TPU v7x, 32 devices: a whole 2x2x4 slice. The times are simulated.
32 devices in a mesh: grp: 2 (over x), gx: 8 (over z, y), gy: 2 (over core).
Axes of the slice: x: 2, y: 2, z: 4, core: 2. Of those that a mesh axis runs over, the one named last changes fastest.
Arguments:
- loaded_fields: bfloat16 [2, 32, 16, 128], P(None, ('grp', 'gx'), 'gy'), parts along dimension 1, may hold values from -6 to 6
- brick_home: int32 [16], P('grp'), parts along dimension 0, may hold values from 0 to 7, each once
- liquid_mask: int32 [32, 16, 128], P(('grp', 'gx'), 'gy'), parts along dimension 0, may hold values 0 or 1
- density_class: int32 [32, 16, 128], P(('grp', 'gx'), 'gy'), parts along dimension 0, may hold values from 0 to 3
- inverse_density: float32 [4], replicated, may hold values from 0.25 to 4
- conv_a: bfloat16 [27, 64, 3], replicated, may hold values from -0.625 to 0.625
- bias_a: float32 [64], replicated, may hold values from -3 to 3
- conv_b: bfloat16 [27, 64, 64], replicated, may hold values from -0.15625 to 0.15625
- bias_b: float32 [64], replicated, may hold values from -3 to 3
- conv_c: bfloat16 [27, 64, 64], replicated, may hold values from -0.15625 to 0.15625
- bias_c: float32 [64], replicated, may hold values from -3 to 3
- head_weight: bfloat16 [64], replicated, may hold values from -0.75 to 0.75
- head_bias: float32 [1], replicated, may hold values from -3 to 3
Outputs:
- pressure: float32 [32, 16, 128], P(('grp', 'gx'), 'gy'), parts along dimension 0
- loss: float32 [2], P('grp'), parts along dimension 0
- grad_conv_a: float32 [54, 64, 3], P('grp'), parts along dimension 0
- grad_bias_a: float32 [128], P('grp'), parts along dimension 0
- grad_conv_b: float32 [54, 64, 64], P('grp'), parts along dimension 0
- grad_bias_b: float32 [128], P('grp'), parts along dimension 0
- grad_conv_c: float32 [54, 64, 64], P('grp'), parts along dimension 0
- grad_bias_c: float32 [128], P('grp'), parts along dimension 0
- grad_head_weight: float32 [128], P('grp'), parts along dimension 0
There are 2 independent parts, one for each index of `grp`. A program takes and returns all parts, laid end to end along the dimension named above; an argument that names none is the same for every part. Nothing has to cross between parts.
Inputs may be any that keep to these rules, and one draw needn't show every extreme that they name: `brick_home`: a permutation of 0 to 7.
All inputs are finite; a program needn't handle non-finite values. No bound on the sum of `liquid_mask` on one device may be relied on, other than what follows from the above.
Results may differ from a plain program's by a relative error of at most 0.0041.
The roundings to bfloat16 on the way count: a program that leaves them out, or rounds other values in their place, can miss the bound.
Values may be sent and summed in bfloat16 or wider, within the bound.
No kernel may reach another device: no remote copies, remote signals or barrier semaphores. Data moves between devices by JAX's collectives and lax.ppermute only.
A program may use at most 64 MiB of HBM per device.

v0:
```python
import functools

import jax
import jax.numpy as jnp
from jax import lax
from jax.experimental import pallas as pl
from jax.experimental.pallas import tpu as pltpu
from jax.sharding import PartitionSpec as P

F32 = jnp.float32
BF16 = jnp.bfloat16
AXES = ("gx", "gy")
HID = 64
NZ = 128
NY = 16
PLANES = 16
MID = 7
WROWS = 864
ROWS = 896


def shift_right(v):
    lane = lax.broadcasted_iota(jnp.int32, v.shape, v.ndim - 1)
    return jnp.where(lane == 0, 0.0, pltpu.roll(v, 1, v.ndim - 1))


def shift_left(v):
    lane = lax.broadcasted_iota(jnp.int32, v.shape, v.ndim - 1)
    return jnp.where(lane == NZ - 1, 0.0, pltpu.roll(v, NZ - 1, v.ndim - 1))


def dot_nn(a, b):
    return jnp.dot(a, b, preferred_element_type=F32)


def dot_nt(a, b):
    return lax.dot_general(a, b, (((1,), (1,)), ((), ())), preferred_element_type=F32)


def step_kernel(
    pos_ref,
    home_ref,
    invd_ref,
    hb_ref,
    gath_ref,
    wa_ref,
    wb_ref,
    wc_ref,
    wbt_ref,
    wct_ref,
    ba_ref,
    bb_ref,
    bc_ref,
    hw_ref,
    p_out,
    keep_ref,
    send_ref,
    inv_ref,
    x0s,
    liq,
    scl,
    f1,
    h1,
    h2,
    h3o,
    s1,
    s2,
    s3,
    pf,
    rs,
    gs,
    g3,
    g2,
    g1,
    gcat,
    hcat,
    acc,
    *,
    n_slots,
    cells,
):
    gx = pos_ref[0]
    gy = pos_ref[1]
    for s in range(n_slots):
        inv_ref[home_ref[s]] = s

    def zero_rims(ref):
        z = jnp.zeros(ref.shape[2:], ref.dtype)

        def body(i, c):
            ref[i, 0] = z
            ref[i, NY + 1] = z
            return c

        lax.fori_loop(0, ref.shape[0], body, 0)

    for ref in (x0s, h1, h2, g3, g2):
        zero_rims(ref)
    for ref in (liq, scl, pf, rs, f1):
        ref[...] = jnp.zeros(ref.shape, F32)

    def load_plane(X, c):
        xg = 2 * gx - MID + X
        ok = jnp.where((xg >= 0) & (xg < 2 * n_slots), 1.0, 0.0).astype(F32)
        xc = jnp.clip(xg, 0, 2 * n_slots - 1)
        home = xc // 2
        half = xc - 2 * home
        slot = inv_ref[home]
        for y in range(NY):
            fb = gath_ref[2 * slot + y // 8, half, y % 8].astype(F32) * ok
            mb = gath_ref[2 * home + y // 8, half, y % 8].astype(F32)
            lq = mb[2:3] * ok
            cl = mb[3:4]
            sc = jnp.zeros((1, NZ), F32)
            for k in range(4):
                sc = jnp.where(cl == k, invd_ref[k], sc)
            row4 = lax.broadcasted_iota(jnp.int32, (4, NZ), 0)
            base = jnp.where(row4 < 2, fb, jnp.where(row4 == 2, mb * ok, 0.0))
            k12 = jnp.concatenate(
                [shift_right(base), base, shift_left(base), jnp.zeros((4, NZ), F32)], axis=0
            )
            x0s[X, y + 1] = k12.astype(BF16)
            liq[X, y + 1 : y + 2, :] = lq
            scl[X, y + 1 : y + 2, :] = sc * lq
            f1[X, y + 1 : y + 2, :] = fb[1:2]
        return c

    lax.fori_loop(0, PLANES, load_plane, 0)

    def taps(src, X, y):
        out = []
        for a in range(3):
            for b in range(3):
                out.append(
                    jnp.concatenate([src[X + a - 1, y + b - 1], src[X + a - 1, y + b]], axis=1)
                )
        return jnp.concatenate(out, axis=0)

    def lane_taps(Y):
        res = []
        for k in range(2):
            part = Y[:, k * NZ : (k + 1) * NZ]
            res.append(
                part[HID : 2 * HID]
                + shift_right(part[:HID])
                + shift_left(part[2 * HID :])
            )
        return res

    def sweep(x_lo, x_n, ry, body):
        y_lo = gy * (8 - ry) + 1

        def plane(i, c):
            def pair(j, c2):
                body(x_lo + i, y_lo + 2 * j)
                return c2

            return lax.fori_loop(0, (8 + ry) // 2, pair, c)

        lax.fori_loop(0, x_n, plane, 0)

    def activate(z):
        sig = 0.5 * jnp.tanh(0.5 * z) + 0.5
        return z * sig, sig

    def slope_of(z, sig):
        return sig * (1.0 + z * (1.0 - sig))

    def layer1(X, y):
        Y = dot_nn(wa_ref[...], taps(x0s, X, y))
        for k in range(2):
            z = Y[:, k * NZ : (k + 1) * NZ] + ba_ref[...]
            m = liq[X, pl.ds(y + k, 1), :]
            act, sig = activate(z)
            h1[X, y + k] = (act * m).astype(BF16)

            @pl.when((X >= MID) & (X < MID + 2))
            def _():
                s1[X - MID, y + k] = slope_of(z, sig) * m

    sweep(MID - 6, 14, 6, layer1)

    def layer2(X, y):
        zs = lane_taps(dot_nn(wb_ref[...], taps(h1, X, y)))
        for k in range(2):
            z = zs[k] + bb_ref[...]
            m = liq[X, pl.ds(y + k, 1), :]
            act, sig = activate(z)
            h2[X, y + k] = (act * m).astype(BF16)

            @pl.when((X >= MID - 1) & (X < MID + 3))
            def _():
                s2[X - MID + 1, y + k] = slope_of(z, sig) * m

    sweep(MID - 5, 12, 6, layer2)

    def layer3(X, y):
        zs = lane_taps(dot_nn(wc_ref[...], taps(h2, X, y)))
        for k in range(2):
            z = zs[k] + bc_ref[...]
            m = liq[X, pl.ds(y + k, 1), :]
            act, sig = activate(z)
            h3 = (act * m).astype(BF16)
            score = jnp.sum(hw_ref[...] * h3.astype(F32), axis=0, keepdims=True)
            pf[X, pl.ds(y + k, 1), :] = m * (score + hb_ref[0])

            @pl.when((X >= MID - 2) & (X < MID + 4))
            def _():
                s3[X - MID + 2, y + k] = slope_of(z, sig) * m

            @pl.when((X >= MID) & (X < MID + 2))
            def _():
                h3o[X - MID, y + k] = h3

    sweep(MID - 4, 10, 4, layer3)

    def operator(val, X):
        v = val[X, 1 : NY + 1, :]
        s = scl[X, 1 : NY + 1, :]
        q = liq[X, 1 : NY + 1, :]

        def term(nv, ns, nq):
            return 0.5 * (s * nq + ns * q) * (nv - v)

        total = term(val[X + 1, 1 : NY + 1, :], scl[X + 1, 1 : NY + 1, :], liq[X + 1, 1 : NY + 1, :])
        total += term(val[X - 1, 1 : NY + 1, :], scl[X - 1, 1 : NY + 1, :], liq[X - 1, 1 : NY + 1, :])
        total += term(val[X, 2 : NY + 2, :], scl[X, 2 : NY + 2, :], liq[X, 2 : NY + 2, :])
        total += term(val[X, 0:NY, :], scl[X, 0:NY, :], liq[X, 0:NY, :])
        total += term(shift_left(v), shift_left(s), shift_left(q))
        total += term(shift_right(v), shift_right(s), shift_right(q))
        return total

    for X in range(MID - 3, MID + 5):
        rs[X, 1 : NY + 1, :] = (
            operator(pf, X) - liq[X, 1 : NY + 1, :] * f1[X, 1 : NY + 1, :]
        )
    own_y = pl.ds(pl.multiple_of(gy * 8, 8) + 1, 8)
    loss = jnp.zeros((8, NZ), F32)
    for k in range(2):
        p_out[k] = pf[MID + k, own_y, :]
        r = rs[MID + k, own_y, :]
        loss += r * r
    loss = jnp.sum(jnp.sum(loss, axis=0, keepdims=True), axis=1, keepdims=True) / cells
    for X in range(PLANES):
        rs[X] = rs[X] * (2.0 / cells)
    for X in range(MID - 2, MID + 4):
        gs[X - MID + 2, 1 : NY + 1, :] = liq[X, 1 : NY + 1, :] * operator(rs, X)

    def back3(X, y):
        for k in range(2):
            g = gs[X - MID + 2, pl.ds(y + k, 1), :]
            g3[X - MID + 2, y + k] = (g * hw_ref[...] * s3[X - MID + 2, y + k]).astype(BF16)

    sweep(MID - 2, 6, 2, back3)

    acc[...] = jnp.zeros(acc.shape, F32)
    y_own = gy * 8 + 1

    def head_grad(i, hacc):
        X = i // 8
        y = y_own + i - 8 * X
        return hacc + gs[X + 2, pl.ds(y, 1), :] * h3o[X, y].astype(F32)

    head = lax.fori_loop(0, 16, head_grad, jnp.zeros((HID, NZ), F32))

    def weight_grad(g_ref, g_off, h_ref, which):
        for i in range(16):
            X, dy = i // 8, i % 8
            y = y_own + dy
            g = g_ref[g_off + X, y].astype(F32)
            cols = slice(i * NZ, (i + 1) * NZ)
            gcat[0:HID, cols] = shift_left(g).astype(BF16)
            gcat[HID : 2 * HID, cols] = g.astype(BF16)
            gcat[2 * HID : 3 * HID, cols] = shift_right(g).astype(BF16)
            for a in range(3):
                for b in range(3):
                    k = 3 * a + b
                    hcat[k * HID : (k + 1) * HID, cols] = h_ref[MID + X + a - 1, y + b - 1]
        W = dot_nt(gcat[...], hcat[...])
        for a in range(3):
            for b in range(3):
                for e in range(3):
                    t = 9 * a + 3 * b + e
                    k = 3 * a + b
                    blk = W[e * HID : (e + 1) * HID, k * HID : (k + 1) * HID]
                    acc[which, t * 32 : (t + 1) * 32, 0:HID] = blk[:32]
                    acc[which, t * 32 : (t + 1) * 32, HID:NZ] = blk[32:]

    def lane_sum(g_ref, g_off):
        def body(i, c):
            X = i // 8
            return c + g_ref[g_off + X, y_own + i - 8 * X].astype(F32)

        return lax.fori_loop(0, 16, body, jnp.zeros((HID, NZ), F32))

    weight_grad(g3, 2, h2, 1)
    bias_c = lane_sum(g3, 2)

    def back2(X, y):
        bs = lane_taps(dot_nn(wct_ref[...], taps(g3, X - MID + 2, y)))
        for k in range(2):
            g2[X - MID + 1, y + k] = (bs[k] * s2[X - MID + 1, y + k]).astype(BF16)

    sweep(MID - 1, 4, 2, back2)
    weight_grad(g2, 1, h1, 0)
    bias_b = lane_sum(g2, 1)

    def back1(X, y):
        bs = lane_taps(dot_nn(wbt_ref[...], taps(g2, X - MID + 1, y)))
        for k in range(2):
            g1[X - MID, y + k] = (bs[k] * s1[X - MID, y + k]).astype(BF16)

    sweep(MID, 2, 0, back1)
    bias_a = lane_sum(g1, 0)

    for i in range(16):
        X, dy = i // 8, i % 8
        y = y_own + dy
        cols = slice(i * NZ, (i + 1) * NZ)
        gcat[0:HID, cols] = g1[X, y]
        for a in range(3):
            for b in range(3):
                k = 3 * a + b
                hcat[k * 16 : (k + 1) * 16, cols] = x0s[MID + X + a - 1, y + b - 1]
    A = dot_nt(hcat[0:144, :], gcat[0:HID, :])
    for k in range(8):
        blk = A[16 * k : 16 * k + 12]
        which, spot = k // 4, k % 4
        r0 = WROWS + 12 * (spot % 2)
        c0 = HID * (spot // 2)
        acc[which, r0 : r0 + 12, c0 : c0 + HID] = blk
    acc[1, WROWS + 24 : WROWS + 32, 0:HID] = A[128:136]
    acc[1, WROWS + 24 : WROWS + 28, HID:NZ] = A[136:140]
    sums = [
        jnp.sum(v, axis=1, keepdims=True).reshape(1, HID) for v in (bias_a, bias_b, bias_c, head)
    ]
    for j in range(2):
        pair = jnp.concatenate([sums[2 * j], sums[2 * j + 1]], axis=1)
        acc[0, WROWS + 24 + j : WROWS + 25 + j, :] = pair
    acc[0, WROWS + 26 : WROWS + 27, :] = jnp.broadcast_to(loss, (1, NZ))
    keep_ref[...] = acc[gy]
    send_ref[...] = acc[1 - gy]


def forward_lhs(w):
    w = w.reshape(3, 3, 3, HID, HID)
    return w.transpose(2, 3, 0, 1, 4).reshape(3 * HID, 9 * HID)


def backward_lhs(w):
    w = w.reshape(3, 3, 3, HID, HID)[::-1, ::-1, ::-1]
    return w.transpose(2, 4, 0, 1, 3).reshape(3 * HID, 9 * HID)


def first_lhs(w):
    w = w.reshape(9, 3, HID, 3)
    w = jnp.pad(w, ((0, 0), (0, 1), (0, 0), (0, 1)))
    w = w.transpose(2, 0, 1, 3).reshape(HID, 9, 16)
    return w.reshape(HID, 144)


def partner(value, bit, count):
    return lax.ppermute(value, AXES, [(i, i ^ bit) for i in range(count)])


def gather_all(block, me, count):
    value = block[None]
    bit = 1
    while bit < count:
        other = partner(value, bit, count)
        upper = (me & bit) != 0
        value = jnp.where(
            upper, jnp.concatenate([other, value]), jnp.concatenate([value, other])
        )
        bit *= 2
    return value


def on_device(
    loaded_fields,
    brick_home,
    liquid_mask,
    density_class,
    inverse_density,
    conv_a,
    bias_a,
    conv_b,
    bias_b,
    conv_c,
    bias_c,
    head_weight,
    head_bias,
):
    n_slots = lax.axis_size("gx")
    count = n_slots * lax.axis_size("gy")
    gx = lax.axis_index("gx")
    gy = lax.axis_index("gy")
    me = gx * 2 + gy
    block = jnp.stack(
        [
            loaded_fields[0],
            loaded_fields[1],
            liquid_mask.astype(BF16),
            density_class.astype(BF16),
        ],
        axis=2,
    )
    gath = gather_all(block, me, count)
    cells = 2 * n_slots * NY * NZ

    def wide(v):
        return jnp.broadcast_to(v.astype(F32)[:, None], (HID, NZ))

    smem = pl.BlockSpec(memory_space=pltpu.SMEM)
    vmem = pl.BlockSpec(memory_space=pltpu.VMEM)
    yy = NY + 2
    pressure, keep, send = pl.pallas_call(
        functools.partial(step_kernel, n_slots=n_slots, cells=cells),
        out_shape=(
            jax.ShapeDtypeStruct((2, 8, NZ), F32),
            jax.ShapeDtypeStruct((ROWS, NZ), F32),
            jax.ShapeDtypeStruct((ROWS, NZ), F32),
        ),
        in_specs=[smem] * 4 + [vmem] * 10,
        out_specs=(vmem, vmem, vmem),
        scratch_shapes=[
            pltpu.SMEM((n_slots,), jnp.int32),
            pltpu.VMEM((PLANES, yy, 16, NZ), BF16),
            pltpu.VMEM((PLANES, yy, NZ), F32),
            pltpu.VMEM((PLANES, yy, NZ), F32),
            pltpu.VMEM((PLANES, yy, NZ), F32),
            pltpu.VMEM((PLANES, yy, HID, NZ), BF16),
            pltpu.VMEM((PLANES, yy, HID, NZ), BF16),
            pltpu.VMEM((2, yy, HID, NZ), BF16),
            pltpu.VMEM((2, yy, HID, NZ), F32),
            pltpu.VMEM((4, yy, HID, NZ), F32),
            pltpu.VMEM((6, yy, HID, NZ), F32),
            pltpu.VMEM((PLANES, yy, NZ), F32),
            pltpu.VMEM((PLANES, yy, NZ), F32),
            pltpu.VMEM((6, yy, NZ), F32),
            pltpu.VMEM((6, yy, HID, NZ), BF16),
            pltpu.VMEM((4, yy, HID, NZ), BF16),
            pltpu.VMEM((2, yy, HID, NZ), BF16),
            pltpu.VMEM((3 * HID, 16 * NZ), BF16),
            pltpu.VMEM((9 * HID, 16 * NZ), BF16),
            pltpu.VMEM((2, ROWS, NZ), F32),
        ],
        compiler_params=pltpu.CompilerParams(vmem_limit_bytes=56 * 1024 * 1024),
        name="step",
    )(
        jnp.stack([gx, gy]).astype(jnp.int32),
        brick_home,
        inverse_density,
        head_bias,
        gath,
        first_lhs(conv_a),
        forward_lhs(conv_b),
        forward_lhs(conv_c),
        backward_lhs(conv_b),
        backward_lhs(conv_c),
        wide(bias_a),
        wide(bias_b),
        wide(bias_c),
        wide(head_weight),
    )

    def pack(v):
        return v

    del pack
    total = keep + partner(send, 1, count)
    bits = []
    bit = 2
    while bit < count:
        bits.append(bit)
        bit *= 2
    for bit in bits:
        half = total.shape[0] // 2
        upper = (me & bit) != 0
        low, high = total[:half], total[half:]
        got = partner(jnp.where(upper, low, high), bit, count)
        total = jnp.where(upper, high, low) + got
    for bit in bits[::-1]:
        other = partner(total, bit, count)
        upper = (me & bit) != 0
        total = jnp.where(
            upper, jnp.concatenate([other, total]), jnp.concatenate([total, other])
        )
    other = partner(total, 1, count)
    first = jnp.where(gy == 0, total, other)
    second = jnp.where(gy == 0, other, total)

    def weights(v):
        v = v[:WROWS].reshape(27, 32, 2, HID)
        return v.transpose(0, 2, 1, 3).reshape(27, HID, HID)

    def blocks(v):
        v = v[WROWS : WROWS + 24].reshape(2, 12, 2, HID)
        return v.transpose(2, 0, 1, 3).reshape(4, 12, HID)

    last = jnp.concatenate(
        [second[WROWS + 24 : WROWS + 32, :HID], second[WROWS + 24 : WROWS + 28, HID:]], axis=0
    )
    parts = jnp.concatenate([blocks(first), blocks(second), last[None]], axis=0)
    grad_a = parts.reshape(27, 4, HID)[:, :3].transpose(0, 2, 1)
    tail = first[WROWS + 24 : WROWS + 27]
    return (
        pressure,
        tail[2, :1],
        grad_a,
        tail[0, :HID],
        weights(first),
        tail[0, HID:],
        weights(second),
        tail[1, :HID],
        tail[1, HID:],
    )


def solution(mesh):
    grid = P(("grp", "gx"), "gy", None)
    part = P("grp")
    stack = P("grp", None, None)
    return jax.shard_map(
        on_device,
        mesh=mesh,
        in_specs=(P(None, ("grp", "gx"), "gy", None), part, grid, grid) + (P(),) * 9,
        out_specs=(grid, part, stack, part, stack, part, stack, part, part),
        check_vma=False,
    )
```

profile of v0, /device:TPU:0, one launch (start us, length us, event | category | flops | bytes accessed | tf_op | source)
XLA Modules:
  0.0 167.1 jit_solution(760654836918513045)
XLA Ops:
  0.7 0.8 convert_bitcast_fusion.1
  3.4 0.8 collective-permute-done
  4.3 2.9 %collective-permute-start.1 = (bf16[2,2,8,4,128]{4,3,2,1,0:T(4,128)(2,1)S(1)}, bf16[2,2,8,4,128]{4,3,2,1,0:T(4,128)(2,1)S(1)}, u32[]{:S(2)}, u32[]{:S(2)}) collective-permute-start(bf16[2,2,8,4,128]{4,3,2,1,0:T(4,128)(2,1)S(1)} %maximum_select_fusion.6), channel_id=1, source_target_pairs={{0,2},{1,3},{2,0},{3,1},{4,6},{5,7},{6,4},{7,5},{8,10},{9,11},{10,... | collective-permute-start | bytes 98312 | tf_op jit(solution)/shard_map/ppermute | solution.py:363
  7.2 1.9 %collective-permute-done.1 = bf16[2,2,8,4,128]{4,3,2,1,0:T(4,128)(2,1)S(1)} collective-permute-done((bf16[2,2,8,4,128]{4,3,2,1,0:T(4,128)(2,1)S(1)}, bf16[2,2,8,4,128]{4,3,2,1,0:T(4,128)(2,1)S(1)}, u32[]{:S(2)}, u32[]{:S(2)}) %collective-permute-start.1) | collective-permute-done | bytes 32800 | tf_op jit(solution)/shard_map/ppermute | solution.py:363
  9.2 2.1 %collective-permute-start.2 = (bf16[4,2,8,4,128]{4,3,2,1,0:T(4,128)(2,1)S(1)}, bf16[4,2,8,4,128]{4,3,2,1,0:T(4,128)(2,1)S(1)}, u32[]{:S(2)}, u32[]{:S(2)}) collective-permute-start(bf16[4,2,8,4,128]{4,3,2,1,0:T(4,128)(2,1)S(1)} %maximum_select_fusion.5), channel_id=1, source_target_pairs={{0,4},{1,5},{2,6},{3,7},{4,0},{5,1},{6,2},{7,3},{8,12},{9,13},{10,... | collective-permute-start | bytes 196616 | tf_op jit(solution)/shard_map/ppermute | solution.py:363
  11.3 2.2 %collective-permute-done.2 = bf16[4,2,8,4,128]{4,3,2,1,0:T(4,128)(2,1)S(1)} collective-permute-done((bf16[4,2,8,4,128]{4,3,2,1,0:T(4,128)(2,1)S(1)}, bf16[4,2,8,4,128]{4,3,2,1,0:T(4,128)(2,1)S(1)}, u32[]{:S(2)}, u32[]{:S(2)}) %collective-permute-start.2) | collective-permute-done | bytes 65568 | tf_op jit(solution)/shard_map/ppermute | solution.py:363
  13.7 3.1 %collective-permute-start.3 = (bf16[8,2,8,4,128]{4,3,2,1,0:T(4,128)(2,1)S(1)}, bf16[8,2,8,4,128]{4,3,2,1,0:T(4,128)(2,1)S(1)}, u32[]{:S(2)}, u32[]{:S(2)}) collective-permute-start(bf16[8,2,8,4,128]{4,3,2,1,0:T(4,128)(2,1)S(1)} %maximum_select_fusion.3), channel_id=1, source_target_pairs={{0,8},{1,9},{2,10},{3,11},{4,12},{5,13},{6,14},{7,15},{8,0},{9,1},... | collective-permute-start | bytes 393224 | tf_op jit(solution)/shard_map/ppermute | solution.py:363
  16.8 0.8 copy.36
  18.7 0.8 copy.37
  21.3 2.3 %rev.6 = bf16[3,3,3,64,64]{3,1,0,4,2:T(4,128)(2,1)S(1)} reverse(bf16[3,3,3,64,64]{3,1,0,4,2:T(4,128)(2,1)S(1)} %copy.36), dimensions={0,1,2} | reverse | bytes 442368 | tf_op jit(solution)/shard_map/rev | solution.py:351
  23.6 1.1 reshape.77.wbt_ref
  24.7 1.1 reshape.74.wb_ref
  25.8 2.3 %rev.7 = bf16[3,3,3,64,64]{3,1,0,4,2:T(4,128)(2,1)S(1)} reverse(bf16[3,3,3,64,64]{3,1,0,4,2:T(4,128)(2,1)S(1)} %copy.37), dimensions={0,1,2} | reverse | bytes 442368 | tf_op jit(solution)/shard_map/rev | solution.py:351
  28.2 1.1 reshape.78.wct_ref
  29.3 1.1 reshape.76.wc_ref
  30.9 1.0 maximum_select_fusion.1.gath_ref
  34.7 87.9 %step.1 = (f32[2,8,128]{2,1,0:T(8,128)}, f32[896,128]{1,0:T(8,128)}, f32[896,128]{1,0:T(8,128)}) custom-call(s32[2]{0:T(128)} %pad_add_fusion.pos_ref, s32[8]{0:T(128)} %home_ref.1, f32[4]{0:T(128)} %invd_ref.1, f32[1]{0:T(128)S(6)} %copy.51.hb_ref, bf16[16,2,8,4,128]{4,3,2,1,0:T(4,128)(2,1)} %maximum_select_fusion.1.gath_ref, bf16[64,144]{1,0:T(8,128)(2,1)} %copy.38.wa_ref, ...), custom_call_target="tpu_custom_call" | custom-call | tf_op jit(solution)/shard_map/step/pallas_call | solution.py:417
  122.6 2.0 %collective-permute-done.4 = f32[896,128]{1,0:T(8,128)S(1)} collective-permute-done((f32[896,128]{1,0:T(8,128)}, f32[896,128]{1,0:T(8,128)S(1)}, u32[]{:S(2)}, u32[]{:S(2)}) %collective-permute-start.4) | collective-permute-done | bytes 458784 | tf_op jit(solution)/shard_map/ppermute | solution.py:363
  124.6 1.1 add.18
  125.7 1.6 collective-permute-start.5
  127.3 6.1 %collective-permute-done.5 = f32[448,128]{1,0:T(8,128)S(1)} collective-permute-done((f32[448,128]{1,0:T(8,128)S(1)}, f32[448,128]{1,0:T(8,128)S(1)}, u32[]{:S(2)}, u32[]{:S(2)}) %collective-permute-start.5) | collective-permute-done | bytes 229408 | tf_op jit(solution)/shard_map/ppermute | solution.py:363
  133.5 1.6 collective-permute-start.6
  135.1 3.2 %collective-permute-done.6 = f32[224,128]{1,0:T(8,128)S(1)} collective-permute-done((f32[224,128]{1,0:T(8,128)S(1)}, f32[224,128]{1,0:T(8,128)S(1)}, u32[]{:S(2)}, u32[]{:S(2)}) %collective-permute-start.6) | collective-permute-done | bytes 114720 | tf_op jit(solution)/shard_map/ppermute | solution.py:363
  138.6 5.0 %collective-permute-done.7 = f32[112,128]{1,0:T(8,128)S(1)} collective-permute-done((f32[112,128]{1,0:T(8,128)S(1)}, f32[112,128]{1,0:T(8,128)S(1)}, u32[]{:S(2)}, u32[]{:S(2)}) %collective-permute-start.7) | collective-permute-done | bytes 57376 | tf_op jit(solution)/shard_map/ppermute | solution.py:363
  143.7 5.0 %collective-permute-done.8 = f32[112,128]{1,0:T(8,128)S(1)} collective-permute-done((f32[112,128]{1,0:T(8,128)S(1)}, f32[112,128]{1,0:T(8,128)S(1)}, u32[]{:S(2)}, u32[]{:S(2)}) %collective-permute-start.8) | collective-permute-done | bytes 57376 | tf_op jit(solution)/shard_map/ppermute | solution.py:363
  148.7 2.2 %collective-permute-start.9 = (f32[224,128]{1,0:T(8,128)S(1)}, f32[224,128]{1,0:T(8,128)S(1)}, u32[]{:S(2)}, u32[]{:S(2)}) collective-permute-start(f32[224,128]{1,0:T(8,128)S(1)} %maximum_select_fusion.4), channel_id=1, source_target_pairs={{0,4},{1,5},{2,6},{3,7},{4,0},{5,1},{6,2},{7,3},{8,12},{9,13},{10,... | collective-permute-start | bytes 344072 | tf_op jit(solution)/shard_map/ppermute | solution.py:363
  150.9 2.8 %collective-permute-done.9 = f32[224,128]{1,0:T(8,128)S(1)} collective-permute-done((f32[224,128]{1,0:T(8,128)S(1)}, f32[224,128]{1,0:T(8,128)S(1)}, u32[]{:S(2)}, u32[]{:S(2)}) %collective-permute-start.9) | collective-permute-done | bytes 114720 | tf_op jit(solution)/shard_map/ppermute | solution.py:363
  153.7 1.5 collective-permute-start.10
  155.2 4.6 %collective-permute-done.10 = f32[448,128]{1,0:T(8,128)S(1)} collective-permute-done((f32[448,128]{1,0:T(8,128)S(1)}, f32[448,128]{1,0:T(8,128)S(1)}, u32[]{:S(2)}, u32[]{:S(2)}) %collective-permute-start.10) | collective-permute-done | bytes 229408 | tf_op jit(solution)/shard_map/ppermute | solution.py:363
  159.9 1.8 %collective-permute-done.11 = f32[896,128]{1,0:T(8,128)S(1)} collective-permute-done((f32[896,128]{1,0:T(8,128)S(1)}, f32[896,128]{1,0:T(8,128)S(1)}, u32[]{:S(2)}, u32[]{:S(2)}) %collective-permute-start.11) | collective-permute-done | bytes 458784 | tf_op jit(solution)/shard_map/ppermute | solution.py:363
  164.5 1.0 copy.43
  166.1 1.0 copy.44
  (71 shorter events, 11.6 us)
Async XLA Ops:
  0.6 16.2 %copy-start = (bf16[27,64,64]{2,1,0:T(8,128)(2,1)S(1)}, bf16[27,64,64]{2,1,0:T(8,128)(2,1)}, u32[]{:S(2)}) copy-start(bf16[27,64,64]{2,1,0:T(8,128)(2,1)} %param.20) | copy-start | bytes 663556
  2.9 1.4 collective-permute-start
  4.3 4.8 %collective-permute-start.1 = (bf16[2,2,8,4,128]{4,3,2,1,0:T(4,128)(2,1)S(1)}, bf16[2,2,8,4,128]{4,3,2,1,0:T(4,128)(2,1)S(1)}, u32[]{:S(2)}, u32[]{:S(2)}) collective-permute-start(bf16[2,2,8,4,128]{4,3,2,1,0:T(4,128)(2,1)S(1)} %maximum_select_fusion.6), channel_id=1, source_target_pairs={{0,2},{1,3},{2,0},{3,1},{4,6},{5,7},{6,4},{7,5},{8,10},{9,11},{10,... | collective-permute-start | bytes 98312 | tf_op jit(solution)/shard_map/ppermute | solution.py:363
  9.2 4.4 %collective-permute-start.2 = (bf16[4,2,8,4,128]{4,3,2,1,0:T(4,128)(2,1)S(1)}, bf16[4,2,8,4,128]{4,3,2,1,0:T(4,128)(2,1)S(1)}, u32[]{:S(2)}, u32[]{:S(2)}) collective-permute-start(bf16[4,2,8,4,128]{4,3,2,1,0:T(4,128)(2,1)S(1)} %maximum_select_fusion.5), channel_id=1, source_target_pairs={{0,4},{1,5},{2,6},{3,7},{4,0},{5,1},{6,2},{7,3},{8,12},{9,13},{10,... | collective-permute-start | bytes 196616 | tf_op jit(solution)/shard_map/ppermute | solution.py:363
  13.7 17.2 %collective-permute-start.3 = (bf16[8,2,8,4,128]{4,3,2,1,0:T(4,128)(2,1)S(1)}, bf16[8,2,8,4,128]{4,3,2,1,0:T(4,128)(2,1)S(1)}, u32[]{:S(2)}, u32[]{:S(2)}) collective-permute-start(bf16[8,2,8,4,128]{4,3,2,1,0:T(4,128)(2,1)S(1)} %maximum_select_fusion.3), channel_id=1, source_target_pairs={{0,8},{1,9},{2,10},{3,11},{4,12},{5,13},{6,14},{7,15},{8,0},{9,1},... | collective-permute-start | bytes 393224 | tf_op jit(solution)/shard_map/ppermute | solution.py:363
  17.6 1.0 copy-start.1
  19.5 1.1 copy-start.2
  30.9 1.0 copy-start.3
  31.9 0.7 copy-start.4
  32.6 0.7 copy-start.5
  33.3 0.7 copy-start.6
  122.6 2.0 %collective-permute-start.4 = (f32[896,128]{1,0:T(8,128)}, f32[896,128]{1,0:T(8,128)S(1)}, u32[]{:S(2)}, u32[]{:S(2)}) collective-permute-start(f32[896,128]{1,0:T(8,128)} %get-tuple-element.14), channel_id=1, source_target_pairs={{0,1},{1,0},{2,3},{3,2},{4,5},{5,4},{6,7},{7,6},{8,9},{9,8},{10,11... | collective-permute-start | bytes 1376264 | tf_op jit(solution)/shard_map/ppermute | solution.py:363
  125.7 7.7 %collective-permute-start.5 = (f32[448,128]{1,0:T(8,128)S(1)}, f32[448,128]{1,0:T(8,128)S(1)}, u32[]{:S(2)}, u32[]{:S(2)}) collective-permute-start(f32[448,128]{1,0:T(8,128)S(1)} %slice_select_fusion), channel_id=1, source_target_pairs={{0,2},{1,3},{2,0},{3,1},{4,6},{5,7},{6,4},{7,5},{8,10},{9,11},{10,... | collective-permute-start | bytes 688136 | tf_op jit(solution)/shard_map/ppermute | solution.py:363
  133.5 4.9 %collective-permute-start.6 = (f32[224,128]{1,0:T(8,128)S(1)}, f32[224,128]{1,0:T(8,128)S(1)}, u32[]{:S(2)}, u32[]{:S(2)}) collective-permute-start(f32[224,128]{1,0:T(8,128)S(1)} %slice_select_fusion.1), channel_id=1, source_target_pairs={{0,4},{1,5},{2,6},{3,7},{4,0},{5,1},{6,2},{7,3},{8,12},{9,13},{10,... | collective-permute-start | bytes 344072 | tf_op jit(solution)/shard_map/ppermute | solution.py:363
  138.4 5.1 %collective-permute-start.7 = (f32[112,128]{1,0:T(8,128)S(1)}, f32[112,128]{1,0:T(8,128)S(1)}, u32[]{:S(2)}, u32[]{:S(2)}) collective-permute-start(f32[112,128]{1,0:T(8,128)S(1)} %slice_select_fusion.2), channel_id=1, source_target_pairs={{0,8},{1,9},{2,10},{3,11},{4,12},{5,13},{6,14},{7,15},{8,0},{9,1},... | collective-permute-start | bytes 172040 | tf_op jit(solution)/shard_map/ppermute | solution.py:363
  143.5 5.2 %collective-permute-start.8 = (f32[112,128]{1,0:T(8,128)S(1)}, f32[112,128]{1,0:T(8,128)S(1)}, u32[]{:S(2)}, u32[]{:S(2)}) collective-permute-start(f32[112,128]{1,0:T(8,128)S(1)} %select_add_fusion.2), channel_id=1, source_target_pairs={{0,8},{1,9},{2,10},{3,11},{4,12},{5,13},{6,14},{7,15},{8,0},{9,1},... | collective-permute-start | bytes 172040 | tf_op jit(solution)/shard_map/ppermute | solution.py:363
  148.7 5.0 %collective-permute-start.9 = (f32[224,128]{1,0:T(8,128)S(1)}, f32[224,128]{1,0:T(8,128)S(1)}, u32[]{:S(2)}, u32[]{:S(2)}) collective-permute-start(f32[224,128]{1,0:T(8,128)S(1)} %maximum_select_fusion.4), channel_id=1, source_target_pairs={{0,4},{1,5},{2,6},{3,7},{4,0},{5,1},{6,2},{7,3},{8,12},{9,13},{10,... | collective-permute-start | bytes 344072 | tf_op jit(solution)/shard_map/ppermute | solution.py:363
  153.7 6.1 %collective-permute-start.10 = (f32[448,128]{1,0:T(8,128)S(1)}, f32[448,128]{1,0:T(8,128)S(1)}, u32[]{:S(2)}, u32[]{:S(2)}) collective-permute-start(f32[448,128]{1,0:T(8,128)S(1)} %maximum_select_fusion.2), channel_id=1, source_target_pairs={{0,2},{1,3},{2,0},{3,1},{4,6},{5,7},{6,4},{7,5},{8,10},{9,11},{10,... | collective-permute-start | bytes 688136 | tf_op jit(solution)/shard_map/ppermute | solution.py:363
  159.8 1.9 %collective-permute-start.11 = (f32[896,128]{1,0:T(8,128)S(1)}, f32[896,128]{1,0:T(8,128)S(1)}, u32[]{:S(2)}, u32[]{:S(2)}) collective-permute-start(f32[896,128]{1,0:T(8,128)S(1)} %maximum_select_fusion), channel_id=1, source_target_pairs={{0,1},{1,0},{2,3},{3,2},{4,5},{5,4},{6,7},{7,6},{8,9},{9,8},{10,11... | collective-permute-start | bytes 1376264 | tf_op jit(solution)/shard_map/ppermute | solution.py:363
where the time goes:
time: 167 us
  Pallas kernels  87.9 us (53%)
  waiting for transfers between devices  35.4 us (21%)
  local copies, waits for them, and re-layouts  21.5 us (13%)
  starting transfers between devices  16.1 us (10%)
  other arithmetic  4.67 us (3%)
    pallas_call x1, Pallas kernels, on_device(): pl.pallas_call(functools.partial(step_kernel, n_slots=n_slots, cells=cell...  87.9 us
    ppermute x12, waiting for transfers between devices, partner(): return lax.ppermute(value, AXES, [(i, i ^ bit) for i in range(count)])  35.4 us
    ppermute x12, starting transfers between devices, partner(): return lax.ppermute(value, AXES, [(i, i ^ bit) for i in range(count)])  16.1 us
    rev x2, local copies, waits for them, and re-layouts, backward_lhs(): w = w.reshape(3, 3, 3, HID, HID)[::-1, ::-1, ::-1]  4.67 us
  transfers between devices with their start and end apart: 12, of which 11 were waited for; matrix products, arithmetic and copies ran while one was open for 8% of the time, Pallas kernels for 0%

commit v1 on v0

v1 whole, which is shorter than its diff:
```python
import functools

import jax
import jax.numpy as jnp
from jax import lax
from jax.experimental import pallas as pl
from jax.experimental.pallas import tpu as pltpu
from jax.sharding import PartitionSpec as P

F32 = jnp.float32
BF16 = jnp.bfloat16
AXES = ("gx", "gy")
HID = 64
NZ = 128
NY = 16
YY = NY + 2
PLANES = 12
MID = 5
FRAME = 12
WROWS = 864
ROWS = 896
TAIL = 16
VMEM_LIMIT = 40 * 1024 * 1024


def shift_right(v):
    lane = lax.broadcasted_iota(jnp.int32, v.shape, v.ndim - 1)
    return jnp.where(lane == 0, 0.0, pltpu.roll(v, 1, v.ndim - 1))


def shift_left(v):
    lane = lax.broadcasted_iota(jnp.int32, v.shape, v.ndim - 1)
    return jnp.where(lane == NZ - 1, 0.0, pltpu.roll(v, NZ - 1, v.ndim - 1))


def dot_nn(a, b):
    return jnp.dot(a, b, preferred_element_type=F32)


def dot_nt(a, b):
    return lax.dot_general(a, b, (((1,), (1,)), ((), ())), preferred_element_type=F32)


def taps(src, X, y):
    out = []
    for a in range(3):
        for b in range(3):
            out.append(
                jnp.concatenate([src[X + a - 1, y + b - 1], src[X + a - 1, y + b]], axis=1)
            )
    return jnp.concatenate(out, axis=0)


def lane_taps(Y, k):
    part = Y[:, k * NZ : (k + 1) * NZ]
    return part[HID : 2 * HID] + shift_right(part[:HID]) + shift_left(part[2 * HID :])


def activate(z):
    sig = 0.5 * jnp.tanh(0.5 * z) + 0.5
    return z * sig, sig


def slope_of(z, sig):
    return sig * (1.0 + z * (1.0 - sig))


def lhs_kernel(wa_ref, wb_ref, wc_ref, fa, fb, fc, tb, tc):
    fa[...] = jnp.zeros(fa.shape, BF16)
    for k in range(9):
        for e in range(3):
            c = 16 * k + 4 * e
            fa[:, c : c + 3] = wa_ref[3 * k + e]
    for w, fwd, bwd in ((wb_ref, fb, tb), (wc_ref, fc, tc)):
        for e in range(3):
            rows = slice(e * HID, (e + 1) * HID)
            for k in range(0, 9, 2):
                c = k * HID
                lo = w[3 * k + e].astype(F32)
                blo = w[26 - (3 * k + e)].astype(F32)
                if k < 8:
                    hi = w[3 * k + 3 + e].astype(F32)
                    bhi = w[26 - (3 * k + 3 + e)].astype(F32)
                    fwd[rows, c : c + 2 * HID] = jnp.concatenate([lo, hi], axis=1).astype(BF16)
                    both = jnp.concatenate([blo, bhi], axis=0)
                    bwd[rows, c : c + 2 * HID] = both.T.astype(BF16)
                else:
                    fwd[rows, c : c + HID] = lo.astype(BF16)
                    both = jnp.concatenate([blo, blo], axis=0)
                    bwd[rows, c : c + HID] = both.T[:, :HID].astype(BF16)


def forward_kernel(
    pos_ref,
    home_ref,
    invd_ref,
    hb_ref,
    gath_ref,
    wa_ref,
    wb_ref,
    wc_ref,
    ba_ref,
    bb_ref,
    bc_ref,
    hw_ref,
    p_out,
    gs_out,
    loss_out,
    head_out,
    x0_out,
    h1_out,
    h2_out,
    s1,
    s2,
    s3,
    inv_ref,
    x0s,
    liq,
    scl,
    f1,
    h1,
    h2,
    h3o,
    pf,
    rs,
    *,
    n_slots,
    cells,
):
    gx = pos_ref[0]
    gy = pos_ref[1]
    for s in range(n_slots):
        inv_ref[home_ref[s]] = s

    for ref in (x0s, h1, h2):
        z = jnp.zeros(ref.shape[2:], ref.dtype)
        for X in range(PLANES):
            ref[X, 0] = z
            ref[X, NY + 1] = z
    for ref in (liq, scl, f1, pf, rs):
        for X in range(PLANES):
            ref[X] = jnp.zeros((YY, NZ), F32)

    def load_plane(X, c):
        xg = 2 * gx - MID + X
        ok = jnp.where((xg >= 0) & (xg < 2 * n_slots), 1.0, 0.0).astype(F32)
        xc = jnp.clip(xg, 0, 2 * n_slots - 1)
        home = xc // 2
        half = xc - 2 * home
        slot = inv_ref[home]
        row4 = lax.broadcasted_iota(jnp.int32, (4, NZ), 0)
        for y in range(NY):
            fb = gath_ref[2 * slot + y // 8, half, y % 8].astype(F32) * ok
            mb = gath_ref[2 * home + y // 8, half, y % 8].astype(F32)
            lq = mb[2:3] * ok
            cl = mb[3:4]
            sc = jnp.zeros((1, NZ), F32)
            for k in range(4):
                sc = jnp.where(cl == k, invd_ref[k], sc)
            base = jnp.where(row4 < 2, fb, jnp.where(row4 == 2, mb * ok, 0.0))
            k12 = jnp.concatenate(
                [shift_right(base), base, shift_left(base), jnp.zeros((4, NZ), F32)], axis=0
            )
            x0s[X, y + 1] = k12.astype(BF16)
            liq[X, y + 1 : y + 2, :] = lq
            scl[X, y + 1 : y + 2, :] = sc * lq
            f1[X, y + 1 : y + 2, :] = fb[1:2]
        return c

    lax.fori_loop(0, PLANES, load_plane, 0)

    def planes(count, body):
        def step(i, c):
            body(i)
            return c

        lax.fori_loop(0, count, step, 0)

    y4 = gy * 4 + 1

    def layer1(X, slot):
        for j in range(6):
            y = y4 + 2 * j
            Y = dot_nn(wa_ref[...], taps(x0s, X, y))
            for k in range(2):
                z = Y[:, k * NZ : (k + 1) * NZ] + ba_ref[...]
                m = liq[X, pl.ds(y + k, 1), :]
                act, sig = activate(z)
                h1[X, y + k] = (act * m).astype(BF16)
                if slot is not None:
                    s1[slot, 2 * j + k] = slope_of(z, sig) * m

    planes(8, lambda i: layer1(1 + i + 2 * (i // 4), None))
    planes(2, lambda i: layer1(MID + i, i))

    def layer2(X, slot):
        for j in range(6):
            y = y4 + 2 * j
            Y = dot_nn(wb_ref[...], taps(h1, X, y))
            for k in range(2):
                z = lane_taps(Y, k) + bb_ref[...]
                m = liq[X, pl.ds(y + k, 1), :]
                act, sig = activate(z)
                h2[X, y + k] = (act * m).astype(BF16)
                if slot is not None:
                    s2[slot, 2 * j + k] = slope_of(z, sig) * m

    planes(4, lambda i: layer2(2 + i + 4 * (i // 2), None))
    planes(4, lambda i: layer2(MID - 1 + i, i))

    y2 = gy * 6 + 1

    def layer3(X, slot, own):
        for j in range(5):
            y = y2 + 2 * j
            Y = dot_nn(wc_ref[...], taps(h2, X, y))
            for k in range(2):
                z = lane_taps(Y, k) + bc_ref[...]
                m = liq[X, pl.ds(y + k, 1), :]
                act, sig = activate(z)
                h3 = (act * m).astype(BF16)
                score = jnp.sum(hw_ref[...] * h3.astype(F32), axis=0, keepdims=True)
                pf[X, pl.ds(y + k, 1), :] = m * (score + hb_ref[0])
                s3[slot, 2 * j + k] = slope_of(z, sig) * m
                if own is not None:
                    h3o[own, 2 * j + k] = h3

    planes(4, lambda i: layer3(3 + i + 2 * (i // 2), i + 2 * (i // 2), None))
    planes(2, lambda i: layer3(MID + i, 2 + i, i))

    def operator(val, X):
        v = val[X, 1 : NY + 1, :]
        s = scl[X, 1 : NY + 1, :]
        q = liq[X, 1 : NY + 1, :]

        def term(nv, ns, nq):
            return 0.5 * (s * nq + ns * q) * (nv - v)

        total = term(val[X + 1, 1 : NY + 1, :], scl[X + 1, 1 : NY + 1, :], liq[X + 1, 1 : NY + 1, :])
        total += term(val[X - 1, 1 : NY + 1, :], scl[X - 1, 1 : NY + 1, :], liq[X - 1, 1 : NY + 1, :])
        total += term(val[X, 2 : NY + 2, :], scl[X, 2 : NY + 2, :], liq[X, 2 : NY + 2, :])
        total += term(val[X, 0:NY, :], scl[X, 0:NY, :], liq[X, 0:NY, :])
        total += term(shift_left(v), shift_left(s), shift_left(q))
        total += term(shift_right(v), shift_right(s), shift_right(q))
        return total

    for X in range(MID - 1, MID + 3):
        rs[X, 1 : NY + 1, :] = operator(pf, X) - liq[X, 1 : NY + 1, :] * f1[X, 1 : NY + 1, :]
    own_y = pl.ds(pl.multiple_of(gy * 8, 8) + 1, 8)
    loss = jnp.zeros((8, NZ), F32)
    for k in range(2):
        p_out[k] = pf[MID + k, own_y, :]
        r = rs[MID + k, own_y, :]
        loss += r * r
    loss_out[...] = loss * (1.0 / cells)
    for X in range(MID - 1, MID + 3):
        rs[X] = rs[X] * (2.0 / cells)
    for k in range(2):
        X = MID + k
        pf[k, 1 : NY + 1, :] = liq[X, 1 : NY + 1, :] * operator(rs, X)
    for k in range(2):
        gs_out[k] = pf[k, own_y, :]

    head = jnp.zeros((HID, NZ), F32)
    for i in range(16):
        X, dy = i // 8, i % 8
        head += pf[X, pl.ds(gy * 8 + 1 + dy, 1), :] * h3o[X, gy * 2 + dy].astype(F32)
    head_out[...] = head

    f0 = gy * 6

    def copy_out(i):
        for l in range(FRAME):
            x0_out[i, l] = x0s[MID - 1 + i, f0 + l]
            h1_out[i, l] = h1[MID - 1 + i, f0 + l]
            h2_out[i, l] = h2[MID - 1 + i, f0 + l]

    planes(4, copy_out)


def backward_kernel(
    pos_ref,
    gl_ref,
    gm_ref,
    gr_ref,
    loss_ref,
    head_ref,
    x0_ref,
    h1_ref,
    h2_ref,
    s1,
    s2,
    s3,
    wbt_ref,
    wct_ref,
    hw_ref,
    keep_ref,
    send_ref,
    gs,
    g3,
    g2,
    g1,
    gcat,
    hcat,
    acc,
):
    gy = pos_ref[1]
    for k in range(2):
        gs[k] = gl_ref[k]
        gs[2 + k] = gm_ref[k]
        gs[4 + k] = gr_ref[k]
    for ref in (g3, g2):
        z = jnp.zeros((HID, NZ), BF16)
        for X in range(ref.shape[0]):
            ref[X, 0] = z
            ref[X, FRAME - 1] = z

    def planes(count, body):
        def step(i, c):
            body(i)
            return c

        lax.fori_loop(0, count, step, 0)

    def back3(X):
        for j in range(10):
            g = gs[X, pl.ds(gy * 6 + j, 1), :]
            g3[X, j + 1] = (g * hw_ref[...] * s3[X, j]).astype(BF16)

    planes(6, back3)

    for X in range(2):
        for r in range(WROWS, ROWS, 8):
            acc[X, r : r + 8, :] = jnp.zeros((8, NZ), F32)
    own = gy * 2 + 1

    def weight_grad(g_ref, g_off, h_ref, which):
        bias = jnp.zeros((HID, NZ), F32)
        for i in range(16):
            X, dy = i // 8, i % 8
            y = own + dy
            raw = g_ref[g_off + X, y]
            g = raw.astype(F32)
            bias += g
            cols = slice(i * NZ, (i + 1) * NZ)
            gcat[0:HID, cols] = shift_left(g).astype(BF16)
            gcat[HID : 2 * HID, cols] = raw
            gcat[2 * HID : 3 * HID, cols] = shift_right(g).astype(BF16)
            for a in range(3):
                for b in range(3):
                    k = 3 * a + b
                    hcat[k * HID : (k + 1) * HID, cols] = h_ref[X + a, y + b - 1]
        W = dot_nt(gcat[...], hcat[...])
        for a in range(3):
            for b in range(3):
                for e in range(3):
                    t = 9 * a + 3 * b + e
                    k = 3 * a + b
                    blk = W[e * HID : (e + 1) * HID, k * HID : (k + 1) * HID]
                    acc[which, t * 32 : (t + 1) * 32, 0:HID] = blk[:32]
                    acc[which, t * 32 : (t + 1) * 32, HID:NZ] = blk[32:]
        return bias

    bias_c = weight_grad(g3, 2, h2_ref, 1)

    def back2(X):
        for j in range(5):
            y = 1 + 2 * j
            Y = dot_nn(wct_ref[...], taps(g3, X + 1, y))
            for k in range(2):
                row = gy * 2 + 2 * j + k
                g2[X, y + k] = (lane_taps(Y, k) * s2[X, row]).astype(BF16)

    planes(4, back2)
    bias_b = weight_grad(g2, 1, h1_ref, 0)

    def back1(X):
        for j in range(4):
            y = own + 2 * j
            Y = dot_nn(wbt_ref[...], taps(g2, X + 1, y))
            for k in range(2):
                row = gy * 4 + 2 * j + k
                g1[X, 2 * j + k] = (lane_taps(Y, k) * s1[X, row]).astype(BF16)

    planes(2, back1)
    bias_a = jnp.zeros((HID, NZ), F32)
    for i in range(16):
        X, dy = i // 8, i % 8
        y = own + dy
        cols = slice(i * NZ, (i + 1) * NZ)
        raw = g1[X, dy]
        bias_a += raw.astype(F32)
        gcat[0:HID, cols] = raw
        for a in range(3):
            for b in range(3):
                k = 3 * a + b
                hcat[k * 16 : (k + 1) * 16, cols] = x0_ref[X + a, y + b - 1]
    A = dot_nt(hcat[0:144, :], gcat[0:HID, :])
    for k in range(8):
        blk = A[16 * k : 16 * k + 12]
        which, spot = k // 4, k % 4
        r0 = WROWS + 12 * (spot % 2)
        c0 = HID * (spot // 2)
        acc[which, r0 : r0 + 12, c0 : c0 + HID] = blk
    acc[1, WROWS + 24 : WROWS + 32, 0:HID] = A[128:136]
    acc[1, WROWS + 24 : WROWS + 28, HID:NZ] = A[136:140]
    sums = [
        jnp.sum(v, axis=1, keepdims=True).reshape(1, HID)
        for v in (bias_a, bias_b, bias_c, head_ref[...])
    ]
    total = jnp.sum(jnp.sum(loss_ref[...], axis=0, keepdims=True), axis=1, keepdims=True)
    keep_ref[0:ROWS] = acc[gy]
    send_ref[0:ROWS] = acc[1 - gy]
    for ref in (keep_ref, send_ref):
        ref[ROWS : ROWS + 8, :] = jnp.zeros((8, NZ), F32)
        for j in range(2):
            ref[ROWS + j : ROWS + j + 1, :] = jnp.concatenate(
                [sums[2 * j], sums[2 * j + 1]], axis=1
            )
        ref[ROWS + 2 : ROWS + 3, :] = jnp.broadcast_to(total, (1, NZ))


def partner(value, bit, count):
    return lax.ppermute(value, AXES, [(i, i ^ bit) for i in range(count)])


def gather_all(block, me, count):
    value = block[None]
    bit = 1
    while bit < count:
        other = partner(value, bit, count)
        upper = (me & bit) != 0
        value = jnp.where(
            upper, jnp.concatenate([other, value]), jnp.concatenate([value, other])
        )
        bit *= 2
    return value


def two_parts(v):
    high = rounded(v)
    return high, rounded(v - high)


def rounded(v):
    return lax.reduce_precision(v, 8, 7)


def sum_all(keep, send, me, count):
    total = keep + partner(send, 1, count)
    body, tail = total[:ROWS], total[ROWS:]
    half = ROWS // 2
    upper = (me & 2) != 0
    high, low = two_parts(tail)
    away = lax.dynamic_slice_in_dim(body, jnp.where(upper, 0, half), half)
    sent = jnp.concatenate([rounded(away), high, low]).astype(BF16)
    got = partner(sent, 2, count).astype(F32)
    body = lax.dynamic_slice_in_dim(body, jnp.where(upper, half, 0), half) + got[:half]
    tail = tail + got[half : half + 8] + got[half + 8 :]
    bit = 4
    while bit < count:
        high, low = two_parts(tail)
        body = rounded(body)
        sent = jnp.concatenate([body, high, low]).astype(BF16)
        got = partner(sent, bit, count).astype(F32)
        body = body + got[:half]
        tail = (high + low) + (got[half : half + 8] + got[half + 8 :])
        bit *= 2
    body = body.astype(BF16)
    other = partner(body, 2, count)
    body = jnp.where(upper, jnp.concatenate([other, body]), jnp.concatenate([body, other]))
    other = partner(body, 1, count)
    odd = (me & 1) != 0
    first = jnp.where(odd, other, body)
    second = jnp.where(odd, body, other)
    return first.astype(F32), second.astype(F32), tail


def on_device(
    loaded_fields,
    brick_home,
    liquid_mask,
    density_class,
    inverse_density,
    conv_a,
    bias_a,
    conv_b,
    bias_b,
    conv_c,
    bias_c,
    head_weight,
    head_bias,
):
    n_slots = lax.axis_size("gx")
    count = n_slots * lax.axis_size("gy")
    gx = lax.axis_index("gx")
    gy = lax.axis_index("gy")
    me = gx * 2 + gy
    cells = 2 * n_slots * NY * NZ
    smem = pl.BlockSpec(memory_space=pltpu.SMEM)
    vmem = pl.BlockSpec(memory_space=pltpu.VMEM)
    params = pltpu.CompilerParams(vmem_limit_bytes=VMEM_LIMIT)

    lhs = jax.ShapeDtypeStruct((3 * HID, 9 * HID), BF16)
    wa, wb, wc, wbt, wct = pl.pallas_call(
        lhs_kernel,
        out_shape=(jax.ShapeDtypeStruct((HID, 144), BF16), lhs, lhs, lhs, lhs),
        in_specs=[vmem] * 3,
        out_specs=(vmem,) * 5,
        compiler_params=params,
        name="lhs",
    )(conv_a, conv_b, conv_c)

    block = jnp.stack(
        [
            loaded_fields[0],
            loaded_fields[1],
            liquid_mask.astype(BF16),
            density_class.astype(BF16),
        ],
        axis=2,
    )
    gath = gather_all(block, me, count)

    def wide(v):
        return jnp.broadcast_to(v.astype(F32)[:, None], (HID, NZ))

    pos = jnp.stack([gx, gy]).astype(jnp.int32)
    head_wide = wide(head_weight)

    def shaped(shape, kind):
        return jax.ShapeDtypeStruct(shape, kind)

    (pressure, score, loss, head, x0o, h1o, h2o, s1, s2, s3) = pl.pallas_call(
        functools.partial(forward_kernel, n_slots=n_slots, cells=cells),
        out_shape=(
            shaped((2, 8, NZ), F32),
            shaped((2, 8, NZ), F32),
            shaped((8, NZ), F32),
            shaped((HID, NZ), F32),
            shaped((4, FRAME, 16, NZ), BF16),
            shaped((4, FRAME, HID, NZ), BF16),
            shaped((4, FRAME, HID, NZ), BF16),
            shaped((2, 12, HID, NZ), F32),
            shaped((4, 12, HID, NZ), F32),
            shaped((6, 10, HID, NZ), F32),
        ),
        in_specs=[smem] * 4 + [vmem] * 8,
        out_specs=(vmem,) * 10,
        scratch_shapes=[
            pltpu.SMEM((n_slots,), jnp.int32),
            pltpu.VMEM((PLANES, YY, 16, NZ), BF16),
            pltpu.VMEM((PLANES, YY, NZ), F32),
            pltpu.VMEM((PLANES, YY, NZ), F32),
            pltpu.VMEM((PLANES, YY, NZ), F32),
            pltpu.VMEM((PLANES, YY, HID, NZ), BF16),
            pltpu.VMEM((PLANES, YY, HID, NZ), BF16),
            pltpu.VMEM((2, 10, HID, NZ), BF16),
            pltpu.VMEM((PLANES, YY, NZ), F32),
            pltpu.VMEM((PLANES, YY, NZ), F32),
        ],
        compiler_params=params,
        name="forward",
    )(
        pos,
        brick_home,
        inverse_density,
        head_bias,
        gath,
        wa,
        wb,
        wc,
        wide(bias_a),
        wide(bias_b),
        wide(bias_c),
        head_wide,
    )

    other = partner(score, 1, count)
    middle = jnp.where(
        gy == 0, jnp.concatenate([score, other], 1), jnp.concatenate([other, score], 1)
    )
    up = [(i, i + 1) for i in range(n_slots - 1)]
    left = lax.ppermute(middle, "gx", up)
    right = lax.ppermute(middle, "gx", [(j, i) for i, j in up])

    keep, send = pl.pallas_call(
        backward_kernel,
        out_shape=(shaped((ROWS + 8, NZ), F32), shaped((ROWS + 8, NZ), F32)),
        in_specs=[smem] + [vmem] * 14,
        out_specs=(vmem, vmem),
        scratch_shapes=[
            pltpu.VMEM((6, NY, NZ), F32),
            pltpu.VMEM((6, FRAME, HID, NZ), BF16),
            pltpu.VMEM((4, FRAME, HID, NZ), BF16),
            pltpu.VMEM((2, 8, HID, NZ), BF16),
            pltpu.VMEM((3 * HID, 16 * NZ), BF16),
            pltpu.VMEM((9 * HID, 16 * NZ), BF16),
            pltpu.VMEM((2, ROWS, NZ), F32),
        ],
        compiler_params=params,
        name="backward",
    )(
        pos,
        left,
        middle,
        right,
        loss,
        head,
        x0o,
        h1o,
        h2o,
        s1,
        s2,
        s3,
        wbt,
        wct,
        head_wide,
    )

    first, second, tail = sum_all(keep, send, me, count)

    def weights(v):
        v = v[:WROWS].reshape(27, 32, 2, HID)
        return v.transpose(0, 2, 1, 3).reshape(27, HID, HID)

    def blocks(v):
        v = v[WROWS : WROWS + 24].reshape(2, 12, 2, HID)
        return v.transpose(2, 0, 1, 3).reshape(4, 12, HID)

    last = jnp.concatenate(
        [second[WROWS + 24 : WROWS + 32, :HID], second[WROWS + 24 : WROWS + 28, HID:]], axis=0
    )
    parts = jnp.concatenate([blocks(first), blocks(second), last[None]], axis=0)
    grad_a = parts.reshape(27, 4, HID)[:, :3].transpose(0, 2, 1)
    return (
        pressure,
        tail[2, :1],
        grad_a,
        tail[0, :HID],
        weights(first),
        tail[0, HID:],
        weights(second),
        tail[1, :HID],
        tail[1, HID:],
    )


def solution(mesh):
    grid = P(("grp", "gx"), "gy", None)
    part = P("grp")
    stack = P("grp", None, None)
    return jax.shard_map(
        on_device,
        mesh=mesh,
        in_specs=(P(None, ("grp", "gx"), "gy", None), part, grid, grid) + (P(),) * 9,
        out_specs=(grid, part, stack, part, stack, part, stack, part, part),
        check_vma=False,
    )
```

time: 167 us -> 103 us (0.62)
  Pallas kernels: 87.9 us -> 24.9 us
  waiting for transfers between devices: 35.4 us -> 28.4 us
  starting transfers between devices: 16.1 us -> 21 us
    pallas_call x1 -> x3, Pallas kernels: 87.9 us -> 24.9 us  [the longest x1 16 us: on_device(): pl.pallas_call(functools.partial(forward_kernel, n_slots=n_slots, cells=c...]
    unnamed x15 -> x52, local copies, waits for them, and re-layouts: 1.27 us -> 16.3 us
    ppermute x12 -> x11, waiting for transfers between devices: 35.4 us -> 24.1 us  [partner(): return lax.ppermute(value, AXES, [(i, i ^ bit) for i in range(count)])]
    reshape x9 -> x0, local copies, waits for them, and re-layouts: 6.77 us -> none  [the longest x4 2.38 us: forward_lhs(): w = w.reshape(3, 3, 3, HID, HID)]
    ppermute x0 -> x2, starting transfers between devices: none -> 4.73 us  [the longest x1 3.44 us: on_device(): left = lax.ppermute(middle, 'gx', up)]
    rev x2 -> x0, local copies, waits for them, and re-layouts: 4.67 us -> none  [backward_lhs(): w = w.reshape(3, 3, 3, HID, HID)[::-1, ::-1, ::-1]]
    ppermute x0 -> x2, waiting for transfers between devices: none -> 4.33 us  [the longest x1 4.21 us: on_device(): right = lax.ppermute(middle, 'gx', [(j, i) for i, j in up])]
    broadcast_in_dim x4, local copies, waits for them, and re-layouts: 2.74 us -> 0.28 us  [wide(): return jnp.broadcast_to(v.astype(F32)[:, None], (HID, NZ))]
  transfers between devices with their start and end apart: 12 -> 13, of which waited for: 11 -> 12; matrix products, arithmetic and copies ran while one was open for 8% -> 2% of each run, Pallas kernels for 0% -> 1%
where the time goes in v1:
time: 103 us; the launch traced here: 102 us
  waiting for transfers between devices  28.4 us (28%)
  Pallas kernels  24.9 us (24%)
  local copies, waits for them, and re-layouts  22 us (21%)
  starting transfers between devices  21 us (20%)
  other arithmetic  4.39 us (4%)
  between operations  1.67 us (2%)
    ppermute x11, waiting for transfers between devices, partner(): return lax.ppermute(value, AXES, [(i, i ^ bit) for i in range(count)])  24.1 us
    unnamed x52, local copies, waits for them, and re-layouts  16.3 us
    ppermute x11, starting transfers between devices, partner(): return lax.ppermute(value, AXES, [(i, i ^ bit) for i in range(count)])  16.2 us
    pallas_call x1, Pallas kernels, on_device(): pl.pallas_call(functools.partial(forward_kernel, n_slots=n_slots, cells=c...  16 us
    pallas_call x1, Pallas kernels, on_device(): pl.pallas_call(backward_kernel, out_shape=(shaped((ROWS + 8, NZ), F32), s...  8.21 us
    ppermute x1, waiting for transfers between devices, on_device(): right = lax.ppermute(middle, 'gx', [(j, i) for i, j in up])  4.21 us
    ppermute x1, starting transfers between devices, on_device(): left = lax.ppermute(middle, 'gx', up)  3.44 us
  transfers between devices with their start and end apart: 13, of which 12 were waited for; matrix products, arithmetic and copies ran while one was open for 2% of the time, Pallas kernels for 1%

profile of v1, /device:TPU:0, one launch (start us, length us, event | category | flops | bytes accessed | tf_op | source)
XLA Modules:
  0.0 102.3 jit_solution(7470322157126573821)
XLA Ops:
  4.3 2.9 %collective-permute-start.1 = (bf16[2,2,8,4,128]{4,3,2,1,0:T(4,128)(2,1)S(1)}, bf16[2,2,8,4,128]{4,3,2,1,0:T(4,128)(2,1)S(1)}, u32[]{:S(2)}, u32[]{:S(2)}) collective-permute-start(bf16[2,2,8,4,128]{4,3,2,1,0:T(4,128)(2,1)S(1)} %maximum_select_fusion.4), channel_id=1, source_target_pairs={{0,2},{1,3},{2,0},{3,1},{4,6},{5,7},{6,4},{7,5},{8,10},{9,11},{10,... | collective-permute-start | bytes 98312 | tf_op jit(solution)/shard_map/ppermute | solution.py:424
  7.2 1.9 %collective-permute-done.1 = bf16[2,2,8,4,128]{4,3,2,1,0:T(4,128)(2,1)S(1)} collective-permute-done((bf16[2,2,8,4,128]{4,3,2,1,0:T(4,128)(2,1)S(1)}, bf16[2,2,8,4,128]{4,3,2,1,0:T(4,128)(2,1)S(1)}, u32[]{:S(2)}, u32[]{:S(2)}) %collective-permute-start.1) | collective-permute-done | bytes 32800 | tf_op jit(solution)/shard_map/ppermute | solution.py:424
  9.2 2.1 %collective-permute-start.2 = (bf16[4,2,8,4,128]{4,3,2,1,0:T(4,128)(2,1)S(1)}, bf16[4,2,8,4,128]{4,3,2,1,0:T(4,128)(2,1)S(1)}, u32[]{:S(2)}, u32[]{:S(2)}) collective-permute-start(bf16[4,2,8,4,128]{4,3,2,1,0:T(4,128)(2,1)S(1)} %maximum_select_fusion.3), channel_id=1, source_target_pairs={{0,4},{1,5},{2,6},{3,7},{4,0},{5,1},{6,2},{7,3},{8,12},{9,13},{10,... | collective-permute-start | bytes 196616 | tf_op jit(solution)/shard_map/ppermute | solution.py:424
  11.3 2.2 %collective-permute-done.2 = bf16[4,2,8,4,128]{4,3,2,1,0:T(4,128)(2,1)S(1)} collective-permute-done((bf16[4,2,8,4,128]{4,3,2,1,0:T(4,128)(2,1)S(1)}, bf16[4,2,8,4,128]{4,3,2,1,0:T(4,128)(2,1)S(1)}, u32[]{:S(2)}, u32[]{:S(2)}) %collective-permute-start.2) | collective-permute-done | bytes 65568 | tf_op jit(solution)/shard_map/ppermute | solution.py:424
  13.7 3.1 %collective-permute-start.3 = (bf16[8,2,8,4,128]{4,3,2,1,0:T(4,128)(2,1)S(1)}, bf16[8,2,8,4,128]{4,3,2,1,0:T(4,128)(2,1)S(1)}, u32[]{:S(2)}, u32[]{:S(2)}) collective-permute-start(bf16[8,2,8,4,128]{4,3,2,1,0:T(4,128)(2,1)S(1)} %maximum_select_fusion.2), channel_id=1, source_target_pairs={{0,8},{1,9},{2,10},{3,11},{4,12},{5,13},{6,14},{7,15},{8,0},{9,1},... | collective-permute-start | bytes 393224 | tf_op jit(solution)/shard_map/ppermute | solution.py:424
  17.5 1.0 %copy.29.wa_ref = bf16[27,64,3]{2,1,0:T(8,128)(2,1)S(1)} copy(bf16[27,64,3]{1,0,2:T(8,128)(2,1)} %param.18) | data formatting | bytes 20736 | tf_op args[5]
  18.5 1.0 copy-done.7
  19.5 1.0 copy-done.8
  22.1 16.0 %forward.1 = (f32[2,8,128]{2,1,0:T(8,128)}, f32[2,8,128]{2,1,0:T(8,128)S(1)}, f32[8,128]{1,0:T(8,128)S(1)}, f32[64,128]{1,0:T(8,128)S(1)}, bf16[4,12,16,128]{3,2...) custom-call(s32[2]{0:T(128)S(1)} %pad_add_fusion.pos_ref, ...), custom_call_target="tpu_custom_call" | custom-call | tf_op jit(solution)/shard_map/forward/pallas_call | solution.py:534
  42.1 1.3 %collective-permute-done.4 = f32[2,8,128]{2,1,0:T(8,128)} collective-permute-done((f32[2,8,128]{2,1,0:T(8,128)S(1)}, f32[2,8,128]{2,1,0:T(8,128)}, u32[]{:S(2)}, u32[]{:S(2)}) %collective-permute-start.4) | collective-permute-done | bytes 8224 | tf_op jit(solution)/shard_map/ppermute | solution.py:424
  44.2 3.4 %collective-permute-start.5 = (f32[2,16,128]{2,1,0:T(8,128)S(1)}, f32[2,16,128]{2,1,0:T(8,128)S(1)}, u32[]{:S(2)}, u32[]{:S(2)}) collective-permute-start(f32[2,16,128]{2,1,0:T(8,128)S(1)} %maximum_select_fusion.5.gm_ref), channel_id=1, source_target_pairs={{0,2},{2,4},{4,6},{6,8},{8,10},{10,12},{12,14},{1,3},{3,5},{5,7},{... | collective-permute-start | bytes 49160 | tf_op jit(solution)/shard_map/ppermute | solution.py:584
  47.6 1.3 %collective-permute-start.6 = (f32[2,16,128]{2,1,0:T(8,128)S(1)}, f32[2,16,128]{2,1,0:T(8,128)S(1)}, u32[]{:S(2)}, u32[]{:S(2)}) collective-permute-start(f32[2,16,128]{2,1,0:T(8,128)S(1)} %maximum_select_fusion.5.gm_ref), channel_id=1, source_target_pairs={{2,0},{4,2},{6,4},{8,6},{10,8},{12,10},{14,12},{3,1},{5,3},{7,5},{... | collective-permute-start | bytes 49160 | tf_op jit(solution)/shard_map/ppermute | solution.py:585
  49.1 4.2 %collective-permute-done.6.gr_ref = f32[2,16,128]{2,1,0:T(8,128)S(1)} collective-permute-done((f32[2,16,128]{2,1,0:T(8,128)S(1)}, f32[2,16,128]{2,1,0:T(8,128)S(1)}, u32[]{:S(2)}, u32[]{:S(2)}) %collective-permute-start.6) | collective-permute-done | bytes 16416 | tf_op jit(solution)/shard_map/ppermute | solution.py:585
  53.3 1.1 %copy-done.1 = bf16[4,12,64,128]{3,2,1,0:T(8,128)(2,1)S(1)} copy-done((bf16[4,12,64,128]{3,2,1,0:T(8,128)(2,1)S(1)}, bf16[4,12,64,128]{3,2,1,0:T(8,128)(2,1)}, u32[]{:S(2)}) %copy-start.1) | copy-done | bytes 786456
  54.4 1.1 %copy-done.3 = bf16[4,12,64,128]{3,2,1,0:T(8,128)(2,1)S(1)} copy-done((bf16[4,12,64,128]{3,2,1,0:T(8,128)(2,1)S(1)}, bf16[4,12,64,128]{3,2,1,0:T(8,128)(2,1)}, u32[]{:S(2)}) %copy-start.3) | copy-done | bytes 786456
  55.5 1.1 %copy-done.5 = f32[2,12,64,128]{3,2,1,0:T(8,128)S(1)} copy-done((f32[2,12,64,128]{3,2,1,0:T(8,128)S(1)}, f32[2,12,64,128]{3,2,1,0:T(8,128)}, u32[]{:S(2)}) %copy-start.5) | copy-done | bytes 786456
  57.4 0.9 copy-done.12
  58.4 0.9 copy-done.14
  59.3 0.9 copy-done.16
  61.0 8.2 %backward.1 = (f32[904,128]{1,0:T(8,128)S(1)}, f32[904,128]{1,0:T(8,128)}) custom-call(s32[2]{0:T(128)S(1)} %pad_add_fusion.pos_ref, f32[2,16,128]{2,1,0:T(8,128)S(1)} %collective-permute-done.5.gl_ref, f32[2,16,128]{2,1,0:T(8,128)S(1)} %maximum_select_fusion.5.gm_ref, f32[2,16,128]{2,1,0:T(8,128)S(1)} %collective-permute-done.6.gr_ref, ...), custom_call_target="tpu_custom_call" | custom-call | tf_op jit(solution)/shard_map/backward/pallas_call | solution.py:587
  70.0 2.0 %collective-permute-done.7 = f32[904,128]{1,0:T(8,128)S(1)} collective-permute-done((f32[904,128]{1,0:T(8,128)}, f32[904,128]{1,0:T(8,128)S(1)}, u32[]{:S(2)}, u32[]{:S(2)}) %collective-permute-start.7) | collective-permute-done | bytes 462880 | tf_op jit(solution)/shard_map/ppermute | solution.py:424
  72.0 1.1 %add.42 = f32[904,128]{1,0:T(8,128)S(1)} add(f32[904,128]{1,0:T(8,128)} %copy-done.6, f32[904,128]{1,0:T(8,128)S(1)} %collective-permute-done.7) | non-fusion elementwise | flops 115712 | bytes 1388544 | tf_op jit(solution)/shard_map/add | solution.py:450
  73.2 2.5 %collective-permute-start.8 = (bf16[464,128]{1,0:T(8,128)(2,1)S(1)}, bf16[464,128]{1,0:T(8,128)(2,1)S(1)}, u32[]{:S(2)}, u32[]{:S(2)}) collective-permute-start(bf16[464,128]{1,0:T(8,128)(2,1)S(1)} %pad_maximum_fusion), channel_id=1, source_target_pairs={{0,2},{1,3},{2,0},{3,1},{4,6},{5,7},{6,4},{7,5},{8,10},{9,11},{10,... | collective-permute-start | bytes 356360 | tf_op jit(solution)/shard_map/ppermute | solution.py:424
  75.7 3.5 %collective-permute-done.8 = bf16[464,128]{1,0:T(8,128)(2,1)S(1)} collective-permute-done((bf16[464,128]{1,0:T(8,128)(2,1)S(1)}, bf16[464,128]{1,0:T(8,128)(2,1)S(1)}, u32[]{:S(2)}, u32[]{:S(2)}) %collective-permute-start.8) | collective-permute-done | bytes 118816 | tf_op jit(solution)/shard_map/ppermute | solution.py:424
  79.3 1.0 collective-permute-start.9
  80.3 3.9 %collective-permute-done.9 = bf16[464,128]{1,0:T(8,128)(2,1)S(1)} collective-permute-done((bf16[464,128]{1,0:T(8,128)(2,1)S(1)}, bf16[464,128]{1,0:T(8,128)(2,1)S(1)}, u32[]{:S(2)}, u32[]{:S(2)}) %collective-permute-start.9) | collective-permute-done | bytes 118816 | tf_op jit(solution)/shard_map/ppermute | solution.py:424
  84.3 2.6 %collective-permute-start.10 = (bf16[464,128]{1,0:T(8,128)(2,1)S(1)}, bf16[464,128]{1,0:T(8,128)(2,1)S(1)}, u32[]{:S(2)}, u32[]{:S(2)}) collective-permute-start(bf16[464,128]{1,0:T(8,128)(2,1)S(1)} %pad_maximum_fusion.2), channel_id=1, source_target_pairs={{0,8},{1,9},{2,10},{3,11},{4,12},{5,13},{6,14},{7,15},{8,0},{9,1},... | collective-permute-start | bytes 356360 | tf_op jit(solution)/shard_map/ppermute | solution.py:424
  86.9 4.6 %collective-permute-done.10 = bf16[464,128]{1,0:T(8,128)(2,1)S(1)} collective-permute-done((bf16[464,128]{1,0:T(8,128)(2,1)S(1)}, bf16[464,128]{1,0:T(8,128)(2,1)S(1)}, u32[]{:S(2)}, u32[]{:S(2)}) %collective-permute-start.10) | collective-permute-done | bytes 118816 | tf_op jit(solution)/shard_map/ppermute | solution.py:424
  91.5 1.5 %collective-permute-start.11 = (bf16[448,128]{1,0:T(8,128)(2,1)S(1)}, bf16[448,128]{1,0:T(8,128)(2,1)S(1)}, u32[]{:S(2)}, u32[]{:S(2)}) collective-permute-start(bf16[448,128]{1,0:T(8,128)(2,1)S(1)} %fusion), channel_id=1, source_target_pairs={{0,2},{1,3},{2,0},{3,1},{4,6},{5,7},{6,4},{7,5},{8,10},{9,11},{10,... | collective-permute-start | bytes 344072 | tf_op jit(solution)/shard_map/ppermute | solution.py:424
  93.0 3.4 %collective-permute-done.11 = bf16[448,128]{1,0:T(8,128)(2,1)S(1)} collective-permute-done((bf16[448,128]{1,0:T(8,128)(2,1)S(1)}, bf16[448,128]{1,0:T(8,128)(2,1)S(1)}, u32[]{:S(2)}, u32[]{:S(2)}) %collective-permute-start.11) | collective-permute-done | bytes 114720 | tf_op jit(solution)/shard_map/ppermute | solution.py:424
  99.7 1.0 copy.34
  101.3 1.0 copy.35
  (109 shorter events, 16.6 us)
Async XLA Ops:
  0.6 21.0 %copy-start.21 = (f32[64]{0:T(128)S(1)}, f32[64]{0:T(128)}, u32[]{:S(2)}) copy-start(f32[64]{0:T(128)} %param.19) | copy-start | bytes 772
  0.7 21.1 %copy-start.22 = (f32[64]{0:T(128)S(1)}, f32[64]{0:T(128)}, u32[]{:S(2)}) copy-start(f32[64]{0:T(128)} %param.21) | copy-start | bytes 772
  0.7 21.3 %copy-start.23 = (f32[64]{0:T(128)S(1)}, f32[64]{0:T(128)}, u32[]{:S(2)}) copy-start(f32[64]{0:T(128)} %param.23) | copy-start | bytes 772
  0.7 21.4 %copy-start.24 = (bf16[64]{0:T(256)(128)(2,1)S(1)}, bf16[64]{0:T(256)(128)(2,1)}, u32[]{:S(2)}) copy-start(bf16[64]{0:T(256)(128)(2,1)} %param.24) | copy-start | bytes 388
  2.9 1.4 %collective-permute-start = (bf16[1,2,8,4,128]{4,3,2,1,0:T(4,128)(2,1)S(1)}, bf16[1,2,8,4,128]{4,3,2,1,0:T(4,128)(2,1)S(1)}, u32[]{:S(2)}, u32[]{:S(2)}) collective-permute-start(bf16[1,2,8,4,128]{4,3,2,1,0:T(4,128)(2,1)S(1)} %maximum_bitcast_fusion), channel_id=1, source_target_pairs={{0,1},{1,0},{2,3},{3,2},{4,5},{5,4},{6,7},{7,6},{8,9},{9,8},{10,11... | collective-permute-start | bytes 49160 | tf_op jit(solution)/shard_map/ppermute | solution.py:424
  4.3 4.8 %collective-permute-start.1 = (bf16[2,2,8,4,128]{4,3,2,1,0:T(4,128)(2,1)S(1)}, bf16[2,2,8,4,128]{4,3,2,1,0:T(4,128)(2,1)S(1)}, u32[]{:S(2)}, u32[]{:S(2)}) collective-permute-start(bf16[2,2,8,4,128]{4,3,2,1,0:T(4,128)(2,1)S(1)} %maximum_select_fusion.4), channel_id=1, source_target_pairs={{0,2},{1,3},{2,0},{3,1},{4,6},{5,7},{6,4},{7,5},{8,10},{9,11},{10,... | collective-permute-start | bytes 98312 | tf_op jit(solution)/shard_map/ppermute | solution.py:424
  9.2 4.4 %collective-permute-start.2 = (bf16[4,2,8,4,128]{4,3,2,1,0:T(4,128)(2,1)S(1)}, bf16[4,2,8,4,128]{4,3,2,1,0:T(4,128)(2,1)S(1)}, u32[]{:S(2)}, u32[]{:S(2)}) collective-permute-start(bf16[4,2,8,4,128]{4,3,2,1,0:T(4,128)(2,1)S(1)} %maximum_select_fusion.3), channel_id=1, source_target_pairs={{0,4},{1,5},{2,6},{3,7},{4,0},{5,1},{6,2},{7,3},{8,12},{9,13},{10,... | collective-permute-start | bytes 196616 | tf_op jit(solution)/shard_map/ppermute | solution.py:424
  13.7 7.6 %collective-permute-start.3 = (bf16[8,2,8,4,128]{4,3,2,1,0:T(4,128)(2,1)S(1)}, bf16[8,2,8,4,128]{4,3,2,1,0:T(4,128)(2,1)S(1)}, u32[]{:S(2)}, u32[]{:S(2)}) collective-permute-start(bf16[8,2,8,4,128]{4,3,2,1,0:T(4,128)(2,1)S(1)} %maximum_select_fusion.2), channel_id=1, source_target_pairs={{0,8},{1,9},{2,10},{3,11},{4,12},{5,13},{6,14},{7,15},{8,0},{9,1},... | collective-permute-start | bytes 393224 | tf_op jit(solution)/shard_map/ppermute | solution.py:424
  18.5 1.0 copy-start.7
  19.5 1.0 copy-start.8
  20.6 1.5 %copy-start.19 = (s32[8]{0:T(128)S(1)}, s32[8]{0:T(128)}, u32[]{:S(2)}) copy-start(s32[8]{0:T(128)} %home_ref.1) | copy-start | bytes 100
  20.6 1.5 %copy-start.20 = (f32[4]{0:T(128)S(1)}, f32[4]{0:T(128)}, u32[]{:S(2)}) copy-start(f32[4]{0:T(128)} %invd_ref.1) | copy-start | bytes 52
  21.2 0.8 copy-start.13
  22.1 16.0 %copy-start.9 = (f32[64,128]{1,0:T(8,128)}, f32[64,128]{1,0:T(8,128)S(1)}, u32[]{:S(2)}) copy-start(f32[64,128]{1,0:T(8,128)S(1)} %broadcast_in_dim.16.hw_ref) | copy-start | bytes 98308
  38.1 0.9 copy-start
  39.0 0.9 copy-start.2
  39.9 0.9 copy-start.4
  42.1 1.3 %collective-permute-start.4 = (f32[2,8,128]{2,1,0:T(8,128)S(1)}, f32[2,8,128]{2,1,0:T(8,128)}, u32[]{:S(2)}, u32[]{:S(2)}) collective-permute-start(f32[2,8,128]{2,1,0:T(8,128)S(1)} %get-tuple-element.30), channel_id=1, source_target_pairs={{0,1},{1,0},{2,3},{3,2},{4,5},{5,4},{6,7},{7,6},{8,9},{9,8},{10,11... | collective-permute-start | bytes 24584 | tf_op jit(solution)/shard_map/ppermute | solution.py:424
  44.2 4.9 %collective-permute-start.5 = (f32[2,16,128]{2,1,0:T(8,128)S(1)}, f32[2,16,128]{2,1,0:T(8,128)S(1)}, u32[]{:S(2)}, u32[]{:S(2)}) collective-permute-start(f32[2,16,128]{2,1,0:T(8,128)S(1)} %maximum_select_fusion.5.gm_ref), channel_id=1, source_target_pairs={{0,2},{2,4},{4,6},{6,8},{8,10},{10,12},{12,14},{1,3},{3,5},{5,7},{... | collective-permute-start | bytes 49160 | tf_op jit(solution)/shard_map/ppermute | solution.py:584
  47.6 5.6 %collective-permute-start.6 = (f32[2,16,128]{2,1,0:T(8,128)S(1)}, f32[2,16,128]{2,1,0:T(8,128)S(1)}, u32[]{:S(2)}, u32[]{:S(2)}) collective-permute-start(f32[2,16,128]{2,1,0:T(8,128)S(1)} %maximum_select_fusion.5.gm_ref), channel_id=1, source_target_pairs={{2,0},{4,2},{6,4},{8,6},{10,8},{12,10},{14,12},{3,1},{5,3},{7,5},{... | collective-permute-start | bytes 49160 | tf_op jit(solution)/shard_map/ppermute | solution.py:585
  53.3 1.1 %copy-start.1 = (bf16[4,12,64,128]{3,2,1,0:T(8,128)(2,1)S(1)}, bf16[4,12,64,128]{3,2,1,0:T(8,128)(2,1)}, u32[]{:S(2)}) copy-start(bf16[4,12,64,128]{3,2,1,0:T(8,128)(2,1)} %copy-done) | copy-start | bytes 2359300
  54.4 1.1 %copy-start.3 = (bf16[4,12,64,128]{3,2,1,0:T(8,128)(2,1)S(1)}, bf16[4,12,64,128]{3,2,1,0:T(8,128)(2,1)}, u32[]{:S(2)}) copy-start(bf16[4,12,64,128]{3,2,1,0:T(8,128)(2,1)} %copy-done.2) | copy-start | bytes 2359300
  55.5 1.1 %copy-start.5 = (f32[2,12,64,128]{3,2,1,0:T(8,128)S(1)}, f32[2,12,64,128]{3,2,1,0:T(8,128)}, u32[]{:S(2)}) copy-start(f32[2,12,64,128]{3,2,1,0:T(8,128)} %copy-done.4) | copy-start | bytes 2359300
  57.4 0.9 copy-start.12
  58.4 0.9 copy-start.14
  59.3 0.9 copy-start.16
  70.0 2.0 %collective-permute-start.7 = (f32[904,128]{1,0:T(8,128)}, f32[904,128]{1,0:T(8,128)S(1)}, u32[]{:S(2)}, u32[]{:S(2)}) collective-permute-start(f32[904,128]{1,0:T(8,128)} %get-tuple-element.42), channel_id=1, source_target_pairs={{0,1},{1,0},{2,3},{3,2},{4,5},{5,4},{6,7},{7,6},{8,9},{9,8},{10,11... | collective-permute-start | bytes 1388552 | tf_op jit(solution)/shard_map/ppermute | solution.py:424
  73.2 6.0 %collective-permute-start.8 = (bf16[464,128]{1,0:T(8,128)(2,1)S(1)}, bf16[464,128]{1,0:T(8,128)(2,1)S(1)}, u32[]{:S(2)}, u32[]{:S(2)}) collective-permute-start(bf16[464,128]{1,0:T(8,128)(2,1)S(1)} %pad_maximum_fusion), channel_id=1, source_target_pairs={{0,2},{1,3},{2,0},{3,1},{4,6},{5,7},{6,4},{7,5},{8,10},{9,11},{10,... | collective-permute-start | bytes 356360 | tf_op jit(solution)/shard_map/ppermute | solution.py:424
  79.3 4.9 %collective-permute-start.9 = (bf16[464,128]{1,0:T(8,128)(2,1)S(1)}, bf16[464,128]{1,0:T(8,128)(2,1)S(1)}, u32[]{:S(2)}, u32[]{:S(2)}) collective-permute-start(bf16[464,128]{1,0:T(8,128)(2,1)S(1)} %pad_maximum_fusion.1), channel_id=1, source_target_pairs={{0,4},{1,5},{2,6},{3,7},{4,0},{5,1},{6,2},{7,3},{8,12},{9,13},{10,... | collective-permute-start | bytes 356360 | tf_op jit(solution)/shard_map/ppermute | solution.py:424
  84.3 7.1 %collective-permute-start.10 = (bf16[464,128]{1,0:T(8,128)(2,1)S(1)}, bf16[464,128]{1,0:T(8,128)(2,1)S(1)}, u32[]{:S(2)}, u32[]{:S(2)}) collective-permute-start(bf16[464,128]{1,0:T(8,128)(2,1)S(1)} %pad_maximum_fusion.2), channel_id=1, source_target_pairs={{0,8},{1,9},{2,10},{3,11},{4,12},{5,13},{6,14},{7,15},{8,0},{9,1},... | collective-permute-start | bytes 356360 | tf_op jit(solution)/shard_map/ppermute | solution.py:424
  91.5 4.9 %collective-permute-start.11 = (bf16[448,128]{1,0:T(8,128)(2,1)S(1)}, bf16[448,128]{1,0:T(8,128)(2,1)S(1)}, u32[]{:S(2)}, u32[]{:S(2)}) collective-permute-start(bf16[448,128]{1,0:T(8,128)(2,1)S(1)} %fusion), channel_id=1, source_target_pairs={{0,2},{1,3},{2,0},{3,1},{4,6},{5,7},{6,4},{7,5},{8,10},{9,11},{10,... | collective-permute-start | bytes 344072 | tf_op jit(solution)/shard_map/ppermute | solution.py:424
  96.5 1.6 %collective-permute-start.12 = (bf16[896,128]{1,0:T(8,128)(2,1)S(1)}, bf16[896,128]{1,0:T(8,128)(2,1)S(1)}, u32[]{:S(2)}, u32[]{:S(2)}) collective-permute-start(bf16[896,128]{1,0:T(8,128)(2,1)S(1)} %maximum_select_fusion.1), channel_id=1, source_target_pairs={{0,1},{1,0},{2,3},{3,2},{4,5},{5,4},{6,7},{7,6},{8,9},{9,8},{10,11... | collective-permute-start | bytes 688136 | tf_op jit(solution)/shard_map/ppermute | solution.py:424
  (6 other events, 4.3 us)

commit v2 on v1

--- a/solution.py
+++ b/solution.py
@@ -20,7 +20,9 @@
 WROWS = 864
 ROWS = 896
 TAIL = 16
-VMEM_LIMIT = 40 * 1024 * 1024
+VMEM_LIMIT = 24 * 1024 * 1024
+S1, S2, S3, HEAD, LOSS, S_BLOCKS = 0, 24, 72, 132, 133, 134
+H1, H2, X0, WB, WC, H_BLOCKS = 0, 48, 96, 108, 123, 138
 
 
 def shift_right(v):
@@ -65,13 +67,35 @@
     return sig * (1.0 + z * (1.0 - sig))
 
 
-def lhs_kernel(wa_ref, wb_ref, wc_ref, fa, fb, fc, tb, tc):
-    fa[...] = jnp.zeros(fa.shape, BF16)
-    for k in range(9):
-        for e in range(3):
-            c = 16 * k + 4 * e
-            fa[:, c : c + 3] = wa_ref[3 * k + e]
-    for w, fwd, bwd in ((wb_ref, fb, tb), (wc_ref, fc, tc)):
+def payload_kernel(fields_hbm, liquid_hbm, class_hbm, out_ref, fields, liquid, classes, rows, sems):
+    copies = [
+        pltpu.make_async_copy(src, dst, sems.at[i])
+        for i, (src, dst) in enumerate(
+            ((fields_hbm, fields), (liquid_hbm, liquid), (class_hbm, classes))
+        )
+    ]
+    for copy in copies:
+        copy.start()
+    for copy in copies:
+        copy.wait()
+    for x in range(2):
+        planes = (fields[0, x], fields[1, x], liquid[x], classes[x])
+        for p, plane in enumerate(planes):
+            plane = plane.astype(F32)
+            for y in range(8):
+                rows[x, y, p : p + 1, :] = plane[y : y + 1]
+    out_ref[...] = rows[...].astype(BF16)
+
+
+def lhs_kernel(wa_hbm, wb_hbm, wc_hbm, fa, fb, fc, tb, tc, wa_ref, wb_ref, wc_ref, sems):
+    copies = [
+        pltpu.make_async_copy(src, dst, sems.at[i])
+        for i, (src, dst) in enumerate(((wb_hbm, wb_ref), (wc_hbm, wc_ref), (wa_hbm, wa_ref)))
+    ]
+    for copy in copies:
+        copy.start()
+    for which, (w, fwd, bwd) in enumerate(((wb_ref, fb, tb), (wc_ref, fc, tc))):
+        copies[which].wait()
         for e in range(3):
             rows = slice(e * HID, (e + 1) * HID)
             for k in range(0, 9, 2):
@@ -82,12 +106,19 @@
                     hi = w[3 * k + 3 + e].astype(F32)
                     bhi = w[26 - (3 * k + 3 + e)].astype(F32)
                     fwd[rows, c : c + 2 * HID] = jnp.concatenate([lo, hi], axis=1).astype(BF16)
-                    both = jnp.concatenate([blo, bhi], axis=0)
-                    bwd[rows, c : c + 2 * HID] = both.T.astype(BF16)
                 else:
+                    bhi = blo
                     fwd[rows, c : c + HID] = lo.astype(BF16)
-                    both = jnp.concatenate([blo, blo], axis=0)
-                    bwd[rows, c : c + HID] = both.T[:, :HID].astype(BF16)
+                bwd[3 * (k // 2) + e] = jnp.concatenate([blo, bhi], axis=0).T.astype(BF16)
+    copies[2].wait()
+    tap = lax.broadcasted_iota(jnp.int32, (27, 144), 0)
+    col = lax.broadcasted_iota(jnp.int32, (27, 144), 1)
+    total = jnp.zeros((HID, 144), F32)
+    for ch in range(3):
+        spot = 16 * (tap // 3) + 4 * (tap - 3 * (tap // 3)) + ch
+        pick = jnp.where(col == spot, 1.0, 0.0).astype(BF16)
+        total += dot_nn(wa_ref[ch].astype(F32).T.astype(BF16), pick)
+    fa[...] = total.astype(BF16)
 
 
 def forward_kernel(
@@ -95,24 +126,21 @@
     home_ref,
     invd_ref,
     hb_ref,
-    gath_ref,
+    mine_ref,
+    other_ref,
     wa_ref,
     wb_ref,
     wc_ref,
+    tb_ref,
+    tc_ref,
     ba_ref,
     bb_ref,
     bc_ref,
     hw_ref,
     p_out,
     gs_out,
-    loss_out,
-    head_out,
-    x0_out,
-    h1_out,
-    h2_out,
-    s1,
-    s2,
-    s3,
+    sbuf,
+    hbuf,
     inv_ref,
     x0s,
     liq,
@@ -149,9 +177,11 @@
         half = xc - 2 * home
         slot = inv_ref[home]
         row4 = lax.broadcasted_iota(jnp.int32, (4, NZ), 0)
-        for y in range(NY):
-            fb = gath_ref[2 * slot + y // 8, half, y % 8].astype(F32) * ok
-            mb = gath_ref[2 * home + y // 8, half, y % 8].astype(F32)
+        for i in range(NY):
+            src = (mine_ref, other_ref)[i // 8]
+            fb = src[slot, half, i % 8].astype(F32) * ok
+            mb = src[home, half, i % 8].astype(F32)
+            y = 8 * (gy if i < 8 else 1 - gy) + i % 8
             lq = mb[2:3] * ok
             cl = mb[3:4]
             sc = jnp.zeros((1, NZ), F32)
@@ -162,9 +192,9 @@
                 [shift_right(base), base, shift_left(base), jnp.zeros((4, NZ), F32)], axis=0
             )
             x0s[X, y + 1] = k12.astype(BF16)
-            liq[X, y + 1 : y + 2, :] = lq
-            scl[X, y + 1 : y + 2, :] = sc * lq
-            f1[X, y + 1 : y + 2, :] = fb[1:2]
+            liq[X, pl.ds(y + 1, 1), :] = lq
+            scl[X, pl.ds(y + 1, 1), :] = sc * lq
+            f1[X, pl.ds(y + 1, 1), :] = fb[1:2]
         return c
 
     lax.fori_loop(0, PLANES, load_plane, 0)
@@ -188,7 +218,7 @@
                 act, sig = activate(z)
                 h1[X, y + k] = (act * m).astype(BF16)
                 if slot is not None:
-                    s1[slot, 2 * j + k] = slope_of(z, sig) * m
+                    sbuf[S1 + 12 * slot + 2 * j + k] = slope_of(z, sig) * m
 
     planes(8, lambda i: layer1(1 + i + 2 * (i // 4), None))
     planes(2, lambda i: layer1(MID + i, i))
@@ -203,7 +233,7 @@
                 act, sig = activate(z)
                 h2[X, y + k] = (act * m).astype(BF16)
                 if slot is not None:
-                    s2[slot, 2 * j + k] = slope_of(z, sig) * m
+                    sbuf[S2 + 12 * slot + 2 * j + k] = slope_of(z, sig) * m
 
     planes(4, lambda i: layer2(2 + i + 4 * (i // 2), None))
     planes(4, lambda i: layer2(MID - 1 + i, i))
@@ -221,7 +251,7 @@
                 h3 = (act * m).astype(BF16)
                 score = jnp.sum(hw_ref[...] * h3.astype(F32), axis=0, keepdims=True)
                 pf[X, pl.ds(y + k, 1), :] = m * (score + hb_ref[0])
-                s3[slot, 2 * j + k] = slope_of(z, sig) * m
+                sbuf[S3 + 10 * slot + 2 * j + k] = slope_of(z, sig) * m
                 if own is not None:
                     h3o[own, 2 * j + k] = h3
 
@@ -252,7 +282,7 @@
         p_out[k] = pf[MID + k, own_y, :]
         r = rs[MID + k, own_y, :]
         loss += r * r
-    loss_out[...] = loss * (1.0 / cells)
+    sbuf[LOSS, 0:8, :] = loss * (1.0 / cells)
     for X in range(MID - 1, MID + 3):
         rs[X] = rs[X] * (2.0 / cells)
     for k in range(2):
@@ -265,34 +295,33 @@
     for i in range(16):
         X, dy = i // 8, i % 8
         head += pf[X, pl.ds(gy * 8 + 1 + dy, 1), :] * h3o[X, gy * 2 + dy].astype(F32)
-    head_out[...] = head
+    sbuf[HEAD] = head
 
     f0 = gy * 6
 
     def copy_out(i):
         for l in range(FRAME):
-            x0_out[i, l] = x0s[MID - 1 + i, f0 + l]
-            h1_out[i, l] = h1[MID - 1 + i, f0 + l]
-            h2_out[i, l] = h2[MID - 1 + i, f0 + l]
+            r = (l % 4) * 16
+            hbuf[X0 + 3 * i + l // 4, r : r + 16, :] = x0s[MID - 1 + i, f0 + l]
+            hbuf[H1 + FRAME * i + l] = h1[MID - 1 + i, f0 + l]
+            hbuf[H2 + FRAME * i + l] = h2[MID - 1 + i, f0 + l]
 
     planes(4, copy_out)
+    for r in range(15):
+        hbuf[WB + r] = tb_ref[r]
+        hbuf[WC + r] = tc_ref[r]
 
 
 def backward_kernel(
     pos_ref,
-    gl_ref,
     gm_ref,
-    gr_ref,
-    loss_ref,
-    head_ref,
-    x0_ref,
-    h1_ref,
-    h2_ref,
-    s1,
-    s2,
-    s3,
-    wbt_ref,
-    wct_ref,
+    gmo_ref,
+    p1_ref,
+    p1o_ref,
+    p2_ref,
+    p2o_ref,
+    sbuf,
+    hbuf,
     hw_ref,
     keep_ref,
     send_ref,
@@ -303,12 +332,27 @@
     gcat,
     hcat,
     acc,
+    wbt_ref,
+    wct_ref,
 ):
     gy = pos_ref[1]
-    for k in range(2):
-        gs[k] = gl_ref[k]
-        gs[2 + k] = gm_ref[k]
-        gs[4 + k] = gr_ref[k]
+    even = pos_ref[0] % 2 == 0
+    own_half = pl.ds(pl.multiple_of(8 * gy, 8), 8)
+    far_half = pl.ds(pl.multiple_of(8 - 8 * gy, 8), 8)
+    for half, gm, p1, p2 in (
+        (own_half, gm_ref, p1_ref, p2_ref),
+        (far_half, gmo_ref, p1o_ref, p2o_ref),
+    ):
+        for k in range(2):
+            gs[k, half, :] = jnp.where(even, p2[k], p1[k])
+            gs[2 + k, half, :] = gm[k]
+            gs[4 + k, half, :] = jnp.where(even, p1[k], p2[k])
+    for base, ref in ((WB, wbt_ref), (WC, wct_ref)):
+        for e in range(3):
+            rows = slice(e * HID, (e + 1) * HID)
+            for t in range(4):
+                ref[rows, t * NZ : (t + 1) * NZ] = hbuf[base + 3 * t + e]
+            ref[rows, 4 * NZ : 4 * NZ + HID] = hbuf[base + 12 + e][:, :HID]
     for ref in (g3, g2):
         z = jnp.zeros((HID, NZ), BF16)
         for X in range(ref.shape[0]):
@@ -325,7 +369,7 @@
     def back3(X):
         for j in range(10):
             g = gs[X, pl.ds(gy * 6 + j, 1), :]
-            g3[X, j + 1] = (g * hw_ref[...] * s3[X, j]).astype(BF16)
+            g3[X, j + 1] = (g * hw_ref[...] * sbuf[S3 + 10 * X + j]).astype(BF16)
 
     planes(6, back3)
 
@@ -334,7 +378,7 @@
             acc[X, r : r + 8, :] = jnp.zeros((8, NZ), F32)
     own = gy * 2 + 1
 
-    def weight_grad(g_ref, g_off, h_ref, which):
+    def weight_grad(g_ref, g_off, h_base, which):
         bias = jnp.zeros((HID, NZ), F32)
         for i in range(16):
             X, dy = i // 8, i % 8
@@ -349,7 +393,7 @@
             for a in range(3):
                 for b in range(3):
                     k = 3 * a + b
-                    hcat[k * HID : (k + 1) * HID, cols] = h_ref[X + a, y + b - 1]
+                    hcat[k * HID : (k + 1) * HID, cols] = hbuf[h_base + FRAME * (X + a) + y + b - 1]
         W = dot_nt(gcat[...], hcat[...])
         for a in range(3):
             for b in range(3):
@@ -361,7 +405,7 @@
                     acc[which, t * 32 : (t + 1) * 32, HID:NZ] = blk[32:]
         return bias
 
-    bias_c = weight_grad(g3, 2, h2_ref, 1)
+    bias_c = weight_grad(g3, 2, H2, 1)
 
     def back2(X):
         for j in range(5):
@@ -369,10 +413,10 @@
             Y = dot_nn(wct_ref[...], taps(g3, X + 1, y))
             for k in range(2):
                 row = gy * 2 + 2 * j + k
-                g2[X, y + k] = (lane_taps(Y, k) * s2[X, row]).astype(BF16)
+                g2[X, y + k] = (lane_taps(Y, k) * sbuf[S2 + 12 * X + row]).astype(BF16)
 
     planes(4, back2)
-    bias_b = weight_grad(g2, 1, h1_ref, 0)
+    bias_b = weight_grad(g2, 1, H1, 0)
 
     def back1(X):
         for j in range(4):
@@ -380,7 +424,7 @@
             Y = dot_nn(wbt_ref[...], taps(g2, X + 1, y))
             for k in range(2):
                 row = gy * 4 + 2 * j + k
-                g1[X, 2 * j + k] = (lane_taps(Y, k) * s1[X, row]).astype(BF16)
+                g1[X, 2 * j + k] = (lane_taps(Y, k) * sbuf[S1 + 12 * X + row]).astype(BF16)
 
     planes(2, back1)
     bias_a = jnp.zeros((HID, NZ), F32)
@@ -394,7 +438,11 @@
         for a in range(3):
             for b in range(3):
                 k = 3 * a + b
-                hcat[k * 16 : (k + 1) * 16, cols] = x0_ref[X + a, y + b - 1]
+                l = y + b - 1
+                q = l // 4
+                hcat[k * 16 : (k + 1) * 16, cols] = hbuf[
+                    X0 + 3 * (X + a) + q, pl.ds(pl.multiple_of((l - 4 * q) * 16, 16), 16), :
+                ]
     A = dot_nt(hcat[0:144, :], gcat[0:HID, :])
     for k in range(8):
         blk = A[16 * k : 16 * k + 12]
@@ -406,9 +454,9 @@
     acc[1, WROWS + 24 : WROWS + 28, HID:NZ] = A[136:140]
     sums = [
         jnp.sum(v, axis=1, keepdims=True).reshape(1, HID)
-        for v in (bias_a, bias_b, bias_c, head_ref[...])
+        for v in (bias_a, bias_b, bias_c, sbuf[HEAD])
     ]
-    total = jnp.sum(jnp.sum(loss_ref[...], axis=0, keepdims=True), axis=1, keepdims=True)
+    total = jnp.sum(jnp.sum(sbuf[LOSS, 0:8, :], axis=0, keepdims=True), axis=1, keepdims=True)
     keep_ref[0:ROWS] = acc[gy]
     send_ref[0:ROWS] = acc[1 - gy]
     for ref in (keep_ref, send_ref):
@@ -420,13 +468,45 @@
         ref[ROWS + 2 : ROWS + 3, :] = jnp.broadcast_to(total, (1, NZ))
 
 
+def finish_kernel(pos_ref, a_ref, b_ref, c_ref, d_ref, gb_hbm, gc_hbm, ga_ref, stage, first, sems):
+    gy = pos_ref[1]
+    upper = (pos_ref[0]) % 2
+
+    def unpack(ref, which, half):
+        for j in range(14):
+            v = ref[32 * j : 32 * j + 32].astype(F32)
+            stage[which, 14 * half + j, 0:32, :] = v[:, :HID]
+            stage[which, 14 * half + j, 32:HID, :] = v[:, HID:]
+
+    unpack(a_ref, gy, upper)
+    unpack(b_ref, gy, 1 - upper)
+    unpack(c_ref, 1 - gy, upper)
+    unpack(d_ref, 1 - gy, 1 - upper)
+    copies = [
+        pltpu.make_async_copy(stage.at[i, pl.ds(0, 27)], dst, sems.at[i])
+        for i, dst in enumerate((gb_hbm, gc_hbm))
+    ]
+    for copy in copies:
+        copy.start()
+    first[0:24] = stage[0, 27, 0:24]
+    first[24:48] = stage[0, 27, 32:56]
+    first[48:72] = stage[1, 27, 0:24]
+    first[72:96] = stage[1, 27, 32:56]
+    first[96:104] = stage[1, 27, 24:32]
+    first[104:108] = stage[1, 27, 56:60]
+    for ch in range(3):
+        ga_ref[ch] = first[pl.ds(ch, 27, stride=4), :]
+    for copy in copies:
+        copy.wait()
+
+
 def partner(value, bit, count):
     return lax.ppermute(value, AXES, [(i, i ^ bit) for i in range(count)])
 
 
 def gather_all(block, me, count):
     value = block[None]
-    bit = 1
+    bit = 2
     while bit < count:
         other = partner(value, bit, count)
         upper = (me & bit) != 0
@@ -467,13 +547,9 @@
         tail = (high + low) + (got[half : half + 8] + got[half + 8 :])
         bit *= 2
     body = body.astype(BF16)
-    other = partner(body, 2, count)
-    body = jnp.where(upper, jnp.concatenate([other, body]), jnp.concatenate([body, other]))
-    other = partner(body, 1, count)
-    odd = (me & 1) != 0
-    first = jnp.where(odd, other, body)
-    second = jnp.where(odd, body, other)
-    return first.astype(F32), second.astype(F32), tail
+    beside = partner(body, 2, count)
+    far = partner(body, 1, count)
+    return body, beside, far, partner(beside, 1, count), tail
 
 
 def on_device(
@@ -501,26 +577,45 @@
     vmem = pl.BlockSpec(memory_space=pltpu.VMEM)
     params = pltpu.CompilerParams(vmem_limit_bytes=VMEM_LIMIT)
 
-    lhs = jax.ShapeDtypeStruct((3 * HID, 9 * HID), BF16)
+    hbm = pl.BlockSpec(memory_space=pl.ANY)
+
+    def shaped(shape, kind):
+        return jax.ShapeDtypeStruct(shape, kind)
+
+    block = pl.pallas_call(
+        payload_kernel,
+        out_shape=shaped((2, 8, 4, NZ), BF16),
+        in_specs=[hbm] * 3,
+        out_specs=vmem,
+        scratch_shapes=[
+            pltpu.VMEM((2, 2, 8, NZ), BF16),
+            pltpu.VMEM((2, 8, NZ), jnp.int32),
+            pltpu.VMEM((2, 8, NZ), jnp.int32),
+            pltpu.VMEM((2, 8, 4, NZ), F32),
+            pltpu.SemaphoreType.DMA((3,)),
+        ],
+        compiler_params=params,
+        name="payload",
+    )(loaded_fields, liquid_mask, density_class)
+    mine = gather_all(block, me, count)
+    across = partner(mine, 1, count)
+
+    lhs = shaped((3 * HID, 9 * HID), BF16)
+    turned = shaped((15, HID, NZ), BF16)
     wa, wb, wc, wbt, wct = pl.pallas_call(
         lhs_kernel,
-        out_shape=(jax.ShapeDtypeStruct((HID, 144), BF16), lhs, lhs, lhs, lhs),
-        in_specs=[vmem] * 3,
+        out_shape=(shaped((HID, 144), BF16), lhs, lhs, turned, turned),
+        in_specs=[hbm] * 3,
         out_specs=(vmem,) * 5,
+        scratch_shapes=[
+            pltpu.VMEM((3, 27, HID), BF16),
+            pltpu.VMEM((27, HID, HID), BF16),
+            pltpu.VMEM((27, HID, HID), BF16),
+            pltpu.SemaphoreType.DMA((3,)),
+        ],
         compiler_params=params,
         name="lhs",
-    )(conv_a, conv_b, conv_c)
-
-    block = jnp.stack(
-        [
-            loaded_fields[0],
-            loaded_fields[1],
-            liquid_mask.astype(BF16),
-            density_class.astype(BF16),
-        ],
-        axis=2,
-    )
-    gath = gather_all(block, me, count)
+    )(conv_a.transpose(2, 0, 1), conv_b, conv_c)
 
     def wide(v):
         return jnp.broadcast_to(v.astype(F32)[:, None], (HID, NZ))
@@ -528,25 +623,16 @@
     pos = jnp.stack([gx, gy]).astype(jnp.int32)
     head_wide = wide(head_weight)
 
-    def shaped(shape, kind):
-        return jax.ShapeDtypeStruct(shape, kind)
-
-    (pressure, score, loss, head, x0o, h1o, h2o, s1, s2, s3) = pl.pallas_call(
+    pressure, score, sbuf, hbuf = pl.pallas_call(
         functools.partial(forward_kernel, n_slots=n_slots, cells=cells),
         out_shape=(
             shaped((2, 8, NZ), F32),
             shaped((2, 8, NZ), F32),
-            shaped((8, NZ), F32),
-            shaped((HID, NZ), F32),
-            shaped((4, FRAME, 16, NZ), BF16),
-            shaped((4, FRAME, HID, NZ), BF16),
-            shaped((4, FRAME, HID, NZ), BF16),
-            shaped((2, 12, HID, NZ), F32),
-            shaped((4, 12, HID, NZ), F32),
-            shaped((6, 10, HID, NZ), F32),
+            shaped((S_BLOCKS, HID, NZ), F32),
+            shaped((H_BLOCKS, HID, NZ), BF16),
         ),
-        in_specs=[smem] * 4 + [vmem] * 8,
-        out_specs=(vmem,) * 10,
+        in_specs=[smem] * 4 + [vmem] * 11,
+        out_specs=(vmem,) * 4,
         scratch_shapes=[
             pltpu.SMEM((n_slots,), jnp.int32),
             pltpu.VMEM((PLANES, YY, 16, NZ), BF16),
@@ -566,28 +652,29 @@
         brick_home,
         inverse_density,
         head_bias,
-        gath,
+        mine,
+        across,
         wa,
         wb,
         wc,
+        wbt,
+        wct,
         wide(bias_a),
         wide(bias_b),
         wide(bias_c),
         head_wide,
     )
 
-    other = partner(score, 1, count)
-    middle = jnp.where(
-        gy == 0, jnp.concatenate([score, other], 1), jnp.concatenate([other, score], 1)
-    )
-    up = [(i, i + 1) for i in range(n_slots - 1)]
-    left = lax.ppermute(middle, "gx", up)
-    right = lax.ppermute(middle, "gx", [(j, i) for i, j in up])
+    swap1 = lax.ppermute(score, "gx", [(i, i ^ 1) for i in range(n_slots)])
+    swap2 = lax.ppermute(score, "gx", [(i, ((i + 1) ^ 1) - 1) for i in range(1, n_slots - 1)])
+    scores = []
+    for value in (score, swap1, swap2):
+        scores += [value, partner(value, 1, count)]
 
     keep, send = pl.pallas_call(
         backward_kernel,
         out_shape=(shaped((ROWS + 8, NZ), F32), shaped((ROWS + 8, NZ), F32)),
-        in_specs=[smem] + [vmem] * 14,
+        in_specs=[smem] + [vmem] * 9,
         out_specs=(vmem, vmem),
         scratch_shapes=[
             pltpu.VMEM((6, NY, NZ), F32),
@@ -597,50 +684,42 @@
             pltpu.VMEM((3 * HID, 16 * NZ), BF16),
             pltpu.VMEM((9 * HID, 16 * NZ), BF16),
             pltpu.VMEM((2, ROWS, NZ), F32),
+            pltpu.VMEM((3 * HID, 9 * HID), BF16),
+            pltpu.VMEM((3 * HID, 9 * HID), BF16),
         ],
         compiler_params=params,
         name="backward",
     )(
         pos,
-        left,
-        middle,
-        right,
-        loss,
-        head,
-        x0o,
-        h1o,
-        h2o,
-        s1,
-        s2,
-        s3,
-        wbt,
-        wct,
+        *scores,
+        sbuf,
+        hbuf,
         head_wide,
     )
 
-    first, second, tail = sum_all(keep, send, me, count)
-
-    def weights(v):
-        v = v[:WROWS].reshape(27, 32, 2, HID)
-        return v.transpose(0, 2, 1, 3).reshape(27, HID, HID)
-
-    def blocks(v):
-        v = v[WROWS : WROWS + 24].reshape(2, 12, 2, HID)
-        return v.transpose(2, 0, 1, 3).reshape(4, 12, HID)
-
-    last = jnp.concatenate(
-        [second[WROWS + 24 : WROWS + 32, :HID], second[WROWS + 24 : WROWS + 28, HID:]], axis=0
-    )
-    parts = jnp.concatenate([blocks(first), blocks(second), last[None]], axis=0)
-    grad_a = parts.reshape(27, 4, HID)[:, :3].transpose(0, 2, 1)
+    *pieces, tail = sum_all(keep, send, me, count)
+    weights = shaped((27, HID, HID), F32)
+    grad_b, grad_c, grad_a = pl.pallas_call(
+        finish_kernel,
+        out_shape=(weights, weights, shaped((3, 27, HID), F32)),
+        in_specs=[smem] + [vmem] * 4,
+        out_specs=(hbm, hbm, vmem),
+        scratch_shapes=[
+            pltpu.VMEM((2, 28, HID, HID), F32),
+            pltpu.VMEM((112, HID), F32),
+            pltpu.SemaphoreType.DMA((2,)),
+        ],
+        compiler_params=params,
+        name="finish",
+    )(pos, *pieces)
     return (
         pressure,
         tail[2, :1],
-        grad_a,
+        grad_a.transpose(1, 2, 0),
         tail[0, :HID],
-        weights(first),
+        grad_b,
         tail[0, HID:],
-        weights(second),
+        grad_c,
         tail[1, :HID],
         tail[1, HID:],
     )

time: 103 us -> 88.4 us (0.86)
  local copies, waits for them, and re-layouts: 22 us -> 10.2 us
  waiting for transfers between devices: 28.4 us -> 24.2 us
  other arithmetic: 4.39 us -> 0.64 us
  starting transfers between devices: 21 us -> 23.9 us
  Pallas kernels: 24.9 us -> 27.6 us
    unnamed x52 -> x16, local copies, waits for them, and re-layouts: 16.3 us -> 6.15 us
    ppermute x11 -> x14, starting transfers between devices: 16.2 us -> 21.4 us  [partner(): return lax.ppermute(value, AXES, [(i, i ^ bit) for i in range(count)])]
    ppermute x2, waiting for transfers between devices: 4.33 us -> 0.86 us  [the longest x1 0.86 us: on_device(): swap1 = lax.ppermute(score, 'gx', [(i, i ^ 1) for i in range(n_slots)])]
    pallas_call x1 -> x3, Pallas kernels: 0.67 us -> 3.98 us  [the longest x1 2.59 us: on_device(): pl.pallas_call(finish_kernel, out_shape=(weights, weights, shaped((3, 27,...]
    broadcast_in_dim x4, local copies, waits for them, and re-layouts: 0.28 us -> 2.92 us  [wide(): return jnp.broadcast_to(v.astype(F32)[:, None], (HID, NZ))]
    ppermute x2, starting transfers between devices: 4.73 us -> 2.5 us  [the longest x1 1.85 us: on_device(): swap1 = lax.ppermute(score, 'gx', [(i, i ^ 1) for i in range(n_slots)])]
    transpose x3 -> x0, local copies, waits for them, and re-layouts: 2.05 us -> none  [the longest x2 2.04 us: weights(): return v.transpose(0, 2, 1, 3).reshape(27, HID, HID)]
    another operation x10 -> x8, other arithmetic: 1.57 us -> 0.14 us  [the longest x2 1.43 us: on_device(): jnp.stack([loaded_fields[0], loaded_fields[1], liquid_mask.astype(BF16),...]
  transfers between devices with their start and end apart: 13 -> 16, of which waited for: 12 -> 12; matrix products, arithmetic and copies ran while one was open for 2% -> 1% of each run, Pallas kernels for 1% -> 2%
where the time goes in v2:
time: 88.4 us; the launch traced here: 88 us
  Pallas kernels  27.6 us (31%)
  waiting for transfers between devices  24.2 us (27%)
  starting transfers between devices  23.9 us (27%)
  local copies, waits for them, and re-layouts  10.2 us (12%)
  between operations  1.48 us (2%)
    ppermute x14, waiting for transfers between devices, partner(): return lax.ppermute(value, AXES, [(i, i ^ bit) for i in range(count)])  23.3 us
    ppermute x14, starting transfers between devices, partner(): return lax.ppermute(value, AXES, [(i, i ^ bit) for i in range(count)])  21.4 us
    pallas_call x1, Pallas kernels, on_device(): pl.pallas_call(functools.partial(forward_kernel, n_slots=n_slots, cells=c...  16.1 us
    pallas_call x1, Pallas kernels, on_device(): pl.pallas_call(backward_kernel, out_shape=(shaped((ROWS + 8, NZ), F32), s...  7.49 us
    unnamed x16, local copies, waits for them, and re-layouts  6.15 us
    broadcast_in_dim x4, local copies, waits for them, and re-layouts, wide(): return jnp.broadcast_to(v.astype(F32)[:, None], (HID, NZ))  2.92 us
    pallas_call x1, Pallas kernels, on_device(): pl.pallas_call(finish_kernel, out_shape=(weights, weights, shaped((3, 27,...  2.59 us
    ppermute x1, starting transfers between devices, on_device(): swap1 = lax.ppermute(score, 'gx', [(i, i ^ 1) for i in range(n_slots)])  1.85 us
  transfers between devices with their start and end apart: 16, of which 12 were waited for; matrix products, arithmetic and copies ran while one was open for 1% of the time, Pallas kernels for 2%

profile of v2, /device:TPU:0, one launch (start us, length us, event | category | flops | bytes accessed | tf_op | source)
XLA Modules:
  0.0 88.0 jit_solution(23226207228000062)
XLA Ops:
  0.7 0.7 copy-done.3
  1.3 0.7 copy-done.4
  2.0 0.7 copy-done.5
  2.8 3.0 %collective-permute-start = (bf16[1,2,8,4,128]{4,3,2,1,0:T(4,128)(2,1)S(1)}, bf16[1,2,8,4,128]{4,3,2,1,0:T(4,128)(2,1)S(1)}, u32[]{:S(2)}, u32[]{:S(2)}) collective-permute-start(bf16[1,2,8,4,128]{4,3,2,1,0:T(4,128)(2,1)S(1)} %bitcast.14), channel_id=1, source_target_pairs={{0,2},{1,3},{2,0},{3,1},{4,6},{5,7},{6,4},{7,5},{8,10},{9,11},{10,... | collective-permute-start | bytes 49160 | tf_op jit(solution)/shard_map/ppermute | solution.py:504
  5.8 1.7 %collective-permute-done = bf16[1,2,8,4,128]{4,3,2,1,0:T(4,128)(2,1)S(1)} collective-permute-done((bf16[1,2,8,4,128]{4,3,2,1,0:T(4,128)(2,1)S(1)}, bf16[1,2,8,4,128]{4,3,2,1,0:T(4,128)(2,1)S(1)}, u32[]{:S(2)}, u32[]{:S(2)}) %collective-permute-start) | collective-permute-done | bytes 16416 | tf_op jit(solution)/shard_map/ppermute | solution.py:504
  7.6 2.1 %collective-permute-start.1 = (bf16[2,2,8,4,128]{4,3,2,1,0:T(4,128)(2,1)S(1)}, bf16[2,2,8,4,128]{4,3,2,1,0:T(4,128)(2,1)S(1)}, u32[]{:S(2)}, u32[]{:S(2)}) collective-permute-start(bf16[2,2,8,4,128]{4,3,2,1,0:T(4,128)(2,1)S(1)} %maximum_select_fusion.2), channel_id=1, source_target_pairs={{0,4},{1,5},{2,6},{3,7},{4,0},{5,1},{6,2},{7,3},{8,12},{9,13},{10,... | collective-permute-start | bytes 98312 | tf_op jit(solution)/shard_map/ppermute | solution.py:504
  9.7 1.9 %collective-permute-done.1 = bf16[2,2,8,4,128]{4,3,2,1,0:T(4,128)(2,1)S(1)} collective-permute-done((bf16[2,2,8,4,128]{4,3,2,1,0:T(4,128)(2,1)S(1)}, bf16[2,2,8,4,128]{4,3,2,1,0:T(4,128)(2,1)S(1)}, u32[]{:S(2)}, u32[]{:S(2)}) %collective-permute-start.1) | collective-permute-done | bytes 32800 | tf_op jit(solution)/shard_map/ppermute | solution.py:504
  11.7 3.1 %collective-permute-start.2 = (bf16[4,2,8,4,128]{4,3,2,1,0:T(4,128)(2,1)S(1)}, bf16[4,2,8,4,128]{4,3,2,1,0:T(4,128)(2,1)S(1)}, u32[]{:S(2)}, u32[]{:S(2)}) collective-permute-start(bf16[4,2,8,4,128]{4,3,2,1,0:T(4,128)(2,1)S(1)} %maximum_select_fusion.1), channel_id=1, source_target_pairs={{0,8},{1,9},{2,10},{3,11},{4,12},{5,13},{6,14},{7,15},{8,0},{9,1},... | collective-permute-start | bytes 196616 | tf_op jit(solution)/shard_map/ppermute | solution.py:504
  14.8 2.2 %collective-permute-done.2 = bf16[4,2,8,4,128]{4,3,2,1,0:T(4,128)(2,1)S(1)} collective-permute-done((bf16[4,2,8,4,128]{4,3,2,1,0:T(4,128)(2,1)S(1)}, bf16[4,2,8,4,128]{4,3,2,1,0:T(4,128)(2,1)S(1)}, u32[]{:S(2)}, u32[]{:S(2)}) %collective-permute-start.2) | collective-permute-done | bytes 65568 | tf_op jit(solution)/shard_map/ppermute | solution.py:504
  17.9 1.0 %copy-done = bf16[27,64,64]{2,1,0:T(8,128)(2,1)S(1)} copy-done((bf16[27,64,64]{2,1,0:T(8,128)(2,1)S(1)}, bf16[27,64,64]{2,1,0:T(8,128)(2,1)}, u32[]{:S(2)}) %copy-start) | copy-done | bytes 221208
  18.9 1.0 %copy-done.1 = bf16[27,64,64]{2,1,0:T(8,128)(2,1)S(1)} copy-done((bf16[27,64,64]{2,1,0:T(8,128)(2,1)S(1)}, bf16[27,64,64]{2,1,0:T(8,128)(2,1)}, u32[]{:S(2)}) %copy-start.1) | copy-done | bytes 221208
  19.9 0.7 copy-done.2
  20.7 1.3 %lhs.1 = (bf16[64,144]{1,0:T(8,128)(2,1)S(1)}, bf16[192,576]{1,0:T(8,128)(2,1)S(1)}, bf16[192,576]{1,0:T(8,128)(2,1)S(1)}, bf16[15,64,128]{2,1,0:T(8,128)(2,1)S(1)}, bf16[15,64,128]{2,1,0:T(8,128)(2,1)S(1)}) custom-call(bf16[3,27,64]{2,1,0:T(8,128)(2,1)S(1)} %bitcast.16, bf16[27,64,64]{2,1,0:T(8,128)(2,1)S(1)} %copy-done, bf16[27,64,64]{2,1,0:T(8,128)(2,1)S(1)} %copy-done.1), custom_call_target="tpu_custom_call" | custom-call | tf_op jit(solution)/shard_map/lhs/pallas_call | solution.py:605
  22.1 0.7 broadcast_in_dim.14.hw_ref
  22.8 0.7 broadcast_in_dim.11.ba_ref
  23.5 0.7 broadcast_in_dim.12.bb_ref
  24.3 0.7 broadcast_in_dim.13.bc_ref
  26.3 16.1 %forward.1 = (f32[2,8,128]{2,1,0:T(8,128)}, f32[2,8,128]{2,1,0:T(8,128)S(1)}, f32[134,64,128]{2,1,0:T(8,128)S(1)}, bf16[138,64,128]{2,1,0:T(8,128)(2,1)S(1)}) custom-call(s32[2]{0:T(128)S(1)} %pad_add_fusion.pos_ref, s32[8]{0:T(128)S(1)} %copy-done.6, f32[4]{0:T(128)S(1)} %copy-done.7, f32[1]{0:T(128)S(6)} %copy.22.hb_ref, ...), custom_call_target="tpu_custom_call" | custom-call | tf_op jit(solution)/shard_map/forward/pallas_call | solution.py:626
  42.4 1.8 %collective-permute-start.5 = (f32[2,8,128]{2,1,0:T(8,128)S(1)}, f32[2,8,128]{2,1,0:T(8,128)S(1)}, u32[]{:S(2)}, u32[]{:S(2)}) collective-permute-start(f32[2,8,128]{2,1,0:T(8,128)S(1)} %get-tuple-element.29.gm_ref), channel_id=1, source_target_pairs={{0,2},{2,0},{4,6},{6,4},{8,10},{10,8},{12,14},{14,12},{1,3},{3,1},... | collective-permute-start | bytes 24584 | tf_op jit(solution)/shard_map/ppermute | solution.py:668
  45.2 0.9 collective-permute-done.5.p1_ref
  47.4 7.5 %backward.1 = (f32[904,128]{1,0:T(8,128)S(1)}, f32[904,128]{1,0:T(8,128)S(1)}) custom-call(s32[2]{0:T(128)S(1)} %pad_add_fusion.pos_ref, f32[2,8,128]{2,1,0:T(8,128)S(1)} %get-tuple-element.29.gm_ref, f32[2,8,128]{2,1,0:T(8,128)S(1)} %collective-permute-done.4.gmo_ref, f32[2,8,128]{2,1,0:T(8,128)S(1)} %collective-permute-done.5.p1_ref, ...), custom_call_target="tpu_custom_call" | custom-call | tf_op jit(solution)/shard_map/backward/pallas_call | solution.py:674
  55.3 1.5 %collective-permute-done.9 = f32[904,128]{1,0:T(8,128)S(1)} collective-permute-done((f32[904,128]{1,0:T(8,128)S(1)}, f32[904,128]{1,0:T(8,128)S(1)}, u32[]{:S(2)}, u32[]{:S(2)}) %collective-permute-start.9) | collective-permute-done | bytes 462880 | tf_op jit(solution)/shard_map/ppermute | solution.py:504
  57.0 4.7 %collective-permute-start.10 = (bf16[464,128]{1,0:T(8,128)(2,1)S(1)}, bf16[464,128]{1,0:T(8,128)(2,1)S(1)}, u32[]{:S(2)}, u32[]{:S(2)}) collective-permute-start(bf16[464,128]{1,0:T(8,128)(2,1)S(1)} %pad_maximum_fusion), channel_id=1, source_target_pairs={{0,2},{1,3},{2,0},{3,1},{4,6},{5,7},{6,4},{7,5},{8,10},{9,11},{10,... | collective-permute-start | bytes 356360 | tf_op jit(solution)/shard_map/ppermute | solution.py:504
  61.7 3.6 %collective-permute-done.10 = bf16[464,128]{1,0:T(8,128)(2,1)S(1)} collective-permute-done((bf16[464,128]{1,0:T(8,128)(2,1)S(1)}, bf16[464,128]{1,0:T(8,128)(2,1)S(1)}, u32[]{:S(2)}, u32[]{:S(2)}) %collective-permute-start.10) | collective-permute-done | bytes 118816 | tf_op jit(solution)/shard_map/ppermute | solution.py:504
  65.3 3.2 %collective-permute-start.11 = (bf16[464,128]{1,0:T(8,128)(2,1)S(1)}, bf16[464,128]{1,0:T(8,128)(2,1)S(1)}, u32[]{:S(2)}, u32[]{:S(2)}) collective-permute-start(bf16[464,128]{1,0:T(8,128)(2,1)S(1)} %pad_maximum_fusion.1), channel_id=1, source_target_pairs={{0,4},{1,5},{2,6},{3,7},{4,0},{5,1},{6,2},{7,3},{8,12},{9,13},{10,... | collective-permute-start | bytes 356360 | tf_op jit(solution)/shard_map/ppermute | solution.py:504
  68.5 2.8 %collective-permute-done.11 = bf16[464,128]{1,0:T(8,128)(2,1)S(1)} collective-permute-done((bf16[464,128]{1,0:T(8,128)(2,1)S(1)}, bf16[464,128]{1,0:T(8,128)(2,1)S(1)}, u32[]{:S(2)}, u32[]{:S(2)}) %collective-permute-start.11) | collective-permute-done | bytes 118816 | tf_op jit(solution)/shard_map/ppermute | solution.py:504
  71.5 3.2 %collective-permute-start.12 = (bf16[464,128]{1,0:T(8,128)(2,1)S(1)}, bf16[464,128]{1,0:T(8,128)(2,1)S(1)}, u32[]{:S(2)}, u32[]{:S(2)}) collective-permute-start(bf16[464,128]{1,0:T(8,128)(2,1)S(1)} %pad_maximum_fusion.2), channel_id=1, source_target_pairs={{0,8},{1,9},{2,10},{3,11},{4,12},{5,13},{6,14},{7,15},{8,0},{9,1},... | collective-permute-start | bytes 356360 | tf_op jit(solution)/shard_map/ppermute | solution.py:504
  74.7 4.4 %collective-permute-done.12 = bf16[464,128]{1,0:T(8,128)(2,1)S(1)} collective-permute-done((bf16[464,128]{1,0:T(8,128)(2,1)S(1)}, bf16[464,128]{1,0:T(8,128)(2,1)S(1)}, u32[]{:S(2)}, u32[]{:S(2)}) %collective-permute-start.12) | collective-permute-done | bytes 118816 | tf_op jit(solution)/shard_map/ppermute | solution.py:504
  79.2 0.7 collective-permute-start.13
  80.4 3.7 %collective-permute-done.13.b_ref = bf16[448,128]{1,0:T(8,128)(2,1)S(1)} collective-permute-done((bf16[448,128]{1,0:T(8,128)(2,1)S(1)}, bf16[448,128]{1,0:T(8,128)(2,1)S(1)}, u32[]{:S(2)}, u32[]{:S(2)}) %collective-permute-start.13) | collective-permute-done | bytes 114720 | tf_op jit(solution)/shard_map/ppermute | solution.py:504
  84.6 0.7 collective-permute-done.15.d_ref
  85.4 2.6 %finish.1 = (f32[27,64,64]{2,1,0:T(8,128)}, f32[27,64,64]{2,1,0:T(8,128)}, f32[3,27,64]{2,1,0:T(8,128)}) custom-call(s32[2]{0:T(128)S(1)} %pad_add_fusion.pos_ref, bf16[448,128]{1,0:T(8,128)(2,1)S(1)} %fusion.a_ref, bf16[448,128]{1,0:T(8,128)(2,1)S(1)} %collective-permute-done.13.b_ref, bf16[448,128]{1,0:T(8,128)(2,1)S(1)} %collective-permute-done.14.c_ref, ...), custom_call_target="tpu_custom_call" | custom-call | tf_op jit(solution)/shard_map/finish/pallas_call | solution.py:702
  (49 shorter events, 5.9 us)
Async XLA Ops:
  0.6 0.7 copy-start.3
  1.3 0.7 copy-start.4
  2.0 0.7 copy-start.5
  2.8 4.8 %collective-permute-start = (bf16[1,2,8,4,128]{4,3,2,1,0:T(4,128)(2,1)S(1)}, bf16[1,2,8,4,128]{4,3,2,1,0:T(4,128)(2,1)S(1)}, u32[]{:S(2)}, u32[]{:S(2)}) collective-permute-start(bf16[1,2,8,4,128]{4,3,2,1,0:T(4,128)(2,1)S(1)} %bitcast.14), channel_id=1, source_target_pairs={{0,2},{1,3},{2,0},{3,1},{4,6},{5,7},{6,4},{7,5},{8,10},{9,11},{10,... | collective-permute-start | bytes 49160 | tf_op jit(solution)/shard_map/ppermute | solution.py:504
  7.6 4.0 %collective-permute-start.1 = (bf16[2,2,8,4,128]{4,3,2,1,0:T(4,128)(2,1)S(1)}, bf16[2,2,8,4,128]{4,3,2,1,0:T(4,128)(2,1)S(1)}, u32[]{:S(2)}, u32[]{:S(2)}) collective-permute-start(bf16[2,2,8,4,128]{4,3,2,1,0:T(4,128)(2,1)S(1)} %maximum_select_fusion.2), channel_id=1, source_target_pairs={{0,4},{1,5},{2,6},{3,7},{4,0},{5,1},{6,2},{7,3},{8,12},{9,13},{10,... | collective-permute-start | bytes 98312 | tf_op jit(solution)/shard_map/ppermute | solution.py:504
  11.7 5.3 %collective-permute-start.2 = (bf16[4,2,8,4,128]{4,3,2,1,0:T(4,128)(2,1)S(1)}, bf16[4,2,8,4,128]{4,3,2,1,0:T(4,128)(2,1)S(1)}, u32[]{:S(2)}, u32[]{:S(2)}) collective-permute-start(bf16[4,2,8,4,128]{4,3,2,1,0:T(4,128)(2,1)S(1)} %maximum_select_fusion.1), channel_id=1, source_target_pairs={{0,8},{1,9},{2,10},{3,11},{4,12},{5,13},{6,14},{7,15},{8,0},{9,1},... | collective-permute-start | bytes 196616 | tf_op jit(solution)/shard_map/ppermute | solution.py:504
  17.2 4.9 %collective-permute-start.3 = (bf16[8,2,8,4,128]{4,3,2,1,0:T(4,128)(2,1)S(1)}, bf16[8,2,8,4,128]{4,3,2,1,0:T(4,128)(2,1)S(1)}, u32[]{:S(2)}, u32[]{:S(2)}) collective-permute-start(bf16[8,2,8,4,128]{4,3,2,1,0:T(4,128)(2,1)S(1)} %maximum_select_fusion.mine_ref), channel_id=1, source_target_pairs={{0,1},{1,0},{2,3},{3,2},{4,5},{5,4},{6,7},{7,6},{8,9},{9,8},{10,11... | collective-permute-start | bytes 393224 | tf_op jit(solution)/shard_map/ppermute | solution.py:504
  17.9 1.0 %copy-start = (bf16[27,64,64]{2,1,0:T(8,128)(2,1)S(1)}, bf16[27,64,64]{2,1,0:T(8,128)(2,1)}, u32[]{:S(2)}) copy-start(bf16[27,64,64]{2,1,0:T(8,128)(2,1)} %wb_hbm.1) | copy-start | bytes 663556
  18.9 1.0 %copy-start.1 = (bf16[27,64,64]{2,1,0:T(8,128)(2,1)S(1)}, bf16[27,64,64]{2,1,0:T(8,128)(2,1)}, u32[]{:S(2)}) copy-start(bf16[27,64,64]{2,1,0:T(8,128)(2,1)} %wc_hbm.1) | copy-start | bytes 663556
  19.9 0.7 copy-start.2
  25.0 0.7 copy-start.6
  25.7 0.7 copy-start.7
  42.4 3.7 %collective-permute-start.5 = (f32[2,8,128]{2,1,0:T(8,128)S(1)}, f32[2,8,128]{2,1,0:T(8,128)S(1)}, u32[]{:S(2)}, u32[]{:S(2)}) collective-permute-start(f32[2,8,128]{2,1,0:T(8,128)S(1)} %get-tuple-element.29.gm_ref), channel_id=1, source_target_pairs={{0,2},{2,0},{4,6},{6,4},{8,10},{10,8},{12,14},{14,12},{1,3},{3,1},... | collective-permute-start | bytes 24584 | tf_op jit(solution)/shard_map/ppermute | solution.py:668
  44.3 1.8 %collective-permute-start.7 = (f32[2,8,128]{2,1,0:T(8,128)S(1)}, f32[2,8,128]{2,1,0:T(8,128)S(1)}, u32[]{:S(2)}, u32[]{:S(2)}) collective-permute-start(f32[2,8,128]{2,1,0:T(8,128)S(1)} %get-tuple-element.29.gm_ref), channel_id=1, source_target_pairs={{2,4},{4,2},{6,8},{8,6},{10,12},{12,10},{3,5},{5,3},{7,9},{9,7},{1... | collective-permute-start | bytes 24584 | tf_op jit(solution)/shard_map/ppermute | solution.py:669
  44.9 1.7 %collective-permute-start.4 = (f32[2,8,128]{2,1,0:T(8,128)S(1)}, f32[2,8,128]{2,1,0:T(8,128)S(1)}, u32[]{:S(2)}, u32[]{:S(2)}) collective-permute-start(f32[2,8,128]{2,1,0:T(8,128)S(1)} %get-tuple-element.29.gm_ref), channel_id=1, source_target_pairs={{0,1},{1,0},{2,3},{3,2},{4,5},{5,4},{6,7},{7,6},{8,9},{9,8},{10,11... | collective-permute-start | bytes 24584 | tf_op jit(solution)/shard_map/ppermute | solution.py:504
  46.1 1.2 %collective-permute-start.6 = (f32[2,8,128]{2,1,0:T(8,128)S(1)}, f32[2,8,128]{2,1,0:T(8,128)S(1)}, u32[]{:S(2)}, u32[]{:S(2)}) collective-permute-start(f32[2,8,128]{2,1,0:T(8,128)S(1)} %collective-permute-done.5.p1_ref), channel_id=1, source_target_pairs={{0,1},{1,0},{2,3},{3,2},{4,5},{5,4},{6,7},{7,6},{8,9},{9,8},{10,11... | collective-permute-start | bytes 24584 | tf_op jit(solution)/shard_map/ppermute | solution.py:504
  46.1 1.3 %collective-permute-start.8 = (f32[2,8,128]{2,1,0:T(8,128)S(1)}, f32[2,8,128]{2,1,0:T(8,128)S(1)}, u32[]{:S(2)}, u32[]{:S(2)}) collective-permute-start(f32[2,8,128]{2,1,0:T(8,128)S(1)} %collective-permute-done.7.p2_ref), channel_id=1, source_target_pairs={{0,1},{1,0},{2,3},{3,2},{4,5},{5,4},{6,7},{7,6},{8,9},{9,8},{10,11... | collective-permute-start | bytes 24584 | tf_op jit(solution)/shard_map/ppermute | solution.py:504
  54.9 1.9 %collective-permute-start.9 = (f32[904,128]{1,0:T(8,128)S(1)}, f32[904,128]{1,0:T(8,128)S(1)}, u32[]{:S(2)}, u32[]{:S(2)}) collective-permute-start(f32[904,128]{1,0:T(8,128)S(1)} %get-tuple-element.33), channel_id=1, source_target_pairs={{0,1},{1,0},{2,3},{3,2},{4,5},{5,4},{6,7},{7,6},{8,9},{9,8},{10,11... | collective-permute-start | bytes 1388552 | tf_op jit(solution)/shard_map/ppermute | solution.py:504
  57.0 8.3 %collective-permute-start.10 = (bf16[464,128]{1,0:T(8,128)(2,1)S(1)}, bf16[464,128]{1,0:T(8,128)(2,1)S(1)}, u32[]{:S(2)}, u32[]{:S(2)}) collective-permute-start(bf16[464,128]{1,0:T(8,128)(2,1)S(1)} %pad_maximum_fusion), channel_id=1, source_target_pairs={{0,2},{1,3},{2,0},{3,1},{4,6},{5,7},{6,4},{7,5},{8,10},{9,11},{10,... | collective-permute-start | bytes 356360 | tf_op jit(solution)/shard_map/ppermute | solution.py:504
  65.3 6.0 %collective-permute-start.11 = (bf16[464,128]{1,0:T(8,128)(2,1)S(1)}, bf16[464,128]{1,0:T(8,128)(2,1)S(1)}, u32[]{:S(2)}, u32[]{:S(2)}) collective-permute-start(bf16[464,128]{1,0:T(8,128)(2,1)S(1)} %pad_maximum_fusion.1), channel_id=1, source_target_pairs={{0,4},{1,5},{2,6},{3,7},{4,0},{5,1},{6,2},{7,3},{8,12},{9,13},{10,... | collective-permute-start | bytes 356360 | tf_op jit(solution)/shard_map/ppermute | solution.py:504
  71.5 7.7 %collective-permute-start.12 = (bf16[464,128]{1,0:T(8,128)(2,1)S(1)}, bf16[464,128]{1,0:T(8,128)(2,1)S(1)}, u32[]{:S(2)}, u32[]{:S(2)}) collective-permute-start(bf16[464,128]{1,0:T(8,128)(2,1)S(1)} %pad_maximum_fusion.2), channel_id=1, source_target_pairs={{0,8},{1,9},{2,10},{3,11},{4,12},{5,13},{6,14},{7,15},{8,0},{9,1},... | collective-permute-start | bytes 356360 | tf_op jit(solution)/shard_map/ppermute | solution.py:504
  79.2 4.9 %collective-permute-start.13 = (bf16[448,128]{1,0:T(8,128)(2,1)S(1)}, bf16[448,128]{1,0:T(8,128)(2,1)S(1)}, u32[]{:S(2)}, u32[]{:S(2)}) collective-permute-start(bf16[448,128]{1,0:T(8,128)(2,1)S(1)} %fusion.a_ref), channel_id=1, source_target_pairs={{0,2},{1,3},{2,0},{3,1},{4,6},{5,7},{6,4},{7,5},{8,10},{9,11},{10,... | collective-permute-start | bytes 344072 | tf_op jit(solution)/shard_map/ppermute | solution.py:504
  79.9 4.8 %collective-permute-start.14 = (bf16[448,128]{1,0:T(8,128)(2,1)S(1)}, bf16[448,128]{1,0:T(8,128)(2,1)S(1)}, u32[]{:S(2)}, u32[]{:S(2)}) collective-permute-start(bf16[448,128]{1,0:T(8,128)(2,1)S(1)} %fusion.a_ref), channel_id=1, source_target_pairs={{0,1},{1,0},{2,3},{3,2},{4,5},{5,4},{6,7},{7,6},{8,9},{9,8},{10,11... | collective-permute-start | bytes 344072 | tf_op jit(solution)/shard_map/ppermute | solution.py:504
  84.1 1.3 %collective-permute-start.15 = (bf16[448,128]{1,0:T(8,128)(2,1)S(1)}, bf16[448,128]{1,0:T(8,128)(2,1)S(1)}, u32[]{:S(2)}, u32[]{:S(2)}) collective-permute-start(bf16[448,128]{1,0:T(8,128)(2,1)S(1)} %collective-permute-done.13.b_ref), channel_id=1, source_target_pairs={{0,1},{1,0},{2,3},{3,2},{4,5},{5,4},{6,7},{7,6},{8,9},{9,8},{10,11... | collective-permute-start | bytes 344072 | tf_op jit(solution)/shard_map/ppermute | solution.py:504

commit v3 on v2

--- a/solution.py
+++ b/solution.py
@@ -87,10 +87,42 @@
     out_ref[...] = rows[...].astype(BF16)
 
 
-def lhs_kernel(wa_hbm, wb_hbm, wc_hbm, fa, fb, fc, tb, tc, wa_ref, wb_ref, wc_ref, sems):
+def lhs_kernel(
+    wb_hbm,
+    wc_hbm,
+    wa_hbm,
+    ba_hbm,
+    bb_hbm,
+    bc_hbm,
+    hw_hbm,
+    fa,
+    fb,
+    fc,
+    tb,
+    tc,
+    wide_ref,
+    wb_ref,
+    wc_ref,
+    wa_ref,
+    ba_ref,
+    bb_ref,
+    bc_ref,
+    hw_ref,
+    sems,
+):
     copies = [
         pltpu.make_async_copy(src, dst, sems.at[i])
-        for i, (src, dst) in enumerate(((wb_hbm, wb_ref), (wc_hbm, wc_ref), (wa_hbm, wa_ref)))
+        for i, (src, dst) in enumerate(
+            (
+                (wb_hbm, wb_ref),
+                (wc_hbm, wc_ref),
+                (wa_hbm, wa_ref),
+                (ba_hbm, ba_ref),
+                (bb_hbm, bb_ref),
+                (bc_hbm, bc_ref),
+                (hw_hbm, hw_ref),
+            )
+        )
     ]
     for copy in copies:
         copy.start()
@@ -119,12 +151,15 @@
         pick = jnp.where(col == spot, 1.0, 0.0).astype(BF16)
         total += dot_nn(wa_ref[ch].astype(F32).T.astype(BF16), pick)
     fa[...] = total.astype(BF16)
+    for i, ref in enumerate((ba_ref, bb_ref, bc_ref, hw_ref)):
+        copies[3 + i].wait()
+        wide_ref[i] = jnp.broadcast_to(ref[...].astype(F32), (NZ, HID)).T
 
 
 def forward_kernel(
     pos_ref,
-    home_ref,
-    invd_ref,
+    home_hbm,
+    invd_hbm,
     hb_ref,
     mine_ref,
     other_ref,
@@ -133,14 +168,14 @@
     wc_ref,
     tb_ref,
     tc_ref,
-    ba_ref,
-    bb_ref,
-    bc_ref,
-    hw_ref,
+    wide_ref,
     p_out,
     gs_out,
     sbuf,
     hbuf,
+    home_ref,
+    invd_ref,
+    sems,
     inv_ref,
     x0s,
     liq,
@@ -157,8 +192,14 @@
 ):
     gx = pos_ref[0]
     gy = pos_ref[1]
-    for s in range(n_slots):
-        inv_ref[home_ref[s]] = s
+    copies = [
+        pltpu.make_async_copy(src, dst, sems.at[i])
+        for i, (src, dst) in enumerate(
+            ((home_hbm, home_ref), (invd_hbm, invd_ref))
+        )
+    ]
+    for copy in copies:
+        copy.start()
 
     for ref in (x0s, h1, h2):
         z = jnp.zeros(ref.shape[2:], ref.dtype)
@@ -168,6 +209,10 @@
     for ref in (liq, scl, f1, pf, rs):
         for X in range(PLANES):
             ref[X] = jnp.zeros((YY, NZ), F32)
+    for copy in copies:
+        copy.wait()
+    for s in range(n_slots):
+        inv_ref[home_ref[s]] = s
 
     def load_plane(X, c):
         xg = 2 * gx - MID + X
@@ -213,7 +258,7 @@
             y = y4 + 2 * j
             Y = dot_nn(wa_ref[...], taps(x0s, X, y))
             for k in range(2):
-                z = Y[:, k * NZ : (k + 1) * NZ] + ba_ref[...]
+                z = Y[:, k * NZ : (k + 1) * NZ] + wide_ref[0]
                 m = liq[X, pl.ds(y + k, 1), :]
                 act, sig = activate(z)
                 h1[X, y + k] = (act * m).astype(BF16)
@@ -228,7 +273,7 @@
             y = y4 + 2 * j
             Y = dot_nn(wb_ref[...], taps(h1, X, y))
             for k in range(2):
-                z = lane_taps(Y, k) + bb_ref[...]
+                z = lane_taps(Y, k) + wide_ref[1]
                 m = liq[X, pl.ds(y + k, 1), :]
                 act, sig = activate(z)
                 h2[X, y + k] = (act * m).astype(BF16)
@@ -245,11 +290,11 @@
             y = y2 + 2 * j
             Y = dot_nn(wc_ref[...], taps(h2, X, y))
             for k in range(2):
-                z = lane_taps(Y, k) + bc_ref[...]
+                z = lane_taps(Y, k) + wide_ref[2]
                 m = liq[X, pl.ds(y + k, 1), :]
                 act, sig = activate(z)
                 h3 = (act * m).astype(BF16)
-                score = jnp.sum(hw_ref[...] * h3.astype(F32), axis=0, keepdims=True)
+                score = jnp.sum(wide_ref[3] * h3.astype(F32), axis=0, keepdims=True)
                 pf[X, pl.ds(y + k, 1), :] = m * (score + hb_ref[0])
                 sbuf[S3 + 10 * slot + 2 * j + k] = slope_of(z, sig) * m
                 if own is not None:
@@ -322,7 +367,7 @@
     p2o_ref,
     sbuf,
     hbuf,
-    hw_ref,
+    wide_ref,
     keep_ref,
     send_ref,
     gs,
@@ -369,7 +414,7 @@
     def back3(X):
         for j in range(10):
             g = gs[X, pl.ds(gy * 6 + j, 1), :]
-            g3[X, j + 1] = (g * hw_ref[...] * sbuf[S3 + 10 * X + j]).astype(BF16)
+            g3[X, j + 1] = (g * wide_ref[3] * sbuf[S3 + 10 * X + j]).astype(BF16)
 
     planes(6, back3)
 
@@ -504,17 +549,10 @@
     return lax.ppermute(value, AXES, [(i, i ^ bit) for i in range(count)])
 
 
-def gather_all(block, me, count):
-    value = block[None]
-    bit = 2
-    while bit < count:
-        other = partner(value, bit, count)
-        upper = (me & bit) != 0
-        value = jnp.where(
-            upper, jnp.concatenate([other, value]), jnp.concatenate([value, other])
-        )
-        bit *= 2
-    return value
+def gather_stage(value, bit, me, count):
+    other = partner(value, bit, count)
+    upper = (me & bit) != 0
+    return jnp.where(upper, jnp.concatenate([other, value]), jnp.concatenate([value, other]))
 
 
 def two_parts(v):
@@ -582,6 +620,9 @@
     def shaped(shape, kind):
         return jax.ShapeDtypeStruct(shape, kind)
 
+    def off_chip(v):
+        return pltpu.with_memory_space_constraint(v, pltpu.HBM)
+
     block = pl.pallas_call(
         payload_kernel,
         out_shape=shaped((2, 8, 4, NZ), BF16),
@@ -596,32 +637,52 @@
         ],
         compiler_params=params,
         name="payload",
-    )(loaded_fields, liquid_mask, density_class)
-    mine = gather_all(block, me, count)
-    across = partner(mine, 1, count)
-
+    )(*map(off_chip, (loaded_fields, liquid_mask, density_class)))
+    mine = block[None]
+    bit = 2
+    while 2 * bit < count:
+        mine = gather_stage(mine, bit, me, count)
+        bit *= 2
+    weights = (
+        conv_b,
+        conv_c,
+        conv_a.transpose(2, 0, 1),
+        *(v.reshape(1, HID) for v in (bias_a, bias_b, bias_c, head_weight)),
+    )
+    mine, weights = lax.optimization_barrier((mine, weights))
     lhs = shaped((3 * HID, 9 * HID), BF16)
     turned = shaped((15, HID, NZ), BF16)
-    wa, wb, wc, wbt, wct = pl.pallas_call(
+    made = pl.pallas_call(
         lhs_kernel,
-        out_shape=(shaped((HID, 144), BF16), lhs, lhs, turned, turned),
-        in_specs=[hbm] * 3,
-        out_specs=(vmem,) * 5,
+        out_shape=(
+            shaped((HID, 144), BF16),
+            lhs,
+            lhs,
+            turned,
+            turned,
+            shaped((4, HID, NZ), F32),
+        ),
+        in_specs=[hbm] * 7,
+        out_specs=(vmem,) * 6,
         scratch_shapes=[
-            pltpu.VMEM((3, 27, HID), BF16),
             pltpu.VMEM((27, HID, HID), BF16),
             pltpu.VMEM((27, HID, HID), BF16),
-            pltpu.SemaphoreType.DMA((3,)),
+            pltpu.VMEM((3, 27, HID), BF16),
+            pltpu.VMEM((1, HID), F32),
+            pltpu.VMEM((1, HID), F32),
+            pltpu.VMEM((1, HID), F32),
+            pltpu.VMEM((1, HID), BF16),
+            pltpu.SemaphoreType.DMA((7,)),
         ],
         compiler_params=params,
         name="lhs",
-    )(conv_a.transpose(2, 0, 1), conv_b, conv_c)
-
-    def wide(v):
-        return jnp.broadcast_to(v.astype(F32)[:, None], (HID, NZ))
+    )(*map(off_chip, weights))
+    mine = gather_stage(mine, bit, me, count)
+    mine, made = lax.optimization_barrier((mine, made))
+    across = partner(mine, 1, count)
+    wide = made[5]
 
     pos = jnp.stack([gx, gy]).astype(jnp.int32)
-    head_wide = wide(head_weight)
 
     pressure, score, sbuf, hbuf = pl.pallas_call(
         functools.partial(forward_kernel, n_slots=n_slots, cells=cells),
@@ -631,9 +692,12 @@
             shaped((S_BLOCKS, HID, NZ), F32),
             shaped((H_BLOCKS, HID, NZ), BF16),
         ),
-        in_specs=[smem] * 4 + [vmem] * 11,
+        in_specs=[smem] + [hbm] * 2 + [smem] + [vmem] * 8,
         out_specs=(vmem,) * 4,
         scratch_shapes=[
+            pltpu.SMEM((n_slots,), jnp.int32),
+            pltpu.SMEM((4,), F32),
+            pltpu.SemaphoreType.DMA((2,)),
             pltpu.SMEM((n_slots,), jnp.int32),
             pltpu.VMEM((PLANES, YY, 16, NZ), BF16),
             pltpu.VMEM((PLANES, YY, NZ), F32),
@@ -649,20 +713,12 @@
         name="forward",
     )(
         pos,
-        brick_home,
-        inverse_density,
+        off_chip(brick_home),
+        off_chip(inverse_density),
         head_bias,
         mine,
         across,
-        wa,
-        wb,
-        wc,
-        wbt,
-        wct,
-        wide(bias_a),
-        wide(bias_b),
-        wide(bias_c),
-        head_wide,
+        *made,
     )
 
     swap1 = lax.ppermute(score, "gx", [(i, i ^ 1) for i in range(n_slots)])
@@ -694,7 +750,7 @@
         *scores,
         sbuf,
         hbuf,
-        head_wide,
+        wide,
     )
 
     *pieces, tail = sum_all(keep, send, me, count)

time: 88.4 us -> 79.7 us (0.902)
  local copies, waits for them, and re-layouts: 10.2 us -> 1.14 us
  Pallas kernels: 27.6 us -> 29.6 us
  waiting for transfers between devices: 24.2 us -> 22.8 us
    unnamed x16 -> x0, local copies, waits for them, and re-layouts: 6.15 us -> none
    broadcast_in_dim x4 -> x0, local copies, waits for them, and re-layouts: 2.92 us -> none  [wide(): return jnp.broadcast_to(v.astype(F32)[:, None], (HID, NZ))]
    ppermute x14, waiting for transfers between devices: 23.3 us -> 21.7 us  [partner(): return lax.ppermute(value, AXES, [(i, i ^ bit) for i in range(count)])]
  transfers between devices with their start and end apart: 16 -> 16, of which waited for: 12 -> 12; matrix products, arithmetic and copies ran while one was open for 1% -> 1% of each run, Pallas kernels for 2% -> 3%
where the time goes in v3:
time: 79.7 us; the launch traced here: 79.4 us
  Pallas kernels  29.6 us (37%)
  starting transfers between devices  23.7 us (30%)
  waiting for transfers between devices  22.8 us (29%)
  between operations  1.47 us (2%)
  local copies, waits for them, and re-layouts  1.14 us (1%)
    ppermute x14, waiting for transfers between devices, partner(): return lax.ppermute(value, AXES, [(i, i ^ bit) for i in range(count)])  21.7 us
    ppermute x14, starting transfers between devices, partner(): return lax.ppermute(value, AXES, [(i, i ^ bit) for i in range(count)])  21.2 us
    pallas_call x1, Pallas kernels, on_device(): pl.pallas_call(functools.partial(forward_kernel, n_slots=n_slots, cells=c...  16.5 us
    pallas_call x1, Pallas kernels, on_device(): pl.pallas_call(backward_kernel, out_shape=(shaped((ROWS + 8, NZ), F32), s...  7.47 us
    pallas_call x1, Pallas kernels, on_device(): pl.pallas_call(finish_kernel, out_shape=(weights, weights, shaped((3, 27,...  2.59 us
    pallas_call x1, Pallas kernels, on_device(): pl.pallas_call(lhs_kernel, out_shape=(shaped((HID, 144), BF16), lhs, lhs,...  2.19 us
    ppermute x1, starting transfers between devices, on_device(): swap1 = lax.ppermute(score, 'gx', [(i, i ^ 1) for i in range(n_slots)])  1.91 us
  transfers between devices with their start and end apart: 16, of which 12 were waited for; matrix products, arithmetic and copies ran while one was open for 1% of the time, Pallas kernels for 3%

profile of v3, /device:TPU:0, one launch (start us, length us, event | category | flops | bytes accessed | tf_op | source)
XLA Modules:
  0.0 79.4 jit_solution(5107491437904417971)
XLA Ops:
  0.6 0.8 payload.1
  1.4 3.0 %collective-permute-start = (bf16[1,2,8,4,128]{4,3,2,1,0:T(4,128)(2,1)S(1)}, bf16[1,2,8,4,128]{4,3,2,1,0:T(4,128)(2,1)S(1)}, u32[]{:S(2)}, u32[]{:S(2)}) collective-permute-start(bf16[1,2,8,4,128]{4,3,2,1,0:T(4,128)(2,1)S(1)} %bitcast.18), channel_id=1, source_target_pairs={{0,2},{1,3},{2,0},{3,1},{4,6},{5,7},{6,4},{7,5},{8,10},{9,11},{10,... | collective-permute-start | bytes 49160 | tf_op jit(solution)/shard_map/ppermute | solution.py:549
  4.5 1.7 %collective-permute-done = bf16[1,2,8,4,128]{4,3,2,1,0:T(4,128)(2,1)S(1)} collective-permute-done((bf16[1,2,8,4,128]{4,3,2,1,0:T(4,128)(2,1)S(1)}, bf16[1,2,8,4,128]{4,3,2,1,0:T(4,128)(2,1)S(1)}, u32[]{:S(2)}, u32[]{:S(2)}) %collective-permute-start) | collective-permute-done | bytes 16416 | tf_op jit(solution)/shard_map/ppermute | solution.py:549
  6.2 2.1 %collective-permute-start.1 = (bf16[2,2,8,4,128]{4,3,2,1,0:T(4,128)(2,1)S(1)}, bf16[2,2,8,4,128]{4,3,2,1,0:T(4,128)(2,1)S(1)}, u32[]{:S(2)}, u32[]{:S(2)}) collective-permute-start(bf16[2,2,8,4,128]{4,3,2,1,0:T(4,128)(2,1)S(1)} %maximum_select_fusion.2), channel_id=1, source_target_pairs={{0,4},{1,5},{2,6},{3,7},{4,0},{5,1},{6,2},{7,3},{8,12},{9,13},{10,... | collective-permute-start | bytes 98312 | tf_op jit(solution)/shard_map/ppermute | solution.py:549
  8.3 1.9 %collective-permute-done.1 = bf16[2,2,8,4,128]{4,3,2,1,0:T(4,128)(2,1)S(1)} collective-permute-done((bf16[2,2,8,4,128]{4,3,2,1,0:T(4,128)(2,1)S(1)}, bf16[2,2,8,4,128]{4,3,2,1,0:T(4,128)(2,1)S(1)}, u32[]{:S(2)}, u32[]{:S(2)}) %collective-permute-start.1) | collective-permute-done | bytes 32800 | tf_op jit(solution)/shard_map/ppermute | solution.py:549
  10.3 3.1 %collective-permute-start.2 = (bf16[4,2,8,4,128]{4,3,2,1,0:T(4,128)(2,1)S(1)}, bf16[4,2,8,4,128]{4,3,2,1,0:T(4,128)(2,1)S(1)}, u32[]{:S(2)}, u32[]{:S(2)}) collective-permute-start(bf16[4,2,8,4,128]{4,3,2,1,0:T(4,128)(2,1)S(1)} %maximum_select_fusion.1), channel_id=1, source_target_pairs={{0,8},{1,9},{2,10},{3,11},{4,12},{5,13},{6,14},{7,15},{8,0},{9,1},... | collective-permute-start | bytes 196616 | tf_op jit(solution)/shard_map/ppermute | solution.py:549
  13.4 2.2 %lhs.1 = (bf16[64,144]{1,0:T(8,128)(2,1)S(1)}, bf16[192,576]{1,0:T(8,128)(2,1)S(1)}, bf16[192,576]{1,0:T(8,128)(2,1)S(1)}, bf16[15,64,128]{2,1,0:T(8,128)(2,1)S(...) custom-call(bf16[27,64,64]{2,1,0:T(8,128)(2,1)} %wb_hbm, bf16[27,64,64]{2,1,0:T(8,128)(2,1)} %wc_hbm, ...), custom_call_target="tpu_custom_call" | custom-call | tf_op jit(solution)/shard_map/lhs/pallas_call | solution.py:655
  15.6 0.1 maximum_select_fusion.mine_ref
  16.5 0.1 pad_add_fusion.pos_ref
  16.6 0.6 collective-permute-done.3.other_ref
  17.2 16.5 %forward.1 = (f32[2,8,128]{2,1,0:T(8,128)}, f32[2,8,128]{2,1,0:T(8,128)S(1)}, f32[134,64,128]{2,1,0:T(8,128)S(1)}, bf16[138,64,128]{2,1,0:T(8,128)(2,1)S(1)}) custom-call(s32[2]{0:T(128)S(1)} %pad_add_fusion.pos_ref, s32[8]{0:T(128)} %home_hbm.1, f32[4]{0:T(128)} %invd_hbm.1, f32[1]{0:T(128)S(6)} %copy.22.hb_ref, ...), custom_call_target="tpu_custom_call" | custom-call | tf_op jit(solution)/shard_map/forward/pallas_call | solution.py:687
  33.7 1.9 %collective-permute-start.5 = (f32[2,8,128]{2,1,0:T(8,128)S(1)}, f32[2,8,128]{2,1,0:T(8,128)S(1)}, u32[]{:S(2)}, u32[]{:S(2)}) collective-permute-start(f32[2,8,128]{2,1,0:T(8,128)S(1)} %get-tuple-element.61.gm_ref), channel_id=1, source_target_pairs={{0,2},{2,0},{4,6},{6,4},{8,10},{10,8},{12,14},{14,12},{1,3},{3,1},... | collective-permute-start | bytes 24584 | tf_op jit(solution)/shard_map/ppermute | solution.py:724
  35.7 0.6 collective-permute-start.7
  36.4 1.1 %collective-permute-done.5.p1_ref = f32[2,8,128]{2,1,0:T(8,128)S(1)} collective-permute-done((f32[2,8,128]{2,1,0:T(8,128)S(1)}, f32[2,8,128]{2,1,0:T(8,128)S(1)}, u32[]{:S(2)}, u32[]{:S(2)}) %collective-permute-start.5) | collective-permute-done | bytes 8224 | tf_op jit(solution)/shard_map/ppermute | solution.py:724
  37.5 0.5 collective-permute-start.8
  38.0 0.7 collective-permute-done.6.p1o_ref
  38.6 0.2 collective-permute-done.8.p2o_ref
  38.8 7.5 %backward.1 = (f32[904,128]{1,0:T(8,128)S(1)}, f32[904,128]{1,0:T(8,128)S(1)}) custom-call(s32[2]{0:T(128)S(1)} %pad_add_fusion.pos_ref, f32[2,8,128]{2,1,0:T(8,128)S(1)} %get-tuple-element.61.gm_ref, f32[2,8,128]{2,1,0:T(8,128)S(1)} %collective-permute-done.4.gmo_ref, f32[2,8,128]{2,1,0:T(8,128)S(1)} %collective-permute-done.5.p1_ref, ...), custom_call_target="tpu_custom_call" | custom-call | tf_op jit(solution)/shard_map/backward/pallas_call | solution.py:730
  46.3 0.4 collective-permute-start.9
  46.7 1.5 %collective-permute-done.9 = f32[904,128]{1,0:T(8,128)S(1)} collective-permute-done((f32[904,128]{1,0:T(8,128)S(1)}, f32[904,128]{1,0:T(8,128)S(1)}, u32[]{:S(2)}, u32[]{:S(2)}) %collective-permute-start.9) | collective-permute-done | bytes 462880 | tf_op jit(solution)/shard_map/ppermute | solution.py:549
  48.3 4.7 %collective-permute-start.10 = (bf16[464,128]{1,0:T(8,128)(2,1)S(1)}, bf16[464,128]{1,0:T(8,128)(2,1)S(1)}, u32[]{:S(2)}, u32[]{:S(2)}) collective-permute-start(bf16[464,128]{1,0:T(8,128)(2,1)S(1)} %pad_maximum_fusion), channel_id=1, source_target_pairs={{0,2},{1,3},{2,0},{3,1},{4,6},{5,7},{6,4},{7,5},{8,10},{9,11},{10,... | collective-permute-start | bytes 356360 | tf_op jit(solution)/shard_map/ppermute | solution.py:549
  53.0 3.6 %collective-permute-done.10 = bf16[464,128]{1,0:T(8,128)(2,1)S(1)} collective-permute-done((bf16[464,128]{1,0:T(8,128)(2,1)S(1)}, bf16[464,128]{1,0:T(8,128)(2,1)S(1)}, u32[]{:S(2)}, u32[]{:S(2)}) %collective-permute-start.10) | collective-permute-done | bytes 118816 | tf_op jit(solution)/shard_map/ppermute | solution.py:549
  56.7 3.2 %collective-permute-start.11 = (bf16[464,128]{1,0:T(8,128)(2,1)S(1)}, bf16[464,128]{1,0:T(8,128)(2,1)S(1)}, u32[]{:S(2)}, u32[]{:S(2)}) collective-permute-start(bf16[464,128]{1,0:T(8,128)(2,1)S(1)} %pad_maximum_fusion.1), channel_id=1, source_target_pairs={{0,4},{1,5},{2,6},{3,7},{4,0},{5,1},{6,2},{7,3},{8,12},{9,13},{10,... | collective-permute-start | bytes 356360 | tf_op jit(solution)/shard_map/ppermute | solution.py:549
  59.9 2.8 %collective-permute-done.11 = bf16[464,128]{1,0:T(8,128)(2,1)S(1)} collective-permute-done((bf16[464,128]{1,0:T(8,128)(2,1)S(1)}, bf16[464,128]{1,0:T(8,128)(2,1)S(1)}, u32[]{:S(2)}, u32[]{:S(2)}) %collective-permute-start.11) | collective-permute-done | bytes 118816 | tf_op jit(solution)/shard_map/ppermute | solution.py:549
  62.8 3.3 %collective-permute-start.12 = (bf16[464,128]{1,0:T(8,128)(2,1)S(1)}, bf16[464,128]{1,0:T(8,128)(2,1)S(1)}, u32[]{:S(2)}, u32[]{:S(2)}) collective-permute-start(bf16[464,128]{1,0:T(8,128)(2,1)S(1)} %pad_maximum_fusion.2), channel_id=1, source_target_pairs={{0,8},{1,9},{2,10},{3,11},{4,12},{5,13},{6,14},{7,15},{8,0},{9,1},... | collective-permute-start | bytes 356360 | tf_op jit(solution)/shard_map/ppermute | solution.py:549
  66.1 4.4 %collective-permute-done.12 = bf16[464,128]{1,0:T(8,128)(2,1)S(1)} collective-permute-done((bf16[464,128]{1,0:T(8,128)(2,1)S(1)}, bf16[464,128]{1,0:T(8,128)(2,1)S(1)}, u32[]{:S(2)}, u32[]{:S(2)}) %collective-permute-start.12) | collective-permute-done | bytes 118816 | tf_op jit(solution)/shard_map/ppermute | solution.py:549
  70.6 0.7 collective-permute-start.13
  71.3 0.5 slice.58
  71.8 3.7 %collective-permute-done.13.b_ref = bf16[448,128]{1,0:T(8,128)(2,1)S(1)} collective-permute-done((bf16[448,128]{1,0:T(8,128)(2,1)S(1)}, bf16[448,128]{1,0:T(8,128)(2,1)S(1)}, u32[]{:S(2)}, u32[]{:S(2)}) %collective-permute-start.13) | collective-permute-done | bytes 114720 | tf_op jit(solution)/shard_map/ppermute | solution.py:549
  75.4 0.6 slice_bitcast_fusion
  76.0 0.7 collective-permute-done.15.d_ref
  76.8 2.6 %finish.1 = (f32[27,64,64]{2,1,0:T(8,128)}, f32[27,64,64]{2,1,0:T(8,128)}, f32[3,27,64]{2,1,0:T(8,128)}) custom-call(s32[2]{0:T(128)S(1)} %pad_add_fusion.pos_ref, bf16[448,128]{1,0:T(8,128)(2,1)S(1)} %fusion.a_ref, bf16[448,128]{1,0:T(8,128)(2,1)S(1)} %collective-permute-done.13.b_ref, bf16[448,128]{1,0:T(8,128)(2,1)S(1)} %collective-permute-done.14.c_ref, ...), custom_call_target="tpu_custom_call" | custom-call | tf_op jit(solution)/shard_map/finish/pallas_call | solution.py:758
  (29 shorter events, 0.7 us)
Async XLA Ops:
  1.4 4.8 %collective-permute-start = (bf16[1,2,8,4,128]{4,3,2,1,0:T(4,128)(2,1)S(1)}, bf16[1,2,8,4,128]{4,3,2,1,0:T(4,128)(2,1)S(1)}, u32[]{:S(2)}, u32[]{:S(2)}) collective-permute-start(bf16[1,2,8,4,128]{4,3,2,1,0:T(4,128)(2,1)S(1)} %bitcast.18), channel_id=1, source_target_pairs={{0,2},{1,3},{2,0},{3,1},{4,6},{5,7},{6,4},{7,5},{8,10},{9,11},{10,... | collective-permute-start | bytes 49160 | tf_op jit(solution)/shard_map/ppermute | solution.py:549
  6.2 4.0 %collective-permute-start.1 = (bf16[2,2,8,4,128]{4,3,2,1,0:T(4,128)(2,1)S(1)}, bf16[2,2,8,4,128]{4,3,2,1,0:T(4,128)(2,1)S(1)}, u32[]{:S(2)}, u32[]{:S(2)}) collective-permute-start(bf16[2,2,8,4,128]{4,3,2,1,0:T(4,128)(2,1)S(1)} %maximum_select_fusion.2), channel_id=1, source_target_pairs={{0,4},{1,5},{2,6},{3,7},{4,0},{5,1},{6,2},{7,3},{8,12},{9,13},{10,... | collective-permute-start | bytes 98312 | tf_op jit(solution)/shard_map/ppermute | solution.py:549
  10.3 5.3 %collective-permute-start.2 = (bf16[4,2,8,4,128]{4,3,2,1,0:T(4,128)(2,1)S(1)}, bf16[4,2,8,4,128]{4,3,2,1,0:T(4,128)(2,1)S(1)}, u32[]{:S(2)}, u32[]{:S(2)}) collective-permute-start(bf16[4,2,8,4,128]{4,3,2,1,0:T(4,128)(2,1)S(1)} %maximum_select_fusion.1), channel_id=1, source_target_pairs={{0,8},{1,9},{2,10},{3,11},{4,12},{5,13},{6,14},{7,15},{8,0},{9,1},... | collective-permute-start | bytes 196616 | tf_op jit(solution)/shard_map/ppermute | solution.py:549
  15.8 1.4 %collective-permute-start.3 = (bf16[8,2,8,4,128]{4,3,2,1,0:T(4,128)(2,1)S(1)}, bf16[8,2,8,4,128]{4,3,2,1,0:T(4,128)(2,1)S(1)}, u32[]{:S(2)}, u32[]{:S(2)}) collective-permute-start(bf16[8,2,8,4,128]{4,3,2,1,0:T(4,128)(2,1)S(1)} %maximum_select_fusion.mine_ref), channel_id=1, source_target_pairs={{0,1},{1,0},{2,3},{3,2},{4,5},{5,4},{6,7},{7,6},{8,9},{9,8},{10,11... | collective-permute-start | bytes 393224 | tf_op jit(solution)/shard_map/ppermute | solution.py:549
  33.7 3.7 %collective-permute-start.5 = (f32[2,8,128]{2,1,0:T(8,128)S(1)}, f32[2,8,128]{2,1,0:T(8,128)S(1)}, u32[]{:S(2)}, u32[]{:S(2)}) collective-permute-start(f32[2,8,128]{2,1,0:T(8,128)S(1)} %get-tuple-element.61.gm_ref), channel_id=1, source_target_pairs={{0,2},{2,0},{4,6},{6,4},{8,10},{10,8},{12,14},{14,12},{1,3},{3,1},... | collective-permute-start | bytes 24584 | tf_op jit(solution)/shard_map/ppermute | solution.py:724
  35.7 1.8 %collective-permute-start.7 = (f32[2,8,128]{2,1,0:T(8,128)S(1)}, f32[2,8,128]{2,1,0:T(8,128)S(1)}, u32[]{:S(2)}, u32[]{:S(2)}) collective-permute-start(f32[2,8,128]{2,1,0:T(8,128)S(1)} %get-tuple-element.61.gm_ref), channel_id=1, source_target_pairs={{2,4},{4,2},{6,8},{8,6},{10,12},{12,10},{3,5},{5,3},{7,9},{9,7},{1... | collective-permute-start | bytes 24584 | tf_op jit(solution)/shard_map/ppermute | solution.py:725
  36.3 1.7 %collective-permute-start.4 = (f32[2,8,128]{2,1,0:T(8,128)S(1)}, f32[2,8,128]{2,1,0:T(8,128)S(1)}, u32[]{:S(2)}, u32[]{:S(2)}) collective-permute-start(f32[2,8,128]{2,1,0:T(8,128)S(1)} %get-tuple-element.61.gm_ref), channel_id=1, source_target_pairs={{0,1},{1,0},{2,3},{3,2},{4,5},{5,4},{6,7},{7,6},{8,9},{9,8},{10,11... | collective-permute-start | bytes 24584 | tf_op jit(solution)/shard_map/ppermute | solution.py:549
  37.5 1.2 %collective-permute-start.6 = (f32[2,8,128]{2,1,0:T(8,128)S(1)}, f32[2,8,128]{2,1,0:T(8,128)S(1)}, u32[]{:S(2)}, u32[]{:S(2)}) collective-permute-start(f32[2,8,128]{2,1,0:T(8,128)S(1)} %collective-permute-done.5.p1_ref), channel_id=1, source_target_pairs={{0,1},{1,0},{2,3},{3,2},{4,5},{5,4},{6,7},{7,6},{8,9},{9,8},{10,11... | collective-permute-start | bytes 24584 | tf_op jit(solution)/shard_map/ppermute | solution.py:549
  37.5 1.3 %collective-permute-start.8 = (f32[2,8,128]{2,1,0:T(8,128)S(1)}, f32[2,8,128]{2,1,0:T(8,128)S(1)}, u32[]{:S(2)}, u32[]{:S(2)}) collective-permute-start(f32[2,8,128]{2,1,0:T(8,128)S(1)} %collective-permute-done.7.p2_ref), channel_id=1, source_target_pairs={{0,1},{1,0},{2,3},{3,2},{4,5},{5,4},{6,7},{7,6},{8,9},{9,8},{10,11... | collective-permute-start | bytes 24584 | tf_op jit(solution)/shard_map/ppermute | solution.py:549
  46.3 1.9 %collective-permute-start.9 = (f32[904,128]{1,0:T(8,128)S(1)}, f32[904,128]{1,0:T(8,128)S(1)}, u32[]{:S(2)}, u32[]{:S(2)}) collective-permute-start(f32[904,128]{1,0:T(8,128)S(1)} %get-tuple-element.65), channel_id=1, source_target_pairs={{0,1},{1,0},{2,3},{3,2},{4,5},{5,4},{6,7},{7,6},{8,9},{9,8},{10,11... | collective-permute-start | bytes 1388552 | tf_op jit(solution)/shard_map/ppermute | solution.py:549
  48.3 8.3 %collective-permute-start.10 = (bf16[464,128]{1,0:T(8,128)(2,1)S(1)}, bf16[464,128]{1,0:T(8,128)(2,1)S(1)}, u32[]{:S(2)}, u32[]{:S(2)}) collective-permute-start(bf16[464,128]{1,0:T(8,128)(2,1)S(1)} %pad_maximum_fusion), channel_id=1, source_target_pairs={{0,2},{1,3},{2,0},{3,1},{4,6},{5,7},{6,4},{7,5},{8,10},{9,11},{10,... | collective-permute-start | bytes 356360 | tf_op jit(solution)/shard_map/ppermute | solution.py:549
  56.7 6.0 %collective-permute-start.11 = (bf16[464,128]{1,0:T(8,128)(2,1)S(1)}, bf16[464,128]{1,0:T(8,128)(2,1)S(1)}, u32[]{:S(2)}, u32[]{:S(2)}) collective-permute-start(bf16[464,128]{1,0:T(8,128)(2,1)S(1)} %pad_maximum_fusion.1), channel_id=1, source_target_pairs={{0,4},{1,5},{2,6},{3,7},{4,0},{5,1},{6,2},{7,3},{8,12},{9,13},{10,... | collective-permute-start | bytes 356360 | tf_op jit(solution)/shard_map/ppermute | solution.py:549
  62.8 7.7 %collective-permute-start.12 = (bf16[464,128]{1,0:T(8,128)(2,1)S(1)}, bf16[464,128]{1,0:T(8,128)(2,1)S(1)}, u32[]{:S(2)}, u32[]{:S(2)}) collective-permute-start(bf16[464,128]{1,0:T(8,128)(2,1)S(1)} %pad_maximum_fusion.2), channel_id=1, source_target_pairs={{0,8},{1,9},{2,10},{3,11},{4,12},{5,13},{6,14},{7,15},{8,0},{9,1},... | collective-permute-start | bytes 356360 | tf_op jit(solution)/shard_map/ppermute | solution.py:549
  70.6 4.9 %collective-permute-start.13 = (bf16[448,128]{1,0:T(8,128)(2,1)S(1)}, bf16[448,128]{1,0:T(8,128)(2,1)S(1)}, u32[]{:S(2)}, u32[]{:S(2)}) collective-permute-start(bf16[448,128]{1,0:T(8,128)(2,1)S(1)} %fusion.a_ref), channel_id=1, source_target_pairs={{0,2},{1,3},{2,0},{3,1},{4,6},{5,7},{6,4},{7,5},{8,10},{9,11},{10,... | collective-permute-start | bytes 344072 | tf_op jit(solution)/shard_map/ppermute | solution.py:549
  71.3 4.8 %collective-permute-start.14 = (bf16[448,128]{1,0:T(8,128)(2,1)S(1)}, bf16[448,128]{1,0:T(8,128)(2,1)S(1)}, u32[]{:S(2)}, u32[]{:S(2)}) collective-permute-start(bf16[448,128]{1,0:T(8,128)(2,1)S(1)} %fusion.a_ref), channel_id=1, source_target_pairs={{0,1},{1,0},{2,3},{3,2},{4,5},{5,4},{6,7},{7,6},{8,9},{9,8},{10,11... | collective-permute-start | bytes 344072 | tf_op jit(solution)/shard_map/ppermute | solution.py:549
  75.4 1.3 %collective-permute-start.15 = (bf16[448,128]{1,0:T(8,128)(2,1)S(1)}, bf16[448,128]{1,0:T(8,128)(2,1)S(1)}, u32[]{:S(2)}, u32[]{:S(2)}) collective-permute-start(bf16[448,128]{1,0:T(8,128)(2,1)S(1)} %collective-permute-done.13.b_ref), channel_id=1, source_target_pairs={{0,1},{1,0},{2,3},{3,2},{4,5},{5,4},{6,7},{7,6},{8,9},{9,8},{10,11... | collective-permute-start | bytes 344072 | tf_op jit(solution)/shard_map/ppermute | solution.py:549

commit v4 on v3

--- a/solution.py
+++ b/solution.py
@@ -22,7 +22,7 @@
 TAIL = 16
 VMEM_LIMIT = 24 * 1024 * 1024
 S1, S2, S3, HEAD, LOSS, S_BLOCKS = 0, 24, 72, 132, 133, 134
-H1, H2, X0, WB, WC, H_BLOCKS = 0, 48, 96, 108, 123, 138
+H1, H2, X0, WB, WC, H_BLOCKS = 0, 48, 96, 108, 144, 180
 
 
 def shift_right(v):
@@ -53,8 +53,18 @@
     return jnp.concatenate(out, axis=0)
 
 
-def lane_taps(Y, k):
-    part = Y[:, k * NZ : (k + 1) * NZ]
+def pair_taps(src, X, y):
+    out = []
+    for b in range(3):
+        for x in range(4):
+            out.append(
+                jnp.concatenate([src[X + x - 1, y + b - 1], src[X + x - 1, y + b]], axis=1)
+            )
+    return jnp.concatenate(out, axis=0)
+
+
+def lane_taps(Y, d, k):
+    part = Y[d * 3 * HID : (d + 1) * 3 * HID, k * NZ : (k + 1) * NZ]
     return part[HID : 2 * HID] + shift_right(part[:HID]) + shift_left(part[2 * HID :])
 
 
@@ -87,23 +97,56 @@
     out_ref[...] = rows[...].astype(BF16)
 
 
-def lhs_kernel(
-    wb_hbm,
+def conv_lhs(w, fwd, bwd):
+    zero = jnp.zeros((HID, HID), F32)
+    for b in range(3):
+        for e in range(3):
+            ahead = [w[9 * a + 3 * b + e].astype(F32) for a in range(3)]
+            back = [w[26 - (9 * a + 3 * b + e)].astype(F32) for a in range(3)]
+            for d in range(2):
+                for half in range(2):
+                    low, high = 2 * half - d, 2 * half + 1 - d
+                    rows = slice((3 * d + e) * HID, (3 * d + e + 1) * HID)
+                    tile = 2 * b + half
+                    pick = [
+                        [v[a] if 0 <= a <= 2 else zero for a in (low, high)] for v in (ahead, back)
+                    ]
+                    fwd[rows, tile * NZ : (tile + 1) * NZ] = jnp.concatenate(
+                        pick[0], axis=1
+                    ).astype(BF16)
+                    bwd[6 * tile + 3 * d + e] = jnp.concatenate(pick[1], axis=0).T.astype(BF16)
+
+
+def second_lhs_kernel(wb_hbm, wa_hbm, fa, fb, tb, wb_ref, wa_ref, sems):
+    copies = [
+        pltpu.make_async_copy(src, dst, sems.at[i])
+        for i, (src, dst) in enumerate(((wb_hbm, wb_ref), (wa_hbm, wa_ref)))
+    ]
+    for copy in copies:
+        copy.start()
+    for copy in copies:
+        copy.wait()
+    conv_lhs(wb_ref, fb, tb)
+    tap = lax.broadcasted_iota(jnp.int32, (27, 144), 0)
+    col = lax.broadcasted_iota(jnp.int32, (27, 144), 1)
+    total = jnp.zeros((HID, 144), F32)
+    for ch in range(3):
+        spot = 16 * (tap // 3) + 4 * (tap - 3 * (tap // 3)) + ch
+        pick = jnp.where(col == spot, 1.0, 0.0).astype(BF16)
+        total += dot_nn(wa_ref[ch].astype(F32).T.astype(BF16), pick)
+    fa[...] = total.astype(BF16)
+
+
+def third_lhs_kernel(
     wc_hbm,
-    wa_hbm,
     ba_hbm,
     bb_hbm,
     bc_hbm,
     hw_hbm,
-    fa,
-    fb,
     fc,
-    tb,
     tc,
     wide_ref,
-    wb_ref,
     wc_ref,
-    wa_ref,
     ba_ref,
     bb_ref,
     bc_ref,
@@ -114,9 +157,7 @@
         pltpu.make_async_copy(src, dst, sems.at[i])
         for i, (src, dst) in enumerate(
             (
-                (wb_hbm, wb_ref),
                 (wc_hbm, wc_ref),
-                (wa_hbm, wa_ref),
                 (ba_hbm, ba_ref),
                 (bb_hbm, bb_ref),
                 (bc_hbm, bc_ref),
@@ -126,34 +167,11 @@
     ]
     for copy in copies:
         copy.start()
-    for which, (w, fwd, bwd) in enumerate(((wb_ref, fb, tb), (wc_ref, fc, tc))):
-        copies[which].wait()
-        for e in range(3):
-            rows = slice(e * HID, (e + 1) * HID)
-            for k in range(0, 9, 2):
-                c = k * HID
-                lo = w[3 * k + e].astype(F32)
-                blo = w[26 - (3 * k + e)].astype(F32)
-                if k < 8:
-                    hi = w[3 * k + 3 + e].astype(F32)
-                    bhi = w[26 - (3 * k + 3 + e)].astype(F32)
-                    fwd[rows, c : c + 2 * HID] = jnp.concatenate([lo, hi], axis=1).astype(BF16)
-                else:
-                    bhi = blo
-                    fwd[rows, c : c + HID] = lo.astype(BF16)
-                bwd[3 * (k // 2) + e] = jnp.concatenate([blo, bhi], axis=0).T.astype(BF16)
-    copies[2].wait()
-    tap = lax.broadcasted_iota(jnp.int32, (27, 144), 0)
-    col = lax.broadcasted_iota(jnp.int32, (27, 144), 1)
-    total = jnp.zeros((HID, 144), F32)
-    for ch in range(3):
-        spot = 16 * (tap // 3) + 4 * (tap - 3 * (tap // 3)) + ch
-        pick = jnp.where(col == spot, 1.0, 0.0).astype(BF16)
-        total += dot_nn(wa_ref[ch].astype(F32).T.astype(BF16), pick)
-    fa[...] = total.astype(BF16)
+    for copy in copies:
+        copy.wait()
     for i, ref in enumerate((ba_ref, bb_ref, bc_ref, hw_ref)):
-        copies[3 + i].wait()
         wide_ref[i] = jnp.broadcast_to(ref[...].astype(F32), (NZ, HID)).T
+    conv_lhs(wc_ref, fc, tc)
 
 
 def forward_kernel(
@@ -165,8 +183,8 @@
     other_ref,
     wa_ref,
     wb_ref,
+    tb_ref,
     wc_ref,
-    tb_ref,
     tc_ref,
     wide_ref,
     p_out,
@@ -271,37 +289,38 @@
     def layer2(X, slot):
         for j in range(6):
             y = y4 + 2 * j
-            Y = dot_nn(wb_ref[...], taps(h1, X, y))
-            for k in range(2):
-                z = lane_taps(Y, k) + wide_ref[1]
-                m = liq[X, pl.ds(y + k, 1), :]
-                act, sig = activate(z)
-                h2[X, y + k] = (act * m).astype(BF16)
-                if slot is not None:
-                    sbuf[S2 + 12 * slot + 2 * j + k] = slope_of(z, sig) * m
-
-    planes(4, lambda i: layer2(2 + i + 4 * (i // 2), None))
-    planes(4, lambda i: layer2(MID - 1 + i, i))
+            Y = dot_nn(wb_ref[...], pair_taps(h1, X, y))
+            for d in range(2):
+                for k in range(2):
+                    z = lane_taps(Y, d, k) + wide_ref[1]
+                    m = liq[X + d, pl.ds(y + k, 1), :]
+                    act, sig = activate(z)
+                    h2[X + d, y + k] = (act * m).astype(BF16)
+                    if slot is not None:
+                        sbuf[S2 + 12 * (slot + d) + 2 * j + k] = slope_of(z, sig) * m
+
+    planes(2, lambda i: layer2(2 + 6 * i, None))
+    planes(2, lambda i: layer2(MID - 1 + 2 * i, 2 * i))
 
     y2 = gy * 6 + 1
 
-    def layer3(X, slot, own):
+    def layer3(i):
+        X = MID - 2 + 2 * i
         for j in range(5):
             y = y2 + 2 * j
-            Y = dot_nn(wc_ref[...], taps(h2, X, y))
-            for k in range(2):
-                z = lane_taps(Y, k) + wide_ref[2]
-                m = liq[X, pl.ds(y + k, 1), :]
-                act, sig = activate(z)
-                h3 = (act * m).astype(BF16)
-                score = jnp.sum(wide_ref[3] * h3.astype(F32), axis=0, keepdims=True)
-                pf[X, pl.ds(y + k, 1), :] = m * (score + hb_ref[0])
-                sbuf[S3 + 10 * slot + 2 * j + k] = slope_of(z, sig) * m
-                if own is not None:
-                    h3o[own, 2 * j + k] = h3
-
-    planes(4, lambda i: layer3(3 + i + 2 * (i // 2), i + 2 * (i // 2), None))
-    planes(2, lambda i: layer3(MID + i, 2 + i, i))
+            Y = dot_nn(wc_ref[...], pair_taps(h2, X, y))
+            for d in range(2):
+                for k in range(2):
+                    z = lane_taps(Y, d, k) + wide_ref[2]
+                    m = liq[X + d, pl.ds(y + k, 1), :]
+                    act, sig = activate(z)
+                    h3 = (act * m).astype(BF16)
+                    score = jnp.sum(wide_ref[3] * h3.astype(F32), axis=0, keepdims=True)
+                    pf[X + d, pl.ds(y + k, 1), :] = m * (score + hb_ref[0])
+                    sbuf[S3 + 10 * (2 * i + d) + 2 * j + k] = slope_of(z, sig) * m
+                    h3o[2 * i + d, 2 * j + k] = h3
+
+    planes(3, layer3)
 
     def operator(val, X):
         v = val[X, 1 : NY + 1, :]
@@ -339,7 +358,7 @@
     head = jnp.zeros((HID, NZ), F32)
     for i in range(16):
         X, dy = i // 8, i % 8
-        head += pf[X, pl.ds(gy * 8 + 1 + dy, 1), :] * h3o[X, gy * 2 + dy].astype(F32)
+        head += pf[X, pl.ds(gy * 8 + 1 + dy, 1), :] * h3o[2 + X, gy * 2 + dy].astype(F32)
     sbuf[HEAD] = head
 
     f0 = gy * 6
@@ -352,7 +371,7 @@
             hbuf[H2 + FRAME * i + l] = h2[MID - 1 + i, f0 + l]
 
     planes(4, copy_out)
-    for r in range(15):
+    for r in range(36):
         hbuf[WB + r] = tb_ref[r]
         hbuf[WC + r] = tc_ref[r]
 
@@ -361,10 +380,10 @@
     pos_ref,
     gm_ref,
     gmo_ref,
+    p2_ref,
+    p2o_ref,
     p1_ref,
     p1o_ref,
-    p2_ref,
-    p2o_ref,
     sbuf,
     hbuf,
     wide_ref,
@@ -377,8 +396,6 @@
     gcat,
     hcat,
     acc,
-    wbt_ref,
-    wct_ref,
 ):
     gy = pos_ref[1]
     even = pos_ref[0] % 2 == 0
@@ -392,12 +409,12 @@
             gs[k, half, :] = jnp.where(even, p2[k], p1[k])
             gs[2 + k, half, :] = gm[k]
             gs[4 + k, half, :] = jnp.where(even, p1[k], p2[k])
-    for base, ref in ((WB, wbt_ref), (WC, wct_ref)):
-        for e in range(3):
-            rows = slice(e * HID, (e + 1) * HID)
-            for t in range(4):
-                ref[rows, t * NZ : (t + 1) * NZ] = hbuf[base + 3 * t + e]
-            ref[rows, 4 * NZ : 4 * NZ + HID] = hbuf[base + 12 + e][:, :HID]
+    def lhs_at(base):
+        tiles = [
+            jnp.concatenate([hbuf[base + 6 * t + r] for r in range(6)], axis=0) for t in range(6)
+        ]
+        return jnp.concatenate(tiles, axis=1)
+
     for ref in (g3, g2):
         z = jnp.zeros((HID, NZ), BF16)
         for X in range(ref.shape[0]):
@@ -452,26 +469,29 @@
 
     bias_c = weight_grad(g3, 2, H2, 1)
 
-    def back2(X):
+    def back2(i):
+        X = 2 * i
         for j in range(5):
             y = 1 + 2 * j
-            Y = dot_nn(wct_ref[...], taps(g3, X + 1, y))
-            for k in range(2):
-                row = gy * 2 + 2 * j + k
-                g2[X, y + k] = (lane_taps(Y, k) * sbuf[S2 + 12 * X + row]).astype(BF16)
-
-    planes(4, back2)
+            Y = dot_nn(lhs_at(WC), pair_taps(g3, X + 1, y))
+            for d in range(2):
+                for k in range(2):
+                    row = gy * 2 + 2 * j + k
+                    g2[X + d, y + k] = (
+                        lane_taps(Y, d, k) * sbuf[S2 + 12 * (X + d) + row]
+                    ).astype(BF16)
+
+    planes(2, back2)
     bias_b = weight_grad(g2, 1, H1, 0)
 
-    def back1(X):
-        for j in range(4):
-            y = own + 2 * j
-            Y = dot_nn(wbt_ref[...], taps(g2, X + 1, y))
+    for j in range(4):
+        y = own + 2 * j
+        Y = dot_nn(lhs_at(WB), pair_taps(g2, 1, y))
+        for d in range(2):
             for k in range(2):
                 row = gy * 4 + 2 * j + k
-                g1[X, 2 * j + k] = (lane_taps(Y, k) * sbuf[S1 + 12 * X + row]).astype(BF16)
-
-    planes(2, back1)
+                g1[d, 2 * j + k] = (lane_taps(Y, d, k) * sbuf[S1 + 12 * d + row]).astype(BF16)
+
     bias_a = jnp.zeros((HID, NZ), F32)
     for i in range(16):
         X, dy = i // 8, i % 8
@@ -638,47 +658,63 @@
         compiler_params=params,
         name="payload",
     )(*map(off_chip, (loaded_fields, liquid_mask, density_class)))
+    lhs = shaped((6 * HID, 12 * HID), BF16)
+    turned = shaped((36, HID, NZ), BF16)
+    vector = pltpu.VMEM((1, HID), F32)
+
+    def layouts2(args):
+        return pl.pallas_call(
+            second_lhs_kernel,
+            out_shape=(shaped((HID, 144), BF16), lhs, turned),
+            in_specs=[hbm] * 2,
+            out_specs=(vmem,) * 3,
+            scratch_shapes=[
+                pltpu.VMEM((27, HID, HID), BF16),
+                pltpu.VMEM((3, 27, HID), BF16),
+                pltpu.SemaphoreType.DMA((2,)),
+            ],
+            compiler_params=params,
+            name="lhs2",
+        )(*map(off_chip, args))
+
+    def layouts3(args):
+        return pl.pallas_call(
+            third_lhs_kernel,
+            out_shape=(lhs, turned, shaped((4, HID, NZ), F32)),
+            in_specs=[hbm] * 5,
+            out_specs=(vmem,) * 3,
+            scratch_shapes=[
+                pltpu.VMEM((27, HID, HID), BF16),
+                vector,
+                vector,
+                vector,
+                pltpu.VMEM((1, HID), BF16),
+                pltpu.SemaphoreType.DMA((5,)),
+            ],
+            compiler_params=params,
+            name="lhs3",
+        )(*map(off_chip, args))
+
+    jobs = [
+        (layouts2, (conv_b, conv_a.transpose(2, 0, 1))),
+        (layouts3, (conv_c, *(v.reshape(1, HID) for v in (bias_a, bias_b, bias_c, head_weight)))),
+    ]
+    made = []
     mine = block[None]
     bit = 2
-    while 2 * bit < count:
-        mine = gather_stage(mine, bit, me, count)
+    while bit < count:
+        if bit > 2 and jobs:
+            job, args = jobs.pop(0)
+            mine, args = lax.optimization_barrier((mine, args))
+            results = job(args)
+            mine = gather_stage(mine, bit, me, count)
+            mine, results = lax.optimization_barrier((mine, results))
+            made += results
+        else:
+            mine = gather_stage(mine, bit, me, count)
         bit *= 2
-    weights = (
-        conv_b,
-        conv_c,
-        conv_a.transpose(2, 0, 1),
-        *(v.reshape(1, HID) for v in (bias_a, bias_b, bias_c, head_weight)),
-    )
-    mine, weights = lax.optimization_barrier((mine, weights))
-    lhs = shaped((3 * HID, 9 * HID), BF16)
-    turned = shaped((15, HID, NZ), BF16)
-    made = pl.pallas_call(
-        lhs_kernel,
-        out_shape=(
-            shaped((HID, 144), BF16),
-            lhs,
-            lhs,
-            turned,
-            turned,
-            shaped((4, HID, NZ), F32),
-        ),
-        in_specs=[hbm] * 7,
-        out_specs=(vmem,) * 6,
-        scratch_shapes=[
-            pltpu.VMEM((27, HID, HID), BF16),
-            pltpu.VMEM((27, HID, HID), BF16),
-            pltpu.VMEM((3, 27, HID), BF16),
-            pltpu.VMEM((1, HID), F32),
-            pltpu.VMEM((1, HID), F32),
-            pltpu.VMEM((1, HID), F32),
-            pltpu.VMEM((1, HID), BF16),
-            pltpu.SemaphoreType.DMA((7,)),
-        ],
-        compiler_params=params,
-        name="lhs",
-    )(*map(off_chip, weights))
-    mine = gather_stage(mine, bit, me, count)
-    mine, made = lax.optimization_barrier((mine, made))
+    for job, args in jobs:
+        made += job(args)
     across = partner(mine, 1, count)
     wide = made[5]
 
@@ -705,7 +741,7 @@
             pltpu.VMEM((PLANES, YY, NZ), F32),
             pltpu.VMEM((PLANES, YY, HID, NZ), BF16),
             pltpu.VMEM((PLANES, YY, HID, NZ), BF16),
-            pltpu.VMEM((2, 10, HID, NZ), BF16),
+            pltpu.VMEM((6, 10, HID, NZ), BF16),
             pltpu.VMEM((PLANES, YY, NZ), F32),
             pltpu.VMEM((PLANES, YY, NZ), F32),
         ],
@@ -721,10 +757,10 @@
         *made,
     )
 
+    swap2 = lax.ppermute(score, "gx", [(i, ((i + 1) ^ 1) - 1) for i in range(1, n_slots - 1)])
     swap1 = lax.ppermute(score, "gx", [(i, i ^ 1) for i in range(n_slots)])
-    swap2 = lax.ppermute(score, "gx", [(i, ((i + 1) ^ 1) - 1) for i in range(1, n_slots - 1)])
     scores = []
-    for value in (score, swap1, swap2):
+    for value in (score, swap2, swap1):
         scores += [value, partner(value, 1, count)]
 
     keep, send = pl.pallas_call(
@@ -740,8 +776,6 @@
             pltpu.VMEM((3 * HID, 16 * NZ), BF16),
             pltpu.VMEM((9 * HID, 16 * NZ), BF16),
             pltpu.VMEM((2, ROWS, NZ), F32),
-            pltpu.VMEM((3 * HID, 9 * HID), BF16),
-            pltpu.VMEM((3 * HID, 9 * HID), BF16),
         ],
         compiler_params=params,
         name="backward",

time: 79.7 us -> 76.5 us (0.960)
  Pallas kernels: 29.6 us -> 28 us
  waiting for transfers between devices: 22.8 us -> 22 us
    ppermute x14, starting transfers between devices: 21.2 us -> 17.6 us  [partner(): return lax.ppermute(value, AXES, [(i, i ^ bit) for i in range(count)])]
    ppermute x1, starting transfers between devices: 1.91 us -> 4.68 us  [on_device(): swap1 = lax.ppermute(score, 'gx', [(i, i ^ 1) for i in range(n_slots)])]
    pallas_call x1, Pallas kernels: 16.5 us -> 14.7 us  [on_device(): pl.pallas_call(functools.partial(forward_kernel, n_slots=n_slots, cells=c...]
    pallas_call x1 -> x2, Pallas kernels: 2.19 us -> 3.15 us  [the longest x1 1.6 us: layouts3(): pl.pallas_call(third_lhs_kernel, out_shape=(lhs, turned, shaped((4, HID,...]
    ppermute x14, waiting for transfers between devices: 21.7 us -> 20.9 us  [partner(): return lax.ppermute(value, AXES, [(i, i ^ bit) for i in range(count)])]
  transfers between devices with their start and end apart: 16 -> 16, of which waited for: 12 -> 12; matrix products, arithmetic and copies ran while one was open for 1% -> 2% of each run, Pallas kernels for 3% -> 4%
where the time goes in v4:
time: 76.5 us; the launch traced here: 76.2 us
  Pallas kernels  28 us (37%)
  starting transfers between devices  23 us (30%)
  waiting for transfers between devices  22 us (29%)
  between operations  1.47 us (2%)
  local copies, waits for them, and re-layouts  1.13 us (1%)
    ppermute x14, waiting for transfers between devices, partner(): return lax.ppermute(value, AXES, [(i, i ^ bit) for i in range(count)])  20.9 us
    ppermute x14, starting transfers between devices, partner(): return lax.ppermute(value, AXES, [(i, i ^ bit) for i in range(count)])  17.6 us
    pallas_call x1, Pallas kernels, on_device(): pl.pallas_call(functools.partial(forward_kernel, n_slots=n_slots, cells=c...  14.7 us
    pallas_call x1, Pallas kernels, on_device(): pl.pallas_call(backward_kernel, out_shape=(shaped((ROWS + 8, NZ), F32), s...  6.76 us
    ppermute x1, starting transfers between devices, on_device(): swap1 = lax.ppermute(score, 'gx', [(i, i ^ 1) for i in range(n_slots)])  4.68 us
    pallas_call x1, Pallas kernels, on_device(): pl.pallas_call(finish_kernel, out_shape=(weights, weights, shaped((3, 27,...  2.59 us
    pallas_call x1, Pallas kernels, layouts3(): pl.pallas_call(third_lhs_kernel, out_shape=(lhs, turned, shaped((4, HID,...  1.6 us
    pallas_call x1, Pallas kernels, layouts2(): pl.pallas_call(second_lhs_kernel, out_shape=(shaped((HID, 144), BF16), lh...  1.56 us
  transfers between devices with their start and end apart: 16, of which 12 were waited for; matrix products, arithmetic and copies ran while one was open for 2% of the time, Pallas kernels for 4%

profile of v4, /device:TPU:0, one launch (start us, length us, event | category | flops | bytes accessed | tf_op | source)
XLA Modules:
  0.0 76.2 jit_solution(16307830754976688602)
XLA Ops:
  0.6 0.8 %payload.1 = bf16[2,8,4,128]{3,2,1,0:T(4,128)(2,1)S(1)} custom-call(bf16[2,2,8,128]{3,2,1,0:T(8,128)(2,1)} %fields_hbm.1, s32[2,8,128]{2,1,0:T(8,128)} %liquid_hbm.1, s32[2,8,128]{2,1,0:T(8,128)} %class_hbm.1), custom_call_target="tpu_custom_call" | custom-call | tf_op jit(solution)/shard_map/payload/pallas_call | solution.py:646
  1.4 3.0 %collective-permute-start = (bf16[1,2,8,4,128]{4,3,2,1,0:T(4,128)(2,1)S(1)}, bf16[1,2,8,4,128]{4,3,2,1,0:T(4,128)(2,1)S(1)}, u32[]{:S(2)}, u32[]{:S(2)}) collective-permute-start(bf16[1,2,8,4,128]{4,3,2,1,0:T(4,128)(2,1)S(1)} %bitcast.18), channel_id=1, source_target_pairs={{0,2},{1,3},{2,0},{3,1},{4,6},{5,7},{6,4},{7,5},{8,10},{9,11},{10,... | collective-permute-start | bytes 49160 | tf_op jit(solution)/shard_map/ppermute | solution.py:569
  4.5 1.7 %collective-permute-done = bf16[1,2,8,4,128]{4,3,2,1,0:T(4,128)(2,1)S(1)} collective-permute-done((bf16[1,2,8,4,128]{4,3,2,1,0:T(4,128)(2,1)S(1)}, bf16[1,2,8,4,128]{4,3,2,1,0:T(4,128)(2,1)S(1)}, u32[]{:S(2)}, u32[]{:S(2)}) %collective-permute-start) | collective-permute-done | bytes 16416 | tf_op jit(solution)/shard_map/ppermute | solution.py:569
  6.2 2.1 %collective-permute-start.1 = (bf16[2,2,8,4,128]{4,3,2,1,0:T(4,128)(2,1)S(1)}, bf16[2,2,8,4,128]{4,3,2,1,0:T(4,128)(2,1)S(1)}, u32[]{:S(2)}, u32[]{:S(2)}) collective-permute-start(bf16[2,2,8,4,128]{4,3,2,1,0:T(4,128)(2,1)S(1)} %maximum_select_fusion.2), channel_id=1, source_target_pairs={{0,4},{1,5},{2,6},{3,7},{4,0},{5,1},{6,2},{7,3},{8,12},{9,13},{10,... | collective-permute-start | bytes 98312 | tf_op jit(solution)/shard_map/ppermute | solution.py:569
  8.3 1.6 %lhs2.1 = (bf16[64,144]{1,0:T(8,128)(2,1)S(1)}, bf16[384,768]{1,0:T(8,128)(2,1)S(1)}, bf16[36,64,128]{2,1,0:T(8,128)(2,1)S(1)}) custom-call(bf16[27,64,64]{2,1,0:T(8,128)(2,1)} %wb_hbm, bf16[3,27,64]{2,1,0:T(8,128)(2,1)} %bitcast.20), custom_call_target="tpu_custom_call" | custom-call | tf_op jit(solution)/shard_map/lhs2/pallas_call | solution.py:666
  9.9 0.3 collective-permute-done.1
  10.3 3.1 %collective-permute-start.2 = (bf16[4,2,8,4,128]{4,3,2,1,0:T(4,128)(2,1)S(1)}, bf16[4,2,8,4,128]{4,3,2,1,0:T(4,128)(2,1)S(1)}, u32[]{:S(2)}, u32[]{:S(2)}) collective-permute-start(bf16[4,2,8,4,128]{4,3,2,1,0:T(4,128)(2,1)S(1)} %maximum_select_fusion.1), channel_id=1, source_target_pairs={{0,8},{1,9},{2,10},{3,11},{4,12},{5,13},{6,14},{7,15},{8,0},{9,1},... | collective-permute-start | bytes 196616 | tf_op jit(solution)/shard_map/ppermute | solution.py:569
  13.4 1.6 %lhs3.1 = (bf16[384,768]{1,0:T(8,128)(2,1)S(1)}, bf16[36,64,128]{2,1,0:T(8,128)(2,1)S(1)}, f32[4,64,128]{2,1,0:T(8,128)S(1)}) custom-call(bf16[27,64,64]{2,1,0:T(8,128)(2,1)} %wc_hbm, f32[1,64]{1,0:T(1,128)} %bitcast.21, f32[1,64]{1,0:T(1,128)} %bitcast.22, f32[1,64]{1,0:T(1,128)} %bitcast.23, bf16[1,64]{1,0:T(2,128)(2,1)} %bitcast.24), custom_call_target="tpu_custom_call" | custom-call | tf_op jit(solution)/shard_map/lhs3/pallas_call | solution.py:681
  15.0 0.6 collective-permute-done.2
  15.6 0.1 maximum_select_fusion.mine_ref
  16.6 0.6 collective-permute-done.3.other_ref
  17.2 14.7 %forward.1 = (f32[2,8,128]{2,1,0:T(8,128)}, f32[2,8,128]{2,1,0:T(8,128)S(1)}, f32[134,64,128]{2,1,0:T(8,128)S(1)}, bf16[180,64,128]{2,1,0:T(8,128)(2,1)S(1)}) custom-call(s32[2]{0:T(128)S(1)} %pad_add_fusion.pos_ref, s32[8]{0:T(128)} %home_hbm.1, f32[4]{0:T(128)} %invd_hbm.1, f32[1]{0:T(128)S(6)} %copy.22.hb_ref, ...), custom_call_target="tpu_custom_call" | custom-call | tf_op jit(solution)/shard_map/forward/pallas_call | solution.py:723
  31.9 0.7 collective-permute-start.5
  32.6 4.7 %collective-permute-start.7 = (f32[2,8,128]{2,1,0:T(8,128)S(1)}, f32[2,8,128]{2,1,0:T(8,128)S(1)}, u32[]{:S(2)}, u32[]{:S(2)}) collective-permute-start(f32[2,8,128]{2,1,0:T(8,128)S(1)} %get-tuple-element.65.gm_ref), channel_id=1, source_target_pairs={{0,2},{2,0},{4,6},{6,4},{8,10},{10,8},{12,14},{14,12},{1,3},{3,1},... | collective-permute-start | bytes 24584 | tf_op jit(solution)/shard_map/ppermute | solution.py:761
  37.3 0.5 collective-permute-start.6
  37.8 1.1 %collective-permute-done.7.p1_ref = f32[2,8,128]{2,1,0:T(8,128)S(1)} collective-permute-done((f32[2,8,128]{2,1,0:T(8,128)S(1)}, f32[2,8,128]{2,1,0:T(8,128)S(1)}, u32[]{:S(2)}, u32[]{:S(2)}) %collective-permute-start.7) | collective-permute-done | bytes 8224 | tf_op jit(solution)/shard_map/ppermute | solution.py:761
  38.9 1.2 %collective-permute-done.8.p1o_ref = f32[2,8,128]{2,1,0:T(8,128)S(1)} collective-permute-done((f32[2,8,128]{2,1,0:T(8,128)S(1)}, f32[2,8,128]{2,1,0:T(8,128)S(1)}, u32[]{:S(2)}, u32[]{:S(2)}) %collective-permute-start.8) | collective-permute-done | bytes 8224 | tf_op jit(solution)/shard_map/ppermute | solution.py:569
  40.1 6.8 %backward.1 = (f32[904,128]{1,0:T(8,128)S(1)}, f32[904,128]{1,0:T(8,128)S(1)}) custom-call(s32[2]{0:T(128)S(1)} %pad_add_fusion.pos_ref, f32[2,8,128]{2,1,0:T(8,128)S(1)} %get-tuple-element.65.gm_ref, f32[2,8,128]{2,1,0:T(8,128)S(1)} %collective-permute-done.4.gmo_ref, f32[2,8,128]{2,1,0:T(8,128)S(1)} %collective-permute-done.5.p2_ref, ...), custom_call_target="tpu_custom_call" | custom-call | tf_op jit(solution)/shard_map/backward/pallas_call | solution.py:766
  46.8 0.2 collective-permute-start.9
  47.1 1.7 %collective-permute-done.9 = f32[904,128]{1,0:T(8,128)S(1)} collective-permute-done((f32[904,128]{1,0:T(8,128)S(1)}, f32[904,128]{1,0:T(8,128)S(1)}, u32[]{:S(2)}, u32[]{:S(2)}) %collective-permute-start.9) | collective-permute-done | bytes 462880 | tf_op jit(solution)/shard_map/ppermute | solution.py:569
  48.9 2.1 %collective-permute-start.10 = (bf16[464,128]{1,0:T(8,128)(2,1)S(1)}, bf16[464,128]{1,0:T(8,128)(2,1)S(1)}, u32[]{:S(2)}, u32[]{:S(2)}) collective-permute-start(bf16[464,128]{1,0:T(8,128)(2,1)S(1)} %pad_maximum_fusion), channel_id=1, source_target_pairs={{0,2},{1,3},{2,0},{3,1},{4,6},{5,7},{6,4},{7,5},{8,10},{9,11},{10,... | collective-permute-start | bytes 356360 | tf_op jit(solution)/shard_map/ppermute | solution.py:569
  51.0 3.6 %collective-permute-done.10 = bf16[464,128]{1,0:T(8,128)(2,1)S(1)} collective-permute-done((bf16[464,128]{1,0:T(8,128)(2,1)S(1)}, bf16[464,128]{1,0:T(8,128)(2,1)S(1)}, u32[]{:S(2)}, u32[]{:S(2)}) %collective-permute-start.10) | collective-permute-done | bytes 118816 | tf_op jit(solution)/shard_map/ppermute | solution.py:569
  54.7 1.7 %collective-permute-start.11 = (bf16[464,128]{1,0:T(8,128)(2,1)S(1)}, bf16[464,128]{1,0:T(8,128)(2,1)S(1)}, u32[]{:S(2)}, u32[]{:S(2)}) collective-permute-start(bf16[464,128]{1,0:T(8,128)(2,1)S(1)} %pad_maximum_fusion.1), channel_id=1, source_target_pairs={{0,4},{1,5},{2,6},{3,7},{4,0},{5,1},{6,2},{7,3},{8,12},{9,13},{10,... | collective-permute-start | bytes 356360 | tf_op jit(solution)/shard_map/ppermute | solution.py:569
  56.4 3.2 %collective-permute-done.11 = bf16[464,128]{1,0:T(8,128)(2,1)S(1)} collective-permute-done((bf16[464,128]{1,0:T(8,128)(2,1)S(1)}, bf16[464,128]{1,0:T(8,128)(2,1)S(1)}, u32[]{:S(2)}, u32[]{:S(2)}) %collective-permute-start.11) | collective-permute-done | bytes 118816 | tf_op jit(solution)/shard_map/ppermute | solution.py:569
  59.7 3.2 %collective-permute-start.12 = (bf16[464,128]{1,0:T(8,128)(2,1)S(1)}, bf16[464,128]{1,0:T(8,128)(2,1)S(1)}, u32[]{:S(2)}, u32[]{:S(2)}) collective-permute-start(bf16[464,128]{1,0:T(8,128)(2,1)S(1)} %pad_maximum_fusion.2), channel_id=1, source_target_pairs={{0,8},{1,9},{2,10},{3,11},{4,12},{5,13},{6,14},{7,15},{8,0},{9,1},... | collective-permute-start | bytes 356360 | tf_op jit(solution)/shard_map/ppermute | solution.py:569
  62.9 4.4 %collective-permute-done.12 = bf16[464,128]{1,0:T(8,128)(2,1)S(1)} collective-permute-done((bf16[464,128]{1,0:T(8,128)(2,1)S(1)}, bf16[464,128]{1,0:T(8,128)(2,1)S(1)}, u32[]{:S(2)}, u32[]{:S(2)}) %collective-permute-start.12) | collective-permute-done | bytes 118816 | tf_op jit(solution)/shard_map/ppermute | solution.py:569
  67.4 1.5 %collective-permute-start.13 = (bf16[448,128]{1,0:T(8,128)(2,1)S(1)}, bf16[448,128]{1,0:T(8,128)(2,1)S(1)}, u32[]{:S(2)}, u32[]{:S(2)}) collective-permute-start(bf16[448,128]{1,0:T(8,128)(2,1)S(1)} %fusion.a_ref), channel_id=1, source_target_pairs={{0,2},{1,3},{2,0},{3,1},{4,6},{5,7},{6,4},{7,5},{8,10},{9,11},{10,... | collective-permute-start | bytes 344072 | tf_op jit(solution)/shard_map/ppermute | solution.py:569
  68.9 0.5 slice.58
  69.4 2.8 %collective-permute-done.13.b_ref = bf16[448,128]{1,0:T(8,128)(2,1)S(1)} collective-permute-done((bf16[448,128]{1,0:T(8,128)(2,1)S(1)}, bf16[448,128]{1,0:T(8,128)(2,1)S(1)}, u32[]{:S(2)}, u32[]{:S(2)}) %collective-permute-start.13) | collective-permute-done | bytes 114720 | tf_op jit(solution)/shard_map/ppermute | solution.py:569
  72.3 0.6 slice_bitcast_fusion
  72.9 0.7 collective-permute-done.15.d_ref
  73.6 2.6 %finish.1 = (f32[27,64,64]{2,1,0:T(8,128)}, f32[27,64,64]{2,1,0:T(8,128)}, f32[3,27,64]{2,1,0:T(8,128)}) custom-call(s32[2]{0:T(128)S(1)} %pad_add_fusion.pos_ref, bf16[448,128]{1,0:T(8,128)(2,1)S(1)} %fusion.a_ref, bf16[448,128]{1,0:T(8,128)(2,1)S(1)} %collective-permute-done.13.b_ref, bf16[448,128]{1,0:T(8,128)(2,1)S(1)} %collective-permute-done.14.c_ref, ...), custom_call_target="tpu_custom_call" | custom-call | tf_op jit(solution)/shard_map/finish/pallas_call | solution.py:792
  (30 shorter events, 0.6 us)
Async XLA Ops:
  1.4 4.8 %collective-permute-start = (bf16[1,2,8,4,128]{4,3,2,1,0:T(4,128)(2,1)S(1)}, bf16[1,2,8,4,128]{4,3,2,1,0:T(4,128)(2,1)S(1)}, u32[]{:S(2)}, u32[]{:S(2)}) collective-permute-start(bf16[1,2,8,4,128]{4,3,2,1,0:T(4,128)(2,1)S(1)} %bitcast.18), channel_id=1, source_target_pairs={{0,2},{1,3},{2,0},{3,1},{4,6},{5,7},{6,4},{7,5},{8,10},{9,11},{10,... | collective-permute-start | bytes 49160 | tf_op jit(solution)/shard_map/ppermute | solution.py:569
  6.2 4.0 %collective-permute-start.1 = (bf16[2,2,8,4,128]{4,3,2,1,0:T(4,128)(2,1)S(1)}, bf16[2,2,8,4,128]{4,3,2,1,0:T(4,128)(2,1)S(1)}, u32[]{:S(2)}, u32[]{:S(2)}) collective-permute-start(bf16[2,2,8,4,128]{4,3,2,1,0:T(4,128)(2,1)S(1)} %maximum_select_fusion.2), channel_id=1, source_target_pairs={{0,4},{1,5},{2,6},{3,7},{4,0},{5,1},{6,2},{7,3},{8,12},{9,13},{10,... | collective-permute-start | bytes 98312 | tf_op jit(solution)/shard_map/ppermute | solution.py:569
  10.3 5.3 %collective-permute-start.2 = (bf16[4,2,8,4,128]{4,3,2,1,0:T(4,128)(2,1)S(1)}, bf16[4,2,8,4,128]{4,3,2,1,0:T(4,128)(2,1)S(1)}, u32[]{:S(2)}, u32[]{:S(2)}) collective-permute-start(bf16[4,2,8,4,128]{4,3,2,1,0:T(4,128)(2,1)S(1)} %maximum_select_fusion.1), channel_id=1, source_target_pairs={{0,8},{1,9},{2,10},{3,11},{4,12},{5,13},{6,14},{7,15},{8,0},{9,1},... | collective-permute-start | bytes 196616 | tf_op jit(solution)/shard_map/ppermute | solution.py:569
  15.8 1.4 %collective-permute-start.3 = (bf16[8,2,8,4,128]{4,3,2,1,0:T(4,128)(2,1)S(1)}, bf16[8,2,8,4,128]{4,3,2,1,0:T(4,128)(2,1)S(1)}, u32[]{:S(2)}, u32[]{:S(2)}) collective-permute-start(bf16[8,2,8,4,128]{4,3,2,1,0:T(4,128)(2,1)S(1)} %maximum_select_fusion.mine_ref), channel_id=1, source_target_pairs={{0,1},{1,0},{2,3},{3,2},{4,5},{5,4},{6,7},{7,6},{8,9},{9,8},{10,11... | collective-permute-start | bytes 393224 | tf_op jit(solution)/shard_map/ppermute | solution.py:569
  31.9 5.4 %collective-permute-start.5 = (f32[2,8,128]{2,1,0:T(8,128)S(1)}, f32[2,8,128]{2,1,0:T(8,128)S(1)}, u32[]{:S(2)}, u32[]{:S(2)}) collective-permute-start(f32[2,8,128]{2,1,0:T(8,128)S(1)} %get-tuple-element.65.gm_ref), channel_id=1, source_target_pairs={{2,4},{4,2},{6,8},{8,6},{10,12},{12,10},{3,5},{5,3},{7,9},{9,7},{1... | collective-permute-start | bytes 24584 | tf_op jit(solution)/shard_map/ppermute | solution.py:760
  32.6 6.3 %collective-permute-start.7 = (f32[2,8,128]{2,1,0:T(8,128)S(1)}, f32[2,8,128]{2,1,0:T(8,128)S(1)}, u32[]{:S(2)}, u32[]{:S(2)}) collective-permute-start(f32[2,8,128]{2,1,0:T(8,128)S(1)} %get-tuple-element.65.gm_ref), channel_id=1, source_target_pairs={{0,2},{2,0},{4,6},{6,4},{8,10},{10,8},{12,14},{14,12},{1,3},{3,1},... | collective-permute-start | bytes 24584 | tf_op jit(solution)/shard_map/ppermute | solution.py:761
  37.3 1.6 %collective-permute-start.4 = (f32[2,8,128]{2,1,0:T(8,128)S(1)}, f32[2,8,128]{2,1,0:T(8,128)S(1)}, u32[]{:S(2)}, u32[]{:S(2)}) collective-permute-start(f32[2,8,128]{2,1,0:T(8,128)S(1)} %get-tuple-element.65.gm_ref), channel_id=1, source_target_pairs={{0,1},{1,0},{2,3},{3,2},{4,5},{5,4},{6,7},{7,6},{8,9},{9,8},{10,11... | collective-permute-start | bytes 24584 | tf_op jit(solution)/shard_map/ppermute | solution.py:569
  37.3 1.6 %collective-permute-start.6 = (f32[2,8,128]{2,1,0:T(8,128)S(1)}, f32[2,8,128]{2,1,0:T(8,128)S(1)}, u32[]{:S(2)}, u32[]{:S(2)}) collective-permute-start(f32[2,8,128]{2,1,0:T(8,128)S(1)} %collective-permute-done.5.p2_ref), channel_id=1, source_target_pairs={{0,1},{1,0},{2,3},{3,2},{4,5},{5,4},{6,7},{7,6},{8,9},{9,8},{10,11... | collective-permute-start | bytes 24584 | tf_op jit(solution)/shard_map/ppermute | solution.py:569
  38.9 1.2 %collective-permute-start.8 = (f32[2,8,128]{2,1,0:T(8,128)S(1)}, f32[2,8,128]{2,1,0:T(8,128)S(1)}, u32[]{:S(2)}, u32[]{:S(2)}) collective-permute-start(f32[2,8,128]{2,1,0:T(8,128)S(1)} %collective-permute-done.7.p1_ref), channel_id=1, source_target_pairs={{0,1},{1,0},{2,3},{3,2},{4,5},{5,4},{6,7},{7,6},{8,9},{9,8},{10,11... | collective-permute-start | bytes 24584 | tf_op jit(solution)/shard_map/ppermute | solution.py:569
  46.8 1.9 %collective-permute-start.9 = (f32[904,128]{1,0:T(8,128)S(1)}, f32[904,128]{1,0:T(8,128)S(1)}, u32[]{:S(2)}, u32[]{:S(2)}) collective-permute-start(f32[904,128]{1,0:T(8,128)S(1)} %get-tuple-element.69), channel_id=1, source_target_pairs={{0,1},{1,0},{2,3},{3,2},{4,5},{5,4},{6,7},{7,6},{8,9},{9,8},{10,11... | collective-permute-start | bytes 1388552 | tf_op jit(solution)/shard_map/ppermute | solution.py:569
  48.9 5.6 %collective-permute-start.10 = (bf16[464,128]{1,0:T(8,128)(2,1)S(1)}, bf16[464,128]{1,0:T(8,128)(2,1)S(1)}, u32[]{:S(2)}, u32[]{:S(2)}) collective-permute-start(bf16[464,128]{1,0:T(8,128)(2,1)S(1)} %pad_maximum_fusion), channel_id=1, source_target_pairs={{0,2},{1,3},{2,0},{3,1},{4,6},{5,7},{6,4},{7,5},{8,10},{9,11},{10,... | collective-permute-start | bytes 356360 | tf_op jit(solution)/shard_map/ppermute | solution.py:569
  54.7 4.9 %collective-permute-start.11 = (bf16[464,128]{1,0:T(8,128)(2,1)S(1)}, bf16[464,128]{1,0:T(8,128)(2,1)S(1)}, u32[]{:S(2)}, u32[]{:S(2)}) collective-permute-start(bf16[464,128]{1,0:T(8,128)(2,1)S(1)} %pad_maximum_fusion.1), channel_id=1, source_target_pairs={{0,4},{1,5},{2,6},{3,7},{4,0},{5,1},{6,2},{7,3},{8,12},{9,13},{10,... | collective-permute-start | bytes 356360 | tf_op jit(solution)/shard_map/ppermute | solution.py:569
  59.7 7.7 %collective-permute-start.12 = (bf16[464,128]{1,0:T(8,128)(2,1)S(1)}, bf16[464,128]{1,0:T(8,128)(2,1)S(1)}, u32[]{:S(2)}, u32[]{:S(2)}) collective-permute-start(bf16[464,128]{1,0:T(8,128)(2,1)S(1)} %pad_maximum_fusion.2), channel_id=1, source_target_pairs={{0,8},{1,9},{2,10},{3,11},{4,12},{5,13},{6,14},{7,15},{8,0},{9,1},... | collective-permute-start | bytes 356360 | tf_op jit(solution)/shard_map/ppermute | solution.py:569
  67.4 4.9 %collective-permute-start.13 = (bf16[448,128]{1,0:T(8,128)(2,1)S(1)}, bf16[448,128]{1,0:T(8,128)(2,1)S(1)}, u32[]{:S(2)}, u32[]{:S(2)}) collective-permute-start(bf16[448,128]{1,0:T(8,128)(2,1)S(1)} %fusion.a_ref), channel_id=1, source_target_pairs={{0,2},{1,3},{2,0},{3,1},{4,6},{5,7},{6,4},{7,5},{8,10},{9,11},{10,... | collective-permute-start | bytes 344072 | tf_op jit(solution)/shard_map/ppermute | solution.py:569
  68.9 4.0 %collective-permute-start.14 = (bf16[448,128]{1,0:T(8,128)(2,1)S(1)}, bf16[448,128]{1,0:T(8,128)(2,1)S(1)}, u32[]{:S(2)}, u32[]{:S(2)}) collective-permute-start(bf16[448,128]{1,0:T(8,128)(2,1)S(1)} %fusion.a_ref), channel_id=1, source_target_pairs={{0,1},{1,0},{2,3},{3,2},{4,5},{5,4},{6,7},{7,6},{8,9},{9,8},{10,11... | collective-permute-start | bytes 344072 | tf_op jit(solution)/shard_map/ppermute | solution.py:569
  72.3 1.3 %collective-permute-start.15 = (bf16[448,128]{1,0:T(8,128)(2,1)S(1)}, bf16[448,128]{1,0:T(8,128)(2,1)S(1)}, u32[]{:S(2)}, u32[]{:S(2)}) collective-permute-start(bf16[448,128]{1,0:T(8,128)(2,1)S(1)} %collective-permute-done.13.b_ref), channel_id=1, source_target_pairs={{0,1},{1,0},{2,3},{3,2},{4,5},{5,4},{6,7},{7,6},{8,9},{9,8},{10,11... | collective-permute-start | bytes 344072 | tf_op jit(solution)/shard_map/ppermute | solution.py:569

commit v5 on v4

--- a/solution.py
+++ b/solution.py
@@ -376,6 +376,51 @@
         hbuf[WC + r] = tc_ref[r]
 
 
+def stack_gradient(raw, gcat, cols):
+    g = raw.astype(F32)
+    gcat[0:HID, cols] = shift_left(g).astype(BF16)
+    gcat[HID : 2 * HID, cols] = raw
+    gcat[2 * HID : 3 * HID, cols] = shift_right(g).astype(BF16)
+    return g
+
+
+def store_weights(W, ref):
+    for a in range(3):
+        for b in range(3):
+            for e in range(3):
+                t = 9 * a + 3 * b + e
+                k = 3 * a + b
+                blk = W[e * HID : (e + 1) * HID, k * HID : (k + 1) * HID]
+                ref[t * 32 : (t + 1) * 32, 0:HID] = blk[:32]
+                ref[t * 32 : (t + 1) * 32, HID:NZ] = blk[32:]
+
+
+def early_kernel(pos_ref, score_ref, sbuf, hbuf, wide_ref, gc_ref, bias_ref, cat_ref, gcat, hcat):
+    gy = pos_ref[1]
+    own = gy * 2 + 1
+    bias = jnp.zeros((HID, NZ), F32)
+    for i in range(16):
+        X, dy = i // 8, i % 8
+        y = own + dy
+        g = score_ref[X, dy : dy + 1, :]
+        raw = (g * wide_ref[3] * sbuf[S3 + 10 * (X + 2) + y - 1]).astype(BF16)
+        cols = slice(i * NZ, (i + 1) * NZ)
+        bias += stack_gradient(raw, gcat, cols)
+        for a in range(3):
+            for b in range(3):
+                k = 3 * a + b
+                row = FRAME * (X + a) + y + b - 1
+                hcat[k * HID : (k + 1) * HID, cols] = hbuf[H2 + row]
+                cat_ref[k * HID : (k + 1) * HID, cols] = hbuf[H1 + row]
+                l = y + b - 1
+                q = l // 4
+                cat_ref[9 * HID + k * 16 : 9 * HID + (k + 1) * 16, cols] = hbuf[
+                    X0 + 3 * (X + a) + q, pl.ds(pl.multiple_of((l - 4 * q) * 16, 16), 16), :
+                ]
+    bias_ref[...] = bias
+    store_weights(dot_nt(gcat[...], hcat[...]), gc_ref)
+
+
 def backward_kernel(
     pos_ref,
     gm_ref,
@@ -387,6 +432,9 @@
     sbuf,
     hbuf,
     wide_ref,
+    gc_ref,
+    bias_ref,
+    cat_ref,
     keep_ref,
     send_ref,
     gs,
@@ -394,7 +442,6 @@
     g2,
     g1,
     gcat,
-    hcat,
     acc,
 ):
     gy = pos_ref[1]
@@ -409,6 +456,7 @@
             gs[k, half, :] = jnp.where(even, p2[k], p1[k])
             gs[2 + k, half, :] = gm[k]
             gs[4 + k, half, :] = jnp.where(even, p1[k], p2[k])
+
     def lhs_at(base):
         tiles = [
             jnp.concatenate([hbuf[base + 6 * t + r] for r in range(6)], axis=0) for t in range(6)
@@ -439,35 +487,6 @@
         for r in range(WROWS, ROWS, 8):
             acc[X, r : r + 8, :] = jnp.zeros((8, NZ), F32)
     own = gy * 2 + 1
-
-    def weight_grad(g_ref, g_off, h_base, which):
-        bias = jnp.zeros((HID, NZ), F32)
-        for i in range(16):
-            X, dy = i // 8, i % 8
-            y = own + dy
-            raw = g_ref[g_off + X, y]
-            g = raw.astype(F32)
-            bias += g
-            cols = slice(i * NZ, (i + 1) * NZ)
-            gcat[0:HID, cols] = shift_left(g).astype(BF16)
-            gcat[HID : 2 * HID, cols] = raw
-            gcat[2 * HID : 3 * HID, cols] = shift_right(g).astype(BF16)
-            for a in range(3):
-                for b in range(3):
-                    k = 3 * a + b
-                    hcat[k * HID : (k + 1) * HID, cols] = hbuf[h_base + FRAME * (X + a) + y + b - 1]
-        W = dot_nt(gcat[...], hcat[...])
-        for a in range(3):
-            for b in range(3):
-                for e in range(3):
-                    t = 9 * a + 3 * b + e
-                    k = 3 * a + b
-                    blk = W[e * HID : (e + 1) * HID, k * HID : (k + 1) * HID]
-                    acc[which, t * 32 : (t + 1) * 32, 0:HID] = blk[:32]
-                    acc[which, t * 32 : (t + 1) * 32, HID:NZ] = blk[32:]
-        return bias
-
-    bias_c = weight_grad(g3, 2, H2, 1)
 
     def back2(i):
         X = 2 * i
@@ -482,7 +501,11 @@
                     ).astype(BF16)
 
     planes(2, back2)
-    bias_b = weight_grad(g2, 1, H1, 0)
+    bias_b = jnp.zeros((HID, NZ), F32)
+    for i in range(16):
+        cols = slice(i * NZ, (i + 1) * NZ)
+        bias_b += stack_gradient(g2[1 + i // 8, own + i % 8], gcat, cols)
+    store_weights(dot_nt(gcat[...], cat_ref[0 : 9 * HID, :]), acc.at[0])
 
     for j in range(4):
         y = own + 2 * j
@@ -494,21 +517,10 @@
 
     bias_a = jnp.zeros((HID, NZ), F32)
     for i in range(16):
-        X, dy = i // 8, i % 8
-        y = own + dy
-        cols = slice(i * NZ, (i + 1) * NZ)
-        raw = g1[X, dy]
+        raw = g1[i // 8, i % 8]
         bias_a += raw.astype(F32)
-        gcat[0:HID, cols] = raw
-        for a in range(3):
-            for b in range(3):
-                k = 3 * a + b
-                l = y + b - 1
-                q = l // 4
-                hcat[k * 16 : (k + 1) * 16, cols] = hbuf[
-                    X0 + 3 * (X + a) + q, pl.ds(pl.multiple_of((l - 4 * q) * 16, 16), 16), :
-                ]
-    A = dot_nt(hcat[0:144, :], gcat[0:HID, :])
+        gcat[0:HID, i * NZ : (i + 1) * NZ] = raw
+    A = dot_nt(cat_ref[9 * HID : 9 * HID + 144, :], gcat[0:HID, :])
     for k in range(8):
         blk = A[16 * k : 16 * k + 12]
         which, spot = k // 4, k % 4
@@ -519,9 +531,10 @@
     acc[1, WROWS + 24 : WROWS + 28, HID:NZ] = A[136:140]
     sums = [
         jnp.sum(v, axis=1, keepdims=True).reshape(1, HID)
-        for v in (bias_a, bias_b, bias_c, sbuf[HEAD])
+        for v in (bias_a, bias_b, bias_ref[...], sbuf[HEAD])
     ]
     total = jnp.sum(jnp.sum(sbuf[LOSS, 0:8, :], axis=0, keepdims=True), axis=1, keepdims=True)
+    acc[1, 0:WROWS, :] = gc_ref[...]
     keep_ref[0:ROWS] = acc[gy]
     send_ref[0:ROWS] = acc[1 - gy]
     for ref in (keep_ref, send_ref):
@@ -533,35 +546,58 @@
         ref[ROWS + 2 : ROWS + 3, :] = jnp.broadcast_to(total, (1, NZ))
 
 
-def finish_kernel(pos_ref, a_ref, b_ref, c_ref, d_ref, gb_hbm, gc_hbm, ga_ref, stage, first, sems):
+def unpack_half(pos_ref, half, mine_ref, far_ref, stage, gb_hbm, gc_hbm, sems):
     gy = pos_ref[1]
-    upper = (pos_ref[0]) % 2
-
-    def unpack(ref, which, half):
+    for ref, which in ((mine_ref, gy), (far_ref, 1 - gy)):
         for j in range(14):
             v = ref[32 * j : 32 * j + 32].astype(F32)
-            stage[which, 14 * half + j, 0:32, :] = v[:, :HID]
-            stage[which, 14 * half + j, 32:HID, :] = v[:, HID:]
-
-    unpack(a_ref, gy, upper)
-    unpack(b_ref, gy, 1 - upper)
-    unpack(c_ref, 1 - gy, upper)
-    unpack(d_ref, 1 - gy, 1 - upper)
-    copies = [
-        pltpu.make_async_copy(stage.at[i, pl.ds(0, 27)], dst, sems.at[i])
+            stage[which, j, 0:32, :] = v[:, :HID]
+            stage[which, j, 32:HID, :] = v[:, HID:]
+    most = [
+        pltpu.make_async_copy(stage.at[i, pl.ds(0, 13)], dst.at[pl.ds(14 * half, 13)], sems.at[i])
         for i, dst in enumerate((gb_hbm, gc_hbm))
     ]
-    for copy in copies:
+    rest = [
+        pltpu.make_async_copy(stage.at[i, 13], dst.at[13], sems.at[2 + i])
+        for i, dst in enumerate((gb_hbm, gc_hbm))
+    ]
+    for copy in most:
         copy.start()
-    first[0:24] = stage[0, 27, 0:24]
-    first[24:48] = stage[0, 27, 32:56]
-    first[48:72] = stage[1, 27, 0:24]
-    first[72:96] = stage[1, 27, 32:56]
-    first[96:104] = stage[1, 27, 24:32]
-    first[104:108] = stage[1, 27, 56:60]
+
+    @pl.when(half == 0)
+    def _():
+        for copy in rest:
+            copy.start()
+        for copy in rest:
+            copy.wait()
+
+    return most
+
+
+def near_kernel(pos_ref, mine_ref, far_ref, gb_hbm, gc_hbm, extra_ref, stage, sems):
+    half = pos_ref[0] % 2
+    most = unpack_half(pos_ref, half, mine_ref, far_ref, stage, gb_hbm, gc_hbm, sems)
+    for i in range(2):
+        extra_ref[i] = stage[i, 13]
+    for copy in most:
+        copy.wait()
+
+
+def finish_kernel(
+    pos_ref, mine_ref, far_ref, extra_ref, gb_in, gc_in, gb_hbm, gc_hbm, ga_ref, stage, first, sems
+):
+    half = 1 - pos_ref[0] % 2
+    most = unpack_half(pos_ref, half, mine_ref, far_ref, stage, gb_hbm, gc_hbm, sems)
+    zero, one = [jnp.where(half == 1, stage[i, 13], extra_ref[i]) for i in range(2)]
+    first[0:24] = zero[0:24]
+    first[24:48] = zero[32:56]
+    first[48:72] = one[0:24]
+    first[72:96] = one[32:56]
+    first[96:104] = one[24:32]
+    first[104:108] = one[56:60]
     for ch in range(3):
         ga_ref[ch] = first[pl.ds(ch, 27, stride=4), :]
-    for copy in copies:
+    for copy in most:
         copy.wait()
 
 
@@ -607,7 +643,7 @@
     body = body.astype(BF16)
     beside = partner(body, 2, count)
     far = partner(body, 1, count)
-    return body, beside, far, partner(beside, 1, count), tail
+    return body, far, beside, tail
 
 
 def on_device(
@@ -759,14 +795,32 @@
 
     swap2 = lax.ppermute(score, "gx", [(i, ((i + 1) ^ 1) - 1) for i in range(1, n_slots - 1)])
     swap1 = lax.ppermute(score, "gx", [(i, i ^ 1) for i in range(n_slots)])
-    scores = []
-    for value in (score, swap2, swap1):
+    across_score = partner(score, 1, count)
+    early = pl.pallas_call(
+        early_kernel,
+        out_shape=(
+            shaped((WROWS, NZ), F32),
+            shaped((HID, NZ), F32),
+            shaped((9 * HID + 144, 16 * NZ), BF16),
+        ),
+        in_specs=[smem] + [vmem] * 4,
+        out_specs=(vmem,) * 3,
+        scratch_shapes=[
+            pltpu.VMEM((3 * HID, 16 * NZ), BF16),
+            pltpu.VMEM((9 * HID, 16 * NZ), BF16),
+        ],
+        compiler_params=params,
+        name="early",
+    )(pos, score, sbuf, hbuf, wide)
+    early, swap2, swap1 = lax.optimization_barrier((early, swap2, swap1))
+    scores = [score, across_score]
+    for value in (swap2, swap1):
         scores += [value, partner(value, 1, count)]
 
     keep, send = pl.pallas_call(
         backward_kernel,
         out_shape=(shaped((ROWS + 8, NZ), F32), shaped((ROWS + 8, NZ), F32)),
-        in_specs=[smem] + [vmem] * 9,
+        in_specs=[smem] + [vmem] * 12,
         out_specs=(vmem, vmem),
         scratch_shapes=[
             pltpu.VMEM((6, NY, NZ), F32),
@@ -774,7 +828,6 @@
             pltpu.VMEM((4, FRAME, HID, NZ), BF16),
             pltpu.VMEM((2, 8, HID, NZ), BF16),
             pltpu.VMEM((3 * HID, 16 * NZ), BF16),
-            pltpu.VMEM((9 * HID, 16 * NZ), BF16),
             pltpu.VMEM((2, ROWS, NZ), F32),
         ],
         compiler_params=params,
@@ -785,23 +838,37 @@
         sbuf,
         hbuf,
         wide,
+        *early,
     )
 
-    *pieces, tail = sum_all(keep, send, me, count)
+    body, far, beside, tail = sum_all(keep, send, me, count)
     weights = shaped((27, HID, HID), F32)
+    stage = pltpu.VMEM((2, 14, HID, HID), F32)
+    near = pl.pallas_call(
+        near_kernel,
+        out_shape=(weights, weights, shaped((2, HID, HID), F32)),
+        in_specs=[smem] + [vmem] * 2,
+        out_specs=(hbm, hbm, vmem),
+        scratch_shapes=[stage, pltpu.SemaphoreType.DMA((4,))],
+        compiler_params=params,
+        name="near",
+    )(pos, body, far)
+    near, beside = lax.optimization_barrier((near, beside))
+    half_b, half_c, extra = near
     grad_b, grad_c, grad_a = pl.pallas_call(
         finish_kernel,
         out_shape=(weights, weights, shaped((3, 27, HID), F32)),
-        in_specs=[smem] + [vmem] * 4,
+        in_specs=[smem] + [vmem] * 3 + [hbm] * 2,
         out_specs=(hbm, hbm, vmem),
         scratch_shapes=[
-            pltpu.VMEM((2, 28, HID, HID), F32),
+            stage,
             pltpu.VMEM((112, HID), F32),
-            pltpu.SemaphoreType.DMA((2,)),
+            pltpu.SemaphoreType.DMA((4,)),
         ],
+        input_output_aliases={4: 0, 5: 1},
         compiler_params=params,
         name="finish",
-    )(pos, *pieces)
+    )(pos, beside, partner(beside, 1, count), extra, half_b, half_c)
     return (
         pressure,
         tail[2, :1],

time: 76.5 us -> 76.2 us (level)
  Pallas kernels: 28 us -> 30.1 us
  waiting for transfers between devices: 22 us -> 20.4 us
  starting transfers between devices: 23 us -> 22.1 us
    pallas_call x0 -> x2, Pallas kernels: none -> 3.85 us  [the longest x1 2.22 us: on_device(): pl.pallas_call(early_kernel, out_shape=(shaped((WROWS, NZ), F32), shaped(...]
    pallas_call x1, Pallas kernels: 6.76 us -> 5.43 us  [on_device(): pl.pallas_call(backward_kernel, out_shape=(shaped((ROWS + 8, NZ), F32), s...]
    ppermute x1, waiting for transfers between devices: 1.12 us -> 0.01 us  [on_device(): swap1 = lax.ppermute(score, 'gx', [(i, i ^ 1) for i in range(n_slots)])]
    ppermute x14, starting transfers between devices: 17.6 us -> 16.7 us  [partner(): return lax.ppermute(value, AXES, [(i, i ^ bit) for i in range(count)])]
  transfers between devices with their start and end apart: 16 -> 16, of which waited for: 12 -> 12; matrix products, arithmetic and copies ran while one was open for 2% -> 2% of each run, Pallas kernels for 4% -> 9%
where the time goes in v5:
time: 76.2 us; the launch traced here: 75.9 us
  Pallas kernels  30.1 us (40%)
  starting transfers between devices  22.1 us (29%)
  waiting for transfers between devices  20.4 us (27%)
  between operations  1.5 us (2%)
  local copies, waits for them, and re-layouts  1.14 us (1%)
    ppermute x14, waiting for transfers between devices, partner(): return lax.ppermute(value, AXES, [(i, i ^ bit) for i in range(count)])  20.4 us
    ppermute x14, starting transfers between devices, partner(): return lax.ppermute(value, AXES, [(i, i ^ bit) for i in range(count)])  16.7 us
    pallas_call x1, Pallas kernels, on_device(): pl.pallas_call(functools.partial(forward_kernel, n_slots=n_slots, cells=c...  14.7 us
    pallas_call x1, Pallas kernels, on_device(): pl.pallas_call(backward_kernel, out_shape=(shaped((ROWS + 8, NZ), F32), s...  5.43 us
    ppermute x1, starting transfers between devices, on_device(): swap1 = lax.ppermute(score, 'gx', [(i, i ^ 1) for i in range(n_slots)])  4.68 us
    pallas_call x1, Pallas kernels, on_device(): pl.pallas_call(finish_kernel, out_shape=(weights, weights, shaped((3, 27,...  2.22 us
    pallas_call x1, Pallas kernels, on_device(): pl.pallas_call(early_kernel, out_shape=(shaped((WROWS, NZ), F32), shaped(...  2.22 us
    pallas_call x1, Pallas kernels, on_device(): pl.pallas_call(near_kernel, out_shape=(weights, weights, shaped((2, HID,...  1.62 us
  transfers between devices with their start and end apart: 16, of which 12 were waited for; matrix products, arithmetic and copies ran while one was open for 2% of the time, Pallas kernels for 9%

profile of v5, /device:TPU:0, one launch (start us, length us, event | category | flops | bytes accessed | tf_op | source)
XLA Modules:
  0.0 75.9 jit_solution(15082634963871385744)
XLA Ops:
  0.6 0.8 %payload.1 = bf16[2,8,4,128]{3,2,1,0:T(4,128)(2,1)S(1)} custom-call(bf16[2,2,8,128]{3,2,1,0:T(8,128)(2,1)} %fields_hbm.1, s32[2,8,128]{2,1,0:T(8,128)} %liquid_hbm.1, s32[2,8,128]{2,1,0:T(8,128)} %class_hbm.1), custom_call_target="tpu_custom_call" | custom-call | tf_op jit(solution)/shard_map/payload/pallas_call | solution.py:682
  1.4 3.0 %collective-permute-start = (bf16[1,2,8,4,128]{4,3,2,1,0:T(4,128)(2,1)S(1)}, bf16[1,2,8,4,128]{4,3,2,1,0:T(4,128)(2,1)S(1)}, u32[]{:S(2)}, u32[]{:S(2)}) collective-permute-start(bf16[1,2,8,4,128]{4,3,2,1,0:T(4,128)(2,1)S(1)} %bitcast.18), channel_id=1, source_target_pairs={{0,2},{1,3},{2,0},{3,1},{4,6},{5,7},{6,4},{7,5},{8,10},{9,11},{10,... | collective-permute-start | bytes 49160 | tf_op jit(solution)/shard_map/ppermute | solution.py:605
  4.5 1.7 %collective-permute-done = bf16[1,2,8,4,128]{4,3,2,1,0:T(4,128)(2,1)S(1)} collective-permute-done((bf16[1,2,8,4,128]{4,3,2,1,0:T(4,128)(2,1)S(1)}, bf16[1,2,8,4,128]{4,3,2,1,0:T(4,128)(2,1)S(1)}, u32[]{:S(2)}, u32[]{:S(2)}) %collective-permute-start) | collective-permute-done | bytes 16416 | tf_op jit(solution)/shard_map/ppermute | solution.py:605
  6.2 2.1 %collective-permute-start.1 = (bf16[2,2,8,4,128]{4,3,2,1,0:T(4,128)(2,1)S(1)}, bf16[2,2,8,4,128]{4,3,2,1,0:T(4,128)(2,1)S(1)}, u32[]{:S(2)}, u32[]{:S(2)}) collective-permute-start(bf16[2,2,8,4,128]{4,3,2,1,0:T(4,128)(2,1)S(1)} %maximum_select_fusion.2), channel_id=1, source_target_pairs={{0,4},{1,5},{2,6},{3,7},{4,0},{5,1},{6,2},{7,3},{8,12},{9,13},{10,... | collective-permute-start | bytes 98312 | tf_op jit(solution)/shard_map/ppermute | solution.py:605
  8.3 1.6 %lhs2.1 = (bf16[64,144]{1,0:T(8,128)(2,1)S(1)}, bf16[384,768]{1,0:T(8,128)(2,1)S(1)}, bf16[36,64,128]{2,1,0:T(8,128)(2,1)S(1)}) custom-call(bf16[27,64,64]{2,1,0:T(8,128)(2,1)} %wb_hbm, bf16[3,27,64]{2,1,0:T(8,128)(2,1)} %bitcast.20), custom_call_target="tpu_custom_call" | custom-call | tf_op jit(solution)/shard_map/lhs2/pallas_call | solution.py:702
  9.9 0.3 collective-permute-done.1
  10.3 3.1 %collective-permute-start.2 = (bf16[4,2,8,4,128]{4,3,2,1,0:T(4,128)(2,1)S(1)}, bf16[4,2,8,4,128]{4,3,2,1,0:T(4,128)(2,1)S(1)}, u32[]{:S(2)}, u32[]{:S(2)}) collective-permute-start(bf16[4,2,8,4,128]{4,3,2,1,0:T(4,128)(2,1)S(1)} %maximum_select_fusion.1), channel_id=1, source_target_pairs={{0,8},{1,9},{2,10},{3,11},{4,12},{5,13},{6,14},{7,15},{8,0},{9,1},... | collective-permute-start | bytes 196616 | tf_op jit(solution)/shard_map/ppermute | solution.py:605
  13.4 1.6 %lhs3.1 = (bf16[384,768]{1,0:T(8,128)(2,1)S(1)}, bf16[36,64,128]{2,1,0:T(8,128)(2,1)S(1)}, f32[4,64,128]{2,1,0:T(8,128)S(1)}) custom-call(bf16[27,64,64]{2,1,0:T(8,128)(2,1)} %wc_hbm, f32[1,64]{1,0:T(1,128)} %bitcast.21, f32[1,64]{1,0:T(1,128)} %bitcast.22, f32[1,64]{1,0:T(1,128)} %bitcast.23, bf16[1,64]{1,0:T(2,128)(2,1)} %bitcast.24), custom_call_target="tpu_custom_call" | custom-call | tf_op jit(solution)/shard_map/lhs3/pallas_call | solution.py:717
  15.0 0.6 collective-permute-done.2
  16.6 0.6 collective-permute-done.3.other_ref
  17.2 14.7 %forward.1 = (f32[2,8,128]{2,1,0:T(8,128)}, f32[2,8,128]{2,1,0:T(8,128)S(1)}, f32[134,64,128]{2,1,0:T(8,128)S(1)}, bf16[180,64,128]{2,1,0:T(8,128)(2,1)S(1)}) custom-call(s32[2]{0:T(128)S(1)} %pad_add_fusion.pos_ref, s32[8]{0:T(128)} %home_hbm.1, f32[4]{0:T(128)} %invd_hbm.1, f32[1]{0:T(128)S(6)} %copy.26.hb_ref, ...), custom_call_target="tpu_custom_call" | custom-call | tf_op jit(solution)/shard_map/forward/pallas_call | solution.py:759
  31.9 0.7 collective-permute-start.5
  32.6 4.7 %collective-permute-start.6 = (f32[2,8,128]{2,1,0:T(8,128)S(1)}, f32[2,8,128]{2,1,0:T(8,128)S(1)}, u32[]{:S(2)}, u32[]{:S(2)}) collective-permute-start(f32[2,8,128]{2,1,0:T(8,128)S(1)} %get-tuple-element.80.score_ref.gm_ref), channel_id=1, source_target_pairs={{0,2},{2,0},{4,6},{6,4},{8,10},{10,8},{12,14},{14,12},{1,3},{3,1},... | collective-permute-start | bytes 24584 | tf_op jit(solution)/shard_map/ppermute | solution.py:797
  37.3 2.2 %early.1 = (f32[864,128]{1,0:T(8,128)S(1)}, f32[64,128]{1,0:T(8,128)S(1)}, bf16[720,2048]{1,0:T(8,128)(2,1)S(1)}) custom-call(s32[2]{0:T(128)S(1)} %pad_add_fusion.pos_ref, f32[2,8,128]{2,1,0:T(8,128)S(1)} %get-tuple-element.80.score_ref.gm_ref, f32[134,64,128]{2,1,0:T(8,128)S(1)} %get-tuple-element.81.sbuf, ...), custom_call_target="tpu_custom_call" | custom-call | tf_op jit(solution)/shard_map/early/pallas_call | solution.py:799
  39.5 0.6 collective-permute-start.7
  40.2 0.7 collective-permute-done.7.p2o_ref
  40.9 0.3 collective-permute-done.8.p1o_ref
  41.2 5.4 %backward.1 = (f32[904,128]{1,0:T(8,128)S(1)}, f32[904,128]{1,0:T(8,128)S(1)}) custom-call(s32[2]{0:T(128)S(1)} %pad_add_fusion.pos_ref, f32[2,8,128]{2,1,0:T(8,128)S(1)} %get-tuple-element.80.score_ref.gm_ref, f32[2,8,128]{2,1,0:T(8,128)S(1)} %collective-permute-done.4.gmo_ref, f32[2,8,128]{2,1,0:T(8,128)S(1)} %collective-permute-done.5.p2_ref, ...), custom_call_target="tpu_custom_call" | custom-call | tf_op jit(solution)/shard_map/backward/pallas_call | solution.py:820
  46.9 1.7 %collective-permute-done.9 = f32[904,128]{1,0:T(8,128)S(1)} collective-permute-done((f32[904,128]{1,0:T(8,128)S(1)}, f32[904,128]{1,0:T(8,128)S(1)}, u32[]{:S(2)}, u32[]{:S(2)}) %collective-permute-start.9) | collective-permute-done | bytes 462880 | tf_op jit(solution)/shard_map/ppermute | solution.py:605
  48.7 1.0 %collective-permute-start.10 = (bf16[464,128]{1,0:T(8,128)(2,1)S(1)}, bf16[464,128]{1,0:T(8,128)(2,1)S(1)}, u32[]{:S(2)}, u32[]{:S(2)}) collective-permute-start(bf16[464,128]{1,0:T(8,128)(2,1)S(1)} %pad_maximum_fusion), channel_id=1, source_target_pairs={{0,2},{1,3},{2,0},{3,1},{4,6},{5,7},{6,4},{7,5},{8,10},{9,11},{10,... | collective-permute-start | bytes 356360 | tf_op jit(solution)/shard_map/ppermute | solution.py:605
  49.8 4.3 %collective-permute-done.10 = bf16[464,128]{1,0:T(8,128)(2,1)S(1)} collective-permute-done((bf16[464,128]{1,0:T(8,128)(2,1)S(1)}, bf16[464,128]{1,0:T(8,128)(2,1)S(1)}, u32[]{:S(2)}, u32[]{:S(2)}) %collective-permute-start.10) | collective-permute-done | bytes 118816 | tf_op jit(solution)/shard_map/ppermute | solution.py:605
  54.2 1.7 %collective-permute-start.11 = (bf16[464,128]{1,0:T(8,128)(2,1)S(1)}, bf16[464,128]{1,0:T(8,128)(2,1)S(1)}, u32[]{:S(2)}, u32[]{:S(2)}) collective-permute-start(bf16[464,128]{1,0:T(8,128)(2,1)S(1)} %pad_maximum_fusion.1), channel_id=1, source_target_pairs={{0,4},{1,5},{2,6},{3,7},{4,0},{5,1},{6,2},{7,3},{8,12},{9,13},{10,... | collective-permute-start | bytes 356360 | tf_op jit(solution)/shard_map/ppermute | solution.py:605
  55.9 3.2 %collective-permute-done.11 = bf16[464,128]{1,0:T(8,128)(2,1)S(1)} collective-permute-done((bf16[464,128]{1,0:T(8,128)(2,1)S(1)}, bf16[464,128]{1,0:T(8,128)(2,1)S(1)}, u32[]{:S(2)}, u32[]{:S(2)}) %collective-permute-start.11) | collective-permute-done | bytes 118816 | tf_op jit(solution)/shard_map/ppermute | solution.py:605
  59.2 3.3 %collective-permute-start.12 = (bf16[464,128]{1,0:T(8,128)(2,1)S(1)}, bf16[464,128]{1,0:T(8,128)(2,1)S(1)}, u32[]{:S(2)}, u32[]{:S(2)}) collective-permute-start(bf16[464,128]{1,0:T(8,128)(2,1)S(1)} %pad_maximum_fusion.2), channel_id=1, source_target_pairs={{0,8},{1,9},{2,10},{3,11},{4,12},{5,13},{6,14},{7,15},{8,0},{9,1},... | collective-permute-start | bytes 356360 | tf_op jit(solution)/shard_map/ppermute | solution.py:605
  62.5 4.1 %collective-permute-done.12 = bf16[464,128]{1,0:T(8,128)(2,1)S(1)} collective-permute-done((bf16[464,128]{1,0:T(8,128)(2,1)S(1)}, bf16[464,128]{1,0:T(8,128)(2,1)S(1)}, u32[]{:S(2)}, u32[]{:S(2)}) %collective-permute-start.12) | collective-permute-done | bytes 118816 | tf_op jit(solution)/shard_map/ppermute | solution.py:605
  66.8 1.5 %collective-permute-start.14 = (bf16[448,128]{1,0:T(8,128)(2,1)S(1)}, bf16[448,128]{1,0:T(8,128)(2,1)S(1)}, u32[]{:S(2)}, u32[]{:S(2)}) collective-permute-start(bf16[448,128]{1,0:T(8,128)(2,1)S(1)} %fusion.mine_ref), channel_id=1, source_target_pairs={{0,2},{1,3},{2,0},{3,1},{4,6},{5,7},{6,4},{7,5},{8,10},{9,11},{10,... | collective-permute-start | bytes 344072 | tf_op jit(solution)/shard_map/ppermute | solution.py:605
  68.2 0.5 slice.58
  68.7 1.6 %near.1 = (f32[27,64,64]{2,1,0:T(8,128)}, f32[27,64,64]{2,1,0:T(8,128)}, f32[2,64,64]{2,1,0:T(8,128)S(1)}) custom-call(s32[2]{0:T(128)S(1)} %pad_add_fusion.pos_ref, bf16[448,128]{1,0:T(8,128)(2,1)S(1)} %fusion.mine_ref, bf16[448,128]{1,0:T(8,128)(2,1)S(1)} %collective-permute-done.13.far_ref), custom_call_target="tpu_custom_call" | custom-call | tf_op jit(solution)/shard_map/near/pallas_call | solution.py:847
  70.4 2.0 %collective-permute-done.14.mine_ref = bf16[448,128]{1,0:T(8,128)(2,1)S(1)} collective-permute-done((bf16[448,128]{1,0:T(8,128)(2,1)S(1)}, bf16[448,128]{1,0:T(8,128)(2,1)S(1)}, u32[]{:S(2)}, u32[]{:S(2)}) %collective-permute-start.14) | collective-permute-done | bytes 114720 | tf_op jit(solution)/shard_map/ppermute | solution.py:605
  72.3 0.6 slice_bitcast_fusion
  72.9 0.7 collective-permute-done.15.far_ref
  73.6 2.2 %finish.1 = (f32[27,64,64]{2,1,0:T(8,128)}, f32[27,64,64]{2,1,0:T(8,128)}, f32[3,27,64]{2,1,0:T(8,128)}) custom-call(s32[2]{0:T(128)S(1)} %pad_add_fusion.pos_ref, bf16[448,128]{1,0:T(8,128)(2,1)S(1)} %collective-permute-done.14.mine_ref, bf16[448,128]{1,0:T(8,128)(2,1)S(1)} %collective-permute-done.15.far_ref, ...), custom_call_target="tpu_custom_call", output_to_operand_aliasing={{0}: (4, {}), {1}: (5, {})} | custom-call | tf_op jit(solution)/shard_map/finish/pallas_call | solution.py:858
  (32 shorter events, 1.2 us)
Async XLA Ops:
  1.4 4.8 %collective-permute-start = (bf16[1,2,8,4,128]{4,3,2,1,0:T(4,128)(2,1)S(1)}, bf16[1,2,8,4,128]{4,3,2,1,0:T(4,128)(2,1)S(1)}, u32[]{:S(2)}, u32[]{:S(2)}) collective-permute-start(bf16[1,2,8,4,128]{4,3,2,1,0:T(4,128)(2,1)S(1)} %bitcast.18), channel_id=1, source_target_pairs={{0,2},{1,3},{2,0},{3,1},{4,6},{5,7},{6,4},{7,5},{8,10},{9,11},{10,... | collective-permute-start | bytes 49160 | tf_op jit(solution)/shard_map/ppermute | solution.py:605
  6.2 4.0 %collective-permute-start.1 = (bf16[2,2,8,4,128]{4,3,2,1,0:T(4,128)(2,1)S(1)}, bf16[2,2,8,4,128]{4,3,2,1,0:T(4,128)(2,1)S(1)}, u32[]{:S(2)}, u32[]{:S(2)}) collective-permute-start(bf16[2,2,8,4,128]{4,3,2,1,0:T(4,128)(2,1)S(1)} %maximum_select_fusion.2), channel_id=1, source_target_pairs={{0,4},{1,5},{2,6},{3,7},{4,0},{5,1},{6,2},{7,3},{8,12},{9,13},{10,... | collective-permute-start | bytes 98312 | tf_op jit(solution)/shard_map/ppermute | solution.py:605
  10.3 5.3 %collective-permute-start.2 = (bf16[4,2,8,4,128]{4,3,2,1,0:T(4,128)(2,1)S(1)}, bf16[4,2,8,4,128]{4,3,2,1,0:T(4,128)(2,1)S(1)}, u32[]{:S(2)}, u32[]{:S(2)}) collective-permute-start(bf16[4,2,8,4,128]{4,3,2,1,0:T(4,128)(2,1)S(1)} %maximum_select_fusion.1), channel_id=1, source_target_pairs={{0,8},{1,9},{2,10},{3,11},{4,12},{5,13},{6,14},{7,15},{8,0},{9,1},... | collective-permute-start | bytes 196616 | tf_op jit(solution)/shard_map/ppermute | solution.py:605
  15.8 1.4 %collective-permute-start.3 = (bf16[8,2,8,4,128]{4,3,2,1,0:T(4,128)(2,1)S(1)}, bf16[8,2,8,4,128]{4,3,2,1,0:T(4,128)(2,1)S(1)}, u32[]{:S(2)}, u32[]{:S(2)}) collective-permute-start(bf16[8,2,8,4,128]{4,3,2,1,0:T(4,128)(2,1)S(1)} %maximum_select_fusion.mine_ref), channel_id=1, source_target_pairs={{0,1},{1,0},{2,3},{3,2},{4,5},{5,4},{6,7},{7,6},{8,9},{9,8},{10,11... | collective-permute-start | bytes 393224 | tf_op jit(solution)/shard_map/ppermute | solution.py:605
  31.9 7.6 %collective-permute-start.5 = (f32[2,8,128]{2,1,0:T(8,128)S(1)}, f32[2,8,128]{2,1,0:T(8,128)S(1)}, u32[]{:S(2)}, u32[]{:S(2)}) collective-permute-start(f32[2,8,128]{2,1,0:T(8,128)S(1)} %get-tuple-element.80.score_ref.gm_ref), channel_id=1, source_target_pairs={{2,4},{4,2},{6,8},{8,6},{10,12},{12,10},{3,5},{5,3},{7,9},{9,7},{1... | collective-permute-start | bytes 24584 | tf_op jit(solution)/shard_map/ppermute | solution.py:796
  32.6 6.9 %collective-permute-start.6 = (f32[2,8,128]{2,1,0:T(8,128)S(1)}, f32[2,8,128]{2,1,0:T(8,128)S(1)}, u32[]{:S(2)}, u32[]{:S(2)}) collective-permute-start(f32[2,8,128]{2,1,0:T(8,128)S(1)} %get-tuple-element.80.score_ref.gm_ref), channel_id=1, source_target_pairs={{0,2},{2,0},{4,6},{6,4},{8,10},{10,8},{12,14},{14,12},{1,3},{3,1},... | collective-permute-start | bytes 24584 | tf_op jit(solution)/shard_map/ppermute | solution.py:797
  37.2 2.9 %collective-permute-start.4 = (f32[2,8,128]{2,1,0:T(8,128)S(1)}, f32[2,8,128]{2,1,0:T(8,128)S(1)}, u32[]{:S(2)}, u32[]{:S(2)}) collective-permute-start(f32[2,8,128]{2,1,0:T(8,128)S(1)} %get-tuple-element.80.score_ref.gm_ref), channel_id=1, source_target_pairs={{0,1},{1,0},{2,3},{3,2},{4,5},{5,4},{6,7},{7,6},{8,9},{9,8},{10,11... | collective-permute-start | bytes 24584 | tf_op jit(solution)/shard_map/ppermute | solution.py:605
  39.5 1.4 %collective-permute-start.7 = (f32[2,8,128]{2,1,0:T(8,128)S(1)}, f32[2,8,128]{2,1,0:T(8,128)S(1)}, u32[]{:S(2)}, u32[]{:S(2)}) collective-permute-start(f32[2,8,128]{2,1,0:T(8,128)S(1)} %collective-permute-done.5.p2_ref), channel_id=1, source_target_pairs={{0,1},{1,0},{2,3},{3,2},{4,5},{5,4},{6,7},{7,6},{8,9},{9,8},{10,11... | collective-permute-start | bytes 24584 | tf_op jit(solution)/shard_map/ppermute | solution.py:605
  40.1 1.2 %collective-permute-start.8 = (f32[2,8,128]{2,1,0:T(8,128)S(1)}, f32[2,8,128]{2,1,0:T(8,128)S(1)}, u32[]{:S(2)}, u32[]{:S(2)}) collective-permute-start(f32[2,8,128]{2,1,0:T(8,128)S(1)} %collective-permute-done.6.p1_ref), channel_id=1, source_target_pairs={{0,1},{1,0},{2,3},{3,2},{4,5},{5,4},{6,7},{7,6},{8,9},{9,8},{10,11... | collective-permute-start | bytes 24584 | tf_op jit(solution)/shard_map/ppermute | solution.py:605
  46.7 1.9 %collective-permute-start.9 = (f32[904,128]{1,0:T(8,128)S(1)}, f32[904,128]{1,0:T(8,128)S(1)}, u32[]{:S(2)}, u32[]{:S(2)}) collective-permute-start(f32[904,128]{1,0:T(8,128)S(1)} %get-tuple-element.92), channel_id=1, source_target_pairs={{0,1},{1,0},{2,3},{3,2},{4,5},{5,4},{6,7},{7,6},{8,9},{9,8},{10,11... | collective-permute-start | bytes 1388552 | tf_op jit(solution)/shard_map/ppermute | solution.py:605
  48.7 5.4 %collective-permute-start.10 = (bf16[464,128]{1,0:T(8,128)(2,1)S(1)}, bf16[464,128]{1,0:T(8,128)(2,1)S(1)}, u32[]{:S(2)}, u32[]{:S(2)}) collective-permute-start(bf16[464,128]{1,0:T(8,128)(2,1)S(1)} %pad_maximum_fusion), channel_id=1, source_target_pairs={{0,2},{1,3},{2,0},{3,1},{4,6},{5,7},{6,4},{7,5},{8,10},{9,11},{10,... | collective-permute-start | bytes 356360 | tf_op jit(solution)/shard_map/ppermute | solution.py:605
  54.2 4.9 %collective-permute-start.11 = (bf16[464,128]{1,0:T(8,128)(2,1)S(1)}, bf16[464,128]{1,0:T(8,128)(2,1)S(1)}, u32[]{:S(2)}, u32[]{:S(2)}) collective-permute-start(bf16[464,128]{1,0:T(8,128)(2,1)S(1)} %pad_maximum_fusion.1), channel_id=1, source_target_pairs={{0,4},{1,5},{2,6},{3,7},{4,0},{5,1},{6,2},{7,3},{8,12},{9,13},{10,... | collective-permute-start | bytes 356360 | tf_op jit(solution)/shard_map/ppermute | solution.py:605
  59.2 7.4 %collective-permute-start.12 = (bf16[464,128]{1,0:T(8,128)(2,1)S(1)}, bf16[464,128]{1,0:T(8,128)(2,1)S(1)}, u32[]{:S(2)}, u32[]{:S(2)}) collective-permute-start(bf16[464,128]{1,0:T(8,128)(2,1)S(1)} %pad_maximum_fusion.2), channel_id=1, source_target_pairs={{0,8},{1,9},{2,10},{3,11},{4,12},{5,13},{6,14},{7,15},{8,0},{9,1},... | collective-permute-start | bytes 356360 | tf_op jit(solution)/shard_map/ppermute | solution.py:605
  66.7 2.1 %collective-permute-start.13 = (bf16[448,128]{1,0:T(8,128)(2,1)S(1)}, bf16[448,128]{1,0:T(8,128)(2,1)S(1)}, u32[]{:S(2)}, u32[]{:S(2)}) collective-permute-start(bf16[448,128]{1,0:T(8,128)(2,1)S(1)} %fusion.mine_ref), channel_id=1, source_target_pairs={{0,1},{1,0},{2,3},{3,2},{4,5},{5,4},{6,7},{7,6},{8,9},{9,8},{10,11... | collective-permute-start | bytes 344072 | tf_op jit(solution)/shard_map/ppermute | solution.py:605
  66.8 5.6 %collective-permute-start.14 = (bf16[448,128]{1,0:T(8,128)(2,1)S(1)}, bf16[448,128]{1,0:T(8,128)(2,1)S(1)}, u32[]{:S(2)}, u32[]{:S(2)}) collective-permute-start(bf16[448,128]{1,0:T(8,128)(2,1)S(1)} %fusion.mine_ref), channel_id=1, source_target_pairs={{0,2},{1,3},{2,0},{3,1},{4,6},{5,7},{6,4},{7,5},{8,10},{9,11},{10,... | collective-permute-start | bytes 344072 | tf_op jit(solution)/shard_map/ppermute | solution.py:605
  72.3 1.3 %collective-permute-start.15 = (bf16[448,128]{1,0:T(8,128)(2,1)S(1)}, bf16[448,128]{1,0:T(8,128)(2,1)S(1)}, u32[]{:S(2)}, u32[]{:S(2)}) collective-permute-start(bf16[448,128]{1,0:T(8,128)(2,1)S(1)} %collective-permute-done.14.mine_ref), channel_id=1, source_target_pairs={{0,1},{1,0},{2,3},{3,2},{4,5},{5,4},{6,7},{7,6},{8,9},{9,8},{10,11... | collective-permute-start | bytes 344072 | tf_op jit(solution)/shard_map/ppermute | solution.py:605

commit v6 on v5

--- a/solution.py
+++ b/solution.py
@@ -143,9 +143,13 @@
     bb_hbm,
     bc_hbm,
     hw_hbm,
+    home_hbm,
+    invd_hbm,
     fc,
     tc,
     wide_ref,
+    home_ref,
+    invd_ref,
     wc_ref,
     ba_ref,
     bb_ref,
@@ -162,6 +166,8 @@
                 (bb_hbm, bb_ref),
                 (bc_hbm, bc_ref),
                 (hw_hbm, hw_ref),
+                (home_hbm, home_ref),
+                (invd_hbm, invd_ref),
             )
         )
     ]
@@ -175,9 +181,8 @@
 
 
 def forward_kernel(
-    pos_ref,
-    home_hbm,
-    invd_hbm,
+    home_ref,
+    invd_ref,
     hb_ref,
     mine_ref,
     other_ref,
@@ -187,12 +192,11 @@
     wc_ref,
     tc_ref,
     wide_ref,
-    p_out,
+    p_hbm,
     gs_out,
     sbuf,
     hbuf,
-    home_ref,
-    invd_ref,
+    p_out,
     sems,
     inv_ref,
     x0s,
@@ -208,17 +212,8 @@
     n_slots,
     cells,
 ):
-    gx = pos_ref[0]
-    gy = pos_ref[1]
-    copies = [
-        pltpu.make_async_copy(src, dst, sems.at[i])
-        for i, (src, dst) in enumerate(
-            ((home_hbm, home_ref), (invd_hbm, invd_ref))
-        )
-    ]
-    for copy in copies:
-        copy.start()
-
+    gx = lax.axis_index("gx")
+    gy = lax.axis_index("gy")
     for ref in (x0s, h1, h2):
         z = jnp.zeros(ref.shape[2:], ref.dtype)
         for X in range(PLANES):
@@ -227,8 +222,6 @@
     for ref in (liq, scl, f1, pf, rs):
         for X in range(PLANES):
             ref[X] = jnp.zeros((YY, NZ), F32)
-    for copy in copies:
-        copy.wait()
     for s in range(n_slots):
         inv_ref[home_ref[s]] = s
 
@@ -346,6 +339,8 @@
         p_out[k] = pf[MID + k, own_y, :]
         r = rs[MID + k, own_y, :]
         loss += r * r
+    leave = pltpu.make_async_copy(p_out, p_hbm, sems.at[0])
+    leave.start()
     sbuf[LOSS, 0:8, :] = loss * (1.0 / cells)
     for X in range(MID - 1, MID + 3):
         rs[X] = rs[X] * (2.0 / cells)
@@ -374,6 +369,7 @@
     for r in range(36):
         hbuf[WB + r] = tb_ref[r]
         hbuf[WC + r] = tc_ref[r]
+    leave.wait()
 
 
 def stack_gradient(raw, gcat, cols):
@@ -395,8 +391,8 @@
                 ref[t * 32 : (t + 1) * 32, HID:NZ] = blk[32:]
 
 
-def early_kernel(pos_ref, score_ref, sbuf, hbuf, wide_ref, gc_ref, bias_ref, cat_ref, gcat, hcat):
-    gy = pos_ref[1]
+def early_kernel(score_ref, sbuf, hbuf, wide_ref, gc_ref, bias_ref, cat_ref, gcat, hcat):
+    gy = lax.axis_index("gy")
     own = gy * 2 + 1
     bias = jnp.zeros((HID, NZ), F32)
     for i in range(16):
@@ -422,7 +418,6 @@
 
 
 def backward_kernel(
-    pos_ref,
     gm_ref,
     gmo_ref,
     p2_ref,
@@ -444,8 +439,8 @@
     gcat,
     acc,
 ):
-    gy = pos_ref[1]
-    even = pos_ref[0] % 2 == 0
+    gy = lax.axis_index("gy")
+    even = lax.axis_index("gx") % 2 == 0
     own_half = pl.ds(pl.multiple_of(8 * gy, 8), 8)
     far_half = pl.ds(pl.multiple_of(8 - 8 * gy, 8), 8)
     for half, gm, p1, p2 in (
@@ -546,8 +541,8 @@
         ref[ROWS + 2 : ROWS + 3, :] = jnp.broadcast_to(total, (1, NZ))
 
 
-def unpack_half(pos_ref, half, mine_ref, far_ref, stage, gb_hbm, gc_hbm, sems):
-    gy = pos_ref[1]
+def unpack_half(half, mine_ref, far_ref, stage, gb_hbm, gc_hbm, sems):
+    gy = lax.axis_index("gy")
     for ref, which in ((mine_ref, gy), (far_ref, 1 - gy)):
         for j in range(14):
             v = ref[32 * j : 32 * j + 32].astype(F32)
@@ -574,9 +569,9 @@
     return most
 
 
-def near_kernel(pos_ref, mine_ref, far_ref, gb_hbm, gc_hbm, extra_ref, stage, sems):
-    half = pos_ref[0] % 2
-    most = unpack_half(pos_ref, half, mine_ref, far_ref, stage, gb_hbm, gc_hbm, sems)
+def near_kernel(mine_ref, far_ref, gb_hbm, gc_hbm, extra_ref, stage, sems):
+    half = lax.axis_index("gx") % 2
+    most = unpack_half(half, mine_ref, far_ref, stage, gb_hbm, gc_hbm, sems)
     for i in range(2):
         extra_ref[i] = stage[i, 13]
     for copy in most:
@@ -584,10 +579,10 @@
 
 
 def finish_kernel(
-    pos_ref, mine_ref, far_ref, extra_ref, gb_in, gc_in, gb_hbm, gc_hbm, ga_ref, stage, first, sems
+    mine_ref, far_ref, extra_ref, gb_in, gc_in, gb_hbm, gc_hbm, ga_hbm, stage, first, ga_ref, sems
 ):
-    half = 1 - pos_ref[0] % 2
-    most = unpack_half(pos_ref, half, mine_ref, far_ref, stage, gb_hbm, gc_hbm, sems)
+    half = 1 - lax.axis_index("gx") % 2
+    most = unpack_half(half, mine_ref, far_ref, stage, gb_hbm, gc_hbm, sems)
     zero, one = [jnp.where(half == 1, stage[i, 13], extra_ref[i]) for i in range(2)]
     first[0:24] = zero[0:24]
     first[24:48] = zero[32:56]
@@ -597,6 +592,9 @@
     first[104:108] = one[56:60]
     for ch in range(3):
         ga_ref[ch] = first[pl.ds(ch, 27, stride=4), :]
+    last = pltpu.make_async_copy(ga_ref, ga_hbm, sems.at[4])
+    last.start()
+    last.wait()
     for copy in most:
         copy.wait()
 
@@ -716,16 +714,22 @@
     def layouts3(args):
         return pl.pallas_call(
             third_lhs_kernel,
-            out_shape=(lhs, turned, shaped((4, HID, NZ), F32)),
-            in_specs=[hbm] * 5,
-            out_specs=(vmem,) * 3,
+            out_shape=(
+                lhs,
+                turned,
+                shaped((4, HID, NZ), F32),
+                pltpu.SMEM((n_slots,), jnp.int32),
+                pltpu.SMEM((4,), F32),
+            ),
+            in_specs=[hbm] * 7,
+            out_specs=(vmem,) * 3 + (smem,) * 2,
             scratch_shapes=[
                 pltpu.VMEM((27, HID, HID), BF16),
                 vector,
                 vector,
                 vector,
                 pltpu.VMEM((1, HID), BF16),
-                pltpu.SemaphoreType.DMA((5,)),
+                pltpu.SemaphoreType.DMA((7,)),
             ],
             compiler_params=params,
             name="lhs3",
@@ -733,7 +737,15 @@
 
     jobs = [
         (layouts2, (conv_b, conv_a.transpose(2, 0, 1))),
-        (layouts3, (conv_c, *(v.reshape(1, HID) for v in (bias_a, bias_b, bias_c, head_weight)))),
+        (
+            layouts3,
+            (
+                conv_c,
+                *(v.reshape(1, HID) for v in (bias_a, bias_b, bias_c, head_weight)),
+                brick_home,
+                inverse_density,
+            ),
+        ),
     ]
     made = []
     mine = block[None]
@@ -753,8 +765,8 @@
         made += job(args)
     across = partner(mine, 1, count)
     wide = made[5]
-
-    pos = jnp.stack([gx, gy]).astype(jnp.int32)
+    home, table = [pltpu.with_memory_space_constraint(v, pltpu.SMEM) for v in made[6:]]
+
 
     pressure, score, sbuf, hbuf = pl.pallas_call(
         functools.partial(forward_kernel, n_slots=n_slots, cells=cells),
@@ -764,12 +776,11 @@
             shaped((S_BLOCKS, HID, NZ), F32),
             shaped((H_BLOCKS, HID, NZ), BF16),
         ),
-        in_specs=[smem] + [hbm] * 2 + [smem] + [vmem] * 8,
-        out_specs=(vmem,) * 4,
+        in_specs=[smem] * 3 + [vmem] * 8,
+        out_specs=(hbm,) + (vmem,) * 3,
         scratch_shapes=[
-            pltpu.SMEM((n_slots,), jnp.int32),
-            pltpu.SMEM((4,), F32),
-            pltpu.SemaphoreType.DMA((2,)),
+            pltpu.VMEM((2, 8, NZ), F32),
+            pltpu.SemaphoreType.DMA((1,)),
             pltpu.SMEM((n_slots,), jnp.int32),
             pltpu.VMEM((PLANES, YY, 16, NZ), BF16),
             pltpu.VMEM((PLANES, YY, NZ), F32),
@@ -784,13 +795,12 @@
         compiler_params=params,
         name="forward",
     )(
-        pos,
-        off_chip(brick_home),
-        off_chip(inverse_density),
+        home,
+        table,
         head_bias,
         mine,
         across,
-        *made,
+        *made[:6],
     )
 
     swap2 = lax.ppermute(score, "gx", [(i, ((i + 1) ^ 1) - 1) for i in range(1, n_slots - 1)])
@@ -803,7 +813,7 @@
             shaped((HID, NZ), F32),
             shaped((9 * HID + 144, 16 * NZ), BF16),
         ),
-        in_specs=[smem] + [vmem] * 4,
+        in_specs=[vmem] * 4,
         out_specs=(vmem,) * 3,
         scratch_shapes=[
             pltpu.VMEM((3 * HID, 16 * NZ), BF16),
@@ -811,7 +821,7 @@
         ],
         compiler_params=params,
         name="early",
-    )(pos, score, sbuf, hbuf, wide)
+    )(score, sbuf, hbuf, wide)
     early, swap2, swap1 = lax.optimization_barrier((early, swap2, swap1))
     scores = [score, across_score]
     for value in (swap2, swap1):
@@ -820,7 +830,7 @@
     keep, send = pl.pallas_call(
         backward_kernel,
         out_shape=(shaped((ROWS + 8, NZ), F32), shaped((ROWS + 8, NZ), F32)),
-        in_specs=[smem] + [vmem] * 12,
+        in_specs=[vmem] * 12,
         out_specs=(vmem, vmem),
         scratch_shapes=[
             pltpu.VMEM((6, NY, NZ), F32),
@@ -833,7 +843,6 @@
         compiler_params=params,
         name="backward",
     )(
-        pos,
         *scores,
         sbuf,
         hbuf,
@@ -847,28 +856,29 @@
     near = pl.pallas_call(
         near_kernel,
         out_shape=(weights, weights, shaped((2, HID, HID), F32)),
-        in_specs=[smem] + [vmem] * 2,
+        in_specs=[vmem] * 2,
         out_specs=(hbm, hbm, vmem),
         scratch_shapes=[stage, pltpu.SemaphoreType.DMA((4,))],
         compiler_params=params,
         name="near",
-    )(pos, body, far)
+    )(body, far)
     near, beside = lax.optimization_barrier((near, beside))
     half_b, half_c, extra = near
     grad_b, grad_c, grad_a = pl.pallas_call(
         finish_kernel,
         out_shape=(weights, weights, shaped((3, 27, HID), F32)),
-        in_specs=[smem] + [vmem] * 3 + [hbm] * 2,
-        out_specs=(hbm, hbm, vmem),
+        in_specs=[vmem] * 3 + [hbm] * 2,
+        out_specs=(hbm, hbm, hbm),
         scratch_shapes=[
             stage,
             pltpu.VMEM((112, HID), F32),
-            pltpu.SemaphoreType.DMA((4,)),
+            pltpu.VMEM((3, 27, HID), F32),
+            pltpu.SemaphoreType.DMA((5,)),
         ],
-        input_output_aliases={4: 0, 5: 1},
+        input_output_aliases={3: 0, 4: 1},
         compiler_params=params,
         name="finish",
-    )(pos, beside, partner(beside, 1, count), extra, half_b, half_c)
+    )(beside, partner(beside, 1, count), extra, half_b, half_c)
     return (
         pressure,
         tail[2, :1],

time: 76.2 us -> 73 us (0.958)
  Pallas kernels: 30.1 us -> 26.2 us
  starting transfers between devices: 22.1 us -> 23.2 us
    pallas_call x1, Pallas kernels: 14.7 us -> 13.5 us  [on_device(): pl.pallas_call(functools.partial(forward_kernel, n_slots=n_slots, cells=c...]
    ppermute x14, starting transfers between devices: 16.7 us -> 17.9 us  [partner(): return lax.ppermute(value, AXES, [(i, i ^ bit) for i in range(count)])]
    pallas_call x1, Pallas kernels: 2.22 us -> 1.08 us  [on_device(): pl.pallas_call(finish_kernel, out_shape=(weights, weights, shaped((3, 27,...]
  transfers between devices with their start and end apart: 16 -> 16, of which waited for: 12 -> 12; matrix products, arithmetic and copies ran while one was open for 2% -> 2% of each run, Pallas kernels for 9% -> 8%
where the time goes in v6:
time: 73 us; the launch traced here: 72.7 us
  Pallas kernels  26.2 us (36%)
  starting transfers between devices  23.2 us (32%)
  waiting for transfers between devices  20 us (27%)
  between operations  1.49 us (2%)
  local copies, waits for them, and re-layouts  1.14 us (2%)
    ppermute x14, waiting for transfers between devices, partner(): return lax.ppermute(value, AXES, [(i, i ^ bit) for i in range(count)])  20 us
    ppermute x14, starting transfers between devices, partner(): return lax.ppermute(value, AXES, [(i, i ^ bit) for i in range(count)])  17.9 us
    pallas_call x1, Pallas kernels, on_device(): pl.pallas_call(functools.partial(forward_kernel, n_slots=n_slots, cells=c...  13.5 us
    pallas_call x1, Pallas kernels, on_device(): pl.pallas_call(backward_kernel, out_shape=(shaped((ROWS + 8, NZ), F32), s...  4.93 us
    ppermute x1, starting transfers between devices, on_device(): swap1 = lax.ppermute(score, 'gx', [(i, i ^ 1) for i in range(n_slots)])  4.69 us
    pallas_call x1, Pallas kernels, on_device(): pl.pallas_call(early_kernel, out_shape=(shaped((WROWS, NZ), F32), shaped(...  1.66 us
    pallas_call x1, Pallas kernels, layouts3(): pl.pallas_call(third_lhs_kernel, out_shape=(lhs, turned, shaped((4, HID,...  1.63 us
    pallas_call x1, Pallas kernels, layouts2(): pl.pallas_call(second_lhs_kernel, out_shape=(shaped((HID, 144), BF16), lh...  1.56 us
  transfers between devices with their start and end apart: 16, of which 12 were waited for; matrix products, arithmetic and copies ran while one was open for 2% of the time, Pallas kernels for 8%

profile of v6, /device:TPU:0, one launch (start us, length us, event | category | flops | bytes accessed | tf_op | source)
XLA Modules:
  0.0 72.7 jit_solution(17113704004875990960)
XLA Ops:
  0.6 0.8 %payload.1 = bf16[2,8,4,128]{3,2,1,0:T(4,128)(2,1)S(1)} custom-call(bf16[2,2,8,128]{3,2,1,0:T(8,128)(2,1)} %fields_hbm.1, s32[2,8,128]{2,1,0:T(8,128)} %liquid_hbm.1, s32[2,8,128]{2,1,0:T(8,128)} %class_hbm.1), custom_call_target="tpu_custom_call" | custom-call | tf_op jit(solution)/shard_map/payload/pallas_call | solution.py:680
  1.4 3.0 %collective-permute-start = (bf16[1,2,8,4,128]{4,3,2,1,0:T(4,128)(2,1)S(1)}, bf16[1,2,8,4,128]{4,3,2,1,0:T(4,128)(2,1)S(1)}, u32[]{:S(2)}, u32[]{:S(2)}) collective-permute-start(bf16[1,2,8,4,128]{4,3,2,1,0:T(4,128)(2,1)S(1)} %bitcast.16), channel_id=1, source_target_pairs={{0,2},{1,3},{2,0},{3,1},{4,6},{5,7},{6,4},{7,5},{8,10},{9,11},{10,... | collective-permute-start | bytes 49160 | tf_op jit(solution)/shard_map/ppermute | solution.py:603
  4.5 1.7 %collective-permute-done = bf16[1,2,8,4,128]{4,3,2,1,0:T(4,128)(2,1)S(1)} collective-permute-done((bf16[1,2,8,4,128]{4,3,2,1,0:T(4,128)(2,1)S(1)}, bf16[1,2,8,4,128]{4,3,2,1,0:T(4,128)(2,1)S(1)}, u32[]{:S(2)}, u32[]{:S(2)}) %collective-permute-start) | collective-permute-done | bytes 16416 | tf_op jit(solution)/shard_map/ppermute | solution.py:603
  6.2 2.1 %collective-permute-start.1 = (bf16[2,2,8,4,128]{4,3,2,1,0:T(4,128)(2,1)S(1)}, bf16[2,2,8,4,128]{4,3,2,1,0:T(4,128)(2,1)S(1)}, u32[]{:S(2)}, u32[]{:S(2)}) collective-permute-start(bf16[2,2,8,4,128]{4,3,2,1,0:T(4,128)(2,1)S(1)} %maximum_select_fusion.2), channel_id=1, source_target_pairs={{0,4},{1,5},{2,6},{3,7},{4,0},{5,1},{6,2},{7,3},{8,12},{9,13},{10,... | collective-permute-start | bytes 98312 | tf_op jit(solution)/shard_map/ppermute | solution.py:603
  8.3 1.6 %lhs2.1 = (bf16[64,144]{1,0:T(8,128)(2,1)S(1)}, bf16[384,768]{1,0:T(8,128)(2,1)S(1)}, bf16[36,64,128]{2,1,0:T(8,128)(2,1)S(1)}) custom-call(bf16[27,64,64]{2,1,0:T(8,128)(2,1)} %wb_hbm, bf16[3,27,64]{2,1,0:T(8,128)(2,1)} %bitcast.18), custom_call_target="tpu_custom_call" | custom-call | tf_op jit(solution)/shard_map/lhs2/pallas_call | solution.py:700
  9.9 0.3 collective-permute-done.1
  10.3 3.1 %collective-permute-start.2 = (bf16[4,2,8,4,128]{4,3,2,1,0:T(4,128)(2,1)S(1)}, bf16[4,2,8,4,128]{4,3,2,1,0:T(4,128)(2,1)S(1)}, u32[]{:S(2)}, u32[]{:S(2)}) collective-permute-start(bf16[4,2,8,4,128]{4,3,2,1,0:T(4,128)(2,1)S(1)} %maximum_select_fusion.1), channel_id=1, source_target_pairs={{0,8},{1,9},{2,10},{3,11},{4,12},{5,13},{6,14},{7,15},{8,0},{9,1},... | collective-permute-start | bytes 196616 | tf_op jit(solution)/shard_map/ppermute | solution.py:603
  13.4 1.6 %lhs3.1 = (bf16[384,768]{1,0:T(8,128)(2,1)S(1)}, bf16[36,64,128]{2,1,0:T(8,128)(2,1)S(1)}, f32[4,64,128]{2,1,0:T(8,128)S(1)}, s32[8]{0:T(128)S(4)}, f32[4]{0:T(128)S(4)}) custom-call(bf16[27,64,64]{2,1,0:T(8,128)(2,1)} %wc_hbm, f32[1,64]{1,0:T(1,128)} %bitcast.19, f32[1,64]{1,0:T(1,128)} %bitcast.20, f32[1,64]{1,0:T(1,128)} %bitcast.21, ...), custom_call_target="tpu_custom_call" | custom-call | tf_op jit(solution)/shard_map/lhs3/pallas_call | solution.py:715
  15.0 0.6 collective-permute-done.2
  16.5 0.7 collective-permute-done.3.other_ref
  17.2 13.5 %forward.1 = (f32[2,8,128]{2,1,0:T(8,128)}, f32[2,8,128]{2,1,0:T(8,128)S(1)}, f32[134,64,128]{2,1,0:T(8,128)S(1)}, bf16[180,64,128]{2,1,0:T(8,128)(2,1)S(1)}) custom-call(s32[8]{0:T(128)S(4)} %get-tuple-element.82.home_ref, f32[4]{0:T(128)S(4)} %get-tuple-element.83.invd_ref, f32[1]{0:T(128)S(6)} %copy.26.hb_ref, ...), custom_call_target="tpu_custom_call" | custom-call | tf_op jit(solution)/shard_map/forward/pallas_call | solution.py:771
  30.7 0.7 collective-permute-start.5
  31.4 4.7 %collective-permute-start.6 = (f32[2,8,128]{2,1,0:T(8,128)S(1)}, f32[2,8,128]{2,1,0:T(8,128)S(1)}, u32[]{:S(2)}, u32[]{:S(2)}) collective-permute-start(f32[2,8,128]{2,1,0:T(8,128)S(1)} %get-tuple-element.92.score_ref.gm_ref), channel_id=1, source_target_pairs={{0,2},{2,0},{4,6},{6,4},{8,10},{10,8},{12,14},{14,12},{1,3},{3,1},... | collective-permute-start | bytes 24584 | tf_op jit(solution)/shard_map/ppermute | solution.py:807
  36.1 1.7 %early.1 = (f32[864,128]{1,0:T(8,128)S(1)}, f32[64,128]{1,0:T(8,128)S(1)}, bf16[720,2048]{1,0:T(8,128)(2,1)S(1)}) custom-call(f32[2,8,128]{2,1,0:T(8,128)S(1)} %get-tuple-element.92.score_ref.gm_ref, f32[134,64,128]{2,1,0:T(8,128)S(1)} %get-tuple-element.93.sbuf, bf16[180,64,128]{2,1,0:T(8,128)(2,1)S(1)} %get-tuple-element.94.hbuf, ...), custom_call_target="tpu_custom_call" | custom-call | tf_op jit(solution)/shard_map/early/pallas_call | solution.py:809
  37.8 0.6 collective-permute-start.7
  38.4 0.7 %collective-permute-done.7.p2o_ref = f32[2,8,128]{2,1,0:T(8,128)S(1)} collective-permute-done((f32[2,8,128]{2,1,0:T(8,128)S(1)}, f32[2,8,128]{2,1,0:T(8,128)S(1)}, u32[]{:S(2)}, u32[]{:S(2)}) %collective-permute-start.7) | collective-permute-done | bytes 8224 | tf_op jit(solution)/shard_map/ppermute | solution.py:603
  39.2 0.3 collective-permute-done.8.p1o_ref
  39.5 4.9 %backward.1 = (f32[904,128]{1,0:T(8,128)S(1)}, f32[904,128]{1,0:T(8,128)S(1)}) custom-call(f32[2,8,128]{2,1,0:T(8,128)S(1)} %get-tuple-element.92.score_ref.gm_ref, f32[2,8,128]{2,1,0:T(8,128)S(1)} %collective-permute-done.4.gmo_ref, f32[2,8,128]{2,1,0:T(8,128)S(1)} %collective-permute-done.5.p2_ref, f32[2,8,128]{2,1,0:T(8,128)S(1)} %collective-permute-done.7.p2o_ref, ...), custom_call_target="tpu_custom_call" | custom-call | tf_op jit(solution)/shard_map/backward/pallas_call | solution.py:830
  44.7 1.7 %collective-permute-done.9 = f32[904,128]{1,0:T(8,128)S(1)} collective-permute-done((f32[904,128]{1,0:T(8,128)S(1)}, f32[904,128]{1,0:T(8,128)S(1)}, u32[]{:S(2)}, u32[]{:S(2)}) %collective-permute-start.9) | collective-permute-done | bytes 462880 | tf_op jit(solution)/shard_map/ppermute | solution.py:603
  46.5 1.6 %collective-permute-start.10 = (bf16[464,128]{1,0:T(8,128)(2,1)S(1)}, bf16[464,128]{1,0:T(8,128)(2,1)S(1)}, u32[]{:S(2)}, u32[]{:S(2)}) collective-permute-start(bf16[464,128]{1,0:T(8,128)(2,1)S(1)} %pad_maximum_fusion), channel_id=1, source_target_pairs={{0,2},{1,3},{2,0},{3,1},{4,6},{5,7},{6,4},{7,5},{8,10},{9,11},{10,... | collective-permute-start | bytes 356360 | tf_op jit(solution)/shard_map/ppermute | solution.py:603
  48.1 3.8 %collective-permute-done.10 = bf16[464,128]{1,0:T(8,128)(2,1)S(1)} collective-permute-done((bf16[464,128]{1,0:T(8,128)(2,1)S(1)}, bf16[464,128]{1,0:T(8,128)(2,1)S(1)}, u32[]{:S(2)}, u32[]{:S(2)}) %collective-permute-start.10) | collective-permute-done | bytes 118816 | tf_op jit(solution)/shard_map/ppermute | solution.py:603
  52.0 1.7 %collective-permute-start.11 = (bf16[464,128]{1,0:T(8,128)(2,1)S(1)}, bf16[464,128]{1,0:T(8,128)(2,1)S(1)}, u32[]{:S(2)}, u32[]{:S(2)}) collective-permute-start(bf16[464,128]{1,0:T(8,128)(2,1)S(1)} %pad_maximum_fusion.1), channel_id=1, source_target_pairs={{0,4},{1,5},{2,6},{3,7},{4,0},{5,1},{6,2},{7,3},{8,12},{9,13},{10,... | collective-permute-start | bytes 356360 | tf_op jit(solution)/shard_map/ppermute | solution.py:603
  53.7 3.2 %collective-permute-done.11 = bf16[464,128]{1,0:T(8,128)(2,1)S(1)} collective-permute-done((bf16[464,128]{1,0:T(8,128)(2,1)S(1)}, bf16[464,128]{1,0:T(8,128)(2,1)S(1)}, u32[]{:S(2)}, u32[]{:S(2)}) %collective-permute-start.11) | collective-permute-done | bytes 118816 | tf_op jit(solution)/shard_map/ppermute | solution.py:603
  57.0 3.2 %collective-permute-start.12 = (bf16[464,128]{1,0:T(8,128)(2,1)S(1)}, bf16[464,128]{1,0:T(8,128)(2,1)S(1)}, u32[]{:S(2)}, u32[]{:S(2)}) collective-permute-start(bf16[464,128]{1,0:T(8,128)(2,1)S(1)} %pad_maximum_fusion.2), channel_id=1, source_target_pairs={{0,8},{1,9},{2,10},{3,11},{4,12},{5,13},{6,14},{7,15},{8,0},{9,1},... | collective-permute-start | bytes 356360 | tf_op jit(solution)/shard_map/ppermute | solution.py:603
  60.2 4.1 %collective-permute-done.12 = bf16[464,128]{1,0:T(8,128)(2,1)S(1)} collective-permute-done((bf16[464,128]{1,0:T(8,128)(2,1)S(1)}, bf16[464,128]{1,0:T(8,128)(2,1)S(1)}, u32[]{:S(2)}, u32[]{:S(2)}) %collective-permute-start.12) | collective-permute-done | bytes 118816 | tf_op jit(solution)/shard_map/ppermute | solution.py:603
  64.5 2.0 %collective-permute-start.14 = (bf16[448,128]{1,0:T(8,128)(2,1)S(1)}, bf16[448,128]{1,0:T(8,128)(2,1)S(1)}, u32[]{:S(2)}, u32[]{:S(2)}) collective-permute-start(bf16[448,128]{1,0:T(8,128)(2,1)S(1)} %fusion.mine_ref), channel_id=1, source_target_pairs={{0,2},{1,3},{2,0},{3,1},{4,6},{5,7},{6,4},{7,5},{8,10},{9,11},{10,... | collective-permute-start | bytes 344072 | tf_op jit(solution)/shard_map/ppermute | solution.py:603
  66.5 0.5 slice.58
  67.0 1.1 %near.1 = (f32[27,64,64]{2,1,0:T(8,128)}, f32[27,64,64]{2,1,0:T(8,128)}, f32[2,64,64]{2,1,0:T(8,128)S(1)}) custom-call(bf16[448,128]{1,0:T(8,128)(2,1)S(1)} %fusion.mine_ref, bf16[448,128]{1,0:T(8,128)(2,1)S(1)} %collective-permute-done.13.far_ref), custom_call_target="tpu_custom_call" | custom-call | tf_op jit(solution)/shard_map/near/pallas_call | solution.py:856
  68.1 2.1 %collective-permute-done.14.mine_ref = bf16[448,128]{1,0:T(8,128)(2,1)S(1)} collective-permute-done((bf16[448,128]{1,0:T(8,128)(2,1)S(1)}, bf16[448,128]{1,0:T(8,128)(2,1)S(1)}, u32[]{:S(2)}, u32[]{:S(2)}) %collective-permute-start.14) | collective-permute-done | bytes 114720 | tf_op jit(solution)/shard_map/ppermute | solution.py:603
  70.3 0.6 slice_bitcast_fusion
  70.8 0.7 %collective-permute-done.15.far_ref = bf16[448,128]{1,0:T(8,128)(2,1)S(1)} collective-permute-done((bf16[448,128]{1,0:T(8,128)(2,1)S(1)}, bf16[448,128]{1,0:T(8,128)(2,1)S(1)}, u32[]{:S(2)}, u32[]{:S(2)}) %collective-permute-start.15) | collective-permute-done | bytes 114720 | tf_op jit(solution)/shard_map/ppermute | solution.py:603
  71.6 1.1 %finish.1 = (f32[27,64,64]{2,1,0:T(8,128)}, f32[27,64,64]{2,1,0:T(8,128)}, f32[3,27,64]{2,1,0:T(8,128)}) custom-call(bf16[448,128]{1,0:T(8,128)(2,1)S(1)} %collective-permute-done.14.mine_ref, bf16[448,128]{1,0:T(8,128)(2,1)S(1)} %collective-permute-done.15.far_ref, ...), custom_call_target="tpu_custom_call", output_to_operand_aliasing={{0}: (3, {}), {1}: (4, {})} | custom-call | tf_op jit(solution)/shard_map/finish/pallas_call | solution.py:867
  (31 shorter events, 1.1 us)
Async XLA Ops:
  1.4 4.8 %collective-permute-start = (bf16[1,2,8,4,128]{4,3,2,1,0:T(4,128)(2,1)S(1)}, bf16[1,2,8,4,128]{4,3,2,1,0:T(4,128)(2,1)S(1)}, u32[]{:S(2)}, u32[]{:S(2)}) collective-permute-start(bf16[1,2,8,4,128]{4,3,2,1,0:T(4,128)(2,1)S(1)} %bitcast.16), channel_id=1, source_target_pairs={{0,2},{1,3},{2,0},{3,1},{4,6},{5,7},{6,4},{7,5},{8,10},{9,11},{10,... | collective-permute-start | bytes 49160 | tf_op jit(solution)/shard_map/ppermute | solution.py:603
  6.2 4.0 %collective-permute-start.1 = (bf16[2,2,8,4,128]{4,3,2,1,0:T(4,128)(2,1)S(1)}, bf16[2,2,8,4,128]{4,3,2,1,0:T(4,128)(2,1)S(1)}, u32[]{:S(2)}, u32[]{:S(2)}) collective-permute-start(bf16[2,2,8,4,128]{4,3,2,1,0:T(4,128)(2,1)S(1)} %maximum_select_fusion.2), channel_id=1, source_target_pairs={{0,4},{1,5},{2,6},{3,7},{4,0},{5,1},{6,2},{7,3},{8,12},{9,13},{10,... | collective-permute-start | bytes 98312 | tf_op jit(solution)/shard_map/ppermute | solution.py:603
  10.3 5.3 %collective-permute-start.2 = (bf16[4,2,8,4,128]{4,3,2,1,0:T(4,128)(2,1)S(1)}, bf16[4,2,8,4,128]{4,3,2,1,0:T(4,128)(2,1)S(1)}, u32[]{:S(2)}, u32[]{:S(2)}) collective-permute-start(bf16[4,2,8,4,128]{4,3,2,1,0:T(4,128)(2,1)S(1)} %maximum_select_fusion.1), channel_id=1, source_target_pairs={{0,8},{1,9},{2,10},{3,11},{4,12},{5,13},{6,14},{7,15},{8,0},{9,1},... | collective-permute-start | bytes 196616 | tf_op jit(solution)/shard_map/ppermute | solution.py:603
  15.8 1.4 %collective-permute-start.3 = (bf16[8,2,8,4,128]{4,3,2,1,0:T(4,128)(2,1)S(1)}, bf16[8,2,8,4,128]{4,3,2,1,0:T(4,128)(2,1)S(1)}, u32[]{:S(2)}, u32[]{:S(2)}) collective-permute-start(bf16[8,2,8,4,128]{4,3,2,1,0:T(4,128)(2,1)S(1)} %maximum_select_fusion.mine_ref), channel_id=1, source_target_pairs={{0,1},{1,0},{2,3},{3,2},{4,5},{5,4},{6,7},{7,6},{8,9},{9,8},{10,11... | collective-permute-start | bytes 393224 | tf_op jit(solution)/shard_map/ppermute | solution.py:603
  30.7 7.0 %collective-permute-start.5 = (f32[2,8,128]{2,1,0:T(8,128)S(1)}, f32[2,8,128]{2,1,0:T(8,128)S(1)}, u32[]{:S(2)}, u32[]{:S(2)}) collective-permute-start(f32[2,8,128]{2,1,0:T(8,128)S(1)} %get-tuple-element.92.score_ref.gm_ref), channel_id=1, source_target_pairs={{2,4},{4,2},{6,8},{8,6},{10,12},{12,10},{3,5},{5,3},{7,9},{9,7},{1... | collective-permute-start | bytes 24584 | tf_op jit(solution)/shard_map/ppermute | solution.py:806
  31.4 6.4 %collective-permute-start.6 = (f32[2,8,128]{2,1,0:T(8,128)S(1)}, f32[2,8,128]{2,1,0:T(8,128)S(1)}, u32[]{:S(2)}, u32[]{:S(2)}) collective-permute-start(f32[2,8,128]{2,1,0:T(8,128)S(1)} %get-tuple-element.92.score_ref.gm_ref), channel_id=1, source_target_pairs={{0,2},{2,0},{4,6},{6,4},{8,10},{10,8},{12,14},{14,12},{1,3},{3,1},... | collective-permute-start | bytes 24584 | tf_op jit(solution)/shard_map/ppermute | solution.py:807
  36.1 2.3 %collective-permute-start.4 = (f32[2,8,128]{2,1,0:T(8,128)S(1)}, f32[2,8,128]{2,1,0:T(8,128)S(1)}, u32[]{:S(2)}, u32[]{:S(2)}) collective-permute-start(f32[2,8,128]{2,1,0:T(8,128)S(1)} %get-tuple-element.92.score_ref.gm_ref), channel_id=1, source_target_pairs={{0,1},{1,0},{2,3},{3,2},{4,5},{5,4},{6,7},{7,6},{8,9},{9,8},{10,11... | collective-permute-start | bytes 24584 | tf_op jit(solution)/shard_map/ppermute | solution.py:603
  37.8 1.4 %collective-permute-start.7 = (f32[2,8,128]{2,1,0:T(8,128)S(1)}, f32[2,8,128]{2,1,0:T(8,128)S(1)}, u32[]{:S(2)}, u32[]{:S(2)}) collective-permute-start(f32[2,8,128]{2,1,0:T(8,128)S(1)} %collective-permute-done.5.p2_ref), channel_id=1, source_target_pairs={{0,1},{1,0},{2,3},{3,2},{4,5},{5,4},{6,7},{7,6},{8,9},{9,8},{10,11... | collective-permute-start | bytes 24584 | tf_op jit(solution)/shard_map/ppermute | solution.py:603
  38.3 1.2 %collective-permute-start.8 = (f32[2,8,128]{2,1,0:T(8,128)S(1)}, f32[2,8,128]{2,1,0:T(8,128)S(1)}, u32[]{:S(2)}, u32[]{:S(2)}) collective-permute-start(f32[2,8,128]{2,1,0:T(8,128)S(1)} %collective-permute-done.6.p1_ref), channel_id=1, source_target_pairs={{0,1},{1,0},{2,3},{3,2},{4,5},{5,4},{6,7},{7,6},{8,9},{9,8},{10,11... | collective-permute-start | bytes 24584 | tf_op jit(solution)/shard_map/ppermute | solution.py:603
  44.4 1.9 %collective-permute-start.9 = (f32[904,128]{1,0:T(8,128)S(1)}, f32[904,128]{1,0:T(8,128)S(1)}, u32[]{:S(2)}, u32[]{:S(2)}) collective-permute-start(f32[904,128]{1,0:T(8,128)S(1)} %get-tuple-element.104), channel_id=1, source_target_pairs={{0,1},{1,0},{2,3},{3,2},{4,5},{5,4},{6,7},{7,6},{8,9},{9,8},{10,11... | collective-permute-start | bytes 1388552 | tf_op jit(solution)/shard_map/ppermute | solution.py:603
  46.5 5.4 %collective-permute-start.10 = (bf16[464,128]{1,0:T(8,128)(2,1)S(1)}, bf16[464,128]{1,0:T(8,128)(2,1)S(1)}, u32[]{:S(2)}, u32[]{:S(2)}) collective-permute-start(bf16[464,128]{1,0:T(8,128)(2,1)S(1)} %pad_maximum_fusion), channel_id=1, source_target_pairs={{0,2},{1,3},{2,0},{3,1},{4,6},{5,7},{6,4},{7,5},{8,10},{9,11},{10,... | collective-permute-start | bytes 356360 | tf_op jit(solution)/shard_map/ppermute | solution.py:603
  52.0 4.9 %collective-permute-start.11 = (bf16[464,128]{1,0:T(8,128)(2,1)S(1)}, bf16[464,128]{1,0:T(8,128)(2,1)S(1)}, u32[]{:S(2)}, u32[]{:S(2)}) collective-permute-start(bf16[464,128]{1,0:T(8,128)(2,1)S(1)} %pad_maximum_fusion.1), channel_id=1, source_target_pairs={{0,4},{1,5},{2,6},{3,7},{4,0},{5,1},{6,2},{7,3},{8,12},{9,13},{10,... | collective-permute-start | bytes 356360 | tf_op jit(solution)/shard_map/ppermute | solution.py:603
  57.0 7.4 %collective-permute-start.12 = (bf16[464,128]{1,0:T(8,128)(2,1)S(1)}, bf16[464,128]{1,0:T(8,128)(2,1)S(1)}, u32[]{:S(2)}, u32[]{:S(2)}) collective-permute-start(bf16[464,128]{1,0:T(8,128)(2,1)S(1)} %pad_maximum_fusion.2), channel_id=1, source_target_pairs={{0,8},{1,9},{2,10},{3,11},{4,12},{5,13},{6,14},{7,15},{8,0},{9,1},... | collective-permute-start | bytes 356360 | tf_op jit(solution)/shard_map/ppermute | solution.py:603
  64.5 2.6 %collective-permute-start.13 = (bf16[448,128]{1,0:T(8,128)(2,1)S(1)}, bf16[448,128]{1,0:T(8,128)(2,1)S(1)}, u32[]{:S(2)}, u32[]{:S(2)}) collective-permute-start(bf16[448,128]{1,0:T(8,128)(2,1)S(1)} %fusion.mine_ref), channel_id=1, source_target_pairs={{0,1},{1,0},{2,3},{3,2},{4,5},{5,4},{6,7},{7,6},{8,9},{9,8},{10,11... | collective-permute-start | bytes 344072 | tf_op jit(solution)/shard_map/ppermute | solution.py:603
  64.5 5.7 %collective-permute-start.14 = (bf16[448,128]{1,0:T(8,128)(2,1)S(1)}, bf16[448,128]{1,0:T(8,128)(2,1)S(1)}, u32[]{:S(2)}, u32[]{:S(2)}) collective-permute-start(bf16[448,128]{1,0:T(8,128)(2,1)S(1)} %fusion.mine_ref), channel_id=1, source_target_pairs={{0,2},{1,3},{2,0},{3,1},{4,6},{5,7},{6,4},{7,5},{8,10},{9,11},{10,... | collective-permute-start | bytes 344072 | tf_op jit(solution)/shard_map/ppermute | solution.py:603
  70.3 1.3 %collective-permute-start.15 = (bf16[448,128]{1,0:T(8,128)(2,1)S(1)}, bf16[448,128]{1,0:T(8,128)(2,1)S(1)}, u32[]{:S(2)}, u32[]{:S(2)}) collective-permute-start(bf16[448,128]{1,0:T(8,128)(2,1)S(1)} %collective-permute-done.14.mine_ref), channel_id=1, source_target_pairs={{0,1},{1,0},{2,3},{3,2},{4,5},{5,4},{6,7},{7,6},{8,9},{9,8},{10,11... | collective-permute-start | bytes 344072 | tf_op jit(solution)/shard_map/ppermute | solution.py:603

commit v7 on v6

--- a/solution.py
+++ b/solution.py
@@ -19,7 +19,7 @@
 FRAME = 12
 WROWS = 864
 ROWS = 896
-TAIL = 16
+SPLIT = 4
 VMEM_LIMIT = 24 * 1024 * 1024
 S1, S2, S3, HEAD, LOSS, S_BLOCKS = 0, 24, 72, 132, 133, 134
 H1, H2, X0, WB, WC, H_BLOCKS = 0, 48, 96, 108, 144, 180
@@ -53,14 +53,17 @@
     return jnp.concatenate(out, axis=0)
 
 
-def pair_taps(src, X, y):
+def pair_taps(src, X, y, n):
     out = []
     for b in range(3):
         for x in range(4):
-            out.append(
-                jnp.concatenate([src[X + x - 1, y + b - 1], src[X + x - 1, y + b]], axis=1)
-            )
+            rows = [src[X + x - 1, y + b - 1 + k] for k in range(n)]
+            out.append(jnp.concatenate(rows, axis=1) if n > 1 else rows[0])
     return jnp.concatenate(out, axis=0)
+
+
+def row_groups(count):
+    return [(j, min(2, count - j)) for j in range(0, count, 2)]
 
 
 def lane_taps(Y, d, k):
@@ -239,18 +242,19 @@
             mb = src[home, half, i % 8].astype(F32)
             y = 8 * (gy if i < 8 else 1 - gy) + i % 8
             lq = mb[2:3] * ok
-            cl = mb[3:4]
-            sc = jnp.zeros((1, NZ), F32)
-            for k in range(4):
-                sc = jnp.where(cl == k, invd_ref[k], sc)
             base = jnp.where(row4 < 2, fb, jnp.where(row4 == 2, mb * ok, 0.0))
             k12 = jnp.concatenate(
                 [shift_right(base), base, shift_left(base), jnp.zeros((4, NZ), F32)], axis=0
             )
             x0s[X, y + 1] = k12.astype(BF16)
             liq[X, pl.ds(y + 1, 1), :] = lq
-            scl[X, pl.ds(y + 1, 1), :] = sc * lq
+            scl[X, pl.ds(y + 1, 1), :] = mb[3:4]
             f1[X, pl.ds(y + 1, 1), :] = fb[1:2]
+        cl = scl[X, 1 : NY + 1, :]
+        sc = jnp.zeros((NY, NZ), F32)
+        for k in range(4):
+            sc = jnp.where(cl == k, invd_ref[k], sc)
+        scl[X, 1 : NY + 1, :] = sc * liq[X, 1 : NY + 1, :]
         return c
 
     lax.fori_loop(0, PLANES, load_plane, 0)
@@ -279,18 +283,20 @@
     planes(8, lambda i: layer1(1 + i + 2 * (i // 4), None))
     planes(2, lambda i: layer1(MID + i, i))
 
+    y3 = gy * 5 + 1
+
     def layer2(X, slot):
-        for j in range(6):
-            y = y4 + 2 * j
-            Y = dot_nn(wb_ref[...], pair_taps(h1, X, y))
+        for j, n in row_groups(11):
+            y = y3 + j
+            Y = dot_nn(wb_ref[...], pair_taps(h1, X, y, n))
             for d in range(2):
-                for k in range(2):
+                for k in range(n):
                     z = lane_taps(Y, d, k) + wide_ref[1]
                     m = liq[X + d, pl.ds(y + k, 1), :]
                     act, sig = activate(z)
                     h2[X + d, y + k] = (act * m).astype(BF16)
                     if slot is not None:
-                        sbuf[S2 + 12 * (slot + d) + 2 * j + k] = slope_of(z, sig) * m
+                        sbuf[S2 + 12 * (slot + d) + j + k] = slope_of(z, sig) * m
 
     planes(2, lambda i: layer2(2 + 6 * i, None))
     planes(2, lambda i: layer2(MID - 1 + 2 * i, 2 * i))
@@ -301,7 +307,7 @@
         X = MID - 2 + 2 * i
         for j in range(5):
             y = y2 + 2 * j
-            Y = dot_nn(wc_ref[...], pair_taps(h2, X, y))
+            Y = dot_nn(wc_ref[...], pair_taps(h2, X, y, 2))
             for d in range(2):
                 for k in range(2):
                     z = lane_taps(Y, d, k) + wide_ref[2]
@@ -389,6 +395,11 @@
                 blk = W[e * HID : (e + 1) * HID, k * HID : (k + 1) * HID]
                 ref[t * 32 : (t + 1) * 32, 0:HID] = blk[:32]
                 ref[t * 32 : (t + 1) * 32, HID:NZ] = blk[32:]
+
+
+def channel_sums(first, second):
+    rows = [jnp.sum(v, axis=1, keepdims=True).reshape(1, HID) for v in (first, second)]
+    return jnp.concatenate(rows, axis=1)
 
 
 def early_kernel(score_ref, sbuf, hbuf, wide_ref, gc_ref, bias_ref, cat_ref, gcat, hcat):
@@ -413,8 +424,11 @@
                 cat_ref[9 * HID + k * 16 : 9 * HID + (k + 1) * 16, cols] = hbuf[
                     X0 + 3 * (X + a) + q, pl.ds(pl.multiple_of((l - 4 * q) * 16, 16), 16), :
                 ]
-    bias_ref[...] = bias
     store_weights(dot_nt(gcat[...], hcat[...]), gc_ref)
+    loss = jnp.sum(jnp.sum(sbuf[LOSS, 0:8, :], axis=0, keepdims=True), axis=1, keepdims=True)
+    bias_ref[...] = jnp.zeros((8, NZ), F32)
+    bias_ref[1:2, :] = channel_sums(bias, sbuf[HEAD])
+    bias_ref[2:3, :] = jnp.broadcast_to(loss, (1, NZ))
 
 
 def backward_kernel(
@@ -485,12 +499,12 @@
 
     def back2(i):
         X = 2 * i
-        for j in range(5):
-            y = 1 + 2 * j
-            Y = dot_nn(lhs_at(WC), pair_taps(g3, X + 1, y))
+        for j, n in row_groups(9):
+            y = 1 + gy + j
+            Y = dot_nn(lhs_at(WC), pair_taps(g3, X + 1, y, n))
             for d in range(2):
-                for k in range(2):
-                    row = gy * 2 + 2 * j + k
+                for k in range(n):
+                    row = 2 * gy + j + k
                     g2[X + d, y + k] = (
                         lane_taps(Y, d, k) * sbuf[S2 + 12 * (X + d) + row]
                     ).astype(BF16)
@@ -504,7 +518,7 @@
 
     for j in range(4):
         y = own + 2 * j
-        Y = dot_nn(lhs_at(WB), pair_taps(g2, 1, y))
+        Y = dot_nn(lhs_at(WB), pair_taps(g2, 1, y, 2))
         for d in range(2):
             for k in range(2):
                 row = gy * 4 + 2 * j + k
@@ -524,21 +538,13 @@
         acc[which, r0 : r0 + 12, c0 : c0 + HID] = blk
     acc[1, WROWS + 24 : WROWS + 32, 0:HID] = A[128:136]
     acc[1, WROWS + 24 : WROWS + 28, HID:NZ] = A[136:140]
-    sums = [
-        jnp.sum(v, axis=1, keepdims=True).reshape(1, HID)
-        for v in (bias_a, bias_b, bias_ref[...], sbuf[HEAD])
-    ]
-    total = jnp.sum(jnp.sum(sbuf[LOSS, 0:8, :], axis=0, keepdims=True), axis=1, keepdims=True)
     acc[1, 0:WROWS, :] = gc_ref[...]
     keep_ref[0:ROWS] = acc[gy]
     send_ref[0:ROWS] = acc[1 - gy]
+    sums = channel_sums(bias_a, bias_b)
     for ref in (keep_ref, send_ref):
-        ref[ROWS : ROWS + 8, :] = jnp.zeros((8, NZ), F32)
-        for j in range(2):
-            ref[ROWS + j : ROWS + j + 1, :] = jnp.concatenate(
-                [sums[2 * j], sums[2 * j + 1]], axis=1
-            )
-        ref[ROWS + 2 : ROWS + 3, :] = jnp.broadcast_to(total, (1, NZ))
+        ref[ROWS : ROWS + 8, :] = bias_ref[...]
+        ref[ROWS : ROWS + 1, :] = sums
 
 
 def unpack_half(half, mine_ref, far_ref, stage, gb_hbm, gc_hbm, sems):
@@ -570,7 +576,7 @@
 
 
 def near_kernel(mine_ref, far_ref, gb_hbm, gc_hbm, extra_ref, stage, sems):
-    half = lax.axis_index("gx") % 2
+    half = lax.axis_index("gx") // (SPLIT // 2) % 2
     most = unpack_half(half, mine_ref, far_ref, stage, gb_hbm, gc_hbm, sems)
     for i in range(2):
         extra_ref[i] = stage[i, 13]
@@ -581,7 +587,7 @@
 def finish_kernel(
     mine_ref, far_ref, extra_ref, gb_in, gc_in, gb_hbm, gc_hbm, ga_hbm, stage, first, ga_ref, sems
 ):
-    half = 1 - lax.axis_index("gx") % 2
+    half = 1 - lax.axis_index("gx") // (SPLIT // 2) % 2
     most = unpack_half(half, mine_ref, far_ref, stage, gb_hbm, gc_hbm, sems)
     zero, one = [jnp.where(half == 1, stage[i, 13], extra_ref[i]) for i in range(2)]
     first[0:24] = zero[0:24]
@@ -622,24 +628,25 @@
     total = keep + partner(send, 1, count)
     body, tail = total[:ROWS], total[ROWS:]
     half = ROWS // 2
-    upper = (me & 2) != 0
+    upper = (me & SPLIT) != 0
     high, low = two_parts(tail)
     away = lax.dynamic_slice_in_dim(body, jnp.where(upper, 0, half), half)
     sent = jnp.concatenate([rounded(away), high, low]).astype(BF16)
-    got = partner(sent, 2, count).astype(F32)
+    got = partner(sent, SPLIT, count).astype(F32)
     body = lax.dynamic_slice_in_dim(body, jnp.where(upper, half, 0), half) + got[:half]
     tail = tail + got[half : half + 8] + got[half + 8 :]
-    bit = 4
+    bit = 2
     while bit < count:
-        high, low = two_parts(tail)
-        body = rounded(body)
-        sent = jnp.concatenate([body, high, low]).astype(BF16)
-        got = partner(sent, bit, count).astype(F32)
-        body = body + got[:half]
-        tail = (high + low) + (got[half : half + 8] + got[half + 8 :])
+        if bit != SPLIT:
+            high, low = two_parts(tail)
+            body = rounded(body)
+            sent = jnp.concatenate([body, high, low]).astype(BF16)
+            got = partner(sent, bit, count).astype(F32)
+            body = body + got[:half]
+            tail = (high + low) + (got[half : half + 8] + got[half + 8 :])
         bit *= 2
     body = body.astype(BF16)
-    beside = partner(body, 2, count)
+    beside = partner(body, SPLIT, count)
     far = partner(body, 1, count)
     return body, far, beside, tail
 
@@ -810,7 +817,7 @@
         early_kernel,
         out_shape=(
             shaped((WROWS, NZ), F32),
-            shaped((HID, NZ), F32),
+            shaped((8, NZ), F32),
             shaped((9 * HID + 144, 16 * NZ), BF16),
         ),
         in_specs=[vmem] * 4,

time: 73 us -> 72.6 us (level)
  waiting for transfers between devices: 20 us -> 21.4 us
  starting transfers between devices: 23.2 us -> 21.9 us
    ppermute x14, starting transfers between devices: 17.9 us -> 16.5 us  [partner(): return lax.ppermute(value, AXES, [(i, i ^ bit) for i in range(count)])]
    ppermute x14, waiting for transfers between devices: 20 us -> 21.4 us  [partner(): return lax.ppermute(value, AXES, [(i, i ^ bit) for i in range(count)])]
  transfers between devices with their start and end apart: 16 -> 16, of which waited for: 12 -> 13; matrix products, arithmetic and copies ran while one was open for 2% -> 2% of each run, Pallas kernels for 8% -> 8%
where the time goes in v7:
time: 72.6 us; the launch traced here: 72.3 us
  Pallas kernels  25.9 us (36%)
  starting transfers between devices  21.9 us (30%)
  waiting for transfers between devices  21.4 us (29%)
  between operations  1.49 us (2%)
  local copies, waits for them, and re-layouts  1.14 us (2%)
    ppermute x14, waiting for transfers between devices, partner(): return lax.ppermute(value, AXES, [(i, i ^ bit) for i in range(count)])  21.4 us
    ppermute x14, starting transfers between devices, partner(): return lax.ppermute(value, AXES, [(i, i ^ bit) for i in range(count)])  16.5 us
    pallas_call x1, Pallas kernels, on_device(): pl.pallas_call(functools.partial(forward_kernel, n_slots=n_slots, cells=c...  13.2 us
    pallas_call x1, Pallas kernels, on_device(): pl.pallas_call(backward_kernel, out_shape=(shaped((ROWS + 8, NZ), F32), s...  4.93 us
    ppermute x1, starting transfers between devices, on_device(): swap1 = lax.ppermute(score, 'gx', [(i, i ^ 1) for i in range(n_slots)])  4.68 us
    pallas_call x1, Pallas kernels, on_device(): pl.pallas_call(early_kernel, out_shape=(shaped((WROWS, NZ), F32), shaped(...  1.68 us
    pallas_call x1, Pallas kernels, layouts3(): pl.pallas_call(third_lhs_kernel, out_shape=(lhs, turned, shaped((4, HID,...  1.63 us
    pallas_call x1, Pallas kernels, layouts2(): pl.pallas_call(second_lhs_kernel, out_shape=(shaped((HID, 144), BF16), lh...  1.56 us
  transfers between devices with their start and end apart: 16, of which 13 were waited for; matrix products, arithmetic and copies ran while one was open for 2% of the time, Pallas kernels for 8%

profile of v7, /device:TPU:0, one launch (start us, length us, event | category | flops | bytes accessed | tf_op | source)
XLA Modules:
  0.0 72.3 jit_solution(17706867511879368940)
XLA Ops:
  0.6 0.8 %payload.1 = bf16[2,8,4,128]{3,2,1,0:T(4,128)(2,1)S(1)} custom-call(bf16[2,2,8,128]{3,2,1,0:T(8,128)(2,1)} %fields_hbm.1, s32[2,8,128]{2,1,0:T(8,128)} %liquid_hbm.1, s32[2,8,128]{2,1,0:T(8,128)} %class_hbm.1), custom_call_target="tpu_custom_call" | custom-call | tf_op jit(solution)/shard_map/payload/pallas_call | solution.py:687
  1.4 3.0 %collective-permute-start = (bf16[1,2,8,4,128]{4,3,2,1,0:T(4,128)(2,1)S(1)}, bf16[1,2,8,4,128]{4,3,2,1,0:T(4,128)(2,1)S(1)}, u32[]{:S(2)}, u32[]{:S(2)}) collective-permute-start(bf16[1,2,8,4,128]{4,3,2,1,0:T(4,128)(2,1)S(1)} %bitcast.16), channel_id=1, source_target_pairs={{0,2},{1,3},{2,0},{3,1},{4,6},{5,7},{6,4},{7,5},{8,10},{9,11},{10,... | collective-permute-start | bytes 49160 | tf_op jit(solution)/shard_map/ppermute | solution.py:609
  4.5 1.7 %collective-permute-done = bf16[1,2,8,4,128]{4,3,2,1,0:T(4,128)(2,1)S(1)} collective-permute-done((bf16[1,2,8,4,128]{4,3,2,1,0:T(4,128)(2,1)S(1)}, bf16[1,2,8,4,128]{4,3,2,1,0:T(4,128)(2,1)S(1)}, u32[]{:S(2)}, u32[]{:S(2)}) %collective-permute-start) | collective-permute-done | bytes 16416 | tf_op jit(solution)/shard_map/ppermute | solution.py:609
  6.2 2.1 %collective-permute-start.1 = (bf16[2,2,8,4,128]{4,3,2,1,0:T(4,128)(2,1)S(1)}, bf16[2,2,8,4,128]{4,3,2,1,0:T(4,128)(2,1)S(1)}, u32[]{:S(2)}, u32[]{:S(2)}) collective-permute-start(bf16[2,2,8,4,128]{4,3,2,1,0:T(4,128)(2,1)S(1)} %maximum_select_fusion.2), channel_id=1, source_target_pairs={{0,4},{1,5},{2,6},{3,7},{4,0},{5,1},{6,2},{7,3},{8,12},{9,13},{10,... | collective-permute-start | bytes 98312 | tf_op jit(solution)/shard_map/ppermute | solution.py:609
  8.3 1.6 %lhs2.1 = (bf16[64,144]{1,0:T(8,128)(2,1)S(1)}, bf16[384,768]{1,0:T(8,128)(2,1)S(1)}, bf16[36,64,128]{2,1,0:T(8,128)(2,1)S(1)}) custom-call(bf16[27,64,64]{2,1,0:T(8,128)(2,1)} %wb_hbm, bf16[3,27,64]{2,1,0:T(8,128)(2,1)} %bitcast.18), custom_call_target="tpu_custom_call" | custom-call | tf_op jit(solution)/shard_map/lhs2/pallas_call | solution.py:707
  9.9 0.3 collective-permute-done.1
  10.3 3.1 %collective-permute-start.2 = (bf16[4,2,8,4,128]{4,3,2,1,0:T(4,128)(2,1)S(1)}, bf16[4,2,8,4,128]{4,3,2,1,0:T(4,128)(2,1)S(1)}, u32[]{:S(2)}, u32[]{:S(2)}) collective-permute-start(bf16[4,2,8,4,128]{4,3,2,1,0:T(4,128)(2,1)S(1)} %maximum_select_fusion.1), channel_id=1, source_target_pairs={{0,8},{1,9},{2,10},{3,11},{4,12},{5,13},{6,14},{7,15},{8,0},{9,1},... | collective-permute-start | bytes 196616 | tf_op jit(solution)/shard_map/ppermute | solution.py:609
  13.4 1.6 %lhs3.1 = (bf16[384,768]{1,0:T(8,128)(2,1)S(1)}, bf16[36,64,128]{2,1,0:T(8,128)(2,1)S(1)}, f32[4,64,128]{2,1,0:T(8,128)S(1)}, s32[8]{0:T(128)S(4)}, f32[4]{0:T(128)S(4)}) custom-call(bf16[27,64,64]{2,1,0:T(8,128)(2,1)} %wc_hbm, f32[1,64]{1,0:T(1,128)} %bitcast.19, f32[1,64]{1,0:T(1,128)} %bitcast.20, f32[1,64]{1,0:T(1,128)} %bitcast.21, ...), custom_call_target="tpu_custom_call" | custom-call | tf_op jit(solution)/shard_map/lhs3/pallas_call | solution.py:722
  15.0 0.6 collective-permute-done.2
  16.5 0.7 collective-permute-done.3.other_ref
  17.2 13.2 %forward.1 = (f32[2,8,128]{2,1,0:T(8,128)}, f32[2,8,128]{2,1,0:T(8,128)S(1)}, f32[134,64,128]{2,1,0:T(8,128)S(1)}, bf16[180,64,128]{2,1,0:T(8,128)(2,1)S(1)}) custom-call(s32[8]{0:T(128)S(4)} %get-tuple-element.82.home_ref, f32[4]{0:T(128)S(4)} %get-tuple-element.83.invd_ref, f32[1]{0:T(128)S(6)} %copy.26.hb_ref, ...), custom_call_target="tpu_custom_call" | custom-call | tf_op jit(solution)/shard_map/forward/pallas_call | solution.py:778
  30.4 0.7 collective-permute-start.5
  31.0 4.7 %collective-permute-start.6 = (f32[2,8,128]{2,1,0:T(8,128)S(1)}, f32[2,8,128]{2,1,0:T(8,128)S(1)}, u32[]{:S(2)}, u32[]{:S(2)}) collective-permute-start(f32[2,8,128]{2,1,0:T(8,128)S(1)} %get-tuple-element.92.score_ref.gm_ref), channel_id=1, source_target_pairs={{0,2},{2,0},{4,6},{6,4},{8,10},{10,8},{12,14},{14,12},{1,3},{3,1},... | collective-permute-start | bytes 24584 | tf_op jit(solution)/shard_map/ppermute | solution.py:814
  35.7 1.7 %early.1 = (f32[864,128]{1,0:T(8,128)S(1)}, f32[8,128]{1,0:T(8,128)S(1)}, bf16[720,2048]{1,0:T(8,128)(2,1)S(1)}) custom-call(f32[2,8,128]{2,1,0:T(8,128)S(1)} %get-tuple-element.92.score_ref.gm_ref, f32[134,64,128]{2,1,0:T(8,128)S(1)} %get-tuple-element.93.sbuf, bf16[180,64,128]{2,1,0:T(8,128)(2,1)S(1)} %get-tuple-element.94.hbuf, ...), custom_call_target="tpu_custom_call" | custom-call | tf_op jit(solution)/shard_map/early/pallas_call | solution.py:816
  37.4 0.6 collective-permute-start.7
  38.1 0.7 %collective-permute-done.7.p2o_ref = f32[2,8,128]{2,1,0:T(8,128)S(1)} collective-permute-done((f32[2,8,128]{2,1,0:T(8,128)S(1)}, f32[2,8,128]{2,1,0:T(8,128)S(1)}, u32[]{:S(2)}, u32[]{:S(2)}) %collective-permute-start.7) | collective-permute-done | bytes 8224 | tf_op jit(solution)/shard_map/ppermute | solution.py:609
  38.8 0.3 collective-permute-done.8.p1o_ref
  39.2 4.9 %backward.1 = (f32[904,128]{1,0:T(8,128)S(1)}, f32[904,128]{1,0:T(8,128)S(1)}) custom-call(f32[2,8,128]{2,1,0:T(8,128)S(1)} %get-tuple-element.92.score_ref.gm_ref, f32[2,8,128]{2,1,0:T(8,128)S(1)} %collective-permute-done.4.gmo_ref, f32[2,8,128]{2,1,0:T(8,128)S(1)} %collective-permute-done.5.p2_ref, f32[2,8,128]{2,1,0:T(8,128)S(1)} %collective-permute-done.7.p2o_ref, ...), custom_call_target="tpu_custom_call" | custom-call | tf_op jit(solution)/shard_map/backward/pallas_call | solution.py:837
  44.3 1.7 %collective-permute-done.9 = f32[904,128]{1,0:T(8,128)S(1)} collective-permute-done((f32[904,128]{1,0:T(8,128)S(1)}, f32[904,128]{1,0:T(8,128)S(1)}, u32[]{:S(2)}, u32[]{:S(2)}) %collective-permute-start.9) | collective-permute-done | bytes 462880 | tf_op jit(solution)/shard_map/ppermute | solution.py:609
  46.1 1.7 %collective-permute-start.10 = (bf16[464,128]{1,0:T(8,128)(2,1)S(1)}, bf16[464,128]{1,0:T(8,128)(2,1)S(1)}, u32[]{:S(2)}, u32[]{:S(2)}) collective-permute-start(bf16[464,128]{1,0:T(8,128)(2,1)S(1)} %pad_maximum_fusion), channel_id=1, source_target_pairs={{0,4},{1,5},{2,6},{3,7},{4,0},{5,1},{6,2},{7,3},{8,12},{9,13},{10,... | collective-permute-start | bytes 356360 | tf_op jit(solution)/shard_map/ppermute | solution.py:609
  47.9 3.7 %collective-permute-done.10 = bf16[464,128]{1,0:T(8,128)(2,1)S(1)} collective-permute-done((bf16[464,128]{1,0:T(8,128)(2,1)S(1)}, bf16[464,128]{1,0:T(8,128)(2,1)S(1)}, u32[]{:S(2)}, u32[]{:S(2)}) %collective-permute-start.10) | collective-permute-done | bytes 118816 | tf_op jit(solution)/shard_map/ppermute | solution.py:609
  51.6 1.8 %collective-permute-start.11 = (bf16[464,128]{1,0:T(8,128)(2,1)S(1)}, bf16[464,128]{1,0:T(8,128)(2,1)S(1)}, u32[]{:S(2)}, u32[]{:S(2)}) collective-permute-start(bf16[464,128]{1,0:T(8,128)(2,1)S(1)} %pad_maximum_fusion.1), channel_id=1, source_target_pairs={{0,2},{1,3},{2,0},{3,1},{4,6},{5,7},{6,4},{7,5},{8,10},{9,11},{10,... | collective-permute-start | bytes 356360 | tf_op jit(solution)/shard_map/ppermute | solution.py:609
  53.4 3.1 %collective-permute-done.11 = bf16[464,128]{1,0:T(8,128)(2,1)S(1)} collective-permute-done((bf16[464,128]{1,0:T(8,128)(2,1)S(1)}, bf16[464,128]{1,0:T(8,128)(2,1)S(1)}, u32[]{:S(2)}, u32[]{:S(2)}) %collective-permute-start.11) | collective-permute-done | bytes 118816 | tf_op jit(solution)/shard_map/ppermute | solution.py:609
  56.6 3.2 %collective-permute-start.12 = (bf16[464,128]{1,0:T(8,128)(2,1)S(1)}, bf16[464,128]{1,0:T(8,128)(2,1)S(1)}, u32[]{:S(2)}, u32[]{:S(2)}) collective-permute-start(bf16[464,128]{1,0:T(8,128)(2,1)S(1)} %pad_maximum_fusion.2), channel_id=1, source_target_pairs={{0,8},{1,9},{2,10},{3,11},{4,12},{5,13},{6,14},{7,15},{8,0},{9,1},... | collective-permute-start | bytes 356360 | tf_op jit(solution)/shard_map/ppermute | solution.py:609
  59.9 4.3 %collective-permute-done.12 = bf16[464,128]{1,0:T(8,128)(2,1)S(1)} collective-permute-done((bf16[464,128]{1,0:T(8,128)(2,1)S(1)}, bf16[464,128]{1,0:T(8,128)(2,1)S(1)}, u32[]{:S(2)}, u32[]{:S(2)}) %collective-permute-start.12) | collective-permute-done | bytes 118816 | tf_op jit(solution)/shard_map/ppermute | solution.py:609
  64.3 0.5 collective-permute-start.14
  64.9 0.5 slice.58
  65.7 1.1 %near.1 = (f32[27,64,64]{2,1,0:T(8,128)}, f32[27,64,64]{2,1,0:T(8,128)}, f32[2,64,64]{2,1,0:T(8,128)S(1)}) custom-call(bf16[448,128]{1,0:T(8,128)(2,1)S(1)} %fusion.mine_ref, bf16[448,128]{1,0:T(8,128)(2,1)S(1)} %collective-permute-done.13.far_ref), custom_call_target="tpu_custom_call" | custom-call | tf_op jit(solution)/shard_map/near/pallas_call | solution.py:863
  66.8 3.2 %collective-permute-done.14.mine_ref = bf16[448,128]{1,0:T(8,128)(2,1)S(1)} collective-permute-done((bf16[448,128]{1,0:T(8,128)(2,1)S(1)}, bf16[448,128]{1,0:T(8,128)(2,1)S(1)}, u32[]{:S(2)}, u32[]{:S(2)}) %collective-permute-start.14) | collective-permute-done | bytes 114720 | tf_op jit(solution)/shard_map/ppermute | solution.py:609
  69.9 0.6 slice_bitcast_fusion
  70.5 0.7 %collective-permute-done.15.far_ref = bf16[448,128]{1,0:T(8,128)(2,1)S(1)} collective-permute-done((bf16[448,128]{1,0:T(8,128)(2,1)S(1)}, bf16[448,128]{1,0:T(8,128)(2,1)S(1)}, u32[]{:S(2)}, u32[]{:S(2)}) %collective-permute-start.15) | collective-permute-done | bytes 114720 | tf_op jit(solution)/shard_map/ppermute | solution.py:609
  71.2 1.1 %finish.1 = (f32[27,64,64]{2,1,0:T(8,128)}, f32[27,64,64]{2,1,0:T(8,128)}, f32[3,27,64]{2,1,0:T(8,128)}) custom-call(bf16[448,128]{1,0:T(8,128)(2,1)S(1)} %collective-permute-done.14.mine_ref, bf16[448,128]{1,0:T(8,128)(2,1)S(1)} %collective-permute-done.15.far_ref, ...), custom_call_target="tpu_custom_call", output_to_operand_aliasing={{0}: (3, {}), {1}: (4, {})} | custom-call | tf_op jit(solution)/shard_map/finish/pallas_call | solution.py:874
  (31 shorter events, 1.3 us)
Async XLA Ops:
  1.4 4.8 %collective-permute-start = (bf16[1,2,8,4,128]{4,3,2,1,0:T(4,128)(2,1)S(1)}, bf16[1,2,8,4,128]{4,3,2,1,0:T(4,128)(2,1)S(1)}, u32[]{:S(2)}, u32[]{:S(2)}) collective-permute-start(bf16[1,2,8,4,128]{4,3,2,1,0:T(4,128)(2,1)S(1)} %bitcast.16), channel_id=1, source_target_pairs={{0,2},{1,3},{2,0},{3,1},{4,6},{5,7},{6,4},{7,5},{8,10},{9,11},{10,... | collective-permute-start | bytes 49160 | tf_op jit(solution)/shard_map/ppermute | solution.py:609
  6.2 4.0 %collective-permute-start.1 = (bf16[2,2,8,4,128]{4,3,2,1,0:T(4,128)(2,1)S(1)}, bf16[2,2,8,4,128]{4,3,2,1,0:T(4,128)(2,1)S(1)}, u32[]{:S(2)}, u32[]{:S(2)}) collective-permute-start(bf16[2,2,8,4,128]{4,3,2,1,0:T(4,128)(2,1)S(1)} %maximum_select_fusion.2), channel_id=1, source_target_pairs={{0,4},{1,5},{2,6},{3,7},{4,0},{5,1},{6,2},{7,3},{8,12},{9,13},{10,... | collective-permute-start | bytes 98312 | tf_op jit(solution)/shard_map/ppermute | solution.py:609
  10.3 5.3 %collective-permute-start.2 = (bf16[4,2,8,4,128]{4,3,2,1,0:T(4,128)(2,1)S(1)}, bf16[4,2,8,4,128]{4,3,2,1,0:T(4,128)(2,1)S(1)}, u32[]{:S(2)}, u32[]{:S(2)}) collective-permute-start(bf16[4,2,8,4,128]{4,3,2,1,0:T(4,128)(2,1)S(1)} %maximum_select_fusion.1), channel_id=1, source_target_pairs={{0,8},{1,9},{2,10},{3,11},{4,12},{5,13},{6,14},{7,15},{8,0},{9,1},... | collective-permute-start | bytes 196616 | tf_op jit(solution)/shard_map/ppermute | solution.py:609
  15.8 1.4 %collective-permute-start.3 = (bf16[8,2,8,4,128]{4,3,2,1,0:T(4,128)(2,1)S(1)}, bf16[8,2,8,4,128]{4,3,2,1,0:T(4,128)(2,1)S(1)}, u32[]{:S(2)}, u32[]{:S(2)}) collective-permute-start(bf16[8,2,8,4,128]{4,3,2,1,0:T(4,128)(2,1)S(1)} %maximum_select_fusion.mine_ref), channel_id=1, source_target_pairs={{0,1},{1,0},{2,3},{3,2},{4,5},{5,4},{6,7},{7,6},{8,9},{9,8},{10,11... | collective-permute-start | bytes 393224 | tf_op jit(solution)/shard_map/ppermute | solution.py:609
  30.4 7.0 %collective-permute-start.5 = (f32[2,8,128]{2,1,0:T(8,128)S(1)}, f32[2,8,128]{2,1,0:T(8,128)S(1)}, u32[]{:S(2)}, u32[]{:S(2)}) collective-permute-start(f32[2,8,128]{2,1,0:T(8,128)S(1)} %get-tuple-element.92.score_ref.gm_ref), channel_id=1, source_target_pairs={{2,4},{4,2},{6,8},{8,6},{10,12},{12,10},{3,5},{5,3},{7,9},{9,7},{1... | collective-permute-start | bytes 24584 | tf_op jit(solution)/shard_map/ppermute | solution.py:813
  31.0 6.4 %collective-permute-start.6 = (f32[2,8,128]{2,1,0:T(8,128)S(1)}, f32[2,8,128]{2,1,0:T(8,128)S(1)}, u32[]{:S(2)}, u32[]{:S(2)}) collective-permute-start(f32[2,8,128]{2,1,0:T(8,128)S(1)} %get-tuple-element.92.score_ref.gm_ref), channel_id=1, source_target_pairs={{0,2},{2,0},{4,6},{6,4},{8,10},{10,8},{12,14},{14,12},{1,3},{3,1},... | collective-permute-start | bytes 24584 | tf_op jit(solution)/shard_map/ppermute | solution.py:814
  35.7 2.4 %collective-permute-start.4 = (f32[2,8,128]{2,1,0:T(8,128)S(1)}, f32[2,8,128]{2,1,0:T(8,128)S(1)}, u32[]{:S(2)}, u32[]{:S(2)}) collective-permute-start(f32[2,8,128]{2,1,0:T(8,128)S(1)} %get-tuple-element.92.score_ref.gm_ref), channel_id=1, source_target_pairs={{0,1},{1,0},{2,3},{3,2},{4,5},{5,4},{6,7},{7,6},{8,9},{9,8},{10,11... | collective-permute-start | bytes 24584 | tf_op jit(solution)/shard_map/ppermute | solution.py:609
  37.4 1.4 %collective-permute-start.7 = (f32[2,8,128]{2,1,0:T(8,128)S(1)}, f32[2,8,128]{2,1,0:T(8,128)S(1)}, u32[]{:S(2)}, u32[]{:S(2)}) collective-permute-start(f32[2,8,128]{2,1,0:T(8,128)S(1)} %collective-permute-done.5.p2_ref), channel_id=1, source_target_pairs={{0,1},{1,0},{2,3},{3,2},{4,5},{5,4},{6,7},{7,6},{8,9},{9,8},{10,11... | collective-permute-start | bytes 24584 | tf_op jit(solution)/shard_map/ppermute | solution.py:609
  38.0 1.2 %collective-permute-start.8 = (f32[2,8,128]{2,1,0:T(8,128)S(1)}, f32[2,8,128]{2,1,0:T(8,128)S(1)}, u32[]{:S(2)}, u32[]{:S(2)}) collective-permute-start(f32[2,8,128]{2,1,0:T(8,128)S(1)} %collective-permute-done.6.p1_ref), channel_id=1, source_target_pairs={{0,1},{1,0},{2,3},{3,2},{4,5},{5,4},{6,7},{7,6},{8,9},{9,8},{10,11... | collective-permute-start | bytes 24584 | tf_op jit(solution)/shard_map/ppermute | solution.py:609
  44.1 1.9 %collective-permute-start.9 = (f32[904,128]{1,0:T(8,128)S(1)}, f32[904,128]{1,0:T(8,128)S(1)}, u32[]{:S(2)}, u32[]{:S(2)}) collective-permute-start(f32[904,128]{1,0:T(8,128)S(1)} %get-tuple-element.104), channel_id=1, source_target_pairs={{0,1},{1,0},{2,3},{3,2},{4,5},{5,4},{6,7},{7,6},{8,9},{9,8},{10,11... | collective-permute-start | bytes 1388552 | tf_op jit(solution)/shard_map/ppermute | solution.py:609
  46.1 5.4 %collective-permute-start.10 = (bf16[464,128]{1,0:T(8,128)(2,1)S(1)}, bf16[464,128]{1,0:T(8,128)(2,1)S(1)}, u32[]{:S(2)}, u32[]{:S(2)}) collective-permute-start(bf16[464,128]{1,0:T(8,128)(2,1)S(1)} %pad_maximum_fusion), channel_id=1, source_target_pairs={{0,4},{1,5},{2,6},{3,7},{4,0},{5,1},{6,2},{7,3},{8,12},{9,13},{10,... | collective-permute-start | bytes 356360 | tf_op jit(solution)/shard_map/ppermute | solution.py:609
  51.6 4.9 %collective-permute-start.11 = (bf16[464,128]{1,0:T(8,128)(2,1)S(1)}, bf16[464,128]{1,0:T(8,128)(2,1)S(1)}, u32[]{:S(2)}, u32[]{:S(2)}) collective-permute-start(bf16[464,128]{1,0:T(8,128)(2,1)S(1)} %pad_maximum_fusion.1), channel_id=1, source_target_pairs={{0,2},{1,3},{2,0},{3,1},{4,6},{5,7},{6,4},{7,5},{8,10},{9,11},{10,... | collective-permute-start | bytes 356360 | tf_op jit(solution)/shard_map/ppermute | solution.py:609
  56.6 7.6 %collective-permute-start.12 = (bf16[464,128]{1,0:T(8,128)(2,1)S(1)}, bf16[464,128]{1,0:T(8,128)(2,1)S(1)}, u32[]{:S(2)}, u32[]{:S(2)}) collective-permute-start(bf16[464,128]{1,0:T(8,128)(2,1)S(1)} %pad_maximum_fusion.2), channel_id=1, source_target_pairs={{0,8},{1,9},{2,10},{3,11},{4,12},{5,13},{6,14},{7,15},{8,0},{9,1},... | collective-permute-start | bytes 356360 | tf_op jit(solution)/shard_map/ppermute | solution.py:609
  64.3 1.4 %collective-permute-start.13 = (bf16[448,128]{1,0:T(8,128)(2,1)S(1)}, bf16[448,128]{1,0:T(8,128)(2,1)S(1)}, u32[]{:S(2)}, u32[]{:S(2)}) collective-permute-start(bf16[448,128]{1,0:T(8,128)(2,1)S(1)} %fusion.mine_ref), channel_id=1, source_target_pairs={{0,1},{1,0},{2,3},{3,2},{4,5},{5,4},{6,7},{7,6},{8,9},{9,8},{10,11... | collective-permute-start | bytes 344072 | tf_op jit(solution)/shard_map/ppermute | solution.py:609
  64.3 5.6 %collective-permute-start.14 = (bf16[448,128]{1,0:T(8,128)(2,1)S(1)}, bf16[448,128]{1,0:T(8,128)(2,1)S(1)}, u32[]{:S(2)}, u32[]{:S(2)}) collective-permute-start(bf16[448,128]{1,0:T(8,128)(2,1)S(1)} %fusion.mine_ref), channel_id=1, source_target_pairs={{0,4},{1,5},{2,6},{3,7},{4,0},{5,1},{6,2},{7,3},{8,12},{9,13},{10,... | collective-permute-start | bytes 344072 | tf_op jit(solution)/shard_map/ppermute | solution.py:609
  69.9 1.3 %collective-permute-start.15 = (bf16[448,128]{1,0:T(8,128)(2,1)S(1)}, bf16[448,128]{1,0:T(8,128)(2,1)S(1)}, u32[]{:S(2)}, u32[]{:S(2)}) collective-permute-start(bf16[448,128]{1,0:T(8,128)(2,1)S(1)} %collective-permute-done.14.mine_ref), channel_id=1, source_target_pairs={{0,1},{1,0},{2,3},{3,2},{4,5},{5,4},{6,7},{7,6},{8,9},{9,8},{10,11... | collective-permute-start | bytes 344072 | tf_op jit(solution)/shard_map/ppermute | solution.py:609

commit v8 on v7

--- a/solution.py
+++ b/solution.py
@@ -183,12 +183,63 @@
     conv_lhs(wc_ref, fc, tc)
 
 
+def zero_rims(*refs):
+    for ref in refs:
+        z = jnp.zeros(ref.shape[2:], ref.dtype)
+        for X in range(PLANES):
+            ref[X, 0] = z
+            ref[X, NY + 1] = z
+
+
+def load_half(src, y_first, home_ref, inv_ref, x0s, liq, scl, f1, n_slots):
+    gx = lax.axis_index("gx")
+    for s in range(n_slots):
+        inv_ref[home_ref[s]] = s
+
+    def load_plane(X, c):
+        xg = 2 * gx - MID + X
+        ok = jnp.where((xg >= 0) & (xg < 2 * n_slots), 1.0, 0.0).astype(F32)
+        xc = jnp.clip(xg, 0, 2 * n_slots - 1)
+        home = xc // 2
+        half = xc - 2 * home
+        slot = inv_ref[home]
+        row4 = lax.broadcasted_iota(jnp.int32, (4, NZ), 0)
+        for i in range(8):
+            fb = src[slot, half, i].astype(F32) * ok
+            mb = src[home, half, i].astype(F32)
+            lq = mb[2:3] * ok
+            y = y_first + i
+            base = jnp.where(row4 < 2, fb, jnp.where(row4 == 2, mb * ok, 0.0))
+            k12 = jnp.concatenate(
+                [shift_right(base), base, shift_left(base), jnp.zeros((4, NZ), F32)], axis=0
+            )
+            x0s[X, y + 1] = k12.astype(BF16)
+            liq[X, pl.ds(y + 1, 1), :] = lq
+            scl[X, pl.ds(y + 1, 1), :] = mb[3:4]
+            f1[X, pl.ds(y + 1, 1), :] = fb[1:2]
+        return c
+
+    lax.fori_loop(0, PLANES, load_plane, 0)
+
+
+def prepare_kernel(home_ref, mine_ref, x0s, liq, scl, f1, inv_ref, *, n_slots):
+    zero_rims(x0s)
+    for ref in (liq, scl, f1):
+        for X in range(PLANES):
+            ref[X] = jnp.zeros((YY, NZ), F32)
+    own = 8 * lax.axis_index("gy")
+    load_half(mine_ref, own, home_ref, inv_ref, x0s, liq, scl, f1, n_slots)
+
+
 def forward_kernel(
     home_ref,
     invd_ref,
     hb_ref,
-    mine_ref,
     other_ref,
+    x0s_in,
+    liq_in,
+    scl_in,
+    f1_in,
     wa_ref,
     wb_ref,
     tb_ref,
@@ -217,47 +268,21 @@
 ):
     gx = lax.axis_index("gx")
     gy = lax.axis_index("gy")
-    for ref in (x0s, h1, h2):
-        z = jnp.zeros(ref.shape[2:], ref.dtype)
-        for X in range(PLANES):
-            ref[X, 0] = z
-            ref[X, NY + 1] = z
-    for ref in (liq, scl, f1, pf, rs):
+    zero_rims(h1, h2)
+    for ref in (pf, rs):
         for X in range(PLANES):
             ref[X] = jnp.zeros((YY, NZ), F32)
-    for s in range(n_slots):
-        inv_ref[home_ref[s]] = s
-
-    def load_plane(X, c):
-        xg = 2 * gx - MID + X
-        ok = jnp.where((xg >= 0) & (xg < 2 * n_slots), 1.0, 0.0).astype(F32)
-        xc = jnp.clip(xg, 0, 2 * n_slots - 1)
-        home = xc // 2
-        half = xc - 2 * home
-        slot = inv_ref[home]
-        row4 = lax.broadcasted_iota(jnp.int32, (4, NZ), 0)
-        for i in range(NY):
-            src = (mine_ref, other_ref)[i // 8]
-            fb = src[slot, half, i % 8].astype(F32) * ok
-            mb = src[home, half, i % 8].astype(F32)
-            y = 8 * (gy if i < 8 else 1 - gy) + i % 8
-            lq = mb[2:3] * ok
-            base = jnp.where(row4 < 2, fb, jnp.where(row4 == 2, mb * ok, 0.0))
-            k12 = jnp.concatenate(
-                [shift_right(base), base, shift_left(base), jnp.zeros((4, NZ), F32)], axis=0
-            )
-            x0s[X, y + 1] = k12.astype(BF16)
-            liq[X, pl.ds(y + 1, 1), :] = lq
-            scl[X, pl.ds(y + 1, 1), :] = mb[3:4]
-            f1[X, pl.ds(y + 1, 1), :] = fb[1:2]
+
+    for src, dst in ((x0s_in, x0s), (liq_in, liq), (scl_in, scl), (f1_in, f1)):
+        for X in range(PLANES):
+            dst[X] = src[X]
+    load_half(other_ref, 8 - 8 * gy, home_ref, inv_ref, x0s, liq, scl, f1, n_slots)
+    for X in range(PLANES):
         cl = scl[X, 1 : NY + 1, :]
         sc = jnp.zeros((NY, NZ), F32)
         for k in range(4):
             sc = jnp.where(cl == k, invd_ref[k], sc)
         scl[X, 1 : NY + 1, :] = sc * liq[X, 1 : NY + 1, :]
-        return c
-
-    lax.fori_loop(0, PLANES, load_plane, 0)
 
     def planes(count, body):
         def step(i, c):
@@ -569,26 +594,32 @@
     def _():
         for copy in rest:
             copy.start()
-        for copy in rest:
+
+    def finish():
+        for copy in most:
             copy.wait()
 
-    return most
+        @pl.when(half == 0)
+        def _():
+            for copy in rest:
+                copy.wait()
+
+    return finish
 
 
 def near_kernel(mine_ref, far_ref, gb_hbm, gc_hbm, extra_ref, stage, sems):
     half = lax.axis_index("gx") // (SPLIT // 2) % 2
-    most = unpack_half(half, mine_ref, far_ref, stage, gb_hbm, gc_hbm, sems)
+    wait = unpack_half(half, mine_ref, far_ref, stage, gb_hbm, gc_hbm, sems)
     for i in range(2):
         extra_ref[i] = stage[i, 13]
-    for copy in most:
-        copy.wait()
+    wait()
 
 
 def finish_kernel(
     mine_ref, far_ref, extra_ref, gb_in, gc_in, gb_hbm, gc_hbm, ga_hbm, stage, first, ga_ref, sems
 ):
     half = 1 - lax.axis_index("gx") // (SPLIT // 2) % 2
-    most = unpack_half(half, mine_ref, far_ref, stage, gb_hbm, gc_hbm, sems)
+    wait = unpack_half(half, mine_ref, far_ref, stage, gb_hbm, gc_hbm, sems)
     zero, one = [jnp.where(half == 1, stage[i, 13], extra_ref[i]) for i in range(2)]
     first[0:24] = zero[0:24]
     first[24:48] = zero[32:56]
@@ -600,9 +631,8 @@
         ga_ref[ch] = first[pl.ds(ch, 27, stride=4), :]
     last = pltpu.make_async_copy(ga_ref, ga_hbm, sems.at[4])
     last.start()
+    wait()
     last.wait()
-    for copy in most:
-        copy.wait()
 
 
 def partner(value, bit, count):
@@ -775,6 +805,18 @@
     home, table = [pltpu.with_memory_space_constraint(v, pltpu.SMEM) for v in made[6:]]
 
 
+    plane = shaped((PLANES, YY, NZ), F32)
+    inputs = (shaped((PLANES, YY, 16, NZ), BF16), plane, plane, plane)
+    prepared = pl.pallas_call(
+        functools.partial(prepare_kernel, n_slots=n_slots),
+        out_shape=inputs,
+        in_specs=[smem, vmem],
+        out_specs=(vmem,) * 4,
+        scratch_shapes=[pltpu.SMEM((n_slots,), jnp.int32)],
+        compiler_params=params,
+        name="prepare",
+    )(home, mine)
+
     pressure, score, sbuf, hbuf = pl.pallas_call(
         functools.partial(forward_kernel, n_slots=n_slots, cells=cells),
         out_shape=(
@@ -783,7 +825,7 @@
             shaped((S_BLOCKS, HID, NZ), F32),
             shaped((H_BLOCKS, HID, NZ), BF16),
         ),
-        in_specs=[smem] * 3 + [vmem] * 8,
+        in_specs=[smem] * 3 + [vmem] * 11,
         out_specs=(hbm,) + (vmem,) * 3,
         scratch_shapes=[
             pltpu.VMEM((2, 8, NZ), F32),
@@ -805,8 +847,8 @@
         home,
         table,
         head_bias,
-        mine,
         across,
+        *prepared,
         *made[:6],
     )
 

time: 72.6 us -> 73.1 us (level)
  Pallas kernels: 25.9 us -> 27.1 us
    pallas_call x0 -> x1, Pallas kernels: none -> 1.15 us  [on_device(): pl.pallas_call(functools.partial(prepare_kernel, n_slots=n_slots), out_sh...]
  transfers between devices with their start and end apart: 16 -> 16, of which waited for: 13 -> 12; matrix products, arithmetic and copies ran while one was open for 2% -> 2% of each run, Pallas kernels for 8% -> 10%
where the time goes in v8:
time: 73.1 us; the launch traced here: 72.8 us
  Pallas kernels  27.1 us (37%)
  starting transfers between devices  21.8 us (30%)
  waiting for transfers between devices  20.7 us (28%)
  between operations  1.5 us (2%)
  local copies, waits for them, and re-layouts  1.14 us (2%)
    ppermute x14, waiting for transfers between devices, partner(): return lax.ppermute(value, AXES, [(i, i ^ bit) for i in range(count)])  20.7 us
    ppermute x14, starting transfers between devices, partner(): return lax.ppermute(value, AXES, [(i, i ^ bit) for i in range(count)])  16.5 us
    pallas_call x1, Pallas kernels, on_device(): pl.pallas_call(functools.partial(forward_kernel, n_slots=n_slots, cells=c...  13.2 us
    pallas_call x1, Pallas kernels, on_device(): pl.pallas_call(backward_kernel, out_shape=(shaped((ROWS + 8, NZ), F32), s...  4.92 us
    ppermute x1, starting transfers between devices, on_device(): swap1 = lax.ppermute(score, 'gx', [(i, i ^ 1) for i in range(n_slots)])  4.68 us
    pallas_call x1, Pallas kernels, on_device(): pl.pallas_call(early_kernel, out_shape=(shaped((WROWS, NZ), F32), shaped(...  1.68 us
    pallas_call x1, Pallas kernels, layouts3(): pl.pallas_call(third_lhs_kernel, out_shape=(lhs, turned, shaped((4, HID,...  1.63 us
    pallas_call x1, Pallas kernels, layouts2(): pl.pallas_call(second_lhs_kernel, out_shape=(shaped((HID, 144), BF16), lh...  1.56 us
  transfers between devices with their start and end apart: 16, of which 12 were waited for; matrix products, arithmetic and copies ran while one was open for 2% of the time, Pallas kernels for 10%

profile of v8, /device:TPU:0, one launch (start us, length us, event | category | flops | bytes accessed | tf_op | source)
XLA Modules:
  0.0 72.8 jit_solution(12540219113790411140)
XLA Ops:
  0.6 0.8 %payload.1 = bf16[2,8,4,128]{3,2,1,0:T(4,128)(2,1)S(1)} custom-call(bf16[2,2,8,128]{3,2,1,0:T(8,128)(2,1)} %fields_hbm.1, s32[2,8,128]{2,1,0:T(8,128)} %liquid_hbm.1, s32[2,8,128]{2,1,0:T(8,128)} %class_hbm.1), custom_call_target="tpu_custom_call" | custom-call | tf_op jit(solution)/shard_map/payload/pallas_call | solution.py:717
  1.4 3.0 %collective-permute-start = (bf16[1,2,8,4,128]{4,3,2,1,0:T(4,128)(2,1)S(1)}, bf16[1,2,8,4,128]{4,3,2,1,0:T(4,128)(2,1)S(1)}, u32[]{:S(2)}, u32[]{:S(2)}) collective-permute-start(bf16[1,2,8,4,128]{4,3,2,1,0:T(4,128)(2,1)S(1)} %bitcast.16), channel_id=1, source_target_pairs={{0,2},{1,3},{2,0},{3,1},{4,6},{5,7},{6,4},{7,5},{8,10},{9,11},{10,... | collective-permute-start | bytes 49160 | tf_op jit(solution)/shard_map/ppermute | solution.py:639
  4.5 1.7 %collective-permute-done = bf16[1,2,8,4,128]{4,3,2,1,0:T(4,128)(2,1)S(1)} collective-permute-done((bf16[1,2,8,4,128]{4,3,2,1,0:T(4,128)(2,1)S(1)}, bf16[1,2,8,4,128]{4,3,2,1,0:T(4,128)(2,1)S(1)}, u32[]{:S(2)}, u32[]{:S(2)}) %collective-permute-start) | collective-permute-done | bytes 16416 | tf_op jit(solution)/shard_map/ppermute | solution.py:639
  6.2 2.1 %collective-permute-start.1 = (bf16[2,2,8,4,128]{4,3,2,1,0:T(4,128)(2,1)S(1)}, bf16[2,2,8,4,128]{4,3,2,1,0:T(4,128)(2,1)S(1)}, u32[]{:S(2)}, u32[]{:S(2)}) collective-permute-start(bf16[2,2,8,4,128]{4,3,2,1,0:T(4,128)(2,1)S(1)} %maximum_select_fusion.2), channel_id=1, source_target_pairs={{0,4},{1,5},{2,6},{3,7},{4,0},{5,1},{6,2},{7,3},{8,12},{9,13},{10,... | collective-permute-start | bytes 98312 | tf_op jit(solution)/shard_map/ppermute | solution.py:639
  8.3 1.6 %lhs2.1 = (bf16[64,144]{1,0:T(8,128)(2,1)S(1)}, bf16[384,768]{1,0:T(8,128)(2,1)S(1)}, bf16[36,64,128]{2,1,0:T(8,128)(2,1)S(1)}) custom-call(bf16[27,64,64]{2,1,0:T(8,128)(2,1)} %wb_hbm, bf16[3,27,64]{2,1,0:T(8,128)(2,1)} %bitcast.18), custom_call_target="tpu_custom_call" | custom-call | tf_op jit(solution)/shard_map/lhs2/pallas_call | solution.py:737
  9.9 0.3 collective-permute-done.1
  10.3 3.1 %collective-permute-start.2 = (bf16[4,2,8,4,128]{4,3,2,1,0:T(4,128)(2,1)S(1)}, bf16[4,2,8,4,128]{4,3,2,1,0:T(4,128)(2,1)S(1)}, u32[]{:S(2)}, u32[]{:S(2)}) collective-permute-start(bf16[4,2,8,4,128]{4,3,2,1,0:T(4,128)(2,1)S(1)} %maximum_select_fusion.1), channel_id=1, source_target_pairs={{0,8},{1,9},{2,10},{3,11},{4,12},{5,13},{6,14},{7,15},{8,0},{9,1},... | collective-permute-start | bytes 196616 | tf_op jit(solution)/shard_map/ppermute | solution.py:639
  13.4 1.6 %lhs3.1 = (bf16[384,768]{1,0:T(8,128)(2,1)S(1)}, bf16[36,64,128]{2,1,0:T(8,128)(2,1)S(1)}, f32[4,64,128]{2,1,0:T(8,128)S(1)}, s32[8]{0:T(128)S(4)}, f32[4]{0:T(128)S(4)}) custom-call(bf16[27,64,64]{2,1,0:T(8,128)(2,1)} %wc_hbm, f32[1,64]{1,0:T(1,128)} %bitcast.19, f32[1,64]{1,0:T(1,128)} %bitcast.20, f32[1,64]{1,0:T(1,128)} %bitcast.21, ...), custom_call_target="tpu_custom_call" | custom-call | tf_op jit(solution)/shard_map/lhs3/pallas_call | solution.py:752
  15.0 0.6 collective-permute-done.2
  16.5 1.2 %prepare.1 = (bf16[12,18,16,128]{3,2,1,0:T(8,128)(2,1)S(1)}, f32[12,18,128]{2,1,0:T(8,128)S(1)}, f32[12,18,128]{2,1,0:T(8,128)S(1)}, f32[12,18,128]{2,1,0:T(8,128)S(1)}) custom-call(s32[8]{0:T(128)S(4)} %get-tuple-element.86.home_ref, bf16[8,2,8,4,128]{4,3,2,1,0:T(4,128)(2,1)S(1)} %maximum_select_fusion.mine_ref), custom_call_target="tpu_custom_call" | custom-call | tf_op jit(solution)/shard_map/prepare/pallas_call | solution.py:810
  17.7 13.2 %forward.1 = (f32[2,8,128]{2,1,0:T(8,128)}, f32[2,8,128]{2,1,0:T(8,128)S(1)}, f32[134,64,128]{2,1,0:T(8,128)S(1)}, bf16[180,64,128]{2,1,0:T(8,128)(2,1)S(1)}) custom-call(s32[8]{0:T(128)S(4)} %get-tuple-element.86.home_ref, f32[4]{0:T(128)S(4)} %get-tuple-element.87.invd_ref, f32[1]{0:T(128)S(6)} %copy.26.hb_ref, ...), custom_call_target="tpu_custom_call" | custom-call | tf_op jit(solution)/shard_map/forward/pallas_call | solution.py:820
  30.9 0.7 collective-permute-start.5
  31.6 4.7 %collective-permute-start.6 = (f32[2,8,128]{2,1,0:T(8,128)S(1)}, f32[2,8,128]{2,1,0:T(8,128)S(1)}, u32[]{:S(2)}, u32[]{:S(2)}) collective-permute-start(f32[2,8,128]{2,1,0:T(8,128)S(1)} %get-tuple-element.100.score_ref.gm_ref), channel_id=1, source_target_pairs={{0,2},{2,0},{4,6},{6,4},{8,10},{10,8},{12,14},{14,12},{1,3},{3,1},... | collective-permute-start | bytes 24584 | tf_op jit(solution)/shard_map/ppermute | solution.py:856
  36.2 1.7 %early.1 = (f32[864,128]{1,0:T(8,128)S(1)}, f32[8,128]{1,0:T(8,128)S(1)}, bf16[720,2048]{1,0:T(8,128)(2,1)S(1)}) custom-call(f32[2,8,128]{2,1,0:T(8,128)S(1)} %get-tuple-element.100.score_ref.gm_ref, f32[134,64,128]{2,1,0:T(8,128)S(1)} %get-tuple-element.101.sbuf, bf16[180,64,128]{2,1,0:T(8,128)(2,1)S(1)} %get-tuple-element.102.hbuf, ...), custom_call_target="tpu_custom_call" | custom-call | tf_op jit(solution)/shard_map/early/pallas_call | solution.py:858
  38.0 0.6 collective-permute-start.7
  38.6 0.7 %collective-permute-done.7.p2o_ref = f32[2,8,128]{2,1,0:T(8,128)S(1)} collective-permute-done((f32[2,8,128]{2,1,0:T(8,128)S(1)}, f32[2,8,128]{2,1,0:T(8,128)S(1)}, u32[]{:S(2)}, u32[]{:S(2)}) %collective-permute-start.7) | collective-permute-done | bytes 8224 | tf_op jit(solution)/shard_map/ppermute | solution.py:639
  39.4 0.3 collective-permute-done.8.p1o_ref
  39.7 4.9 %backward.1 = (f32[904,128]{1,0:T(8,128)S(1)}, f32[904,128]{1,0:T(8,128)S(1)}) custom-call(f32[2,8,128]{2,1,0:T(8,128)S(1)} %get-tuple-element.100.score_ref.gm_ref, f32[2,8,128]{2,1,0:T(8,128)S(1)} %collective-permute-done.4.gmo_ref, f32[2,8,128]{2,1,0:T(8,128)S(1)} %collective-permute-done.5.p2_ref, f32[2,8,128]{2,1,0:T(8,128)S(1)} %collective-permute-done.7.p2o_ref, ...), custom_call_target="tpu_custom_call" | custom-call | tf_op jit(solution)/shard_map/backward/pallas_call | solution.py:879
  44.8 1.7 %collective-permute-done.9 = f32[904,128]{1,0:T(8,128)S(1)} collective-permute-done((f32[904,128]{1,0:T(8,128)S(1)}, f32[904,128]{1,0:T(8,128)S(1)}, u32[]{:S(2)}, u32[]{:S(2)}) %collective-permute-start.9) | collective-permute-done | bytes 462880 | tf_op jit(solution)/shard_map/ppermute | solution.py:639
  46.7 1.7 %collective-permute-start.10 = (bf16[464,128]{1,0:T(8,128)(2,1)S(1)}, bf16[464,128]{1,0:T(8,128)(2,1)S(1)}, u32[]{:S(2)}, u32[]{:S(2)}) collective-permute-start(bf16[464,128]{1,0:T(8,128)(2,1)S(1)} %pad_maximum_fusion), channel_id=1, source_target_pairs={{0,4},{1,5},{2,6},{3,7},{4,0},{5,1},{6,2},{7,3},{8,12},{9,13},{10,... | collective-permute-start | bytes 356360 | tf_op jit(solution)/shard_map/ppermute | solution.py:639
  48.4 3.7 %collective-permute-done.10 = bf16[464,128]{1,0:T(8,128)(2,1)S(1)} collective-permute-done((bf16[464,128]{1,0:T(8,128)(2,1)S(1)}, bf16[464,128]{1,0:T(8,128)(2,1)S(1)}, u32[]{:S(2)}, u32[]{:S(2)}) %collective-permute-start.10) | collective-permute-done | bytes 118816 | tf_op jit(solution)/shard_map/ppermute | solution.py:639
  52.1 1.8 %collective-permute-start.11 = (bf16[464,128]{1,0:T(8,128)(2,1)S(1)}, bf16[464,128]{1,0:T(8,128)(2,1)S(1)}, u32[]{:S(2)}, u32[]{:S(2)}) collective-permute-start(bf16[464,128]{1,0:T(8,128)(2,1)S(1)} %pad_maximum_fusion.1), channel_id=1, source_target_pairs={{0,2},{1,3},{2,0},{3,1},{4,6},{5,7},{6,4},{7,5},{8,10},{9,11},{10,... | collective-permute-start | bytes 356360 | tf_op jit(solution)/shard_map/ppermute | solution.py:639
  53.9 3.1 %collective-permute-done.11 = bf16[464,128]{1,0:T(8,128)(2,1)S(1)} collective-permute-done((bf16[464,128]{1,0:T(8,128)(2,1)S(1)}, bf16[464,128]{1,0:T(8,128)(2,1)S(1)}, u32[]{:S(2)}, u32[]{:S(2)}) %collective-permute-start.11) | collective-permute-done | bytes 118816 | tf_op jit(solution)/shard_map/ppermute | solution.py:639
  57.1 3.2 %collective-permute-start.12 = (bf16[464,128]{1,0:T(8,128)(2,1)S(1)}, bf16[464,128]{1,0:T(8,128)(2,1)S(1)}, u32[]{:S(2)}, u32[]{:S(2)}) collective-permute-start(bf16[464,128]{1,0:T(8,128)(2,1)S(1)} %pad_maximum_fusion.2), channel_id=1, source_target_pairs={{0,8},{1,9},{2,10},{3,11},{4,12},{5,13},{6,14},{7,15},{8,0},{9,1},... | collective-permute-start | bytes 356360 | tf_op jit(solution)/shard_map/ppermute | solution.py:639
  60.4 4.3 %collective-permute-done.12 = bf16[464,128]{1,0:T(8,128)(2,1)S(1)} collective-permute-done((bf16[464,128]{1,0:T(8,128)(2,1)S(1)}, bf16[464,128]{1,0:T(8,128)(2,1)S(1)}, u32[]{:S(2)}, u32[]{:S(2)}) %collective-permute-start.12) | collective-permute-done | bytes 118816 | tf_op jit(solution)/shard_map/ppermute | solution.py:639
  64.8 0.5 collective-permute-start.14
  65.4 0.5 slice.58
  66.2 1.1 %near.1 = (f32[27,64,64]{2,1,0:T(8,128)}, f32[27,64,64]{2,1,0:T(8,128)}, f32[2,64,64]{2,1,0:T(8,128)S(1)}) custom-call(bf16[448,128]{1,0:T(8,128)(2,1)S(1)} %fusion.mine_ref, bf16[448,128]{1,0:T(8,128)(2,1)S(1)} %collective-permute-done.13.far_ref), custom_call_target="tpu_custom_call" | custom-call | tf_op jit(solution)/shard_map/near/pallas_call | solution.py:905
  67.3 3.1 %collective-permute-done.14.mine_ref = bf16[448,128]{1,0:T(8,128)(2,1)S(1)} collective-permute-done((bf16[448,128]{1,0:T(8,128)(2,1)S(1)}, bf16[448,128]{1,0:T(8,128)(2,1)S(1)}, u32[]{:S(2)}, u32[]{:S(2)}) %collective-permute-start.14) | collective-permute-done | bytes 114720 | tf_op jit(solution)/shard_map/ppermute | solution.py:639
  70.4 0.6 slice_bitcast_fusion
  71.0 0.7 %collective-permute-done.15.far_ref = bf16[448,128]{1,0:T(8,128)(2,1)S(1)} collective-permute-done((bf16[448,128]{1,0:T(8,128)(2,1)S(1)}, bf16[448,128]{1,0:T(8,128)(2,1)S(1)}, u32[]{:S(2)}, u32[]{:S(2)}) %collective-permute-start.15) | collective-permute-done | bytes 114720 | tf_op jit(solution)/shard_map/ppermute | solution.py:639
  71.7 1.1 %finish.1 = (f32[27,64,64]{2,1,0:T(8,128)}, f32[27,64,64]{2,1,0:T(8,128)}, f32[3,27,64]{2,1,0:T(8,128)}) custom-call(bf16[448,128]{1,0:T(8,128)(2,1)S(1)} %collective-permute-done.14.mine_ref, bf16[448,128]{1,0:T(8,128)(2,1)S(1)} %collective-permute-done.15.far_ref, ...), custom_call_target="tpu_custom_call", output_to_operand_aliasing={{0}: (3, {}), {1}: (4, {})} | custom-call | tf_op jit(solution)/shard_map/finish/pallas_call | solution.py:916
  (32 shorter events, 1.3 us)
Async XLA Ops:
  1.4 4.8 %collective-permute-start = (bf16[1,2,8,4,128]{4,3,2,1,0:T(4,128)(2,1)S(1)}, bf16[1,2,8,4,128]{4,3,2,1,0:T(4,128)(2,1)S(1)}, u32[]{:S(2)}, u32[]{:S(2)}) collective-permute-start(bf16[1,2,8,4,128]{4,3,2,1,0:T(4,128)(2,1)S(1)} %bitcast.16), channel_id=1, source_target_pairs={{0,2},{1,3},{2,0},{3,1},{4,6},{5,7},{6,4},{7,5},{8,10},{9,11},{10,... | collective-permute-start | bytes 49160 | tf_op jit(solution)/shard_map/ppermute | solution.py:639
  6.2 4.0 %collective-permute-start.1 = (bf16[2,2,8,4,128]{4,3,2,1,0:T(4,128)(2,1)S(1)}, bf16[2,2,8,4,128]{4,3,2,1,0:T(4,128)(2,1)S(1)}, u32[]{:S(2)}, u32[]{:S(2)}) collective-permute-start(bf16[2,2,8,4,128]{4,3,2,1,0:T(4,128)(2,1)S(1)} %maximum_select_fusion.2), channel_id=1, source_target_pairs={{0,4},{1,5},{2,6},{3,7},{4,0},{5,1},{6,2},{7,3},{8,12},{9,13},{10,... | collective-permute-start | bytes 98312 | tf_op jit(solution)/shard_map/ppermute | solution.py:639
  10.3 5.3 %collective-permute-start.2 = (bf16[4,2,8,4,128]{4,3,2,1,0:T(4,128)(2,1)S(1)}, bf16[4,2,8,4,128]{4,3,2,1,0:T(4,128)(2,1)S(1)}, u32[]{:S(2)}, u32[]{:S(2)}) collective-permute-start(bf16[4,2,8,4,128]{4,3,2,1,0:T(4,128)(2,1)S(1)} %maximum_select_fusion.1), channel_id=1, source_target_pairs={{0,8},{1,9},{2,10},{3,11},{4,12},{5,13},{6,14},{7,15},{8,0},{9,1},... | collective-permute-start | bytes 196616 | tf_op jit(solution)/shard_map/ppermute | solution.py:639
  15.8 1.9 %collective-permute-start.3 = (bf16[8,2,8,4,128]{4,3,2,1,0:T(4,128)(2,1)S(1)}, bf16[8,2,8,4,128]{4,3,2,1,0:T(4,128)(2,1)S(1)}, u32[]{:S(2)}, u32[]{:S(2)}) collective-permute-start(bf16[8,2,8,4,128]{4,3,2,1,0:T(4,128)(2,1)S(1)} %maximum_select_fusion.mine_ref), channel_id=1, source_target_pairs={{0,1},{1,0},{2,3},{3,2},{4,5},{5,4},{6,7},{7,6},{8,9},{9,8},{10,11... | collective-permute-start | bytes 393224 | tf_op jit(solution)/shard_map/ppermute | solution.py:639
  30.9 7.0 %collective-permute-start.5 = (f32[2,8,128]{2,1,0:T(8,128)S(1)}, f32[2,8,128]{2,1,0:T(8,128)S(1)}, u32[]{:S(2)}, u32[]{:S(2)}) collective-permute-start(f32[2,8,128]{2,1,0:T(8,128)S(1)} %get-tuple-element.100.score_ref.gm_ref), channel_id=1, source_target_pairs={{2,4},{4,2},{6,8},{8,6},{10,12},{12,10},{3,5},{5,3},{7,9},{9,7},{1... | collective-permute-start | bytes 24584 | tf_op jit(solution)/shard_map/ppermute | solution.py:855
  31.6 6.4 %collective-permute-start.6 = (f32[2,8,128]{2,1,0:T(8,128)S(1)}, f32[2,8,128]{2,1,0:T(8,128)S(1)}, u32[]{:S(2)}, u32[]{:S(2)}) collective-permute-start(f32[2,8,128]{2,1,0:T(8,128)S(1)} %get-tuple-element.100.score_ref.gm_ref), channel_id=1, source_target_pairs={{0,2},{2,0},{4,6},{6,4},{8,10},{10,8},{12,14},{14,12},{1,3},{3,1},... | collective-permute-start | bytes 24584 | tf_op jit(solution)/shard_map/ppermute | solution.py:856
  36.2 2.4 %collective-permute-start.4 = (f32[2,8,128]{2,1,0:T(8,128)S(1)}, f32[2,8,128]{2,1,0:T(8,128)S(1)}, u32[]{:S(2)}, u32[]{:S(2)}) collective-permute-start(f32[2,8,128]{2,1,0:T(8,128)S(1)} %get-tuple-element.100.score_ref.gm_ref), channel_id=1, source_target_pairs={{0,1},{1,0},{2,3},{3,2},{4,5},{5,4},{6,7},{7,6},{8,9},{9,8},{10,11... | collective-permute-start | bytes 24584 | tf_op jit(solution)/shard_map/ppermute | solution.py:639
  38.0 1.4 %collective-permute-start.7 = (f32[2,8,128]{2,1,0:T(8,128)S(1)}, f32[2,8,128]{2,1,0:T(8,128)S(1)}, u32[]{:S(2)}, u32[]{:S(2)}) collective-permute-start(f32[2,8,128]{2,1,0:T(8,128)S(1)} %collective-permute-done.5.p2_ref), channel_id=1, source_target_pairs={{0,1},{1,0},{2,3},{3,2},{4,5},{5,4},{6,7},{7,6},{8,9},{9,8},{10,11... | collective-permute-start | bytes 24584 | tf_op jit(solution)/shard_map/ppermute | solution.py:639
  38.5 1.2 %collective-permute-start.8 = (f32[2,8,128]{2,1,0:T(8,128)S(1)}, f32[2,8,128]{2,1,0:T(8,128)S(1)}, u32[]{:S(2)}, u32[]{:S(2)}) collective-permute-start(f32[2,8,128]{2,1,0:T(8,128)S(1)} %collective-permute-done.6.p1_ref), channel_id=1, source_target_pairs={{0,1},{1,0},{2,3},{3,2},{4,5},{5,4},{6,7},{7,6},{8,9},{9,8},{10,11... | collective-permute-start | bytes 24584 | tf_op jit(solution)/shard_map/ppermute | solution.py:639
  44.6 1.9 %collective-permute-start.9 = (f32[904,128]{1,0:T(8,128)S(1)}, f32[904,128]{1,0:T(8,128)S(1)}, u32[]{:S(2)}, u32[]{:S(2)}) collective-permute-start(f32[904,128]{1,0:T(8,128)S(1)} %get-tuple-element.112), channel_id=1, source_target_pairs={{0,1},{1,0},{2,3},{3,2},{4,5},{5,4},{6,7},{7,6},{8,9},{9,8},{10,11... | collective-permute-start | bytes 1388552 | tf_op jit(solution)/shard_map/ppermute | solution.py:639
  46.7 5.4 %collective-permute-start.10 = (bf16[464,128]{1,0:T(8,128)(2,1)S(1)}, bf16[464,128]{1,0:T(8,128)(2,1)S(1)}, u32[]{:S(2)}, u32[]{:S(2)}) collective-permute-start(bf16[464,128]{1,0:T(8,128)(2,1)S(1)} %pad_maximum_fusion), channel_id=1, source_target_pairs={{0,4},{1,5},{2,6},{3,7},{4,0},{5,1},{6,2},{7,3},{8,12},{9,13},{10,... | collective-permute-start | bytes 356360 | tf_op jit(solution)/shard_map/ppermute | solution.py:639
  52.1 4.9 %collective-permute-start.11 = (bf16[464,128]{1,0:T(8,128)(2,1)S(1)}, bf16[464,128]{1,0:T(8,128)(2,1)S(1)}, u32[]{:S(2)}, u32[]{:S(2)}) collective-permute-start(bf16[464,128]{1,0:T(8,128)(2,1)S(1)} %pad_maximum_fusion.1), channel_id=1, source_target_pairs={{0,2},{1,3},{2,0},{3,1},{4,6},{5,7},{6,4},{7,5},{8,10},{9,11},{10,... | collective-permute-start | bytes 356360 | tf_op jit(solution)/shard_map/ppermute | solution.py:639
  57.1 7.5 %collective-permute-start.12 = (bf16[464,128]{1,0:T(8,128)(2,1)S(1)}, bf16[464,128]{1,0:T(8,128)(2,1)S(1)}, u32[]{:S(2)}, u32[]{:S(2)}) collective-permute-start(bf16[464,128]{1,0:T(8,128)(2,1)S(1)} %pad_maximum_fusion.2), channel_id=1, source_target_pairs={{0,8},{1,9},{2,10},{3,11},{4,12},{5,13},{6,14},{7,15},{8,0},{9,1},... | collective-permute-start | bytes 356360 | tf_op jit(solution)/shard_map/ppermute | solution.py:639
  64.8 1.4 %collective-permute-start.13 = (bf16[448,128]{1,0:T(8,128)(2,1)S(1)}, bf16[448,128]{1,0:T(8,128)(2,1)S(1)}, u32[]{:S(2)}, u32[]{:S(2)}) collective-permute-start(bf16[448,128]{1,0:T(8,128)(2,1)S(1)} %fusion.mine_ref), channel_id=1, source_target_pairs={{0,1},{1,0},{2,3},{3,2},{4,5},{5,4},{6,7},{7,6},{8,9},{9,8},{10,11... | collective-permute-start | bytes 344072 | tf_op jit(solution)/shard_map/ppermute | solution.py:639
  64.8 5.6 %collective-permute-start.14 = (bf16[448,128]{1,0:T(8,128)(2,1)S(1)}, bf16[448,128]{1,0:T(8,128)(2,1)S(1)}, u32[]{:S(2)}, u32[]{:S(2)}) collective-permute-start(bf16[448,128]{1,0:T(8,128)(2,1)S(1)} %fusion.mine_ref), channel_id=1, source_target_pairs={{0,4},{1,5},{2,6},{3,7},{4,0},{5,1},{6,2},{7,3},{8,12},{9,13},{10,... | collective-permute-start | bytes 344072 | tf_op jit(solution)/shard_map/ppermute | solution.py:639
  70.4 1.3 %collective-permute-start.15 = (bf16[448,128]{1,0:T(8,128)(2,1)S(1)}, bf16[448,128]{1,0:T(8,128)(2,1)S(1)}, u32[]{:S(2)}, u32[]{:S(2)}) collective-permute-start(bf16[448,128]{1,0:T(8,128)(2,1)S(1)} %collective-permute-done.14.mine_ref), channel_id=1, source_target_pairs={{0,1},{1,0},{2,3},{3,2},{4,5},{5,4},{6,7},{7,6},{8,9},{9,8},{10,11... | collective-permute-start | bytes 344072 | tf_op jit(solution)/shard_map/ppermute | solution.py:639

commit v9 on v7

--- a/solution.py
+++ b/solution.py
@@ -228,7 +228,7 @@
     for s in range(n_slots):
         inv_ref[home_ref[s]] = s
 
-    def load_plane(X, c):
+    def load_plane(X):
         xg = 2 * gx - MID + X
         ok = jnp.where((xg >= 0) & (xg < 2 * n_slots), 1.0, 0.0).astype(F32)
         xc = jnp.clip(xg, 0, 2 * n_slots - 1)
@@ -255,9 +255,13 @@
         for k in range(4):
             sc = jnp.where(cl == k, invd_ref[k], sc)
         scl[X, 1 : NY + 1, :] = sc * liq[X, 1 : NY + 1, :]
+
+    def load_planes(i, c):
+        for k in range(3):
+            load_plane(3 * i + k)
         return c
 
-    lax.fori_loop(0, PLANES, load_plane, 0)
+    lax.fori_loop(0, PLANES // 3, load_planes, 0)
 
     def planes(count, body):
         def step(i, c):
@@ -280,8 +284,14 @@
                 if slot is not None:
                     sbuf[S1 + 12 * slot + 2 * j + k] = slope_of(z, sig) * m
 
-    planes(8, lambda i: layer1(1 + i + 2 * (i // 4), None))
-    planes(2, lambda i: layer1(MID + i, i))
+    def layer1_pair(i):
+        X = 1 + 2 * i + 2 * (i // 2)
+        layer1(X, None)
+        layer1(X + 1, None)
+
+    planes(4, layer1_pair)
+    layer1(MID, 0)
+    layer1(MID + 1, 1)
 
     y3 = gy * 5 + 1
 
@@ -569,26 +579,32 @@
     def _():
         for copy in rest:
             copy.start()
-        for copy in rest:
+
+    def finish():
+        for copy in most:
             copy.wait()
 
-    return most
+        @pl.when(half == 0)
+        def _():
+            for copy in rest:
+                copy.wait()
+
+    return finish
 
 
 def near_kernel(mine_ref, far_ref, gb_hbm, gc_hbm, extra_ref, stage, sems):
     half = lax.axis_index("gx") // (SPLIT // 2) % 2
-    most = unpack_half(half, mine_ref, far_ref, stage, gb_hbm, gc_hbm, sems)
+    wait = unpack_half(half, mine_ref, far_ref, stage, gb_hbm, gc_hbm, sems)
     for i in range(2):
         extra_ref[i] = stage[i, 13]
-    for copy in most:
-        copy.wait()
+    wait()
 
 
 def finish_kernel(
     mine_ref, far_ref, extra_ref, gb_in, gc_in, gb_hbm, gc_hbm, ga_hbm, stage, first, ga_ref, sems
 ):
     half = 1 - lax.axis_index("gx") // (SPLIT // 2) % 2
-    most = unpack_half(half, mine_ref, far_ref, stage, gb_hbm, gc_hbm, sems)
+    wait = unpack_half(half, mine_ref, far_ref, stage, gb_hbm, gc_hbm, sems)
     zero, one = [jnp.where(half == 1, stage[i, 13], extra_ref[i]) for i in range(2)]
     first[0:24] = zero[0:24]
     first[24:48] = zero[32:56]
@@ -600,9 +616,8 @@
         ga_ref[ch] = first[pl.ds(ch, 27, stride=4), :]
     last = pltpu.make_async_copy(ga_ref, ga_hbm, sems.at[4])
     last.start()
+    wait()
     last.wait()
-    for copy in most:
-        copy.wait()
 
 
 def partner(value, bit, count):

time: 72.6 us -> 71.3 us (0.982)
  Pallas kernels: 25.9 us -> 24.5 us
    pallas_call x1, Pallas kernels: 13.2 us -> 11.8 us  [on_device(): pl.pallas_call(functools.partial(forward_kernel, n_slots=n_slots, cells=c...]
where the time goes in v9:
time: 71.3 us; the launch traced here: 71 us
  Pallas kernels  24.5 us (34%)
  starting transfers between devices  21.9 us (31%)
  waiting for transfers between devices  21.3 us (30%)
  between operations  1.49 us (2%)
  local copies, waits for them, and re-layouts  1.14 us (2%)
    ppermute x14, waiting for transfers between devices, partner(): return lax.ppermute(value, AXES, [(i, i ^ bit) for i in range(count)])  21.3 us
    ppermute x14, starting transfers between devices, partner(): return lax.ppermute(value, AXES, [(i, i ^ bit) for i in range(count)])  16.6 us
    pallas_call x1, Pallas kernels, on_device(): pl.pallas_call(functools.partial(forward_kernel, n_slots=n_slots, cells=c...  11.8 us
    pallas_call x1, Pallas kernels, on_device(): pl.pallas_call(backward_kernel, out_shape=(shaped((ROWS + 8, NZ), F32), s...  4.92 us
    ppermute x1, starting transfers between devices, on_device(): swap1 = lax.ppermute(score, 'gx', [(i, i ^ 1) for i in range(n_slots)])  4.68 us
    pallas_call x1, Pallas kernels, on_device(): pl.pallas_call(early_kernel, out_shape=(shaped((WROWS, NZ), F32), shaped(...  1.68 us
    pallas_call x1, Pallas kernels, layouts3(): pl.pallas_call(third_lhs_kernel, out_shape=(lhs, turned, shaped((4, HID,...  1.63 us
    pallas_call x1, Pallas kernels, layouts2(): pl.pallas_call(second_lhs_kernel, out_shape=(shaped((HID, 144), BF16), lh...  1.56 us
  transfers between devices with their start and end apart: 16, of which 13 were waited for; matrix products, arithmetic and copies ran while one was open for 2% of the time, Pallas kernels for 8%

profile of v9, /device:TPU:0, one launch (start us, length us, event | category | flops | bytes accessed | tf_op | source)
XLA Modules:
  0.0 71.0 jit_solution(16377429762565672516)
XLA Ops:
  0.6 0.8 %payload.1 = bf16[2,8,4,128]{3,2,1,0:T(4,128)(2,1)S(1)} custom-call(bf16[2,2,8,128]{3,2,1,0:T(8,128)(2,1)} %fields_hbm.1, s32[2,8,128]{2,1,0:T(8,128)} %liquid_hbm.1, s32[2,8,128]{2,1,0:T(8,128)} %class_hbm.1), custom_call_target="tpu_custom_call" | custom-call | tf_op jit(solution)/shard_map/payload/pallas_call | solution.py:702
  1.4 3.0 %collective-permute-start = (bf16[1,2,8,4,128]{4,3,2,1,0:T(4,128)(2,1)S(1)}, bf16[1,2,8,4,128]{4,3,2,1,0:T(4,128)(2,1)S(1)}, u32[]{:S(2)}, u32[]{:S(2)}) collective-permute-start(bf16[1,2,8,4,128]{4,3,2,1,0:T(4,128)(2,1)S(1)} %bitcast.16), channel_id=1, source_target_pairs={{0,2},{1,3},{2,0},{3,1},{4,6},{5,7},{6,4},{7,5},{8,10},{9,11},{10,... | collective-permute-start | bytes 49160 | tf_op jit(solution)/shard_map/ppermute | solution.py:624
  4.5 1.7 %collective-permute-done = bf16[1,2,8,4,128]{4,3,2,1,0:T(4,128)(2,1)S(1)} collective-permute-done((bf16[1,2,8,4,128]{4,3,2,1,0:T(4,128)(2,1)S(1)}, bf16[1,2,8,4,128]{4,3,2,1,0:T(4,128)(2,1)S(1)}, u32[]{:S(2)}, u32[]{:S(2)}) %collective-permute-start) | collective-permute-done | bytes 16416 | tf_op jit(solution)/shard_map/ppermute | solution.py:624
  6.2 2.1 %collective-permute-start.1 = (bf16[2,2,8,4,128]{4,3,2,1,0:T(4,128)(2,1)S(1)}, bf16[2,2,8,4,128]{4,3,2,1,0:T(4,128)(2,1)S(1)}, u32[]{:S(2)}, u32[]{:S(2)}) collective-permute-start(bf16[2,2,8,4,128]{4,3,2,1,0:T(4,128)(2,1)S(1)} %maximum_select_fusion.2), channel_id=1, source_target_pairs={{0,4},{1,5},{2,6},{3,7},{4,0},{5,1},{6,2},{7,3},{8,12},{9,13},{10,... | collective-permute-start | bytes 98312 | tf_op jit(solution)/shard_map/ppermute | solution.py:624
  8.3 1.6 %lhs2.1 = (bf16[64,144]{1,0:T(8,128)(2,1)S(1)}, bf16[384,768]{1,0:T(8,128)(2,1)S(1)}, bf16[36,64,128]{2,1,0:T(8,128)(2,1)S(1)}) custom-call(bf16[27,64,64]{2,1,0:T(8,128)(2,1)} %wb_hbm, bf16[3,27,64]{2,1,0:T(8,128)(2,1)} %bitcast.18), custom_call_target="tpu_custom_call" | custom-call | tf_op jit(solution)/shard_map/lhs2/pallas_call | solution.py:722
  9.9 0.3 collective-permute-done.1
  10.3 3.1 %collective-permute-start.2 = (bf16[4,2,8,4,128]{4,3,2,1,0:T(4,128)(2,1)S(1)}, bf16[4,2,8,4,128]{4,3,2,1,0:T(4,128)(2,1)S(1)}, u32[]{:S(2)}, u32[]{:S(2)}) collective-permute-start(bf16[4,2,8,4,128]{4,3,2,1,0:T(4,128)(2,1)S(1)} %maximum_select_fusion.1), channel_id=1, source_target_pairs={{0,8},{1,9},{2,10},{3,11},{4,12},{5,13},{6,14},{7,15},{8,0},{9,1},... | collective-permute-start | bytes 196616 | tf_op jit(solution)/shard_map/ppermute | solution.py:624
  13.4 1.6 %lhs3.1 = (bf16[384,768]{1,0:T(8,128)(2,1)S(1)}, bf16[36,64,128]{2,1,0:T(8,128)(2,1)S(1)}, f32[4,64,128]{2,1,0:T(8,128)S(1)}, s32[8]{0:T(128)S(4)}, f32[4]{0:T(128)S(4)}) custom-call(bf16[27,64,64]{2,1,0:T(8,128)(2,1)} %wc_hbm, f32[1,64]{1,0:T(1,128)} %bitcast.19, f32[1,64]{1,0:T(1,128)} %bitcast.20, f32[1,64]{1,0:T(1,128)} %bitcast.21, ...), custom_call_target="tpu_custom_call" | custom-call | tf_op jit(solution)/shard_map/lhs3/pallas_call | solution.py:737
  15.0 0.6 collective-permute-done.2
  16.5 0.7 collective-permute-done.3.other_ref
  17.2 11.8 %forward.1 = (f32[2,8,128]{2,1,0:T(8,128)}, f32[2,8,128]{2,1,0:T(8,128)S(1)}, f32[134,64,128]{2,1,0:T(8,128)S(1)}, bf16[180,64,128]{2,1,0:T(8,128)(2,1)S(1)}) custom-call(s32[8]{0:T(128)S(4)} %get-tuple-element.82.home_ref, f32[4]{0:T(128)S(4)} %get-tuple-element.83.invd_ref, f32[1]{0:T(128)S(6)} %copy.26.hb_ref, ...), custom_call_target="tpu_custom_call" | custom-call | tf_op jit(solution)/shard_map/forward/pallas_call | solution.py:793
  29.0 0.7 collective-permute-start.5
  29.7 4.7 %collective-permute-start.6 = (f32[2,8,128]{2,1,0:T(8,128)S(1)}, f32[2,8,128]{2,1,0:T(8,128)S(1)}, u32[]{:S(2)}, u32[]{:S(2)}) collective-permute-start(f32[2,8,128]{2,1,0:T(8,128)S(1)} %get-tuple-element.92.score_ref.gm_ref), channel_id=1, source_target_pairs={{0,2},{2,0},{4,6},{6,4},{8,10},{10,8},{12,14},{14,12},{1,3},{3,1},... | collective-permute-start | bytes 24584 | tf_op jit(solution)/shard_map/ppermute | solution.py:829
  34.4 1.7 %early.1 = (f32[864,128]{1,0:T(8,128)S(1)}, f32[8,128]{1,0:T(8,128)S(1)}, bf16[720,2048]{1,0:T(8,128)(2,1)S(1)}) custom-call(f32[2,8,128]{2,1,0:T(8,128)S(1)} %get-tuple-element.92.score_ref.gm_ref, f32[134,64,128]{2,1,0:T(8,128)S(1)} %get-tuple-element.93.sbuf, bf16[180,64,128]{2,1,0:T(8,128)(2,1)S(1)} %get-tuple-element.94.hbuf, ...), custom_call_target="tpu_custom_call" | custom-call | tf_op jit(solution)/shard_map/early/pallas_call | solution.py:831
  36.1 0.6 collective-permute-start.7
  36.7 0.7 %collective-permute-done.7.p2o_ref = f32[2,8,128]{2,1,0:T(8,128)S(1)} collective-permute-done((f32[2,8,128]{2,1,0:T(8,128)S(1)}, f32[2,8,128]{2,1,0:T(8,128)S(1)}, u32[]{:S(2)}, u32[]{:S(2)}) %collective-permute-start.7) | collective-permute-done | bytes 8224 | tf_op jit(solution)/shard_map/ppermute | solution.py:624
  37.5 0.3 collective-permute-done.8.p1o_ref
  37.8 4.9 %backward.1 = (f32[904,128]{1,0:T(8,128)S(1)}, f32[904,128]{1,0:T(8,128)S(1)}) custom-call(f32[2,8,128]{2,1,0:T(8,128)S(1)} %get-tuple-element.92.score_ref.gm_ref, f32[2,8,128]{2,1,0:T(8,128)S(1)} %collective-permute-done.4.gmo_ref, f32[2,8,128]{2,1,0:T(8,128)S(1)} %collective-permute-done.5.p2_ref, f32[2,8,128]{2,1,0:T(8,128)S(1)} %collective-permute-done.7.p2o_ref, ...), custom_call_target="tpu_custom_call" | custom-call | tf_op jit(solution)/shard_map/backward/pallas_call | solution.py:852
  42.9 1.7 %collective-permute-done.9 = f32[904,128]{1,0:T(8,128)S(1)} collective-permute-done((f32[904,128]{1,0:T(8,128)S(1)}, f32[904,128]{1,0:T(8,128)S(1)}, u32[]{:S(2)}, u32[]{:S(2)}) %collective-permute-start.9) | collective-permute-done | bytes 462880 | tf_op jit(solution)/shard_map/ppermute | solution.py:624
  44.8 1.7 %collective-permute-start.10 = (bf16[464,128]{1,0:T(8,128)(2,1)S(1)}, bf16[464,128]{1,0:T(8,128)(2,1)S(1)}, u32[]{:S(2)}, u32[]{:S(2)}) collective-permute-start(bf16[464,128]{1,0:T(8,128)(2,1)S(1)} %pad_maximum_fusion), channel_id=1, source_target_pairs={{0,4},{1,5},{2,6},{3,7},{4,0},{5,1},{6,2},{7,3},{8,12},{9,13},{10,... | collective-permute-start | bytes 356360 | tf_op jit(solution)/shard_map/ppermute | solution.py:624
  46.5 3.7 %collective-permute-done.10 = bf16[464,128]{1,0:T(8,128)(2,1)S(1)} collective-permute-done((bf16[464,128]{1,0:T(8,128)(2,1)S(1)}, bf16[464,128]{1,0:T(8,128)(2,1)S(1)}, u32[]{:S(2)}, u32[]{:S(2)}) %collective-permute-start.10) | collective-permute-done | bytes 118816 | tf_op jit(solution)/shard_map/ppermute | solution.py:624
  50.2 1.8 %collective-permute-start.11 = (bf16[464,128]{1,0:T(8,128)(2,1)S(1)}, bf16[464,128]{1,0:T(8,128)(2,1)S(1)}, u32[]{:S(2)}, u32[]{:S(2)}) collective-permute-start(bf16[464,128]{1,0:T(8,128)(2,1)S(1)} %pad_maximum_fusion.1), channel_id=1, source_target_pairs={{0,2},{1,3},{2,0},{3,1},{4,6},{5,7},{6,4},{7,5},{8,10},{9,11},{10,... | collective-permute-start | bytes 356360 | tf_op jit(solution)/shard_map/ppermute | solution.py:624
  52.0 3.1 %collective-permute-done.11 = bf16[464,128]{1,0:T(8,128)(2,1)S(1)} collective-permute-done((bf16[464,128]{1,0:T(8,128)(2,1)S(1)}, bf16[464,128]{1,0:T(8,128)(2,1)S(1)}, u32[]{:S(2)}, u32[]{:S(2)}) %collective-permute-start.11) | collective-permute-done | bytes 118816 | tf_op jit(solution)/shard_map/ppermute | solution.py:624
  55.2 3.3 %collective-permute-start.12 = (bf16[464,128]{1,0:T(8,128)(2,1)S(1)}, bf16[464,128]{1,0:T(8,128)(2,1)S(1)}, u32[]{:S(2)}, u32[]{:S(2)}) collective-permute-start(bf16[464,128]{1,0:T(8,128)(2,1)S(1)} %pad_maximum_fusion.2), channel_id=1, source_target_pairs={{0,8},{1,9},{2,10},{3,11},{4,12},{5,13},{6,14},{7,15},{8,0},{9,1},... | collective-permute-start | bytes 356360 | tf_op jit(solution)/shard_map/ppermute | solution.py:624
  58.5 4.3 %collective-permute-done.12 = bf16[464,128]{1,0:T(8,128)(2,1)S(1)} collective-permute-done((bf16[464,128]{1,0:T(8,128)(2,1)S(1)}, bf16[464,128]{1,0:T(8,128)(2,1)S(1)}, u32[]{:S(2)}, u32[]{:S(2)}) %collective-permute-start.12) | collective-permute-done | bytes 118816 | tf_op jit(solution)/shard_map/ppermute | solution.py:624
  63.0 0.5 collective-permute-start.14
  63.5 0.5 slice.58
  64.3 1.1 %near.1 = (f32[27,64,64]{2,1,0:T(8,128)}, f32[27,64,64]{2,1,0:T(8,128)}, f32[2,64,64]{2,1,0:T(8,128)S(1)}) custom-call(bf16[448,128]{1,0:T(8,128)(2,1)S(1)} %fusion.mine_ref, bf16[448,128]{1,0:T(8,128)(2,1)S(1)} %collective-permute-done.13.far_ref), custom_call_target="tpu_custom_call" | custom-call | tf_op jit(solution)/shard_map/near/pallas_call | solution.py:878
  65.4 3.1 %collective-permute-done.14.mine_ref = bf16[448,128]{1,0:T(8,128)(2,1)S(1)} collective-permute-done((bf16[448,128]{1,0:T(8,128)(2,1)S(1)}, bf16[448,128]{1,0:T(8,128)(2,1)S(1)}, u32[]{:S(2)}, u32[]{:S(2)}) %collective-permute-start.14) | collective-permute-done | bytes 114720 | tf_op jit(solution)/shard_map/ppermute | solution.py:624
  68.5 0.6 slice_bitcast_fusion
  69.1 0.7 %collective-permute-done.15.far_ref = bf16[448,128]{1,0:T(8,128)(2,1)S(1)} collective-permute-done((bf16[448,128]{1,0:T(8,128)(2,1)S(1)}, bf16[448,128]{1,0:T(8,128)(2,1)S(1)}, u32[]{:S(2)}, u32[]{:S(2)}) %collective-permute-start.15) | collective-permute-done | bytes 114720 | tf_op jit(solution)/shard_map/ppermute | solution.py:624
  69.9 1.1 %finish.1 = (f32[27,64,64]{2,1,0:T(8,128)}, f32[27,64,64]{2,1,0:T(8,128)}, f32[3,27,64]{2,1,0:T(8,128)}) custom-call(bf16[448,128]{1,0:T(8,128)(2,1)S(1)} %collective-permute-done.14.mine_ref, bf16[448,128]{1,0:T(8,128)(2,1)S(1)} %collective-permute-done.15.far_ref, ...), custom_call_target="tpu_custom_call", output_to_operand_aliasing={{0}: (3, {}), {1}: (4, {})} | custom-call | tf_op jit(solution)/shard_map/finish/pallas_call | solution.py:889
  (31 shorter events, 1.3 us)
Async XLA Ops:
  1.4 4.8 %collective-permute-start = (bf16[1,2,8,4,128]{4,3,2,1,0:T(4,128)(2,1)S(1)}, bf16[1,2,8,4,128]{4,3,2,1,0:T(4,128)(2,1)S(1)}, u32[]{:S(2)}, u32[]{:S(2)}) collective-permute-start(bf16[1,2,8,4,128]{4,3,2,1,0:T(4,128)(2,1)S(1)} %bitcast.16), channel_id=1, source_target_pairs={{0,2},{1,3},{2,0},{3,1},{4,6},{5,7},{6,4},{7,5},{8,10},{9,11},{10,... | collective-permute-start | bytes 49160 | tf_op jit(solution)/shard_map/ppermute | solution.py:624
  6.2 4.0 %collective-permute-start.1 = (bf16[2,2,8,4,128]{4,3,2,1,0:T(4,128)(2,1)S(1)}, bf16[2,2,8,4,128]{4,3,2,1,0:T(4,128)(2,1)S(1)}, u32[]{:S(2)}, u32[]{:S(2)}) collective-permute-start(bf16[2,2,8,4,128]{4,3,2,1,0:T(4,128)(2,1)S(1)} %maximum_select_fusion.2), channel_id=1, source_target_pairs={{0,4},{1,5},{2,6},{3,7},{4,0},{5,1},{6,2},{7,3},{8,12},{9,13},{10,... | collective-permute-start | bytes 98312 | tf_op jit(solution)/shard_map/ppermute | solution.py:624
  10.3 5.3 %collective-permute-start.2 = (bf16[4,2,8,4,128]{4,3,2,1,0:T(4,128)(2,1)S(1)}, bf16[4,2,8,4,128]{4,3,2,1,0:T(4,128)(2,1)S(1)}, u32[]{:S(2)}, u32[]{:S(2)}) collective-permute-start(bf16[4,2,8,4,128]{4,3,2,1,0:T(4,128)(2,1)S(1)} %maximum_select_fusion.1), channel_id=1, source_target_pairs={{0,8},{1,9},{2,10},{3,11},{4,12},{5,13},{6,14},{7,15},{8,0},{9,1},... | collective-permute-start | bytes 196616 | tf_op jit(solution)/shard_map/ppermute | solution.py:624
  15.8 1.4 %collective-permute-start.3 = (bf16[8,2,8,4,128]{4,3,2,1,0:T(4,128)(2,1)S(1)}, bf16[8,2,8,4,128]{4,3,2,1,0:T(4,128)(2,1)S(1)}, u32[]{:S(2)}, u32[]{:S(2)}) collective-permute-start(bf16[8,2,8,4,128]{4,3,2,1,0:T(4,128)(2,1)S(1)} %maximum_select_fusion.mine_ref), channel_id=1, source_target_pairs={{0,1},{1,0},{2,3},{3,2},{4,5},{5,4},{6,7},{7,6},{8,9},{9,8},{10,11... | collective-permute-start | bytes 393224 | tf_op jit(solution)/shard_map/ppermute | solution.py:624
  29.0 7.0 %collective-permute-start.5 = (f32[2,8,128]{2,1,0:T(8,128)S(1)}, f32[2,8,128]{2,1,0:T(8,128)S(1)}, u32[]{:S(2)}, u32[]{:S(2)}) collective-permute-start(f32[2,8,128]{2,1,0:T(8,128)S(1)} %get-tuple-element.92.score_ref.gm_ref), channel_id=1, source_target_pairs={{2,4},{4,2},{6,8},{8,6},{10,12},{12,10},{3,5},{5,3},{7,9},{9,7},{1... | collective-permute-start | bytes 24584 | tf_op jit(solution)/shard_map/ppermute | solution.py:828
  29.7 6.4 %collective-permute-start.6 = (f32[2,8,128]{2,1,0:T(8,128)S(1)}, f32[2,8,128]{2,1,0:T(8,128)S(1)}, u32[]{:S(2)}, u32[]{:S(2)}) collective-permute-start(f32[2,8,128]{2,1,0:T(8,128)S(1)} %get-tuple-element.92.score_ref.gm_ref), channel_id=1, source_target_pairs={{0,2},{2,0},{4,6},{6,4},{8,10},{10,8},{12,14},{14,12},{1,3},{3,1},... | collective-permute-start | bytes 24584 | tf_op jit(solution)/shard_map/ppermute | solution.py:829
  34.3 2.4 %collective-permute-start.4 = (f32[2,8,128]{2,1,0:T(8,128)S(1)}, f32[2,8,128]{2,1,0:T(8,128)S(1)}, u32[]{:S(2)}, u32[]{:S(2)}) collective-permute-start(f32[2,8,128]{2,1,0:T(8,128)S(1)} %get-tuple-element.92.score_ref.gm_ref), channel_id=1, source_target_pairs={{0,1},{1,0},{2,3},{3,2},{4,5},{5,4},{6,7},{7,6},{8,9},{9,8},{10,11... | collective-permute-start | bytes 24584 | tf_op jit(solution)/shard_map/ppermute | solution.py:624
  36.1 1.4 %collective-permute-start.7 = (f32[2,8,128]{2,1,0:T(8,128)S(1)}, f32[2,8,128]{2,1,0:T(8,128)S(1)}, u32[]{:S(2)}, u32[]{:S(2)}) collective-permute-start(f32[2,8,128]{2,1,0:T(8,128)S(1)} %collective-permute-done.5.p2_ref), channel_id=1, source_target_pairs={{0,1},{1,0},{2,3},{3,2},{4,5},{5,4},{6,7},{7,6},{8,9},{9,8},{10,11... | collective-permute-start | bytes 24584 | tf_op jit(solution)/shard_map/ppermute | solution.py:624
  36.6 1.2 %collective-permute-start.8 = (f32[2,8,128]{2,1,0:T(8,128)S(1)}, f32[2,8,128]{2,1,0:T(8,128)S(1)}, u32[]{:S(2)}, u32[]{:S(2)}) collective-permute-start(f32[2,8,128]{2,1,0:T(8,128)S(1)} %collective-permute-done.6.p1_ref), channel_id=1, source_target_pairs={{0,1},{1,0},{2,3},{3,2},{4,5},{5,4},{6,7},{7,6},{8,9},{9,8},{10,11... | collective-permute-start | bytes 24584 | tf_op jit(solution)/shard_map/ppermute | solution.py:624
  42.7 1.9 %collective-permute-start.9 = (f32[904,128]{1,0:T(8,128)S(1)}, f32[904,128]{1,0:T(8,128)S(1)}, u32[]{:S(2)}, u32[]{:S(2)}) collective-permute-start(f32[904,128]{1,0:T(8,128)S(1)} %get-tuple-element.104), channel_id=1, source_target_pairs={{0,1},{1,0},{2,3},{3,2},{4,5},{5,4},{6,7},{7,6},{8,9},{9,8},{10,11... | collective-permute-start | bytes 1388552 | tf_op jit(solution)/shard_map/ppermute | solution.py:624
  44.8 5.4 %collective-permute-start.10 = (bf16[464,128]{1,0:T(8,128)(2,1)S(1)}, bf16[464,128]{1,0:T(8,128)(2,1)S(1)}, u32[]{:S(2)}, u32[]{:S(2)}) collective-permute-start(bf16[464,128]{1,0:T(8,128)(2,1)S(1)} %pad_maximum_fusion), channel_id=1, source_target_pairs={{0,4},{1,5},{2,6},{3,7},{4,0},{5,1},{6,2},{7,3},{8,12},{9,13},{10,... | collective-permute-start | bytes 356360 | tf_op jit(solution)/shard_map/ppermute | solution.py:624
  50.2 4.9 %collective-permute-start.11 = (bf16[464,128]{1,0:T(8,128)(2,1)S(1)}, bf16[464,128]{1,0:T(8,128)(2,1)S(1)}, u32[]{:S(2)}, u32[]{:S(2)}) collective-permute-start(bf16[464,128]{1,0:T(8,128)(2,1)S(1)} %pad_maximum_fusion.1), channel_id=1, source_target_pairs={{0,2},{1,3},{2,0},{3,1},{4,6},{5,7},{6,4},{7,5},{8,10},{9,11},{10,... | collective-permute-start | bytes 356360 | tf_op jit(solution)/shard_map/ppermute | solution.py:624
  55.2 7.6 %collective-permute-start.12 = (bf16[464,128]{1,0:T(8,128)(2,1)S(1)}, bf16[464,128]{1,0:T(8,128)(2,1)S(1)}, u32[]{:S(2)}, u32[]{:S(2)}) collective-permute-start(bf16[464,128]{1,0:T(8,128)(2,1)S(1)} %pad_maximum_fusion.2), channel_id=1, source_target_pairs={{0,8},{1,9},{2,10},{3,11},{4,12},{5,13},{6,14},{7,15},{8,0},{9,1},... | collective-permute-start | bytes 356360 | tf_op jit(solution)/shard_map/ppermute | solution.py:624
  62.9 1.4 %collective-permute-start.13 = (bf16[448,128]{1,0:T(8,128)(2,1)S(1)}, bf16[448,128]{1,0:T(8,128)(2,1)S(1)}, u32[]{:S(2)}, u32[]{:S(2)}) collective-permute-start(bf16[448,128]{1,0:T(8,128)(2,1)S(1)} %fusion.mine_ref), channel_id=1, source_target_pairs={{0,1},{1,0},{2,3},{3,2},{4,5},{5,4},{6,7},{7,6},{8,9},{9,8},{10,11... | collective-permute-start | bytes 344072 | tf_op jit(solution)/shard_map/ppermute | solution.py:624
  63.0 5.6 %collective-permute-start.14 = (bf16[448,128]{1,0:T(8,128)(2,1)S(1)}, bf16[448,128]{1,0:T(8,128)(2,1)S(1)}, u32[]{:S(2)}, u32[]{:S(2)}) collective-permute-start(bf16[448,128]{1,0:T(8,128)(2,1)S(1)} %fusion.mine_ref), channel_id=1, source_target_pairs={{0,4},{1,5},{2,6},{3,7},{4,0},{5,1},{6,2},{7,3},{8,12},{9,13},{10,... | collective-permute-start | bytes 344072 | tf_op jit(solution)/shard_map/ppermute | solution.py:624
  68.5 1.3 %collective-permute-start.15 = (bf16[448,128]{1,0:T(8,128)(2,1)S(1)}, bf16[448,128]{1,0:T(8,128)(2,1)S(1)}, u32[]{:S(2)}, u32[]{:S(2)}) collective-permute-start(bf16[448,128]{1,0:T(8,128)(2,1)S(1)} %collective-permute-done.14.mine_ref), channel_id=1, source_target_pairs={{0,1},{1,0},{2,3},{3,2},{4,5},{5,4},{6,7},{7,6},{8,9},{9,8},{10,11... | collective-permute-start | bytes 344072 | tf_op jit(solution)/shard_map/ppermute | solution.py:624

commit v10 on v9

--- a/solution.py
+++ b/solution.py
@@ -257,11 +257,11 @@
         scl[X, 1 : NY + 1, :] = sc * liq[X, 1 : NY + 1, :]
 
     def load_planes(i, c):
-        for k in range(3):
-            load_plane(3 * i + k)
+        for k in range(6):
+            load_plane(6 * i + k)
         return c
 
-    lax.fori_loop(0, PLANES // 3, load_planes, 0)
+    lax.fori_loop(0, PLANES // 6, load_planes, 0)
 
     def planes(count, body):
         def step(i, c):
@@ -284,12 +284,11 @@
                 if slot is not None:
                     sbuf[S1 + 12 * slot + 2 * j + k] = slope_of(z, sig) * m
 
-    def layer1_pair(i):
-        X = 1 + 2 * i + 2 * (i // 2)
-        layer1(X, None)
-        layer1(X + 1, None)
-
-    planes(4, layer1_pair)
+    def layer1_side(i):
+        for k in range(4):
+            layer1(1 + 6 * i + k, None)
+
+    planes(2, layer1_side)
     layer1(MID, 0)
     layer1(MID + 1, 1)
 
@@ -308,8 +307,10 @@
                     if slot is not None:
                         sbuf[S2 + 12 * (slot + d) + j + k] = slope_of(z, sig) * m
 
-    planes(2, lambda i: layer2(2 + 6 * i, None))
-    planes(2, lambda i: layer2(MID - 1 + 2 * i, 2 * i))
+    for i in range(2):
+        layer2(2 + 6 * i, None)
+    for i in range(2):
+        layer2(MID - 1 + 2 * i, 2 * i)
 
     y2 = gy * 6 + 1
 
@@ -329,7 +330,8 @@
                     sbuf[S3 + 10 * (2 * i + d) + 2 * j + k] = slope_of(z, sig) * m
                     h3o[2 * i + d, 2 * j + k] = h3
 
-    planes(3, layer3)
+    for i in range(3):
+        layer3(i)
 
     def operator(val, X):
         v = val[X, 1 : NY + 1, :]
@@ -381,7 +383,8 @@
             hbuf[H1 + FRAME * i + l] = h1[MID - 1 + i, f0 + l]
             hbuf[H2 + FRAME * i + l] = h2[MID - 1 + i, f0 + l]
 
-    planes(4, copy_out)
+    for i in range(4):
+        copy_out(i)
     for r in range(36):
         hbuf[WB + r] = tb_ref[r]
         hbuf[WC + r] = tc_ref[r]
@@ -488,19 +491,13 @@
             ref[X, 0] = z
             ref[X, FRAME - 1] = z
 
-    def planes(count, body):
-        def step(i, c):
-            body(i)
-            return c
-
-        lax.fori_loop(0, count, step, 0)
-
     def back3(X):
         for j in range(10):
             g = gs[X, pl.ds(gy * 6 + j, 1), :]
             g3[X, j + 1] = (g * wide_ref[3] * sbuf[S3 + 10 * X + j]).astype(BF16)
 
-    planes(6, back3)
+    for X in range(6):
+        back3(X)
 
     for X in range(2):
         for r in range(WROWS, ROWS, 8):
@@ -519,7 +516,8 @@
                         lane_taps(Y, d, k) * sbuf[S2 + 12 * (X + d) + row]
                     ).astype(BF16)
 
-    planes(2, back2)
+    for i in range(2):
+        back2(i)
     bias_b = jnp.zeros((HID, NZ), F32)
     for i in range(16):
         cols = slice(i * NZ, (i + 1) * NZ)

time: 71.3 us -> 69.2 us (0.971)
  Pallas kernels: 24.5 us -> 22.1 us
    pallas_call x1, Pallas kernels: 11.8 us -> 9.95 us  [on_device(): pl.pallas_call(functools.partial(forward_kernel, n_slots=n_slots, cells=c...]
  transfers between devices with their start and end apart: 16 -> 16, of which waited for: 13 -> 13; matrix products, arithmetic and copies ran while one was open for 2% -> 2% of each run, Pallas kernels for 8% -> 9%
where the time goes in v10:
time: 69.2 us; the launch traced here: 68.9 us
  Pallas kernels  22.1 us (32%)
  starting transfers between devices  22.1 us (32%)
  waiting for transfers between devices  21.4 us (31%)
  between operations  1.65 us (2%)
  local copies, waits for them, and re-layouts  1.14 us (2%)
    ppermute x14, waiting for transfers between devices, partner(): return lax.ppermute(value, AXES, [(i, i ^ bit) for i in range(count)])  21.4 us
    ppermute x14, starting transfers between devices, partner(): return lax.ppermute(value, AXES, [(i, i ^ bit) for i in range(count)])  16.6 us
    pallas_call x1, Pallas kernels, on_device(): pl.pallas_call(functools.partial(forward_kernel, n_slots=n_slots, cells=c...  9.95 us
    ppermute x1, starting transfers between devices, on_device(): swap1 = lax.ppermute(score, 'gx', [(i, i ^ 1) for i in range(n_slots)])  4.67 us
    pallas_call x1, Pallas kernels, on_device(): pl.pallas_call(backward_kernel, out_shape=(shaped((ROWS + 8, NZ), F32), s...  4.32 us
    pallas_call x1, Pallas kernels, on_device(): pl.pallas_call(early_kernel, out_shape=(shaped((WROWS, NZ), F32), shaped(...  1.68 us
    pallas_call x1, Pallas kernels, layouts3(): pl.pallas_call(third_lhs_kernel, out_shape=(lhs, turned, shaped((4, HID,...  1.63 us
    pallas_call x1, Pallas kernels, layouts2(): pl.pallas_call(second_lhs_kernel, out_shape=(shaped((HID, 144), BF16), lh...  1.56 us
  transfers between devices with their start and end apart: 16, of which 13 were waited for; matrix products, arithmetic and copies ran while one was open for 2% of the time, Pallas kernels for 9%

profile of v10, /device:TPU:0, one launch (start us, length us, event | category | flops | bytes accessed | tf_op | source)
XLA Modules:
  0.0 68.9 jit_solution(1053010639713159125)
XLA Ops:
  0.6 0.8 %payload.1 = bf16[2,8,4,128]{3,2,1,0:T(4,128)(2,1)S(1)} custom-call(bf16[2,2,8,128]{3,2,1,0:T(8,128)(2,1)} %fields_hbm.1, s32[2,8,128]{2,1,0:T(8,128)} %liquid_hbm.1, s32[2,8,128]{2,1,0:T(8,128)} %class_hbm.1), custom_call_target="tpu_custom_call" | custom-call | tf_op jit(solution)/shard_map/payload/pallas_call | solution.py:700
  1.4 3.0 %collective-permute-start = (bf16[1,2,8,4,128]{4,3,2,1,0:T(4,128)(2,1)S(1)}, bf16[1,2,8,4,128]{4,3,2,1,0:T(4,128)(2,1)S(1)}, u32[]{:S(2)}, u32[]{:S(2)}) collective-permute-start(bf16[1,2,8,4,128]{4,3,2,1,0:T(4,128)(2,1)S(1)} %bitcast.16), channel_id=1, source_target_pairs={{0,2},{1,3},{2,0},{3,1},{4,6},{5,7},{6,4},{7,5},{8,10},{9,11},{10,... | collective-permute-start | bytes 49160 | tf_op jit(solution)/shard_map/ppermute | solution.py:622
  4.5 1.7 %collective-permute-done = bf16[1,2,8,4,128]{4,3,2,1,0:T(4,128)(2,1)S(1)} collective-permute-done((bf16[1,2,8,4,128]{4,3,2,1,0:T(4,128)(2,1)S(1)}, bf16[1,2,8,4,128]{4,3,2,1,0:T(4,128)(2,1)S(1)}, u32[]{:S(2)}, u32[]{:S(2)}) %collective-permute-start) | collective-permute-done | bytes 16416 | tf_op jit(solution)/shard_map/ppermute | solution.py:622
  6.2 2.1 %collective-permute-start.1 = (bf16[2,2,8,4,128]{4,3,2,1,0:T(4,128)(2,1)S(1)}, bf16[2,2,8,4,128]{4,3,2,1,0:T(4,128)(2,1)S(1)}, u32[]{:S(2)}, u32[]{:S(2)}) collective-permute-start(bf16[2,2,8,4,128]{4,3,2,1,0:T(4,128)(2,1)S(1)} %maximum_select_fusion.2), channel_id=1, source_target_pairs={{0,4},{1,5},{2,6},{3,7},{4,0},{5,1},{6,2},{7,3},{8,12},{9,13},{10,... | collective-permute-start | bytes 98312 | tf_op jit(solution)/shard_map/ppermute | solution.py:622
  8.3 1.6 %lhs2.1 = (bf16[64,144]{1,0:T(8,128)(2,1)S(1)}, bf16[384,768]{1,0:T(8,128)(2,1)S(1)}, bf16[36,64,128]{2,1,0:T(8,128)(2,1)S(1)}) custom-call(bf16[27,64,64]{2,1,0:T(8,128)(2,1)} %wb_hbm, bf16[3,27,64]{2,1,0:T(8,128)(2,1)} %bitcast.18), custom_call_target="tpu_custom_call" | custom-call | tf_op jit(solution)/shard_map/lhs2/pallas_call | solution.py:720
  9.9 0.3 collective-permute-done.1
  10.3 3.1 %collective-permute-start.2 = (bf16[4,2,8,4,128]{4,3,2,1,0:T(4,128)(2,1)S(1)}, bf16[4,2,8,4,128]{4,3,2,1,0:T(4,128)(2,1)S(1)}, u32[]{:S(2)}, u32[]{:S(2)}) collective-permute-start(bf16[4,2,8,4,128]{4,3,2,1,0:T(4,128)(2,1)S(1)} %maximum_select_fusion.1), channel_id=1, source_target_pairs={{0,8},{1,9},{2,10},{3,11},{4,12},{5,13},{6,14},{7,15},{8,0},{9,1},... | collective-permute-start | bytes 196616 | tf_op jit(solution)/shard_map/ppermute | solution.py:622
  13.4 1.6 %lhs3.1 = (bf16[384,768]{1,0:T(8,128)(2,1)S(1)}, bf16[36,64,128]{2,1,0:T(8,128)(2,1)S(1)}, f32[4,64,128]{2,1,0:T(8,128)S(1)}, s32[8]{0:T(128)S(4)}, f32[4]{0:T(128)S(4)}) custom-call(bf16[27,64,64]{2,1,0:T(8,128)(2,1)} %wc_hbm, f32[1,64]{1,0:T(1,128)} %bitcast.19, f32[1,64]{1,0:T(1,128)} %bitcast.20, f32[1,64]{1,0:T(1,128)} %bitcast.21, ...), custom_call_target="tpu_custom_call" | custom-call | tf_op jit(solution)/shard_map/lhs3/pallas_call | solution.py:735
  15.0 0.6 collective-permute-done.2
  16.5 0.7 collective-permute-done.3.other_ref
  17.2 10.0 %forward.1 = (f32[2,8,128]{2,1,0:T(8,128)}, f32[2,8,128]{2,1,0:T(8,128)S(1)}, f32[134,64,128]{2,1,0:T(8,128)S(1)}, bf16[180,64,128]{2,1,0:T(8,128)(2,1)S(1)}) custom-call(s32[8]{0:T(128)S(4)} %get-tuple-element.82.home_ref, f32[4]{0:T(128)S(4)} %get-tuple-element.83.invd_ref, f32[1]{0:T(128)S(6)} %copy.26.hb_ref, ...), custom_call_target="tpu_custom_call" | custom-call | tf_op jit(solution)/shard_map/forward/pallas_call | solution.py:791
  27.2 0.8 %collective-permute-start.5 = (f32[2,8,128]{2,1,0:T(8,128)S(1)}, f32[2,8,128]{2,1,0:T(8,128)S(1)}, u32[]{:S(2)}, u32[]{:S(2)}) collective-permute-start(f32[2,8,128]{2,1,0:T(8,128)S(1)} %get-tuple-element.92.score_ref.gm_ref), channel_id=1, source_target_pairs={{2,4},{4,2},{6,8},{8,6},{10,12},{12,10},{3,5},{5,3},{7,9},{9,7},{1... | collective-permute-start | bytes 24584 | tf_op jit(solution)/shard_map/ppermute | solution.py:826
  28.0 4.7 %collective-permute-start.6 = (f32[2,8,128]{2,1,0:T(8,128)S(1)}, f32[2,8,128]{2,1,0:T(8,128)S(1)}, u32[]{:S(2)}, u32[]{:S(2)}) collective-permute-start(f32[2,8,128]{2,1,0:T(8,128)S(1)} %get-tuple-element.92.score_ref.gm_ref), channel_id=1, source_target_pairs={{0,2},{2,0},{4,6},{6,4},{8,10},{10,8},{12,14},{14,12},{1,3},{3,1},... | collective-permute-start | bytes 24584 | tf_op jit(solution)/shard_map/ppermute | solution.py:827
  32.7 1.7 %early.1 = (f32[864,128]{1,0:T(8,128)S(1)}, f32[8,128]{1,0:T(8,128)S(1)}, bf16[720,2048]{1,0:T(8,128)(2,1)S(1)}) custom-call(f32[2,8,128]{2,1,0:T(8,128)S(1)} %get-tuple-element.92.score_ref.gm_ref, f32[134,64,128]{2,1,0:T(8,128)S(1)} %get-tuple-element.93.sbuf, bf16[180,64,128]{2,1,0:T(8,128)(2,1)S(1)} %get-tuple-element.94.hbuf, ...), custom_call_target="tpu_custom_call" | custom-call | tf_op jit(solution)/shard_map/early/pallas_call | solution.py:829
  34.4 0.6 collective-permute-start.7
  35.0 0.7 %collective-permute-done.7.p2o_ref = f32[2,8,128]{2,1,0:T(8,128)S(1)} collective-permute-done((f32[2,8,128]{2,1,0:T(8,128)S(1)}, f32[2,8,128]{2,1,0:T(8,128)S(1)}, u32[]{:S(2)}, u32[]{:S(2)}) %collective-permute-start.7) | collective-permute-done | bytes 8224 | tf_op jit(solution)/shard_map/ppermute | solution.py:622
  35.8 0.3 collective-permute-done.8.p1o_ref
  36.1 4.3 %backward.1 = (f32[904,128]{1,0:T(8,128)S(1)}, f32[904,128]{1,0:T(8,128)S(1)}) custom-call(f32[2,8,128]{2,1,0:T(8,128)S(1)} %get-tuple-element.92.score_ref.gm_ref, f32[2,8,128]{2,1,0:T(8,128)S(1)} %collective-permute-done.4.gmo_ref, f32[2,8,128]{2,1,0:T(8,128)S(1)} %collective-permute-done.5.p2_ref, f32[2,8,128]{2,1,0:T(8,128)S(1)} %collective-permute-done.7.p2o_ref, ...), custom_call_target="tpu_custom_call" | custom-call | tf_op jit(solution)/shard_map/backward/pallas_call | solution.py:850
  40.7 1.6 %collective-permute-done.9 = f32[904,128]{1,0:T(8,128)S(1)} collective-permute-done((f32[904,128]{1,0:T(8,128)S(1)}, f32[904,128]{1,0:T(8,128)S(1)}, u32[]{:S(2)}, u32[]{:S(2)}) %collective-permute-start.9) | collective-permute-done | bytes 462880 | tf_op jit(solution)/shard_map/ppermute | solution.py:622
  42.5 1.7 %collective-permute-start.10 = (bf16[464,128]{1,0:T(8,128)(2,1)S(1)}, bf16[464,128]{1,0:T(8,128)(2,1)S(1)}, u32[]{:S(2)}, u32[]{:S(2)}) collective-permute-start(bf16[464,128]{1,0:T(8,128)(2,1)S(1)} %pad_maximum_fusion), channel_id=1, source_target_pairs={{0,4},{1,5},{2,6},{3,7},{4,0},{5,1},{6,2},{7,3},{8,12},{9,13},{10,... | collective-permute-start | bytes 356360 | tf_op jit(solution)/shard_map/ppermute | solution.py:622
  44.2 3.7 %collective-permute-done.10 = bf16[464,128]{1,0:T(8,128)(2,1)S(1)} collective-permute-done((bf16[464,128]{1,0:T(8,128)(2,1)S(1)}, bf16[464,128]{1,0:T(8,128)(2,1)S(1)}, u32[]{:S(2)}, u32[]{:S(2)}) %collective-permute-start.10) | collective-permute-done | bytes 118816 | tf_op jit(solution)/shard_map/ppermute | solution.py:622
  48.0 1.8 %collective-permute-start.11 = (bf16[464,128]{1,0:T(8,128)(2,1)S(1)}, bf16[464,128]{1,0:T(8,128)(2,1)S(1)}, u32[]{:S(2)}, u32[]{:S(2)}) collective-permute-start(bf16[464,128]{1,0:T(8,128)(2,1)S(1)} %pad_maximum_fusion.1), channel_id=1, source_target_pairs={{0,2},{1,3},{2,0},{3,1},{4,6},{5,7},{6,4},{7,5},{8,10},{9,11},{10,... | collective-permute-start | bytes 356360 | tf_op jit(solution)/shard_map/ppermute | solution.py:622
  49.8 3.1 %collective-permute-done.11 = bf16[464,128]{1,0:T(8,128)(2,1)S(1)} collective-permute-done((bf16[464,128]{1,0:T(8,128)(2,1)S(1)}, bf16[464,128]{1,0:T(8,128)(2,1)S(1)}, u32[]{:S(2)}, u32[]{:S(2)}) %collective-permute-start.11) | collective-permute-done | bytes 118816 | tf_op jit(solution)/shard_map/ppermute | solution.py:622
  53.0 3.3 %collective-permute-start.12 = (bf16[464,128]{1,0:T(8,128)(2,1)S(1)}, bf16[464,128]{1,0:T(8,128)(2,1)S(1)}, u32[]{:S(2)}, u32[]{:S(2)}) collective-permute-start(bf16[464,128]{1,0:T(8,128)(2,1)S(1)} %pad_maximum_fusion.2), channel_id=1, source_target_pairs={{0,8},{1,9},{2,10},{3,11},{4,12},{5,13},{6,14},{7,15},{8,0},{9,1},... | collective-permute-start | bytes 356360 | tf_op jit(solution)/shard_map/ppermute | solution.py:622
  56.3 4.3 %collective-permute-done.12 = bf16[464,128]{1,0:T(8,128)(2,1)S(1)} collective-permute-done((bf16[464,128]{1,0:T(8,128)(2,1)S(1)}, bf16[464,128]{1,0:T(8,128)(2,1)S(1)}, u32[]{:S(2)}, u32[]{:S(2)}) %collective-permute-start.12) | collective-permute-done | bytes 118816 | tf_op jit(solution)/shard_map/ppermute | solution.py:622
  60.8 0.5 collective-permute-start.14
  61.3 0.5 slice.58
  62.1 1.1 %near.1 = (f32[27,64,64]{2,1,0:T(8,128)}, f32[27,64,64]{2,1,0:T(8,128)}, f32[2,64,64]{2,1,0:T(8,128)S(1)}) custom-call(bf16[448,128]{1,0:T(8,128)(2,1)S(1)} %fusion.mine_ref, bf16[448,128]{1,0:T(8,128)(2,1)S(1)} %collective-permute-done.13.far_ref), custom_call_target="tpu_custom_call" | custom-call | tf_op jit(solution)/shard_map/near/pallas_call | solution.py:876
  63.2 3.1 %collective-permute-done.14.mine_ref = bf16[448,128]{1,0:T(8,128)(2,1)S(1)} collective-permute-done((bf16[448,128]{1,0:T(8,128)(2,1)S(1)}, bf16[448,128]{1,0:T(8,128)(2,1)S(1)}, u32[]{:S(2)}, u32[]{:S(2)}) %collective-permute-start.14) | collective-permute-done | bytes 114720 | tf_op jit(solution)/shard_map/ppermute | solution.py:622
  66.4 0.6 slice_bitcast_fusion
  66.9 0.7 %collective-permute-done.15.far_ref = bf16[448,128]{1,0:T(8,128)(2,1)S(1)} collective-permute-done((bf16[448,128]{1,0:T(8,128)(2,1)S(1)}, bf16[448,128]{1,0:T(8,128)(2,1)S(1)}, u32[]{:S(2)}, u32[]{:S(2)}) %collective-permute-start.15) | collective-permute-done | bytes 114720 | tf_op jit(solution)/shard_map/ppermute | solution.py:622
  67.7 1.1 %finish.1 = (f32[27,64,64]{2,1,0:T(8,128)}, f32[27,64,64]{2,1,0:T(8,128)}, f32[3,27,64]{2,1,0:T(8,128)}) custom-call(bf16[448,128]{1,0:T(8,128)(2,1)S(1)} %collective-permute-done.14.mine_ref, bf16[448,128]{1,0:T(8,128)(2,1)S(1)} %collective-permute-done.15.far_ref, ...), custom_call_target="tpu_custom_call", output_to_operand_aliasing={{0}: (3, {}), {1}: (4, {})} | custom-call | tf_op jit(solution)/shard_map/finish/pallas_call | solution.py:887
  (31 shorter events, 1.4 us)
Async XLA Ops:
  1.4 4.8 %collective-permute-start = (bf16[1,2,8,4,128]{4,3,2,1,0:T(4,128)(2,1)S(1)}, bf16[1,2,8,4,128]{4,3,2,1,0:T(4,128)(2,1)S(1)}, u32[]{:S(2)}, u32[]{:S(2)}) collective-permute-start(bf16[1,2,8,4,128]{4,3,2,1,0:T(4,128)(2,1)S(1)} %bitcast.16), channel_id=1, source_target_pairs={{0,2},{1,3},{2,0},{3,1},{4,6},{5,7},{6,4},{7,5},{8,10},{9,11},{10,... | collective-permute-start | bytes 49160 | tf_op jit(solution)/shard_map/ppermute | solution.py:622
  6.2 4.0 %collective-permute-start.1 = (bf16[2,2,8,4,128]{4,3,2,1,0:T(4,128)(2,1)S(1)}, bf16[2,2,8,4,128]{4,3,2,1,0:T(4,128)(2,1)S(1)}, u32[]{:S(2)}, u32[]{:S(2)}) collective-permute-start(bf16[2,2,8,4,128]{4,3,2,1,0:T(4,128)(2,1)S(1)} %maximum_select_fusion.2), channel_id=1, source_target_pairs={{0,4},{1,5},{2,6},{3,7},{4,0},{5,1},{6,2},{7,3},{8,12},{9,13},{10,... | collective-permute-start | bytes 98312 | tf_op jit(solution)/shard_map/ppermute | solution.py:622
  10.3 5.3 %collective-permute-start.2 = (bf16[4,2,8,4,128]{4,3,2,1,0:T(4,128)(2,1)S(1)}, bf16[4,2,8,4,128]{4,3,2,1,0:T(4,128)(2,1)S(1)}, u32[]{:S(2)}, u32[]{:S(2)}) collective-permute-start(bf16[4,2,8,4,128]{4,3,2,1,0:T(4,128)(2,1)S(1)} %maximum_select_fusion.1), channel_id=1, source_target_pairs={{0,8},{1,9},{2,10},{3,11},{4,12},{5,13},{6,14},{7,15},{8,0},{9,1},... | collective-permute-start | bytes 196616 | tf_op jit(solution)/shard_map/ppermute | solution.py:622
  15.8 1.4 %collective-permute-start.3 = (bf16[8,2,8,4,128]{4,3,2,1,0:T(4,128)(2,1)S(1)}, bf16[8,2,8,4,128]{4,3,2,1,0:T(4,128)(2,1)S(1)}, u32[]{:S(2)}, u32[]{:S(2)}) collective-permute-start(bf16[8,2,8,4,128]{4,3,2,1,0:T(4,128)(2,1)S(1)} %maximum_select_fusion.mine_ref), channel_id=1, source_target_pairs={{0,1},{1,0},{2,3},{3,2},{4,5},{5,4},{6,7},{7,6},{8,9},{9,8},{10,11... | collective-permute-start | bytes 393224 | tf_op jit(solution)/shard_map/ppermute | solution.py:622
  27.2 7.2 %collective-permute-start.5 = (f32[2,8,128]{2,1,0:T(8,128)S(1)}, f32[2,8,128]{2,1,0:T(8,128)S(1)}, u32[]{:S(2)}, u32[]{:S(2)}) collective-permute-start(f32[2,8,128]{2,1,0:T(8,128)S(1)} %get-tuple-element.92.score_ref.gm_ref), channel_id=1, source_target_pairs={{2,4},{4,2},{6,8},{8,6},{10,12},{12,10},{3,5},{5,3},{7,9},{9,7},{1... | collective-permute-start | bytes 24584 | tf_op jit(solution)/shard_map/ppermute | solution.py:826
  28.0 6.4 %collective-permute-start.6 = (f32[2,8,128]{2,1,0:T(8,128)S(1)}, f32[2,8,128]{2,1,0:T(8,128)S(1)}, u32[]{:S(2)}, u32[]{:S(2)}) collective-permute-start(f32[2,8,128]{2,1,0:T(8,128)S(1)} %get-tuple-element.92.score_ref.gm_ref), channel_id=1, source_target_pairs={{0,2},{2,0},{4,6},{6,4},{8,10},{10,8},{12,14},{14,12},{1,3},{3,1},... | collective-permute-start | bytes 24584 | tf_op jit(solution)/shard_map/ppermute | solution.py:827
  32.7 2.4 %collective-permute-start.4 = (f32[2,8,128]{2,1,0:T(8,128)S(1)}, f32[2,8,128]{2,1,0:T(8,128)S(1)}, u32[]{:S(2)}, u32[]{:S(2)}) collective-permute-start(f32[2,8,128]{2,1,0:T(8,128)S(1)} %get-tuple-element.92.score_ref.gm_ref), channel_id=1, source_target_pairs={{0,1},{1,0},{2,3},{3,2},{4,5},{5,4},{6,7},{7,6},{8,9},{9,8},{10,11... | collective-permute-start | bytes 24584 | tf_op jit(solution)/shard_map/ppermute | solution.py:622
  34.4 1.4 %collective-permute-start.7 = (f32[2,8,128]{2,1,0:T(8,128)S(1)}, f32[2,8,128]{2,1,0:T(8,128)S(1)}, u32[]{:S(2)}, u32[]{:S(2)}) collective-permute-start(f32[2,8,128]{2,1,0:T(8,128)S(1)} %collective-permute-done.5.p2_ref), channel_id=1, source_target_pairs={{0,1},{1,0},{2,3},{3,2},{4,5},{5,4},{6,7},{7,6},{8,9},{9,8},{10,11... | collective-permute-start | bytes 24584 | tf_op jit(solution)/shard_map/ppermute | solution.py:622
  35.0 1.2 %collective-permute-start.8 = (f32[2,8,128]{2,1,0:T(8,128)S(1)}, f32[2,8,128]{2,1,0:T(8,128)S(1)}, u32[]{:S(2)}, u32[]{:S(2)}) collective-permute-start(f32[2,8,128]{2,1,0:T(8,128)S(1)} %collective-permute-done.6.p1_ref), channel_id=1, source_target_pairs={{0,1},{1,0},{2,3},{3,2},{4,5},{5,4},{6,7},{7,6},{8,9},{9,8},{10,11... | collective-permute-start | bytes 24584 | tf_op jit(solution)/shard_map/ppermute | solution.py:622
  40.5 1.9 %collective-permute-start.9 = (f32[904,128]{1,0:T(8,128)S(1)}, f32[904,128]{1,0:T(8,128)S(1)}, u32[]{:S(2)}, u32[]{:S(2)}) collective-permute-start(f32[904,128]{1,0:T(8,128)S(1)} %get-tuple-element.104), channel_id=1, source_target_pairs={{0,1},{1,0},{2,3},{3,2},{4,5},{5,4},{6,7},{7,6},{8,9},{9,8},{10,11... | collective-permute-start | bytes 1388552 | tf_op jit(solution)/shard_map/ppermute | solution.py:622
  42.5 5.4 %collective-permute-start.10 = (bf16[464,128]{1,0:T(8,128)(2,1)S(1)}, bf16[464,128]{1,0:T(8,128)(2,1)S(1)}, u32[]{:S(2)}, u32[]{:S(2)}) collective-permute-start(bf16[464,128]{1,0:T(8,128)(2,1)S(1)} %pad_maximum_fusion), channel_id=1, source_target_pairs={{0,4},{1,5},{2,6},{3,7},{4,0},{5,1},{6,2},{7,3},{8,12},{9,13},{10,... | collective-permute-start | bytes 356360 | tf_op jit(solution)/shard_map/ppermute | solution.py:622
  48.0 4.9 %collective-permute-start.11 = (bf16[464,128]{1,0:T(8,128)(2,1)S(1)}, bf16[464,128]{1,0:T(8,128)(2,1)S(1)}, u32[]{:S(2)}, u32[]{:S(2)}) collective-permute-start(bf16[464,128]{1,0:T(8,128)(2,1)S(1)} %pad_maximum_fusion.1), channel_id=1, source_target_pairs={{0,2},{1,3},{2,0},{3,1},{4,6},{5,7},{6,4},{7,5},{8,10},{9,11},{10,... | collective-permute-start | bytes 356360 | tf_op jit(solution)/shard_map/ppermute | solution.py:622
  53.0 7.6 %collective-permute-start.12 = (bf16[464,128]{1,0:T(8,128)(2,1)S(1)}, bf16[464,128]{1,0:T(8,128)(2,1)S(1)}, u32[]{:S(2)}, u32[]{:S(2)}) collective-permute-start(bf16[464,128]{1,0:T(8,128)(2,1)S(1)} %pad_maximum_fusion.2), channel_id=1, source_target_pairs={{0,8},{1,9},{2,10},{3,11},{4,12},{5,13},{6,14},{7,15},{8,0},{9,1},... | collective-permute-start | bytes 356360 | tf_op jit(solution)/shard_map/ppermute | solution.py:622
  60.7 1.4 %collective-permute-start.13 = (bf16[448,128]{1,0:T(8,128)(2,1)S(1)}, bf16[448,128]{1,0:T(8,128)(2,1)S(1)}, u32[]{:S(2)}, u32[]{:S(2)}) collective-permute-start(bf16[448,128]{1,0:T(8,128)(2,1)S(1)} %fusion.mine_ref), channel_id=1, source_target_pairs={{0,1},{1,0},{2,3},{3,2},{4,5},{5,4},{6,7},{7,6},{8,9},{9,8},{10,11... | collective-permute-start | bytes 344072 | tf_op jit(solution)/shard_map/ppermute | solution.py:622
  60.8 5.6 %collective-permute-start.14 = (bf16[448,128]{1,0:T(8,128)(2,1)S(1)}, bf16[448,128]{1,0:T(8,128)(2,1)S(1)}, u32[]{:S(2)}, u32[]{:S(2)}) collective-permute-start(bf16[448,128]{1,0:T(8,128)(2,1)S(1)} %fusion.mine_ref), channel_id=1, source_target_pairs={{0,4},{1,5},{2,6},{3,7},{4,0},{5,1},{6,2},{7,3},{8,12},{9,13},{10,... | collective-permute-start | bytes 344072 | tf_op jit(solution)/shard_map/ppermute | solution.py:622
  66.4 1.3 %collective-permute-start.15 = (bf16[448,128]{1,0:T(8,128)(2,1)S(1)}, bf16[448,128]{1,0:T(8,128)(2,1)S(1)}, u32[]{:S(2)}, u32[]{:S(2)}) collective-permute-start(bf16[448,128]{1,0:T(8,128)(2,1)S(1)} %collective-permute-done.14.mine_ref), channel_id=1, source_target_pairs={{0,1},{1,0},{2,3},{3,2},{4,5},{5,4},{6,7},{7,6},{8,9},{9,8},{10,11... | collective-permute-start | bytes 344072 | tf_op jit(solution)/shard_map/ppermute | solution.py:622

commit v11 on v10

--- a/solution.py
+++ b/solution.py
@@ -288,7 +288,8 @@
         for k in range(4):
             layer1(1 + 6 * i + k, None)
 
-    planes(2, layer1_side)
+    for i in range(2):
+        layer1_side(i)
     layer1(MID, 0)
     layer1(MID + 1, 1)
 

time: 69.2 us -> 69 us (level)
  no operation moved by 1% of the time
where the time goes in v11:
time: 69 us; the launch traced here: 68.7 us
  starting transfers between devices  22.1 us (32%)
  Pallas kernels  21.9 us (32%)
  waiting for transfers between devices  21.4 us (31%)
  between operations  1.65 us (2%)
  local copies, waits for them, and re-layouts  1.14 us (2%)
    ppermute x14, waiting for transfers between devices, partner(): return lax.ppermute(value, AXES, [(i, i ^ bit) for i in range(count)])  21.4 us
    ppermute x14, starting transfers between devices, partner(): return lax.ppermute(value, AXES, [(i, i ^ bit) for i in range(count)])  16.6 us
    pallas_call x1, Pallas kernels, on_device(): pl.pallas_call(functools.partial(forward_kernel, n_slots=n_slots, cells=c...  9.72 us
    ppermute x1, starting transfers between devices, on_device(): swap1 = lax.ppermute(score, 'gx', [(i, i ^ 1) for i in range(n_slots)])  4.68 us
    pallas_call x1, Pallas kernels, on_device(): pl.pallas_call(backward_kernel, out_shape=(shaped((ROWS + 8, NZ), F32), s...  4.32 us
    pallas_call x1, Pallas kernels, on_device(): pl.pallas_call(early_kernel, out_shape=(shaped((WROWS, NZ), F32), shaped(...  1.68 us
    pallas_call x1, Pallas kernels, layouts3(): pl.pallas_call(third_lhs_kernel, out_shape=(lhs, turned, shaped((4, HID,...  1.63 us
    pallas_call x1, Pallas kernels, layouts2(): pl.pallas_call(second_lhs_kernel, out_shape=(shaped((HID, 144), BF16), lh...  1.56 us
  transfers between devices with their start and end apart: 16, of which 13 were waited for; matrix products, arithmetic and copies ran while one was open for 2% of the time, Pallas kernels for 9%

profile of v11, /device:TPU:0, one launch (start us, length us, event | category | flops | bytes accessed | tf_op | source)
XLA Modules:
  0.0 68.7 jit_solution(6897424698471503913)
XLA Ops:
  0.6 0.8 %payload.1 = bf16[2,8,4,128]{3,2,1,0:T(4,128)(2,1)S(1)} custom-call(bf16[2,2,8,128]{3,2,1,0:T(8,128)(2,1)} %fields_hbm.1, s32[2,8,128]{2,1,0:T(8,128)} %liquid_hbm.1, s32[2,8,128]{2,1,0:T(8,128)} %class_hbm.1), custom_call_target="tpu_custom_call" | custom-call | tf_op jit(solution)/shard_map/payload/pallas_call | solution.py:701
  1.4 3.0 %collective-permute-start = (bf16[1,2,8,4,128]{4,3,2,1,0:T(4,128)(2,1)S(1)}, bf16[1,2,8,4,128]{4,3,2,1,0:T(4,128)(2,1)S(1)}, u32[]{:S(2)}, u32[]{:S(2)}) collective-permute-start(bf16[1,2,8,4,128]{4,3,2,1,0:T(4,128)(2,1)S(1)} %bitcast.16), channel_id=1, source_target_pairs={{0,2},{1,3},{2,0},{3,1},{4,6},{5,7},{6,4},{7,5},{8,10},{9,11},{10,... | collective-permute-start | bytes 49160 | tf_op jit(solution)/shard_map/ppermute | solution.py:623
  4.5 1.7 %collective-permute-done = bf16[1,2,8,4,128]{4,3,2,1,0:T(4,128)(2,1)S(1)} collective-permute-done((bf16[1,2,8,4,128]{4,3,2,1,0:T(4,128)(2,1)S(1)}, bf16[1,2,8,4,128]{4,3,2,1,0:T(4,128)(2,1)S(1)}, u32[]{:S(2)}, u32[]{:S(2)}) %collective-permute-start) | collective-permute-done | bytes 16416 | tf_op jit(solution)/shard_map/ppermute | solution.py:623
  6.2 2.1 %collective-permute-start.1 = (bf16[2,2,8,4,128]{4,3,2,1,0:T(4,128)(2,1)S(1)}, bf16[2,2,8,4,128]{4,3,2,1,0:T(4,128)(2,1)S(1)}, u32[]{:S(2)}, u32[]{:S(2)}) collective-permute-start(bf16[2,2,8,4,128]{4,3,2,1,0:T(4,128)(2,1)S(1)} %maximum_select_fusion.2), channel_id=1, source_target_pairs={{0,4},{1,5},{2,6},{3,7},{4,0},{5,1},{6,2},{7,3},{8,12},{9,13},{10,... | collective-permute-start | bytes 98312 | tf_op jit(solution)/shard_map/ppermute | solution.py:623
  8.3 1.6 %lhs2.1 = (bf16[64,144]{1,0:T(8,128)(2,1)S(1)}, bf16[384,768]{1,0:T(8,128)(2,1)S(1)}, bf16[36,64,128]{2,1,0:T(8,128)(2,1)S(1)}) custom-call(bf16[27,64,64]{2,1,0:T(8,128)(2,1)} %wb_hbm, bf16[3,27,64]{2,1,0:T(8,128)(2,1)} %bitcast.18), custom_call_target="tpu_custom_call" | custom-call | tf_op jit(solution)/shard_map/lhs2/pallas_call | solution.py:721
  9.9 0.3 collective-permute-done.1
  10.3 3.1 %collective-permute-start.2 = (bf16[4,2,8,4,128]{4,3,2,1,0:T(4,128)(2,1)S(1)}, bf16[4,2,8,4,128]{4,3,2,1,0:T(4,128)(2,1)S(1)}, u32[]{:S(2)}, u32[]{:S(2)}) collective-permute-start(bf16[4,2,8,4,128]{4,3,2,1,0:T(4,128)(2,1)S(1)} %maximum_select_fusion.1), channel_id=1, source_target_pairs={{0,8},{1,9},{2,10},{3,11},{4,12},{5,13},{6,14},{7,15},{8,0},{9,1},... | collective-permute-start | bytes 196616 | tf_op jit(solution)/shard_map/ppermute | solution.py:623
  13.4 1.6 %lhs3.1 = (bf16[384,768]{1,0:T(8,128)(2,1)S(1)}, bf16[36,64,128]{2,1,0:T(8,128)(2,1)S(1)}, f32[4,64,128]{2,1,0:T(8,128)S(1)}, s32[8]{0:T(128)S(4)}, f32[4]{0:T(128)S(4)}) custom-call(bf16[27,64,64]{2,1,0:T(8,128)(2,1)} %wc_hbm, f32[1,64]{1,0:T(1,128)} %bitcast.19, f32[1,64]{1,0:T(1,128)} %bitcast.20, f32[1,64]{1,0:T(1,128)} %bitcast.21, ...), custom_call_target="tpu_custom_call" | custom-call | tf_op jit(solution)/shard_map/lhs3/pallas_call | solution.py:736
  15.0 0.6 collective-permute-done.2
  16.5 0.7 %collective-permute-done.3.other_ref = bf16[8,2,8,4,128]{4,3,2,1,0:T(4,128)(2,1)S(1)} collective-permute-done((bf16[8,2,8,4,128]{4,3,2,1,0:T(4,128)(2,1)S(1)}, bf16[8,2,8,4,128]{4,3,2,1,0:T(4,128)(2,1)S(1)}, u32[]{:S(2)}, u32[]{:S(2)}) %collective-permute-start.3) | collective-permute-done | bytes 131104 | tf_op jit(solution)/shard_map/ppermute | solution.py:623
  17.2 9.7 %forward.1 = (f32[2,8,128]{2,1,0:T(8,128)}, f32[2,8,128]{2,1,0:T(8,128)S(1)}, f32[134,64,128]{2,1,0:T(8,128)S(1)}, bf16[180,64,128]{2,1,0:T(8,128)(2,1)S(1)}) custom-call(s32[8]{0:T(128)S(4)} %get-tuple-element.82.home_ref, f32[4]{0:T(128)S(4)} %get-tuple-element.83.invd_ref, f32[1]{0:T(128)S(6)} %copy.26.hb_ref, ...), custom_call_target="tpu_custom_call" | custom-call | tf_op jit(solution)/shard_map/forward/pallas_call | solution.py:792
  26.9 0.8 %collective-permute-start.5 = (f32[2,8,128]{2,1,0:T(8,128)S(1)}, f32[2,8,128]{2,1,0:T(8,128)S(1)}, u32[]{:S(2)}, u32[]{:S(2)}) collective-permute-start(f32[2,8,128]{2,1,0:T(8,128)S(1)} %get-tuple-element.92.score_ref.gm_ref), channel_id=1, source_target_pairs={{2,4},{4,2},{6,8},{8,6},{10,12},{12,10},{3,5},{5,3},{7,9},{9,7},{1... | collective-permute-start | bytes 24584 | tf_op jit(solution)/shard_map/ppermute | solution.py:827
  27.8 4.7 %collective-permute-start.6 = (f32[2,8,128]{2,1,0:T(8,128)S(1)}, f32[2,8,128]{2,1,0:T(8,128)S(1)}, u32[]{:S(2)}, u32[]{:S(2)}) collective-permute-start(f32[2,8,128]{2,1,0:T(8,128)S(1)} %get-tuple-element.92.score_ref.gm_ref), channel_id=1, source_target_pairs={{0,2},{2,0},{4,6},{6,4},{8,10},{10,8},{12,14},{14,12},{1,3},{3,1},... | collective-permute-start | bytes 24584 | tf_op jit(solution)/shard_map/ppermute | solution.py:828
  32.5 1.7 %early.1 = (f32[864,128]{1,0:T(8,128)S(1)}, f32[8,128]{1,0:T(8,128)S(1)}, bf16[720,2048]{1,0:T(8,128)(2,1)S(1)}) custom-call(f32[2,8,128]{2,1,0:T(8,128)S(1)} %get-tuple-element.92.score_ref.gm_ref, f32[134,64,128]{2,1,0:T(8,128)S(1)} %get-tuple-element.93.sbuf, bf16[180,64,128]{2,1,0:T(8,128)(2,1)S(1)} %get-tuple-element.94.hbuf, ...), custom_call_target="tpu_custom_call" | custom-call | tf_op jit(solution)/shard_map/early/pallas_call | solution.py:830
  34.2 0.6 collective-permute-start.7
  34.8 0.7 %collective-permute-done.7.p2o_ref = f32[2,8,128]{2,1,0:T(8,128)S(1)} collective-permute-done((f32[2,8,128]{2,1,0:T(8,128)S(1)}, f32[2,8,128]{2,1,0:T(8,128)S(1)}, u32[]{:S(2)}, u32[]{:S(2)}) %collective-permute-start.7) | collective-permute-done | bytes 8224 | tf_op jit(solution)/shard_map/ppermute | solution.py:623
  35.6 0.3 collective-permute-done.8.p1o_ref
  35.9 4.3 %backward.1 = (f32[904,128]{1,0:T(8,128)S(1)}, f32[904,128]{1,0:T(8,128)S(1)}) custom-call(f32[2,8,128]{2,1,0:T(8,128)S(1)} %get-tuple-element.92.score_ref.gm_ref, f32[2,8,128]{2,1,0:T(8,128)S(1)} %collective-permute-done.4.gmo_ref, f32[2,8,128]{2,1,0:T(8,128)S(1)} %collective-permute-done.5.p2_ref, f32[2,8,128]{2,1,0:T(8,128)S(1)} %collective-permute-done.7.p2o_ref, ...), custom_call_target="tpu_custom_call" | custom-call | tf_op jit(solution)/shard_map/backward/pallas_call | solution.py:851
  40.5 1.6 %collective-permute-done.9 = f32[904,128]{1,0:T(8,128)S(1)} collective-permute-done((f32[904,128]{1,0:T(8,128)S(1)}, f32[904,128]{1,0:T(8,128)S(1)}, u32[]{:S(2)}, u32[]{:S(2)}) %collective-permute-start.9) | collective-permute-done | bytes 462880 | tf_op jit(solution)/shard_map/ppermute | solution.py:623
  42.3 1.7 %collective-permute-start.10 = (bf16[464,128]{1,0:T(8,128)(2,1)S(1)}, bf16[464,128]{1,0:T(8,128)(2,1)S(1)}, u32[]{:S(2)}, u32[]{:S(2)}) collective-permute-start(bf16[464,128]{1,0:T(8,128)(2,1)S(1)} %pad_maximum_fusion), channel_id=1, source_target_pairs={{0,4},{1,5},{2,6},{3,7},{4,0},{5,1},{6,2},{7,3},{8,12},{9,13},{10,... | collective-permute-start | bytes 356360 | tf_op jit(solution)/shard_map/ppermute | solution.py:623
  44.0 3.7 %collective-permute-done.10 = bf16[464,128]{1,0:T(8,128)(2,1)S(1)} collective-permute-done((bf16[464,128]{1,0:T(8,128)(2,1)S(1)}, bf16[464,128]{1,0:T(8,128)(2,1)S(1)}, u32[]{:S(2)}, u32[]{:S(2)}) %collective-permute-start.10) | collective-permute-done | bytes 118816 | tf_op jit(solution)/shard_map/ppermute | solution.py:623
  47.8 1.8 %collective-permute-start.11 = (bf16[464,128]{1,0:T(8,128)(2,1)S(1)}, bf16[464,128]{1,0:T(8,128)(2,1)S(1)}, u32[]{:S(2)}, u32[]{:S(2)}) collective-permute-start(bf16[464,128]{1,0:T(8,128)(2,1)S(1)} %pad_maximum_fusion.1), channel_id=1, source_target_pairs={{0,2},{1,3},{2,0},{3,1},{4,6},{5,7},{6,4},{7,5},{8,10},{9,11},{10,... | collective-permute-start | bytes 356360 | tf_op jit(solution)/shard_map/ppermute | solution.py:623
  49.6 3.1 %collective-permute-done.11 = bf16[464,128]{1,0:T(8,128)(2,1)S(1)} collective-permute-done((bf16[464,128]{1,0:T(8,128)(2,1)S(1)}, bf16[464,128]{1,0:T(8,128)(2,1)S(1)}, u32[]{:S(2)}, u32[]{:S(2)}) %collective-permute-start.11) | collective-permute-done | bytes 118816 | tf_op jit(solution)/shard_map/ppermute | solution.py:623
  52.8 3.2 %collective-permute-start.12 = (bf16[464,128]{1,0:T(8,128)(2,1)S(1)}, bf16[464,128]{1,0:T(8,128)(2,1)S(1)}, u32[]{:S(2)}, u32[]{:S(2)}) collective-permute-start(bf16[464,128]{1,0:T(8,128)(2,1)S(1)} %pad_maximum_fusion.2), channel_id=1, source_target_pairs={{0,8},{1,9},{2,10},{3,11},{4,12},{5,13},{6,14},{7,15},{8,0},{9,1},... | collective-permute-start | bytes 356360 | tf_op jit(solution)/shard_map/ppermute | solution.py:623
  56.1 4.3 %collective-permute-done.12 = bf16[464,128]{1,0:T(8,128)(2,1)S(1)} collective-permute-done((bf16[464,128]{1,0:T(8,128)(2,1)S(1)}, bf16[464,128]{1,0:T(8,128)(2,1)S(1)}, u32[]{:S(2)}, u32[]{:S(2)}) %collective-permute-start.12) | collective-permute-done | bytes 118816 | tf_op jit(solution)/shard_map/ppermute | solution.py:623
  60.6 0.5 collective-permute-start.14
  61.1 0.5 slice.58
  61.9 1.1 %near.1 = (f32[27,64,64]{2,1,0:T(8,128)}, f32[27,64,64]{2,1,0:T(8,128)}, f32[2,64,64]{2,1,0:T(8,128)S(1)}) custom-call(bf16[448,128]{1,0:T(8,128)(2,1)S(1)} %fusion.mine_ref, bf16[448,128]{1,0:T(8,128)(2,1)S(1)} %collective-permute-done.13.far_ref), custom_call_target="tpu_custom_call" | custom-call | tf_op jit(solution)/shard_map/near/pallas_call | solution.py:877
  63.0 3.1 %collective-permute-done.14.mine_ref = bf16[448,128]{1,0:T(8,128)(2,1)S(1)} collective-permute-done((bf16[448,128]{1,0:T(8,128)(2,1)S(1)}, bf16[448,128]{1,0:T(8,128)(2,1)S(1)}, u32[]{:S(2)}, u32[]{:S(2)}) %collective-permute-start.14) | collective-permute-done | bytes 114720 | tf_op jit(solution)/shard_map/ppermute | solution.py:623
  66.1 0.6 slice_bitcast_fusion
  66.7 0.7 %collective-permute-done.15.far_ref = bf16[448,128]{1,0:T(8,128)(2,1)S(1)} collective-permute-done((bf16[448,128]{1,0:T(8,128)(2,1)S(1)}, bf16[448,128]{1,0:T(8,128)(2,1)S(1)}, u32[]{:S(2)}, u32[]{:S(2)}) %collective-permute-start.15) | collective-permute-done | bytes 114720 | tf_op jit(solution)/shard_map/ppermute | solution.py:623
  67.4 1.1 %finish.1 = (f32[27,64,64]{2,1,0:T(8,128)}, f32[27,64,64]{2,1,0:T(8,128)}, f32[3,27,64]{2,1,0:T(8,128)}) custom-call(bf16[448,128]{1,0:T(8,128)(2,1)S(1)} %collective-permute-done.14.mine_ref, bf16[448,128]{1,0:T(8,128)(2,1)S(1)} %collective-permute-done.15.far_ref, ...), custom_call_target="tpu_custom_call", output_to_operand_aliasing={{0}: (3, {}), {1}: (4, {})} | custom-call | tf_op jit(solution)/shard_map/finish/pallas_call | solution.py:888
  (31 shorter events, 1.4 us)
Async XLA Ops:
  1.4 4.8 %collective-permute-start = (bf16[1,2,8,4,128]{4,3,2,1,0:T(4,128)(2,1)S(1)}, bf16[1,2,8,4,128]{4,3,2,1,0:T(4,128)(2,1)S(1)}, u32[]{:S(2)}, u32[]{:S(2)}) collective-permute-start(bf16[1,2,8,4,128]{4,3,2,1,0:T(4,128)(2,1)S(1)} %bitcast.16), channel_id=1, source_target_pairs={{0,2},{1,3},{2,0},{3,1},{4,6},{5,7},{6,4},{7,5},{8,10},{9,11},{10,... | collective-permute-start | bytes 49160 | tf_op jit(solution)/shard_map/ppermute | solution.py:623
  6.2 4.0 %collective-permute-start.1 = (bf16[2,2,8,4,128]{4,3,2,1,0:T(4,128)(2,1)S(1)}, bf16[2,2,8,4,128]{4,3,2,1,0:T(4,128)(2,1)S(1)}, u32[]{:S(2)}, u32[]{:S(2)}) collective-permute-start(bf16[2,2,8,4,128]{4,3,2,1,0:T(4,128)(2,1)S(1)} %maximum_select_fusion.2), channel_id=1, source_target_pairs={{0,4},{1,5},{2,6},{3,7},{4,0},{5,1},{6,2},{7,3},{8,12},{9,13},{10,... | collective-permute-start | bytes 98312 | tf_op jit(solution)/shard_map/ppermute | solution.py:623
  10.3 5.3 %collective-permute-start.2 = (bf16[4,2,8,4,128]{4,3,2,1,0:T(4,128)(2,1)S(1)}, bf16[4,2,8,4,128]{4,3,2,1,0:T(4,128)(2,1)S(1)}, u32[]{:S(2)}, u32[]{:S(2)}) collective-permute-start(bf16[4,2,8,4,128]{4,3,2,1,0:T(4,128)(2,1)S(1)} %maximum_select_fusion.1), channel_id=1, source_target_pairs={{0,8},{1,9},{2,10},{3,11},{4,12},{5,13},{6,14},{7,15},{8,0},{9,1},... | collective-permute-start | bytes 196616 | tf_op jit(solution)/shard_map/ppermute | solution.py:623
  15.8 1.4 %collective-permute-start.3 = (bf16[8,2,8,4,128]{4,3,2,1,0:T(4,128)(2,1)S(1)}, bf16[8,2,8,4,128]{4,3,2,1,0:T(4,128)(2,1)S(1)}, u32[]{:S(2)}, u32[]{:S(2)}) collective-permute-start(bf16[8,2,8,4,128]{4,3,2,1,0:T(4,128)(2,1)S(1)} %maximum_select_fusion.mine_ref), channel_id=1, source_target_pairs={{0,1},{1,0},{2,3},{3,2},{4,5},{5,4},{6,7},{7,6},{8,9},{9,8},{10,11... | collective-permute-start | bytes 393224 | tf_op jit(solution)/shard_map/ppermute | solution.py:623
  26.9 7.2 %collective-permute-start.5 = (f32[2,8,128]{2,1,0:T(8,128)S(1)}, f32[2,8,128]{2,1,0:T(8,128)S(1)}, u32[]{:S(2)}, u32[]{:S(2)}) collective-permute-start(f32[2,8,128]{2,1,0:T(8,128)S(1)} %get-tuple-element.92.score_ref.gm_ref), channel_id=1, source_target_pairs={{2,4},{4,2},{6,8},{8,6},{10,12},{12,10},{3,5},{5,3},{7,9},{9,7},{1... | collective-permute-start | bytes 24584 | tf_op jit(solution)/shard_map/ppermute | solution.py:827
  27.8 6.4 %collective-permute-start.6 = (f32[2,8,128]{2,1,0:T(8,128)S(1)}, f32[2,8,128]{2,1,0:T(8,128)S(1)}, u32[]{:S(2)}, u32[]{:S(2)}) collective-permute-start(f32[2,8,128]{2,1,0:T(8,128)S(1)} %get-tuple-element.92.score_ref.gm_ref), channel_id=1, source_target_pairs={{0,2},{2,0},{4,6},{6,4},{8,10},{10,8},{12,14},{14,12},{1,3},{3,1},... | collective-permute-start | bytes 24584 | tf_op jit(solution)/shard_map/ppermute | solution.py:828
  32.5 2.4 %collective-permute-start.4 = (f32[2,8,128]{2,1,0:T(8,128)S(1)}, f32[2,8,128]{2,1,0:T(8,128)S(1)}, u32[]{:S(2)}, u32[]{:S(2)}) collective-permute-start(f32[2,8,128]{2,1,0:T(8,128)S(1)} %get-tuple-element.92.score_ref.gm_ref), channel_id=1, source_target_pairs={{0,1},{1,0},{2,3},{3,2},{4,5},{5,4},{6,7},{7,6},{8,9},{9,8},{10,11... | collective-permute-start | bytes 24584 | tf_op jit(solution)/shard_map/ppermute | solution.py:623
  34.2 1.4 %collective-permute-start.7 = (f32[2,8,128]{2,1,0:T(8,128)S(1)}, f32[2,8,128]{2,1,0:T(8,128)S(1)}, u32[]{:S(2)}, u32[]{:S(2)}) collective-permute-start(f32[2,8,128]{2,1,0:T(8,128)S(1)} %collective-permute-done.5.p2_ref), channel_id=1, source_target_pairs={{0,1},{1,0},{2,3},{3,2},{4,5},{5,4},{6,7},{7,6},{8,9},{9,8},{10,11... | collective-permute-start | bytes 24584 | tf_op jit(solution)/shard_map/ppermute | solution.py:623
  34.7 1.2 %collective-permute-start.8 = (f32[2,8,128]{2,1,0:T(8,128)S(1)}, f32[2,8,128]{2,1,0:T(8,128)S(1)}, u32[]{:S(2)}, u32[]{:S(2)}) collective-permute-start(f32[2,8,128]{2,1,0:T(8,128)S(1)} %collective-permute-done.6.p1_ref), channel_id=1, source_target_pairs={{0,1},{1,0},{2,3},{3,2},{4,5},{5,4},{6,7},{7,6},{8,9},{9,8},{10,11... | collective-permute-start | bytes 24584 | tf_op jit(solution)/shard_map/ppermute | solution.py:623
  40.2 1.9 %collective-permute-start.9 = (f32[904,128]{1,0:T(8,128)S(1)}, f32[904,128]{1,0:T(8,128)S(1)}, u32[]{:S(2)}, u32[]{:S(2)}) collective-permute-start(f32[904,128]{1,0:T(8,128)S(1)} %get-tuple-element.104), channel_id=1, source_target_pairs={{0,1},{1,0},{2,3},{3,2},{4,5},{5,4},{6,7},{7,6},{8,9},{9,8},{10,11... | collective-permute-start | bytes 1388552 | tf_op jit(solution)/shard_map/ppermute | solution.py:623
  42.3 5.4 %collective-permute-start.10 = (bf16[464,128]{1,0:T(8,128)(2,1)S(1)}, bf16[464,128]{1,0:T(8,128)(2,1)S(1)}, u32[]{:S(2)}, u32[]{:S(2)}) collective-permute-start(bf16[464,128]{1,0:T(8,128)(2,1)S(1)} %pad_maximum_fusion), channel_id=1, source_target_pairs={{0,4},{1,5},{2,6},{3,7},{4,0},{5,1},{6,2},{7,3},{8,12},{9,13},{10,... | collective-permute-start | bytes 356360 | tf_op jit(solution)/shard_map/ppermute | solution.py:623
  47.8 4.9 %collective-permute-start.11 = (bf16[464,128]{1,0:T(8,128)(2,1)S(1)}, bf16[464,128]{1,0:T(8,128)(2,1)S(1)}, u32[]{:S(2)}, u32[]{:S(2)}) collective-permute-start(bf16[464,128]{1,0:T(8,128)(2,1)S(1)} %pad_maximum_fusion.1), channel_id=1, source_target_pairs={{0,2},{1,3},{2,0},{3,1},{4,6},{5,7},{6,4},{7,5},{8,10},{9,11},{10,... | collective-permute-start | bytes 356360 | tf_op jit(solution)/shard_map/ppermute | solution.py:623
  52.8 7.6 %collective-permute-start.12 = (bf16[464,128]{1,0:T(8,128)(2,1)S(1)}, bf16[464,128]{1,0:T(8,128)(2,1)S(1)}, u32[]{:S(2)}, u32[]{:S(2)}) collective-permute-start(bf16[464,128]{1,0:T(8,128)(2,1)S(1)} %pad_maximum_fusion.2), channel_id=1, source_target_pairs={{0,8},{1,9},{2,10},{3,11},{4,12},{5,13},{6,14},{7,15},{8,0},{9,1},... | collective-permute-start | bytes 356360 | tf_op jit(solution)/shard_map/ppermute | solution.py:623
  60.5 1.4 %collective-permute-start.13 = (bf16[448,128]{1,0:T(8,128)(2,1)S(1)}, bf16[448,128]{1,0:T(8,128)(2,1)S(1)}, u32[]{:S(2)}, u32[]{:S(2)}) collective-permute-start(bf16[448,128]{1,0:T(8,128)(2,1)S(1)} %fusion.mine_ref), channel_id=1, source_target_pairs={{0,1},{1,0},{2,3},{3,2},{4,5},{5,4},{6,7},{7,6},{8,9},{9,8},{10,11... | collective-permute-start | bytes 344072 | tf_op jit(solution)/shard_map/ppermute | solution.py:623
  60.6 5.6 %collective-permute-start.14 = (bf16[448,128]{1,0:T(8,128)(2,1)S(1)}, bf16[448,128]{1,0:T(8,128)(2,1)S(1)}, u32[]{:S(2)}, u32[]{:S(2)}) collective-permute-start(bf16[448,128]{1,0:T(8,128)(2,1)S(1)} %fusion.mine_ref), channel_id=1, source_target_pairs={{0,4},{1,5},{2,6},{3,7},{4,0},{5,1},{6,2},{7,3},{8,12},{9,13},{10,... | collective-permute-start | bytes 344072 | tf_op jit(solution)/shard_map/ppermute | solution.py:623
  66.1 1.3 %collective-permute-start.15 = (bf16[448,128]{1,0:T(8,128)(2,1)S(1)}, bf16[448,128]{1,0:T(8,128)(2,1)S(1)}, u32[]{:S(2)}, u32[]{:S(2)}) collective-permute-start(bf16[448,128]{1,0:T(8,128)(2,1)S(1)} %collective-permute-done.14.mine_ref), channel_id=1, source_target_pairs={{0,1},{1,0},{2,3},{3,2},{4,5},{5,4},{6,7},{7,6},{8,9},{9,8},{10,11... | collective-permute-start | bytes 344072 | tf_op jit(solution)/shard_map/ppermute | solution.py:623
